TPU v7x, 128 devices: a whole 4x4x4 slice. The times are simulated.
128 devices in a mesh: seq: 16 (over x_hi, z, core), head: 8 (over y, x_lo).
Axes of the slice: x: 4 (x_hi: 2, x_lo: 2; x = x_hi * 2 + x_lo), y: 4, z: 4, core: 2. Of those that a mesh axis runs over, the one named last changes fastest.
Arguments:
- grid_state: bfloat16 [131072, 1024], P('seq', 'head'), may hold values from -6 to 6
- encode_index: int32 [256, 8], P('seq'), may hold values from 0 to 1023, as said below
- encode_weights: bfloat16 [256, 8, 128, 128], P('seq'), may hold values from -0.1875 to 0.1875
- first_gain: float32 [1024], replicated, may hold values from 0.1 to 1.9
- project_in: bfloat16 [1024, 3, 1024], P(None, None, 'head'), may hold values from -8 to 8
- project_out: bfloat16 [1024, 1024], P('head'), may hold values from -0.25 to 0.25
- second_gain: float32 [1024], replicated, may hold values from 0.1 to 1.9
- expand_weights: bfloat16 [1024, 4096], P(None, 'head'), may hold values from -0.1875 to 0.1875
- shrink_weights: bfloat16 [4096, 1024], P('head'), may hold values from -0.125 to 0.125
- decode_index: int32 [1024, 2], P('seq'), may hold values from 0 to 255, as said below
- decode_weights: bfloat16 [1024, 2, 128, 128], P('seq'), may hold values from -0.375 to 0.375
- output_gain: float32 [1024], P('head'), may hold values from 0.1 to 1.9
Outputs:
- grid_output: bfloat16 [131072, 1024], P('seq', 'head')
Inputs may be any that keep to these rules, and one draw needn't show every extreme that they name: `encode_index`: for a mesh block of band b (blocks b * 16 onward), every entry lies in b * 64 - 2048 / 128 to (b + 1) * 64 + 2048 / 128 - 1. `decode_index`: for a grid block of band b (blocks b * 64 onward), every entry lies in b * 16 - 2048 / 256 to (b + 1) * 16 + 2048 / 256 - 1, with the division rounded down.
All inputs are finite; a program needn't handle non-finite values.
Results may differ from a plain program's by a relative error of at most 0.012.
Values may be sent and summed in bfloat16 or wider, within the bound.
No kernel may reach another device: no remote copies, remote signals or barrier semaphores. Data moves between devices by JAX's collectives and lax.ppermute only.
A program may use at most 128 MiB of HBM per device.

v0:
```python
import jax
import jax.numpy as jnp
from jax import lax
from jax.sharding import Mesh
from jax.sharding import PartitionSpec as P

D = 1024
HEAD_DIM = 64
WINDOW = 1120
HEAD = ("head_0", "head_1")


EPSILON = 1e-05


def padded(cells, sides, width):
    for axis, dim in sides:
        count = lax.axis_size(axis)
        ends = count - 1
        head = lax.slice_in_dim(cells, 0, width, axis=dim)
        tail = lax.slice_in_dim(cells, cells.shape[dim] - width, cells.shape[dim], axis=dim)
        cells = jnp.concatenate(
            [
                lax.ppermute(tail, axis, [(i, (i + 1) % count) for i in range(ends)]),
                cells,
                lax.ppermute(head, axis, [((i + 1) % count, i) for i in range(ends)]),
            ],
            axis=dim,
        )
    return cells


def gather_axes(value, axes, dim):
    for axis in reversed(axes):
        value = lax.all_gather(value, axis, axis=dim, tiled=True)
    return value


def passed_along(value, axis, by):
    devices = lax.axis_size(axis)
    pairs = [(i, i + by) for i in range(devices) if 0 <= i + by < devices]
    return lax.ppermute(value, axis, pairs)


def laid_out(pieces, dim):
    lengths = list(pieces.shape[1:])
    lengths[dim] *= pieces.shape[0]
    return jnp.moveaxis(pieces, 0, dim).reshape(lengths)


def copy_for_each(value, axis):
    copies = jnp.broadcast_to(value, (lax.axis_size(axis), *value.shape))
    return lax.all_to_all(copies, axis, split_axis=0, concat_axis=0, tiled=True)


def collect(value, axis, dim):
    return laid_out(copy_for_each(value, axis), dim)


def scatter_axes(value, axes, dim):
    for axis in axes:
        value = lax.psum_scatter(value, axis, scatter_dimension=dim, tiled=True)
    return value


def of_everyone(value, axis):
    return copy_for_each(value, axis).astype(jnp.float32).sum(axis=0)


def layer_norm(values, scales):
    average = jnp.mean(values, axis=1, keepdims=True)
    centred = values - average
    spread = jnp.mean(centred * centred, axis=1, keepdims=True)
    return centred * lax.rsqrt(spread + EPSILON) * scales


def interpolate(source, index_table, offset, weight_table):
    columns = source.shape[1]
    block_rows = weight_table.shape[2]
    blocks = source.reshape(-1, block_rows, columns)
    picked = jnp.take(blocks, index_table - offset, axis=0)
    summed = jnp.einsum("bkij,bkjc->bic", weight_table, picked, preferred_element_type=jnp.float32)
    return summed.reshape(-1, columns)


def window_mask(query_rows, key_count, key_anchor, total_rows):
    query_iota = lax.broadcasted_iota(jnp.int32, (query_rows, key_count), 0)
    key_iota = lax.broadcasted_iota(jnp.int32, (query_rows, key_count), 1)
    distance = key_iota - query_iota
    global_key = key_anchor + key_iota
    return (
        (distance >= 0) & (distance <= 2 * WINDOW) & (global_key >= 0) & (global_key < total_rows)
    )


def softmax_values(scores, allowed, value_block):
    masked = jnp.where(allowed[None], scores, -1e30)
    highest = jnp.max(masked, axis=2, keepdims=True)
    powers = jnp.where(allowed[None], jnp.exp(masked - highest), 0.0)
    probs = (powers / jnp.sum(powers, axis=2, keepdims=True)).astype(jnp.bfloat16)
    context = jnp.einsum("hqk,khd->qhd", probs, value_block, preferred_element_type=jnp.float32)
    return context.astype(jnp.bfloat16)


def on_device(
    grid_state,
    encode_index,
    encode_weights,
    first_gain,
    project_in,
    project_out,
    second_gain,
    expand_weights,
    shrink_weights,
    decode_index,
    decode_weights,
    output_gain,
):
    band_number = lax.axis_index("seq")
    band_count = lax.axis_size("seq")
    head_number = lax.axis_index(HEAD)
    head_count = lax.axis_size(HEAD)
    block_rows = encode_weights.shape[2]
    mesh_blocks = encode_weights.shape[0]
    mesh_rows = mesh_blocks * block_rows
    grid_rows = grid_state.shape[0]
    grid_blocks = grid_rows // block_rows
    columns = grid_state.shape[1]
    heads_here = columns // HEAD_DIM
    mesh_rim = mesh_blocks // 2
    grid_wide = padded(grid_state, (("seq", 0),), mesh_blocks * block_rows)
    mesh_start = interpolate(
        grid_wide, encode_index, band_number * grid_blocks - mesh_blocks, encode_weights
    ).astype(jnp.bfloat16)
    whole_start = gather_axes(mesh_start, HEAD, 1)
    first_norm = layer_norm(whole_start.astype(jnp.float32), first_gain).astype(jnp.bfloat16)
    projected = jnp.dot(
        first_norm,
        project_in.reshape(project_in.shape[0], 3 * columns),
        preferred_element_type=jnp.float32,
    ).astype(jnp.bfloat16)
    queries = projected[:, :columns]
    keys_values = projected[:, columns:]
    below_parts = []
    above_parts = []
    rows_needed = min(mesh_rows, WINDOW)
    lower_piece = passed_along(keys_values[mesh_rows - rows_needed :], "seq", 1)
    upper_piece = passed_along(keys_values[:rows_needed], "seq", -1)
    below_parts = [lower_piece] + below_parts
    above_parts = above_parts + [upper_piece]
    extended = jnp.concatenate(below_parts + [keys_values] + above_parts, axis=0)
    query_rows = min(512, mesh_rows)
    key_count = query_rows + 2 * WINDOW
    total_rows = mesh_rows * band_count

    def attend(first_row):
        query_block = lax.dynamic_slice_in_dim(queries, first_row, query_rows, 0).reshape(
            query_rows, heads_here, HEAD_DIM
        )
        key_block = lax.dynamic_slice_in_dim(extended, first_row, key_count, 0)
        key_part = key_block[:, :columns].reshape(key_count, heads_here, HEAD_DIM)
        value_part = key_block[:, columns:].reshape(key_count, heads_here, HEAD_DIM)
        scores = jnp.einsum(
            "qhd,khd->hqk", query_block, key_part, preferred_element_type=jnp.float32
        ) * HEAD_DIM ** (-0.5)
        allowed = window_mask(
            query_rows, key_count, band_number * mesh_rows - WINDOW + first_row, total_rows
        )
        return softmax_values(scores, allowed, value_part)

    starts = jnp.arange(mesh_rows // query_rows, dtype=jnp.int32) * query_rows
    context = lax.map(attend, starts).reshape(mesh_rows, columns)
    share_rows = mesh_rows // head_count
    context_share = lax.all_to_all(context, HEAD, split_axis=0, concat_axis=1, tiled=True)
    attended = jnp.dot(
        context_share, collect(project_out, HEAD, 0), preferred_element_type=jnp.float32
    )
    start_share = lax.dynamic_slice_in_dim(whole_start, head_number * share_rows, share_rows, 0)
    middle_share = (start_share.astype(jnp.float32) + attended).astype(jnp.bfloat16)
    whole_middle = gather_axes(middle_share, HEAD, 0)
    mesh_middle = lax.dynamic_slice_in_dim(whole_middle, head_number * columns, columns, 1)
    second_norm = layer_norm(whole_middle.astype(jnp.float32), second_gain).astype(jnp.bfloat16)
    hidden = jax.nn.gelu(
        jnp.dot(second_norm, expand_weights, preferred_element_type=jnp.float32)
    ).astype(jnp.bfloat16)
    shrunk = jnp.dot(hidden, shrink_weights, preferred_element_type=jnp.float32)
    shrunk_part = scatter_axes(shrunk.astype(jnp.bfloat16), HEAD, 1).astype(jnp.float32)
    mesh_end = (mesh_middle.astype(jnp.float32) + shrunk_part).astype(jnp.bfloat16)
    mesh_wide = padded(mesh_end, (("seq", 0),), mesh_rim * block_rows)
    back = interpolate(
        mesh_wide, decode_index, band_number * mesh_blocks - mesh_rim, decode_weights
    )
    row_sums, square_sums = (
        of_everyone(jnp.sum(back, axis=1).astype(jnp.bfloat16), HEAD).astype(jnp.float32),
        of_everyone(jnp.sum(back * back, axis=1).astype(jnp.bfloat16), HEAD).astype(jnp.float32),
    )
    average = (row_sums / D)[:, None]
    squares = (square_sums / D)[:, None]
    normed = (back - average) * lax.rsqrt(squares - average * average + EPSILON) * output_gain
    return (grid_state.astype(jnp.float32) + normed).astype(jnp.bfloat16)


def solution(mesh):
    finer = Mesh(mesh.devices.reshape(mesh.shape["seq"], 4, 2), ("seq", "head_0", "head_1"))
    in_specs = (
        P("seq", HEAD),
        P("seq", None),
        P("seq", None, None, None),
        P(),
        P(None, None, HEAD),
        P(HEAD, None),
        P(),
        P(None, HEAD),
        P(HEAD, None),
        P("seq", None),
        P("seq", None, None, None),
        P(HEAD),
    )
    out_specs = P("seq", HEAD)
    return jax.shard_map(
        on_device, mesh=finer, in_specs=in_specs, out_specs=out_specs, check_vma=False
    )
```

profile of v0, /device:TPU:97, one launch (start us, length us, event | category | flops | bytes accessed | tf_op | source)
XLA Modules:
  0.0 508.5 jit_solution(5309884476454887407)
XLA Ops:
  7.9 3.8 collective-permute-start
  14.6 3.2 collective-permute-done
  17.9 8.0 %collective-permute-done.1 = bf16[2048,128]{1,0:T(8,128)(2,1)S(1)} collective-permute-done((bf16[2048,128]{1,0:T(8,128)(2,1)S(1)}, bf16[2048,128]{1,0:T(8,128)(2,1)S(1)}, u32[]{:S(2)}, u32[]{:S(2)}) %collective-permute-start.1) | collective-permute-done | bytes 524320 | tf_op jit(solution)/shard_map/ppermute | solution.py:26
  25.9 10.6 %pad_maximum_fusion = bf16[12288,128]{1,0:T(8,128)(2,1)} fusion(bf16[2048,128]{1,0:T(8,128)(2,1)S(1)} %collective-permute-done.1, bf16[8192,128]{1,0:T(8,128)(2,1)} %param.14, bf16[2048,128]{1,0:T(8,128)(2,1)S(1)} %collective-permute-done), kind=kLoop, calls=%fused_computation.74 | loop fusion | flops 9437184 | bytes 6291456 | tf_op jit(solution)/shard_map/concatenate | solution.py:22
  36.5 4.9 gather_fusion
  41.4 5.7 %fusion.70 = bf16[16,128,128]{1,2,0:T(8,128)(2,1)} fusion(bf16[16,8,128,128]{3,2,1,0:T(8,128)(2,1)} %param.16, bf16[16,8,128,128]{3,2,1,0:T(8,128)(2,1)} %bitcast.90, pred[16,8]{1,0:T(8,128)(4,1)S(1)} %copy.59), kind=kOutput, calls=%fused_computation.82 | convolution fusion | flops 539230208 | bytes 8913024 | tf_op jit(solution)/shard_map/bkij,bkjc->bic/dot_general | solution.py:82
  47.2 22.2 %all-gather.5.cloned.1.call-done = bf16[2048,256]{1,0:T(8,128)(2,1)} async-done(((bf16[2048,128]{1,0:T(8,128)(2,1)}), bf16[2048,256]{1,0:T(8,128)(2,1)}) %all-gather.5.cloned.1.call-update) | async-done | bytes 1048592 | tf_op jit(solution)/shard_map/all_gather | solution.py:35
  69.7 53.5 %all-gather.7.cloned.1.call-done = bf16[2048,1024]{1,0:T(8,128)(2,1)} async-done(((bf16[2048,256]{1,0:T(8,128)(2,1)}), bf16[2048,1024]{1,0:T(8,128)(2,1)}) %all-gather.7.cloned.1.call-update) | async-done | bytes 4194320 | tf_op jit(solution)/shard_map/all_gather | solution.py:35
  123.2 3.0 convert_reduce_fusion.1
  128.1 2.6 fusion.59
  131.8 5.7 %collective-permute-start.2 = (bf16[1120,256]{1,0:T(8,128)(2,1)}, bf16[1120,256]{1,0:T(8,128)(2,1)}, u32[]{:S(2)}, u32[]{:S(2)}) collective-permute-start(bf16[1120,256]{1,0:T(8,128)(2,1)} %get-tuple-element.142), channel_id=1, source_target_pairs={{0,8},{8,16},{16,24},{24,32},{32,40},{40,48},{48,56},{56,64},{64,7... | collective-permute-start | bytes 1720328 | tf_op jit(solution)/shard_map/ppermute | solution.py:42
  137.5 1.9 collective-permute-start.3
  141.1 4.5 all-to-all-start.1
  145.8 11.1 %collective-permute-done.3 = bf16[1120,256]{1,0:T(8,128)(2,1)} collective-permute-done((bf16[1120,256]{1,0:T(8,128)(2,1)}, bf16[1120,256]{1,0:T(8,128)(2,1)}, u32[]{:S(2)}, u32[]{:S(2)}) %collective-permute-start.3) | collective-permute-done | bytes 573472 | tf_op jit(solution)/shard_map/ppermute | solution.py:42
  156.9 2.7 pad_maximum_fusion.1
  159.6 108.3 %while.12 = (s32[]{:T(128)}, bf16[4,512,2,64]{1,3,2,0:T(8,128)(2,1)}, s32[4]{0:T(128)S(1)}, bf16[4288,256]{1,0:T(8,128)(2,1)}, s32[]{:T(128)}, /*index=5*/bf16[2...) while((s32[]{:T(128)}, bf16[4,512,2,64]{1,3,2,0:T(8,128)(2,1)}, ...), condition=%wide.region_5.6_spmd, body=%wide.region_2.0_spmd.sunk | while | flops 749677312 | bytes 37408276 | solution.py:172
  166.8 2.5 fusion.109
  169.3 11.1 %fusion.110 = (f32[2,512]{1,0:T(2,128)S(1)}, f32[2,512,2752]{1,2,0:T(8,128)}) fusion(pred[512,2752]{0,1:T(8,128)(4,1)S(1)} %fusion.109, bf16[512,2,64]{0,2,1:T(8,128)(2,1)S(1)} %bitcast.93, bf16[2752,2,64]{0,2,1:T(8,128)(2,1)} %bitcast.87), kind=kOutput, calls=%fused_computation.110.clone.1 | convolution fusion | flops 374803136 | bytes 13520896 | tf_op jit(solution)/shard_map/while/body/eval_jaxpr/sub | solution.py:99
  180.6 6.0 %fusion.111 = bf16[4,512,2,64]{1,3,2,0:T(8,128)(2,1)} fusion(bf16[4,512,2,64]{1,3,2,0:T(8,128)(2,1)} %get-tuple-element.210, s32[]{:T(128)} %get-tuple-element.209, bf16[2752,2,64]{0,2,1:T(8,128)(2,1)S(1)} %bitcast.88, f32[2,512,2752]{1,2,0:T(8,128)} %get-tuple-element.196, f32[2,512]{1,0:T(2,128)S(1)} %get-tuple-element.197), kind=kOutput, calls=%fused_computation.20.clone.1 | convolution fusion | flops 366411776 | bytes 12112384 | tf_op jit(solution)/shard_map/while/body/eval_jaxpr/hqk,khd->qhd/dot_general | solution.py:101
  193.8 2.5 fusion.109
  196.3 11.1 %fusion.110 = (f32[2,512]{1,0:T(2,128)S(1)}, f32[2,512,2752]{1,2,0:T(8,128)}) fusion(pred[512,2752]{0,1:T(8,128)(4,1)S(1)} %fusion.109, bf16[512,2,64]{0,2,1:T(8,128)(2,1)S(1)} %bitcast.93, bf16[2752,2,64]{0,2,1:T(8,128)(2,1)} %bitcast.87), kind=kOutput, calls=%fused_computation.110.clone.1 | convolution fusion | flops 374803136 | bytes 13520896 | tf_op jit(solution)/shard_map/while/body/eval_jaxpr/sub | solution.py:99
  207.7 6.0 %fusion.111 = bf16[4,512,2,64]{1,3,2,0:T(8,128)(2,1)} fusion(bf16[4,512,2,64]{1,3,2,0:T(8,128)(2,1)} %get-tuple-element.210, s32[]{:T(128)} %get-tuple-element.209, bf16[2752,2,64]{0,2,1:T(8,128)(2,1)S(1)} %bitcast.88, f32[2,512,2752]{1,2,0:T(8,128)} %get-tuple-element.196, f32[2,512]{1,0:T(2,128)S(1)} %get-tuple-element.197), kind=kOutput, calls=%fused_computation.20.clone.1 | convolution fusion | flops 366411776 | bytes 12112384 | tf_op jit(solution)/shard_map/while/body/eval_jaxpr/hqk,khd->qhd/dot_general | solution.py:101
  220.9 2.5 fusion.109
  223.4 11.1 %fusion.110 = (f32[2,512]{1,0:T(2,128)S(1)}, f32[2,512,2752]{1,2,0:T(8,128)}) fusion(pred[512,2752]{0,1:T(8,128)(4,1)S(1)} %fusion.109, bf16[512,2,64]{0,2,1:T(8,128)(2,1)S(1)} %bitcast.93, bf16[2752,2,64]{0,2,1:T(8,128)(2,1)} %bitcast.87), kind=kOutput, calls=%fused_computation.110.clone.1 | convolution fusion | flops 374803136 | bytes 13520896 | tf_op jit(solution)/shard_map/while/body/eval_jaxpr/sub | solution.py:99
  234.8 6.0 %fusion.111 = bf16[4,512,2,64]{1,3,2,0:T(8,128)(2,1)} fusion(bf16[4,512,2,64]{1,3,2,0:T(8,128)(2,1)} %get-tuple-element.210, s32[]{:T(128)} %get-tuple-element.209, bf16[2752,2,64]{0,2,1:T(8,128)(2,1)S(1)} %bitcast.88, f32[2,512,2752]{1,2,0:T(8,128)} %get-tuple-element.196, f32[2,512]{1,0:T(2,128)S(1)} %get-tuple-element.197), kind=kOutput, calls=%fused_computation.20.clone.1 | convolution fusion | flops 366411776 | bytes 12112384 | tf_op jit(solution)/shard_map/while/body/eval_jaxpr/hqk,khd->qhd/dot_general | solution.py:101
  248.0 2.5 fusion.109
  250.5 11.1 %fusion.110 = (f32[2,512]{1,0:T(2,128)S(1)}, f32[2,512,2752]{1,2,0:T(8,128)}) fusion(pred[512,2752]{0,1:T(8,128)(4,1)S(1)} %fusion.109, bf16[512,2,64]{0,2,1:T(8,128)(2,1)S(1)} %bitcast.93, bf16[2752,2,64]{0,2,1:T(8,128)(2,1)} %bitcast.87), kind=kOutput, calls=%fused_computation.110.clone.1 | convolution fusion | flops 374803136 | bytes 13520896 | tf_op jit(solution)/shard_map/while/body/eval_jaxpr/sub | solution.py:99
  261.9 6.0 %fusion.111 = bf16[4,512,2,64]{1,3,2,0:T(8,128)(2,1)} fusion(bf16[4,512,2,64]{1,3,2,0:T(8,128)(2,1)} %get-tuple-element.210, s32[]{:T(128)} %get-tuple-element.209, bf16[2752,2,64]{0,2,1:T(8,128)(2,1)S(1)} %bitcast.88, f32[2,512,2752]{1,2,0:T(8,128)} %get-tuple-element.196, f32[2,512]{1,0:T(2,128)S(1)} %get-tuple-element.197), kind=kOutput, calls=%fused_computation.20.clone.1 | convolution fusion | flops 366411776 | bytes 12112384 | tf_op jit(solution)/shard_map/while/body/eval_jaxpr/hqk,khd->qhd/dot_general | solution.py:101
  267.9 2.3 copy.71
  271.5 3.5 all-to-all-start
  275.1 7.4 %all-to-all-done = bf16[8,256,128]{2,1,0:T(8,128)(2,1)S(1)} async-done(((bf16[8,256,128]{2,1,0:T(8,128)(2,1)}), bf16[8,256,128]{2,1,0:T(8,128)(2,1)S(1)}, u32[]{:S(2)}, u32[]{:S(2)}) %all-to-all-start) | async-done | bytes 524320 | tf_op jit(solution)/shard_map/all_to_all | solution.py:174
  282.5 3.2 fusion.73
  285.7 20.5 %all-gather.9.cloned.1.call-done = bf16[512,1024]{1,0:T(8,128)(2,1)} async-done(((bf16[256,1024]{1,0:T(8,128)(2,1)}), bf16[512,1024]{1,0:T(8,128)(2,1)}) %all-gather.9.cloned.1.call-update) | async-done | bytes 1048592 | tf_op jit(solution)/shard_map/all_gather | solution.py:35
  306.5 50.5 %all-gather.11.cloned.1.call-done = bf16[2048,1024]{1,0:T(8,128)(2,1)} async-done(((bf16[512,1024]{1,0:T(8,128)(2,1)}), bf16[2048,1024]{1,0:T(8,128)(2,1)}) %all-gather.11.cloned.1.call-update) | async-done | bytes 4194320 | tf_op jit(solution)/shard_map/all_gather | solution.py:35
  357.0 3.0 convert_reduce_fusion
  361.9 8.3 %convolution_convert_fusion = bf16[2048,1024]{1,0:T(8,128)(2,1)} fusion(bf16[512,1024]{1,0:T(8,128)(2,1)S(1)} %copy-done, bf16[1024,512]{1,0:T(8,128)(2,1)S(1)} %copy-done.9, bf16[2048,1024]{1,0:T(8,128)(2,1)} %all-gather.11.cloned.1.call-done, f32[1024]{0:T(1024)S(1)} %copy-done.11, f32[2048]{0:T(1024)S(1)} %add_rsqrt_fusion.1, ...), kind=kOutput, calls=%fused_computation.73 | convolution fusion | flops 4316987392 | bytes 10506240 | tf_op jit(solution)/shard_map/dot_general | solution.py:186
  370.2 47.3 %reduce-scatter.5.cloned.1.call-done = bf16[2048,256]{1,0:T(8,128)(2,1)} async-done(((bf16[2048,1024]{1,0:T(8,128)(2,1)}), bf16[2048,256]{1,0:T(8,128)(2,1)}) %reduce-scatter.5.cloned.1.call-update) | async-done | bytes 1048592 | tf_op jit(solution)/shard_map/reduce_scatter | solution.py:62
  417.5 2.3 copy.72
  419.8 22.6 %reduce-scatter.7.cloned.1.call-done = bf16[128,2048]{1,0:T(8,128)(2,1)} async-done(((bf16[256,2048]{1,0:T(8,128)(2,1)}), bf16[128,2048]{1,0:T(8,128)(2,1)}) %reduce-scatter.7.cloned.1.call-update) | async-done | bytes 524304
  445.0 4.6 collective-permute-start.4
  452.9 8.0 %collective-permute-done.5 = bf16[1024,128]{1,0:T(8,128)(2,1)S(1)} collective-permute-done((bf16[1024,128]{1,0:T(8,128)(2,1)S(1)}, bf16[1024,128]{1,0:T(8,128)(2,1)S(1)}, u32[]{:S(2)}, u32[]{:S(2)}) %collective-permute-start.5) | collective-permute-done | bytes 262176 | tf_op jit(solution)/shard_map/ppermute | solution.py:26
  461.0 3.1 gather_fusion.1
  464.1 6.8 %bitcast_reduce_fusion = (bf16[64,128]{1,0:T(8,128)(2,1)S(1)}, bf16[64,128]{1,0:T(8,128)(2,1)S(1)}, f32[64,128,128,1]{1,2,3,0:T(8,128)}) fusion(bf16[64,2,128,128]{3,2,1,0:T(8,128)(2,1)} %param.24, bf16[64,2,128,128]{3,2,1,0:T(8,128)(2,1)} %bitcast.91, pred[64,2]{1,0:T(8,128)(4,1)S(1)} %copy.58), kind=kOutput, calls=%fused_computation.58 | convolution fusion | flops 542097408 | bytes 12615808 | tf_op jit(solution)/shard_map/bkij,bkjc->bic/dot_general | solution.py:82
  473.7 4.0 all-to-all-start.3
  477.9 2.1 reduce.4
  483.3 4.0 all-to-all-start.2
  487.6 5.2 %all-to-all-done.2 = bf16[8,2,4096]{2,1,0:T(2,128)(2,1)} async-done(((bf16[8,2,4096]{2,1,0:T(2,128)(2,1)}), bf16[8,2,4096]{2,1,0:T(2,128)(2,1)}, u32[]{:S(2)}, u32[]{:S(2)}) %all-to-all-start.2) | async-done | bytes 131104 | tf_op jit(solution)/shard_map/all_to_all | solution.py:53
  494.5 7.2 %fusion.45 = bf16[8192,128]{1,0:T(8,128)(2,1)} fusion(f32[64,128,128,1]{1,2,3,0:T(8,128)} %get-tuple-element.148, bf16[8192,128]{1,0:T(8,128)(2,1)S(1)} %copy-done.3, f32[128]{0:T(128)} %param.25, f32[8192]{0:T(1024)S(1)} %get-tuple-element.147, f32[8192]{0:T(1024)S(1)} %get-tuple-element.146), kind=kLoop, calls=%fused_computation.57 | loop fusion | flops 6291456 | bytes 8454656 | tf_op jit(solution)/shard_map/convert_element_type | solution.py:200
  (122 shorter events, 43.2 us)
Async XLA Ops:
  6.5 355.3 %copy-start = (bf16[512,1024]{1,0:T(8,128)(2,1)S(1)}, bf16[512,1024]{1,0:T(8,128)(2,1)}, u32[]{:S(2)}) copy-start(bf16[512,1024]{1,0:T(8,128)(2,1)} %param.22) | copy-start | bytes 3145732
  6.5 62.9 %all-gather.5.cloned.1.call-start = ((), (), s32[]{:S(2)}) async-start(), calls=%async_computation.6 | async-start | bytes 1572864 | tf_op jit(solution)/shard_map/all_gather | solution.py:35
  7.9 10.0 %collective-permute-start = (bf16[2048,128]{1,0:T(8,128)(2,1)S(1)}, bf16[2048,128]{1,0:T(8,128)(2,1)S(1)}, u32[]{:S(2)}, u32[]{:S(2)}) collective-permute-start(bf16[2048,128]{1,0:T(8,128)(2,1)S(1)} %get-tuple-element.140), channel_id=1, source_target_pairs={{0,8},{8,16},{16,24},{24,32},{32,40},{40,48},{48,56},{56,64},{64,7... | collective-permute-start | bytes 1572872 | tf_op jit(solution)/shard_map/ppermute | solution.py:24
  11.8 14.1 %collective-permute-start.1 = (bf16[2048,128]{1,0:T(8,128)(2,1)S(1)}, bf16[2048,128]{1,0:T(8,128)(2,1)S(1)}, u32[]{:S(2)}, u32[]{:S(2)}) collective-permute-start(bf16[2048,128]{1,0:T(8,128)(2,1)S(1)} %get-tuple-element.141), channel_id=1, source_target_pairs={{8,0},{16,8},{24,16},{32,24},{40,32},{48,40},{56,48},{64,56},{72,6... | collective-permute-start | bytes 1572872 | tf_op jit(solution)/shard_map/ppermute | solution.py:26
  41.4 28.0 %copy-start.6 = (bf16[1024,3,128]{2,0,1:T(8,128)(2,1)S(1)}, bf16[1024,3,128]{2,0,1:T(8,128)(2,1)}, u32[]{:S(2)}) copy-start(bf16[1024,3,128]{2,0,1:T(8,128)(2,1)} %param.18) | copy-start | bytes 2359300
  47.1 76.1 %all-gather.7.cloned.1.call-start = ((), (), s32[]{:S(2)}) async-start(), calls=%async_computation.7 | async-start | bytes 5242880 | tf_op jit(solution)/shard_map/all_gather | solution.py:35
  69.7 58.3 %copy-start.10 = (f32[1024]{0:T(1024)S(1)}, f32[1024]{0:T(1024)}, u32[]{:S(2)}) copy-start(f32[1024]{0:T(1024)} %param.17) | copy-start | bytes 12292
  123.2 3.4 copy-start.2
  128.0 11.4 %copy-start.7 = (bf16[128,1024]{1,0:T(8,128)(2,1)S(1)}, bf16[128,1024]{1,0:T(8,128)(2,1)}, u32[]{:S(2)}) copy-start(bf16[128,1024]{1,0:T(8,128)(2,1)} %param.19) | copy-start | bytes 786436
  131.8 14.0 %collective-permute-start.2 = (bf16[1120,256]{1,0:T(8,128)(2,1)}, bf16[1120,256]{1,0:T(8,128)(2,1)}, u32[]{:S(2)}, u32[]{:S(2)}) collective-permute-start(bf16[1120,256]{1,0:T(8,128)(2,1)} %get-tuple-element.142), channel_id=1, source_target_pairs={{0,8},{8,16},{16,24},{24,32},{32,40},{40,48},{48,56},{56,64},{64,7... | collective-permute-start | bytes 1720328 | tf_op jit(solution)/shard_map/ppermute | solution.py:42
  137.5 19.3 %collective-permute-start.3 = (bf16[1120,256]{1,0:T(8,128)(2,1)}, bf16[1120,256]{1,0:T(8,128)(2,1)}, u32[]{:S(2)}, u32[]{:S(2)}) collective-permute-start(bf16[1120,256]{1,0:T(8,128)(2,1)} %get-tuple-element.143), channel_id=1, source_target_pairs={{8,0},{16,8},{24,16},{32,24},{40,32},{48,40},{56,48},{64,56},{72,6... | collective-permute-start | bytes 1720328 | tf_op jit(solution)/shard_map/ppermute | solution.py:42
  141.1 130.5 %all-to-all-start.1 = ((bf16[8,128,1024]{2,1,0:T(8,128)(2,1)}), bf16[8,128,1024]{2,1,0:T(8,128)(2,1)}, u32[]{:S(2)}, u32[]{:S(2)}) async-start(bf16[8,128,1024]{2,1,0:T(8,128)(2,1)} %broadcast_in_dim.85), calls=%async_computation.1 | async-start | bytes 4194304 | tf_op jit(solution)/shard_map/all_to_all | solution.py:53
  159.6 7.2 %copy-start.4 = (bf16[2048,128]{1,0:T(8,128)(2,1)}, bf16[2048,128]{1,0:T(8,128)(2,1)S(1)}, u32[]{:S(2)}) copy-start(bf16[2048,128]{1,0:T(8,128)(2,1)S(1)} %get-tuple-element.225) | copy-start | bytes 1572868 | tf_op jit(solution)/shard_map/while
  180.6 6.0 %copy-start.5 = (bf16[2048,128]{1,0:T(8,128)(2,1)S(1)}, bf16[2048,128]{1,0:T(8,128)(2,1)}, u32[]{:S(2)}) copy-start(bf16[2048,128]{1,0:T(8,128)(2,1)} %copy-done.4) | copy-start | bytes 1572868 | tf_op jit(solution)/shard_map/while
  186.6 7.2 %copy-start.4 = (bf16[2048,128]{1,0:T(8,128)(2,1)}, bf16[2048,128]{1,0:T(8,128)(2,1)S(1)}, u32[]{:S(2)}) copy-start(bf16[2048,128]{1,0:T(8,128)(2,1)S(1)} %get-tuple-element.225) | copy-start | bytes 1572868 | tf_op jit(solution)/shard_map/while
  207.7 6.0 %copy-start.5 = (bf16[2048,128]{1,0:T(8,128)(2,1)S(1)}, bf16[2048,128]{1,0:T(8,128)(2,1)}, u32[]{:S(2)}) copy-start(bf16[2048,128]{1,0:T(8,128)(2,1)} %copy-done.4) | copy-start | bytes 1572868 | tf_op jit(solution)/shard_map/while
  213.7 7.2 %copy-start.4 = (bf16[2048,128]{1,0:T(8,128)(2,1)}, bf16[2048,128]{1,0:T(8,128)(2,1)S(1)}, u32[]{:S(2)}) copy-start(bf16[2048,128]{1,0:T(8,128)(2,1)S(1)} %get-tuple-element.225) | copy-start | bytes 1572868 | tf_op jit(solution)/shard_map/while
  234.8 6.0 %copy-start.5 = (bf16[2048,128]{1,0:T(8,128)(2,1)S(1)}, bf16[2048,128]{1,0:T(8,128)(2,1)}, u32[]{:S(2)}) copy-start(bf16[2048,128]{1,0:T(8,128)(2,1)} %copy-done.4) | copy-start | bytes 1572868 | tf_op jit(solution)/shard_map/while
  240.8 7.2 %copy-start.4 = (bf16[2048,128]{1,0:T(8,128)(2,1)}, bf16[2048,128]{1,0:T(8,128)(2,1)S(1)}, u32[]{:S(2)}) copy-start(bf16[2048,128]{1,0:T(8,128)(2,1)S(1)} %get-tuple-element.225) | copy-start | bytes 1572868 | tf_op jit(solution)/shard_map/while
  261.8 6.0 %copy-start.5 = (bf16[2048,128]{1,0:T(8,128)(2,1)S(1)}, bf16[2048,128]{1,0:T(8,128)(2,1)}, u32[]{:S(2)}) copy-start(bf16[2048,128]{1,0:T(8,128)(2,1)} %copy-done.4) | copy-start | bytes 1572868 | tf_op jit(solution)/shard_map/while
  271.5 11.0 %all-to-all-start = ((bf16[8,256,128]{2,1,0:T(8,128)(2,1)}), bf16[8,256,128]{2,1,0:T(8,128)(2,1)S(1)}, u32[]{:S(2)}, u32[]{:S(2)}) async-start(bf16[8,256,128]{2,1,0:T(8,128)(2,1)} %reshape.172), calls=%async_computation | async-start | bytes 1048576 | tf_op jit(solution)/shard_map/all_to_all | solution.py:174
  275.0 31.2 %all-gather.9.cloned.1.call-start = ((), (), s32[]{:S(2)}) async-start(), calls=%async_computation.8 | async-start | bytes 1572864 | tf_op jit(solution)/shard_map/all_gather | solution.py:35
  285.7 71.3 %all-gather.11.cloned.1.call-start = ((), (), s32[]{:S(2)}) async-start(), calls=%async_computation.9 | async-start | bytes 5242880 | tf_op jit(solution)/shard_map/all_gather | solution.py:35
  306.2 55.7 %copy-start.9 = (bf16[1024,512]{1,0:T(8,128)(2,1)S(1)}, bf16[1024,512]{1,0:T(8,128)(2,1)}, u32[]{:S(2)}) copy-start(bf16[1024,512]{1,0:T(8,128)(2,1)} %param.21) | copy-start | bytes 3145732
  306.2 55.6 %copy-start.11 = (f32[1024]{0:T(1024)S(1)}, f32[1024]{0:T(1024)}, u32[]{:S(2)}) copy-start(f32[1024]{0:T(1024)} %param.20) | copy-start | bytes 12292
  306.3 111.3 %reduce-scatter.5.cloned.1.call-start = ((), (), s32[]{:S(2)}) async-start(), calls=%async_computation.10 | async-start | bytes 5242880 | tf_op jit(solution)/shard_map/reduce_scatter | solution.py:62
  357.0 3.4 copy-start.1
  370.2 81.4 %copy-start.8 = (s32[64,2]{0,1:T(2,128)S(1)}, s32[64,2]{0,1:T(2,128)}, u32[]{:S(2)}) copy-start(s32[64,2]{0,1:T(2,128)} %param.23) | copy-start | bytes 1540
  370.2 72.3 %reduce-scatter.7.cloned.1.call-start = ((), (), s32[]{:S(2)}) async-start(), calls=%async_computation.11 | async-start | bytes 1572864
  445.0 7.9 %collective-permute-start.4 = (bf16[1024,128]{1,0:T(8,128)(2,1)S(1)}, bf16[1024,128]{1,0:T(8,128)(2,1)S(1)}, u32[]{:S(2)}, u32[]{:S(2)}) collective-permute-start(bf16[1024,128]{1,0:T(8,128)(2,1)S(1)} %get-tuple-element.144), channel_id=1, source_target_pairs={{0,8},{8,16},{16,24},{24,32},{32,40},{40,48},{48,56},{56,64},{64,7... | collective-permute-start | bytes 786440 | tf_op jit(solution)/shard_map/ppermute | solution.py:24
  449.6 11.3 %collective-permute-start.5 = (bf16[1024,128]{1,0:T(8,128)(2,1)S(1)}, bf16[1024,128]{1,0:T(8,128)(2,1)S(1)}, u32[]{:S(2)}, u32[]{:S(2)}) collective-permute-start(bf16[1024,128]{1,0:T(8,128)(2,1)S(1)} %get-tuple-element.145), channel_id=1, source_target_pairs={{8,0},{16,8},{24,16},{32,24},{40,32},{48,40},{56,48},{64,56},{72,6... | collective-permute-start | bytes 786440 | tf_op jit(solution)/shard_map/ppermute | solution.py:26
  470.8 23.6 %copy-start.3 = (bf16[8192,128]{1,0:T(8,128)(2,1)S(1)}, bf16[8192,128]{1,0:T(8,128)(2,1)}, u32[]{:S(2)}) copy-start(bf16[8192,128]{1,0:T(8,128)(2,1)} %param.14) | copy-start | bytes 6291460
  473.7 9.6 %all-to-all-start.3 = ((bf16[8,2,4096]{2,1,0:T(2,128)(2,1)}), bf16[8,2,4096]{2,1,0:T(2,128)(2,1)S(1)}, u32[]{:S(2)}, u32[]{:S(2)}) async-start(bf16[8,2,4096]{2,1,0:T(2,128)(2,1)} %reshape.175), calls=%async_computation.4 | async-start | bytes 262144 | tf_op jit(solution)/shard_map/all_to_all | solution.py:53
  483.3 9.6 %all-to-all-start.2 = ((bf16[8,2,4096]{2,1,0:T(2,128)(2,1)}), bf16[8,2,4096]{2,1,0:T(2,128)(2,1)}, u32[]{:S(2)}, u32[]{:S(2)}) async-start(bf16[8,2,4096]{2,1,0:T(2,128)(2,1)} %reshape.177), calls=%async_computation.3 | async-start | bytes 262144 | tf_op jit(solution)/shard_map/all_to_all | solution.py:53
Sparse Core Ops, SparseCore 0:
  47.2 22.1 all-gather.4
  71.0 52.1 all-gather.6
  285.8 20.3 all-gather.8
  307.7 49.2 all-gather.10
  370.3 47.1 reduce-scatter.4
  419.9 22.4 reduce-scatter.6
where the time goes:
time: 511 us; the launch traced here: 508 us
  waiting for transfers between devices  262 us (51%)
  matrix products  94.8 us (19%)
  other arithmetic  45.2 us (9%)
  local copies, waits for them, and re-layouts  42.1 us (8%)
  starting transfers between devices  36.4 us (7%)
  between operations  13.9 us (3%)
  loops' own time  13.8 us (3%)
    all_gather x4, waiting for transfers between devices, gather_axes(): value = lax.all_gather(value, axis, axis=dim, tiled=True)  147 us
    reduce_scatter x1, waiting for transfers between devices, scatter_axes(): value = lax.psum_scatter(value, axis, scatter_dimension=dim, tiled=True)  47.3 us
    sub x4, matrix products, softmax_values(): powers = jnp.where(allowed[None], jnp.exp(masked - highest), 0.0)  44.2 us
    dot_general x4, matrix products, softmax_values(): jnp.einsum('hqk,khd->qhd', probs, value_block, preferred_element_type=jnp...  24.1 us
    unnamed x7, waiting for transfers between devices  22.7 us
    ppermute x2, waiting for transfers between devices, padded(): lax.ppermute(head, axis, [((i + 1) % count, i) for i in range(ends)])  16 us
    another operation x1, loops' own time, on_device(): context = lax.map(attend, starts).reshape(mesh_rows, columns)  13.8 us
    all_to_all x3, starting transfers between devices, copy_for_each(): return lax.all_to_all(copies, axis, split_axis=0, concat_axis=0, tiled=True)  12.5 us
  transfers between devices with their start and end apart: 16, of which 14 were waited for; matrix products, arithmetic and copies ran while one was open for 21% of the time, Pallas kernels for 0%

commit v1 on v0

v1 whole, which is shorter than its diff:
```python
import jax
import jax.numpy as jnp
from jax import lax
from jax.experimental import pallas as pl
from jax.experimental.pallas import tpu as pltpu
from jax.sharding import PartitionSpec as P

D = 1024
HEAD_DIM = 64
WINDOW = 1120
REACH = 1152
BLOCK = 128
EPSILON = 1e-05
LOG2E = 1.4426950408889634
BF = jnp.bfloat16
F32 = jnp.float32
NT = (((1,), (1,)), ((), ()))
TN = (((0,), (0,)), ((), ()))
MIB = 1 << 20


def params(mib):
    return pltpu.CompilerParams(
        dimension_semantics=("arbitrary",), vmem_limit_bytes=mib * MIB
    )


def dot(a, b):
    return jnp.dot(a, b, preferred_element_type=F32)


ANY = pl.BlockSpec(memory_space=pl.ANY)


def whole(shape):
    return pl.BlockSpec(shape, lambda i, *_: (0,) * len(shape))


def encode_kernel(index, low, own, high, weights, out, source, sems):
    step = pl.program_id(0)
    rim = low.shape[0]

    @pl.when(step == 0)
    def _():
        copies = [
            pltpu.make_async_copy(low, source.at[pl.ds(0, rim)], sems.at[0]),
            pltpu.make_async_copy(own, source.at[pl.ds(rim, own.shape[0])], sems.at[1]),
            pltpu.make_async_copy(
                high, source.at[pl.ds(rim + own.shape[0], rim)], sems.at[2]
            ),
        ]
        for c in copies:
            c.start()
        for c in copies:
            c.wait()

    per, slots = weights.shape[0], weights.shape[1]
    for b in range(per):
        left = jnp.concatenate([weights[b, k] for k in range(slots)], axis=1)
        right = jnp.concatenate(
            [source[index[step * per + b, k]] for k in range(slots)], axis=0
        )
        out[b * BLOCK : (b + 1) * BLOCK] = dot(left, right).astype(BF)


def encode(index, low, own, high, weights):
    count, slots = weights.shape[:2]
    per = 2
    blocks = own.shape[0] // BLOCK
    rim = low.shape[0] // BLOCK
    shaped = [v.reshape(-1, BLOCK, BLOCK) for v in (low, own, high)]
    return pl.pallas_call(
        encode_kernel,
        out_shape=jax.ShapeDtypeStruct((count * BLOCK, BLOCK), BF),
        grid_spec=pltpu.PrefetchScalarGridSpec(
            num_scalar_prefetch=1,
            grid=(count // per,),
            in_specs=[
                ANY,
                ANY,
                ANY,
                pl.BlockSpec((per, slots, BLOCK, BLOCK), lambda i, _: (i, 0, 0, 0)),
            ],
            out_specs=pl.BlockSpec((per * BLOCK, BLOCK), lambda i, _: (i, 0)),
            scratch_shapes=[
                pltpu.VMEM((blocks + 2 * rim, BLOCK, BLOCK), BF),
                pltpu.SemaphoreType.DMA((3,)),
            ],
        ),
        compiler_params=params(24),
        name="encode",
    )(index, *shaped, weights)


def project_kernel(
    order, s0, s1, s2, s3, s4, s5, lo6, hi6, lo7, hi7, gain, weights,
    queries, keys_values, share, ordered,
):
    step = pl.program_id(0)
    half = pl.num_programs(0) // 2

    @pl.when(step == 0)
    def _():
        for p in range(8):
            ordered[p * BLOCK : (p + 1) * BLOCK] = weights[order[p]]

    early = step < half
    raw = [s[...] for s in (s0, s1, s2, s3, s4, s5)]
    raw.append(jnp.where(early, lo6[...], hi6[...]))
    raw.append(jnp.where(early, lo7[...], hi7[...]))

    @pl.when(step == order[0])
    def _():
        for p in range(8):
            share[order[p]] = raw[p]

    pieces = [r.astype(F32) for r in raw]
    total = pieces[0]
    for x in pieces[1:]:
        total = total + x
    average = jnp.sum(total, axis=1, keepdims=True) * (1.0 / D)
    pieces = [x - average for x in pieces]
    total = pieces[0] * pieces[0]
    for x in pieces[1:]:
        total = total + x * x
    spread = lax.rsqrt(jnp.sum(total, axis=1, keepdims=True) * (1.0 / D) + EPSILON)
    normed = jnp.concatenate(
        [(x * spread * gain[order[p]]).astype(BF) for p, x in enumerate(pieces)], axis=1
    )
    made = dot(normed, ordered[...]).astype(BF)
    queries[...] = (made[:, :BLOCK].astype(F32) * (HEAD_DIM**-0.5)).astype(BF)
    keys_values[...] = made[:, BLOCK:]


def project(order, slots, gain, weights):
    rows = slots[0].shape[0]
    tile = rows // 8
    full = pl.BlockSpec((tile, BLOCK), lambda i, _: (i, 0))
    early = pl.BlockSpec((tile, BLOCK), lambda i, _: (jnp.minimum(i, 3), 0))
    late = pl.BlockSpec((tile, BLOCK), lambda i, _: (jnp.maximum(i - 4, 0), 0))
    return pl.pallas_call(
        project_kernel,
        out_shape=(
            jax.ShapeDtypeStruct((rows, BLOCK), BF),
            jax.ShapeDtypeStruct((rows, 2 * BLOCK), BF),
            jax.ShapeDtypeStruct((8, tile, BLOCK), BF),
        ),
        grid_spec=pltpu.PrefetchScalarGridSpec(
            num_scalar_prefetch=1,
            grid=(8,),
            in_specs=[full] * 6
            + [early, late, early, late]
            + [whole((8, 1, BLOCK)), whole((8, BLOCK, 3 * BLOCK))],
            out_specs=(
                full,
                pl.BlockSpec((tile, 2 * BLOCK), lambda i, _: (i, 0)),
                whole((8, tile, BLOCK)),
            ),
            scratch_shapes=[pltpu.VMEM((D, 3 * BLOCK), BF)],
        ),
        compiler_params=params(24),
        name="project",
    )(order, *slots, gain.reshape(8, 1, BLOCK), weights.reshape(8, BLOCK, 3 * BLOCK))


TILE = 256
SPAN = TILE + 2 * REACH
CHUNKS = SPAN // TILE


def attend_kernel(edges, queries, low, own, high, out, keys, values, scores, sems):
    step = pl.program_id(0)
    rows = own.shape[0]

    @pl.when(step == 0)
    def _():
        copies = []
        for n, (part, start) in enumerate(
            ((low, 0), (own, REACH), (high, REACH + rows))
        ):
            for m, target in enumerate((keys, values)):
                copies.append(
                    pltpu.make_async_copy(
                        part.at[:, pl.ds(m * BLOCK, BLOCK)],
                        target.at[pl.ds(start, part.shape[0]), pl.ds(0, BLOCK)],
                        sems.at[2 * n + m],
                    )
                )
        for c in copies:
            c.start()
        values[:, BLOCK:] = jnp.ones((values.shape[0], BLOCK), BF)
        first = lax.broadcasted_iota(jnp.int32, (keys.shape[0], BLOCK), 1) == 0
        row = lax.broadcasted_iota(jnp.int32, (keys.shape[0], BLOCK), 0)
        absent = ((row < REACH) & (edges[0] == 1)) | (
            (row >= REACH + rows) & (edges[1] == 1)
        )
        keys[:, BLOCK:] = jnp.where(first & absent, -1e30, 0.0).astype(BF)
        for c in copies:
            c.wait()

    lane = lax.broadcasted_iota(jnp.int32, (TILE, BLOCK), 1)
    q = queries[...]
    zero = jnp.zeros_like(q)
    both = jnp.concatenate(
        [jnp.where(lane < HEAD_DIM, q, zero), jnp.where(lane < HEAD_DIM, zero, q)], axis=0
    )
    mark = jnp.where(
        lax.broadcasted_iota(jnp.int32, (2 * TILE, BLOCK), 1) == 0, 1.0, 0.0
    ).astype(BF)
    stacked = jnp.concatenate([both, mark], axis=1)
    row = lax.broadcasted_iota(jnp.int32, (2 * TILE, TILE), 0) & (TILE - 1)
    column = lax.broadcasted_iota(jnp.int32, (2 * TILE, TILE), 1)
    highest = jnp.full((2 * TILE, BLOCK), -1e30, F32)
    for c in range(CHUNKS):
        part = keys[pl.ds(pl.multiple_of((step + c) * TILE, TILE), TILE)]
        s = lax.dot_general(stacked, part, NT, preferred_element_type=F32)
        least = c * TILE - REACH
        gap = column - row + least
        if least - TILE < -WINDOW:
            s = jnp.where(gap >= -WINDOW, s, -1e30)
        if least + TILE > WINDOW:
            s = jnp.where(gap <= WINDOW, s, -1e30)
        scores[:, c * TILE : (c + 1) * TILE] = s
        highest = jnp.maximum(highest, jnp.maximum(s[:, :BLOCK], s[:, BLOCK:]))
    peak = jnp.max(highest, axis=1, keepdims=True) * LOG2E
    total = jnp.zeros((2 * TILE, 2 * BLOCK), F32)
    for c in range(CHUNKS):
        part = values[pl.ds(pl.multiple_of((step + c) * TILE, TILE), TILE)]
        powers = jnp.exp2(scores[:, c * TILE : (c + 1) * TILE] * LOG2E - peak)
        total = total + dot(powers.astype(BF), part)
    made = total[:, :BLOCK] / total[:, BLOCK:]
    out[...] = jnp.where(lane < HEAD_DIM, made[:TILE], made[TILE:]).astype(BF)


def attend(edges, queries, low, own, high):
    rows = own.shape[0]
    return pl.pallas_call(
        attend_kernel,
        out_shape=jax.ShapeDtypeStruct((rows, BLOCK), BF),
        grid_spec=pltpu.PrefetchScalarGridSpec(
            num_scalar_prefetch=1,
            grid=(rows // TILE,),
            in_specs=[pl.BlockSpec((TILE, BLOCK), lambda i, _: (i, 0)), ANY, ANY, ANY],
            out_specs=pl.BlockSpec((TILE, BLOCK), lambda i, _: (i, 0)),
            scratch_shapes=[
                pltpu.VMEM((rows + 2 * REACH, 2 * BLOCK), BF),
                pltpu.VMEM((rows + 2 * REACH, 2 * BLOCK), BF),
                pltpu.VMEM((2 * TILE, SPAN), F32),
                pltpu.SemaphoreType.DMA((6,)),
            ],
        ),
        compiler_params=params(32),
        name="attend",
    )(edges, queries, low, own, high)


ROWS_E = 64
ROWS_S = 64
ROWS_P = 16
PACK = ROWS_E + ROWS_S + ROWS_P


def pack_weights(position, expand, shrink, project_out):
    part = lax.dynamic_slice_in_dim(expand, position * 2 * ROWS_E, 2 * ROWS_E, 0)
    return jnp.concatenate(
        [
            jnp.concatenate([part[:ROWS_E], part[ROWS_E:]], axis=1),
            lax.dynamic_slice_in_dim(shrink, position * ROWS_S, ROWS_S, 0),
            lax.dynamic_slice_in_dim(project_out, position * ROWS_P, ROWS_P, 0),
        ],
        axis=0,
    )


def gelu(v):
    return 0.5 * v * (1.0 + jnp.tanh(0.7978845608028654 * (v + 0.044715 * v * v * v)))


def forward_kernel(table, *refs):
    parts = refs[:10]
    context, share, gain, out, expand, shrink, outward, sems = refs[10:]
    groups = ([], [], [])
    width = expand.shape[2]
    for n, part in enumerate(parts):
        first = 4 if n % 5 == 4 else 0
        count = part.shape[0]
        where = table[8 + n]
        slots = pl.ds(first, count)

        def copy(group, source, target):
            groups[group].append(
                pltpu.make_async_copy(source, target, sems.at[group, len(groups[group])])
            )

        copy(
            0,
            part.at[:, pl.ds(ROWS_E + ROWS_S, ROWS_P), :],
            outward.at[slots, pl.ds(pl.multiple_of(where * ROWS_P, ROWS_P), ROWS_P), :],
        )
        for side in range(2):
            copy(
                1,
                part.at[:, pl.ds(0, ROWS_E), pl.ds(side * width, width)],
                expand.at[
                    slots,
                    pl.ds(pl.multiple_of(where * 2 * ROWS_E + side * ROWS_E, ROWS_E), ROWS_E),
                    :,
                ],
            )
        copy(
            2,
            part.at[:, pl.ds(ROWS_E, ROWS_S), :],
            shrink.at[slots, pl.ds(pl.multiple_of(where * ROWS_S, ROWS_S), ROWS_S), :],
        )
    for group in groups:
        for c in group:
            c.start()
    for c in groups[0]:
        c.wait()
    total = dot(context[table[0]], outward[0])
    for p in range(1, 8):
        total = total + dot(context[table[p]], outward[p])
    start = jnp.concatenate([share[h] for h in range(8)], axis=1).astype(F32)
    middle = (start + total).astype(BF).astype(F32)
    average = jnp.mean(middle, axis=1, keepdims=True)
    centred = middle - average
    spread = jnp.mean(centred * centred, axis=1, keepdims=True)
    normed = (centred * lax.rsqrt(spread + EPSILON) * gain[...]).astype(BF)
    for c in groups[1]:
        c.wait()
    hidden = [gelu(dot(normed, expand[p])).astype(BF) for p in range(8)]
    for c in groups[2]:
        c.wait()
    total = middle
    for p in range(8):
        total = total + dot(hidden[p], shrink[p])
    done = total.astype(BF)
    for h in range(8):
        out[h] = done[:, h * BLOCK : (h + 1) * BLOCK]


def forward(table, parts, context, share, gain):
    rows = share.shape[1]
    width = D // 2
    return pl.pallas_call(
        forward_kernel,
        out_shape=jax.ShapeDtypeStruct((8, rows, BLOCK), BF),
        grid_spec=pltpu.PrefetchScalarGridSpec(
            num_scalar_prefetch=1,
            grid=(1,),
            in_specs=[ANY] * 10
            + [whole((8, rows, BLOCK)), whole((8, rows, BLOCK)), whole((1, D))],
            out_specs=whole((8, rows, BLOCK)),
            scratch_shapes=[
                pltpu.VMEM((8, D, width), BF),
                pltpu.VMEM((8, width, D), BF),
                pltpu.VMEM((8, BLOCK, D), BF),
                pltpu.SemaphoreType.DMA((3, 20)),
            ],
        ),
        compiler_params=params(48),
        name="forward",
    )(table, *parts, context, share, gain.reshape(1, D))


EACH = 8


def decode_kernel(index, low, own, high, weights, back, sums, source, sems):
    step = pl.program_id(0)
    rim = low.shape[0]

    @pl.when(step == 0)
    def _():
        copies = [
            pltpu.make_async_copy(low, source.at[pl.ds(0, rim)], sems.at[0]),
            pltpu.make_async_copy(own, source.at[pl.ds(rim, own.shape[0])], sems.at[1]),
            pltpu.make_async_copy(
                high, source.at[pl.ds(rim + own.shape[0], rim)], sems.at[2]
            ),
        ]
        for c in copies:
            c.start()
        for c in copies:
            c.wait()

    slots = weights.shape[1]
    ones = jnp.ones((2 * EACH, BLOCK), BF)
    row = lax.broadcasted_iota(jnp.int32, (2 * EACH, BLOCK), 0)
    held = jnp.zeros((2 * EACH, BLOCK), F32)
    for b in range(EACH):
        left = jnp.concatenate([weights[b, k] for k in range(slots)], axis=1)
        right = jnp.concatenate(
            [source[index[step * EACH + b, k]] for k in range(slots)], axis=0
        )
        made = dot(left, right)
        back[b * BLOCK : (b + 1) * BLOCK] = made
        plain = lax.dot_general(ones, made.astype(BF), NT, preferred_element_type=F32)
        square = lax.dot_general(
            ones, (made * made).astype(BF), NT, preferred_element_type=F32
        )
        held = jnp.where(row == b, plain, jnp.where(row == EACH + b, square, held))
    sums[0] = held.astype(BF)


def decode(index, low, own, high, weights):
    count, slots = weights.shape[:2]
    blocks = own.shape[0]
    rim = low.shape[0]
    steps = count // EACH
    return pl.pallas_call(
        decode_kernel,
        out_shape=(
            jax.ShapeDtypeStruct((count * BLOCK, BLOCK), F32),
            jax.ShapeDtypeStruct((steps, 2 * EACH, BLOCK), BF),
        ),
        grid_spec=pltpu.PrefetchScalarGridSpec(
            num_scalar_prefetch=1,
            grid=(steps,),
            in_specs=[
                ANY,
                ANY,
                ANY,
                pl.BlockSpec((EACH, slots, BLOCK, BLOCK), lambda i, _: (i, 0, 0, 0)),
            ],
            out_specs=(
                pl.BlockSpec((EACH * BLOCK, BLOCK), lambda i, _: (i, 0)),
                pl.BlockSpec((1, 2 * EACH, BLOCK), lambda i, _: (i, 0, 0)),
            ),
            scratch_shapes=[
                pltpu.VMEM((blocks + 2 * rim, BLOCK, BLOCK), BF),
                pltpu.SemaphoreType.DMA((3,)),
            ],
        ),
        compiler_params=params(24),
        name="decode",
    )(index, low, own, high, weights)


def finish_kernel(sums, back, state, gain, out):
    count = sums.shape[0]
    stats = jnp.concatenate([sums[h, 0] for h in range(count)], axis=0)
    depth = count * 2 * EACH
    row = lax.broadcasted_iota(jnp.int32, (depth, 2 * EACH * BLOCK), 0)
    column = lax.broadcasted_iota(jnp.int32, (depth, 2 * EACH * BLOCK), 1)
    pick = jnp.where((row % (2 * EACH)) == (column // BLOCK), 1.0, 0.0).astype(BF)
    spread = lax.dot_general(stats, pick, TN, preferred_element_type=F32) * (1.0 / D)
    for b in range(EACH):
        rows = slice(b * BLOCK, (b + 1) * BLOCK)
        average = spread[:, b * BLOCK : (b + 1) * BLOCK]
        squares = spread[:, (EACH + b) * BLOCK : (EACH + b + 1) * BLOCK]
        scale = lax.rsqrt(squares - average * average + EPSILON) * gain[...]
        out[rows] = (
            state[rows].astype(F32) + (back[rows] - average) * scale
        ).astype(BF)


def finish(sums, back, state, gain):
    rows = state.shape[0]
    tile = pl.BlockSpec((EACH * BLOCK, BLOCK), lambda i: (i, 0))
    return pl.pallas_call(
        finish_kernel,
        out_shape=jax.ShapeDtypeStruct((rows, BLOCK), BF),
        grid_spec=pl.GridSpec(
            grid=(rows // (EACH * BLOCK),),
            in_specs=[
                pl.BlockSpec((sums.shape[0], 1, 2 * EACH, BLOCK), lambda i: (0, i, 0, 0)),
                tile,
                tile,
                pl.BlockSpec((1, BLOCK), lambda i: (0, 0)),
            ],
            out_specs=tile,
        ),
        compiler_params=params(24),
        name="finish",
    )(sums, back, state, gain.reshape(1, BLOCK))


def shifted(value, by):
    return lax.ppermute(value, "seq", [(i, i + by) for i in range(16) if 0 <= i + by < 16])


def among(value, axis, count, to):
    return lax.ppermute(value, axis, [(i, to(i)) for i in range(count)])


def head_ring(x):
    half = x.shape[0] // 2
    north = lambda v: among(v, "head", 8, lambda i: (i + 2) % 8)
    south = lambda v: among(v, "head", 8, lambda i: (i - 2) % 8)
    y = among(x, "head", 8, lambda i: i ^ 1)
    xa, xb = north(x), south(x)
    ya, yb = north(y), south(y)
    return (
        x, y, xa, ya, xb, yb,
        north(xa[:half]), south(xb[half:]), north(ya[:half]), south(yb[half:]),
    )


def along_z(i, by):
    return (i // 8) * 8 + ((i // 2 + by) % 4) * 2 + i % 2


def gathered_weights(packed):
    s = head_ring(packed)
    mine = jnp.stack(
        s[:6] + (jnp.concatenate(s[6:8], axis=0), jnp.concatenate(s[8:10], axis=0))
    )
    up = lambda v: among(v, "seq", 16, lambda i: along_z(i, 1))
    down = lambda v: among(v, "seq", 16, lambda i: along_z(i, -1))
    a, b = up(mine), down(mine)
    here = [mine, a, b, up(a[:4]), down(b[4:])]
    return here + [among(v, "seq", 16, lambda i: i ^ 1) for v in here]


def on_device(
    grid_state,
    encode_index,
    encode_weights,
    first_gain,
    project_in,
    project_out,
    second_gain,
    expand_weights,
    shrink_weights,
    decode_index,
    decode_weights,
    output_gain,
):
    band = lax.axis_index("seq")
    bands = lax.axis_size("seq")
    me = lax.axis_index("head")
    mesh_blocks = encode_weights.shape[0]
    mesh_rows = mesh_blocks * BLOCK
    grid_blocks = grid_state.shape[0] // BLOCK
    rim = mesh_blocks * BLOCK
    low = shifted(grid_state[-rim:], 1)
    high = shifted(grid_state[:rim], -1)

    position = band % 8
    parts = gathered_weights(
        pack_weights(position, expand_weights, shrink_weights, project_out)
    )

    mesh_start = encode(
        encode_index - (band * grid_blocks - mesh_blocks), low, grid_state, high, encode_weights
    )
    slots = head_ring(mesh_start)
    partner = me ^ 1
    order = jnp.stack(
        [me, partner] + [(v + by) % 8 for by in (6, 2, 4) for v in (me, partner)]
    ).astype(jnp.int32)
    queries, keys_values, share = project(order, slots, first_gain, project_in)
    below = shifted(keys_values[mesh_rows - REACH :], 1)
    above = shifted(keys_values[:REACH], -1)
    edges = jnp.stack([band == 0, band == bands - 1]).astype(jnp.int32)
    context = attend(edges, queries, below, keys_values, above)
    context = lax.all_to_all(
        context.reshape(8, mesh_rows // 8, BLOCK), "head", 0, 0, tiled=True
    )
    z, core = position // 2, position % 2
    places = [
        ((z + by) % 4) * 2 + side
        for side in (core, 1 - core)
        for by in (0, 3, 1, 2, 2)
    ]
    table = jnp.concatenate([order, jnp.stack(places).astype(jnp.int32)])
    mesh_end = forward(table, parts, context, share, second_gain)
    mesh_end = lax.all_to_all(mesh_end, "head", 0, 0, tiled=True)
    mesh_end = mesh_end.reshape(mesh_blocks, BLOCK, BLOCK)
    edge = mesh_blocks // 2
    back, sums = decode(
        decode_index - (band * mesh_blocks - edge),
        shifted(mesh_end[-edge:], 1),
        mesh_end,
        shifted(mesh_end[:edge], -1),
        decode_weights,
    )
    sums = lax.all_to_all(
        jnp.broadcast_to(sums, (8, *sums.shape)), "head", 0, 0, tiled=True
    )
    return finish(sums, back, grid_state, output_gain)


def solution(mesh):
    in_specs = (
        P("seq", "head"),
        P("seq", None),
        P("seq", None, None, None),
        P(),
        P(None, None, "head"),
        P("head", None),
        P(),
        P(None, "head"),
        P("head", None),
        P("seq", None),
        P("seq", None, None, None),
        P("head"),
    )
    return jax.shard_map(
        on_device, mesh=mesh, in_specs=in_specs, out_specs=P("seq", "head"), check_vma=False
    )
```

time: 511 us -> 268 us (0.52)
  waiting for transfers between devices: 262 us -> 70.1 us
  matrix products: 94.8 us -> 0 us
  Pallas kernels: 0 us -> 68.7 us
  other arithmetic: 45.2 us -> 3.06 us
  blocking collectives: 0 us -> 21 us
  starting transfers between devices: 36.4 us -> 56 us
  loops' own time: 13.8 us -> 0 us
  between operations: 13.9 us -> 0.52 us
  local copies, waits for them, and re-layouts: 42.1 us -> 47.3 us
    all_gather x4 -> x0, waiting for transfers between devices: 147 us -> none  [gather_axes(): value = lax.all_gather(value, axis, axis=dim, tiled=True)]
    pallas_call x0 -> x6, Pallas kernels: none -> 68.7 us  [the longest x1 26 us: attend(): pl.pallas_call(attend_kernel, out_shape=jax.ShapeDtypeStruct((rows, BLOCK...]
    dot_general x9 -> x0, matrix products: 50.6 us -> none  [the longest x4 24.1 us: softmax_values(): jnp.einsum('hqk,khd->qhd', probs, value_block, preferred_element_type=jnp...]
    reduce_scatter x1 -> x0, waiting for transfers between devices: 47.3 us -> none  [scatter_axes(): value = lax.psum_scatter(value, axis, scatter_dimension=dim, tiled=True)]
    sub x4 -> x0, matrix products: 44.2 us -> none  [softmax_values(): powers = jnp.where(allowed[None], jnp.exp(masked - highest), 0.0)]
    ppermute x6 -> x33, starting transfers between devices: 20 us -> 51.9 us  [the longest x6 28.8 us: shifted(): lax.ppermute(value, 'seq', [(i, i + by) for i in range(16) if 0 <= i + by...]
    ppermute x6 -> x33, waiting for transfers between devices: 31.3 us -> 60.9 us  [the longest x27 41.9 us: among(): return lax.ppermute(value, axis, [(i, to(i)) for i in range(count)])]
    unnamed x7 -> x0, waiting for transfers between devices: 22.7 us -> none
  transfers between devices with their start and end apart: 16 -> 34, of which waited for: 14 -> 15; matrix products, arithmetic and copies ran while one was open for 21% -> 9% of each run, Pallas kernels for 0% -> 15%
where the time goes in v1:
time: 268 us; the launch traced here: 267 us
  waiting for transfers between devices  70.1 us (26%)
  Pallas kernels  68.7 us (26%)
  starting transfers between devices  56 us (21%)
  local copies, waits for them, and re-layouts  47.3 us (18%)
  blocking collectives  21 us (8%)
  other arithmetic  3.06 us (1%)
    ppermute x27, waiting for transfers between devices, among(): return lax.ppermute(value, axis, [(i, to(i)) for i in range(count)])  41.9 us
    unnamed x77, local copies, waits for them, and re-layouts  29.3 us
    ppermute x6, starting transfers between devices, shifted(): lax.ppermute(value, 'seq', [(i, i + by) for i in range(16) if 0 <= i + by...  28.8 us
    pallas_call x1, Pallas kernels, attend(): pl.pallas_call(attend_kernel, out_shape=jax.ShapeDtypeStruct((rows, BLOCK...  26 us
    ppermute x27, starting transfers between devices, among(): return lax.ppermute(value, axis, [(i, to(i)) for i in range(count)])  23 us
    ppermute x6, waiting for transfers between devices, shifted(): lax.ppermute(value, 'seq', [(i, i + by) for i in range(16) if 0 <= i + by...  19 us
    pallas_call x1, Pallas kernels, decode(): pl.pallas_call(decode_kernel, out_shape=(jax.ShapeDtypeStruct((count * BL...  13.8 us
    all_to_all x1, blocking collectives, on_device(): mesh_end = lax.all_to_all(mesh_end, 'head', 0, 0, tiled=True)  12.4 us
  transfers between devices with their start and end apart: 34, of which 15 were waited for; matrix products, arithmetic and copies ran while one was open for 9% of the time, Pallas kernels for 15%

profile of v1, /device:TPU:97, one launch (start us, length us, event | category | flops | bytes accessed | tf_op | source)
XLA Modules:
  0.0 266.7 jit_solution(16585474324630302424)
XLA Ops:
  2.8 1.2 collective-permute-start
  4.0 1.3 collective-permute-start.1
  5.3 1.4 collective-permute-start.3
  6.8 2.3 fusion.2
  9.0 4.3 %collective-permute-start.18 = (bf16[2048,128]{1,0:T(8,128)(2,1)}, bf16[2048,128]{1,0:T(8,128)(2,1)}, u32[]{:S(2)}, u32[]{:S(2)}) collective-permute-start(bf16[2048,128]{1,0:T(8,128)(2,1)} %get-tuple-element.16), channel_id=1, source_target_pairs={{0,8},{8,16},{16,24},{24,32},{32,40},{40,48},{48,56},{56,64},{64,7... | collective-permute-start | bytes 1572872 | tf_op jit(solution)/shard_map/ppermute | solution.py:480
  13.3 1.9 collective-permute-start.19
  16.2 2.6 collective-permute-start.4
  18.8 1.7 bitcast_dynamic-update-slice_fusion.4
  22.5 1.7 bitcast_dynamic-update-slice_fusion.3
  24.2 2.7 collective-permute-start.6
  27.8 2.2 copy-done.7
  30.0 4.4 %encode.1.s0 = bf16[2048,128]{1,0:T(8,128)(2,1)S(1)} custom-call(s32[16,8]{1,0:T(8,128)S(1)} %broadcast_subtract_fusion.1.index, bf16[16,128,128]{2,1,0:T(8,128)(2,1)} %bitcast.26.low, bf16[64,128,128]{2,1,0:T(8,128)(2,1)S(1)} %bitcast.48, bf16[16,128,128]{2,1,0:T(8,128)(2,1)} %bitcast.28.high, bf16[16,8,128,128]{3,2,1,0:T(8,128)(2,1)S(1)} %copy-done.7), custom_call_target="tpu_custom_call" | custom-call | tf_op jit(solution)/shard_map/encode/pallas_call | solution.py:72
  34.7 2.7 collective-permute-start.8
  38.1 1.7 bitcast_dynamic-update-slice_fusion.1
  41.9 1.5 collective-permute-start.10
  43.4 2.7 %collective-permute-start.23 = (bf16[2048,128]{1,0:T(8,128)(2,1)S(1)}, bf16[2048,128]{1,0:T(8,128)(2,1)S(1)}, u32[]{:S(2)}, u32[]{:S(2)}) collective-permute-start(bf16[2048,128]{1,0:T(8,128)(2,1)S(1)} %encode.1.s0), channel_id=1, source_target_pairs={{0,6},{1,7},{2,0},{3,1},{4,2},{5,3},{6,4},{7,5},{8,14},{9,15},{10,... | collective-permute-start | bytes 1572872 | tf_op jit(solution)/shard_map/ppermute | solution.py:484
  46.9 1.5 collective-permute-start.22
  48.4 4.7 %collective-permute-done.21.s2 = bf16[2048,128]{1,0:T(8,128)(2,1)S(1)} collective-permute-done((bf16[2048,128]{1,0:T(8,128)(2,1)S(1)}, bf16[2048,128]{1,0:T(8,128)(2,1)S(1)}, u32[]{:S(2)}, u32[]{:S(2)}) %collective-permute-start.21) | collective-permute-done | bytes 524320 | tf_op jit(solution)/shard_map/ppermute | solution.py:484
  54.4 1.7 collective-permute-start.25
  56.9 7.5 %collective-permute-done.22.s3 = bf16[2048,128]{1,0:T(8,128)(2,1)S(1)} collective-permute-done((bf16[2048,128]{1,0:T(8,128)(2,1)S(1)}, bf16[2048,128]{1,0:T(8,128)(2,1)S(1)}, u32[]{:S(2)}, u32[]{:S(2)}) %collective-permute-start.22) | collective-permute-done | bytes 524320 | tf_op jit(solution)/shard_map/ppermute | solution.py:484
  67.4 2.6 collective-permute-done.25.lo6
  70.1 2.8 %copy.26 = bf16[1024,3,128]{2,1,0:T(4,128)(2,1)} copy(bf16[1024,3,128]{2,0,1:T(8,128)(2,1)} %param.16) | data formatting | bytes 1572864 | tf_op jit(solution)/shard_map/reshape | solution.py:163
  72.9 3.2 %reshape.38.weights = bf16[8,128,384]{2,1,0:T(8,128)(2,1)} reshape(bf16[1024,3,128]{2,1,0:T(4,128)(2,1)} %copy.26) | data formatting | bytes 1572864 | tf_op jit(solution)/shard_map/reshape | solution.py:163
  76.2 2.2 collective-permute-done.28.hi7
  85.8 8.3 %project.1 = (bf16[2048,128]{1,0:T(8,128)(2,1)S(1)}, bf16[2048,256]{1,0:T(8,128)(2,1)S(1)}, bf16[8,256,128]{2,1,0:T(8,128)(2,1)S(1)}) custom-call(s32[8]{0:T(128)S(1)} %stack.117.order, bf16[2048,128]{1,0:T(8,128)(2,1)S(1)} %copy-done.10, bf16[2048,128]{1,0:T(8,128)(2,1)S(1)} %copy-done.27, bf16[2048,128]{1,0:T(8,128)(2,1)S(1)} %copy-done.13, ...), custom_call_target="tpu_custom_call" | custom-call | tf_op jit(solution)/shard_map/project/pallas_call | solution.py:141
  94.3 11.9 %collective-permute-start.29 = (bf16[1152,256]{1,0:T(8,128)(2,1)S(1)}, bf16[1152,256]{1,0:T(8,128)(2,1)S(1)}, u32[]{:S(2)}, u32[]{:S(2)}) collective-permute-start(bf16[1152,256]{1,0:T(8,128)(2,1)S(1)} %get-tuple-element.18), channel_id=1, source_target_pairs={{0,8},{8,16},{16,24},{24,32},{32,40},{40,48},{48,56},{56,64},{64,7... | collective-permute-start | bytes 1769480 | tf_op jit(solution)/shard_map/ppermute | solution.py:480
  106.2 1.9 collective-permute-start.30
  108.3 1.4 slice.84
  110.5 1.4 slice.85
  111.9 1.2 collective-permute-done.29.low
  113.9 7.3 %collective-permute-done.30.high = bf16[1152,256]{1,0:T(8,128)(2,1)S(1)} collective-permute-done((bf16[1152,256]{1,0:T(8,128)(2,1)S(1)}, bf16[1152,256]{1,0:T(8,128)(2,1)S(1)}, u32[]{:S(2)}, u32[]{:S(2)}) %collective-permute-start.30) | collective-permute-done | bytes 589856 | tf_op jit(solution)/shard_map/ppermute | solution.py:480
  122.0 15.1 %collective-permute-done.11.refs_3_ = bf16[4,144,1024]{2,1,0:T(8,128)(2,1)} collective-permute-done((bf16[4,144,1024]{2,1,0:T(8,128)(2,1)S(1)}, bf16[4,144,1024]{2,1,0:T(8,128)(2,1)}, u32[]{:S(2)}, u32[]{:S(2)}) %collective-permute-start.11) | collective-permute-done | bytes 1179680 | tf_op jit(solution)/shard_map/ppermute | solution.py:484
  137.1 1.3 collective-permute-start.16
  138.4 8.0 %collective-permute-done.12.refs_4_ = bf16[4,144,1024]{2,1,0:T(8,128)(2,1)} collective-permute-done((bf16[4,144,1024]{2,1,0:T(8,128)(2,1)S(1)}, bf16[4,144,1024]{2,1,0:T(8,128)(2,1)}, u32[]{:S(2)}, u32[]{:S(2)}) %collective-permute-start.12) | collective-permute-done | bytes 1179680 | tf_op jit(solution)/shard_map/ppermute | solution.py:484
  146.5 1.2 copy-done.3
  150.9 26.0 %attend.1 = bf16[2048,128]{1,0:T(8,128)(2,1)S(1)} custom-call(s32[2]{0:T(128)S(1)} %add_convert_fusion.edges, bf16[2048,128]{1,0:T(8,128)(2,1)S(1)} %copy-done.29, bf16[1152,256]{1,0:T(8,128)(2,1)S(1)} %copy-done.21, bf16[2048,256]{1,0:T(8,128)(2,1)S(1)} %copy-done.3, bf16[1152,256]{1,0:T(8,128)(2,1)S(1)} %copy-done.23), custom_call_target="tpu_custom_call" | custom-call | tf_op jit(solution)/shard_map/attend/pallas_call | solution.py:237
  177.7 4.1 %all-to-all-start = ((bf16[8,256,128]{2,1,0:T(8,128)(2,1)}), bf16[8,256,128]{2,1,0:T(8,128)(2,1)}, u32[]{:S(2)}, u32[]{:S(2)}) async-start(bf16[8,256,128]{2,1,0:T(8,128)(2,1)} %bitcast.50), calls=%async_computation | async-start | bytes 1048576 | tf_op jit(solution)/shard_map/all_to_all | solution.py:558
  182.0 9.2 %all-to-all-done.refs_10_ = bf16[8,256,128]{2,1,0:T(8,128)(2,1)} async-done(((bf16[8,256,128]{2,1,0:T(8,128)(2,1)}), bf16[8,256,128]{2,1,0:T(8,128)(2,1)}, u32[]{:S(2)}, u32[]{:S(2)}) %all-to-all-start) | async-done | bytes 524320 | tf_op jit(solution)/shard_map/all_to_all | solution.py:558
  192.3 11.3 %forward.1 = bf16[8,256,128]{2,1,0:T(8,128)(2,1)S(1)} custom-call(s32[18]{0:T(128)S(1)} %concatenate.16.table, bf16[8,144,1024]{2,1,0:T(8,128)(2,1)} %fusion.1.refs_0_, bf16[8,144,1024]{2,1,0:T(8,128)(2,1)} %collective-permute-done.9.refs_1_, bf16[8,144,1024]{2,1,0:T(8,128)(2,1)} %collective-permute-done.10.refs_2_, ...), custom_call_target="tpu_custom_call" | custom-call | tf_op jit(solution)/shard_map/forward/pallas_call | solution.py:345
  203.6 12.4 %all_to_all.15 = bf16[8,256,128]{2,1,0:T(8,128)(2,1)S(1)} all-to-all(bf16[8,256,128]{2,1,0:T(8,128)(2,1)S(1)} %forward.1), channel_id=1, replica_groups=mesh['seq'=16,'head'=8] {'head'}, dimensions={0} | all-to-all | bytes 1048576 | tf_op jit(solution)/shard_map/all_to_all | solution.py:569
  217.7 6.8 %collective-permute-start.31 = (bf16[8,128,128]{2,1,0:T(8,128)(2,1)}, bf16[8,128,128]{2,1,0:T(8,128)(2,1)S(1)}, u32[]{:S(2)}, u32[]{:S(2)}) collective-permute-start(bf16[8,128,128]{2,1,0:T(8,128)(2,1)} %bitcast.32), channel_id=1, source_target_pairs={{0,8},{8,16},{16,24},{24,32},{32,40},{40,48},{48,56},{56,64},{64,7... | collective-permute-start | bytes 786440 | tf_op jit(solution)/shard_map/ppermute | solution.py:480
  224.5 1.9 collective-permute-start.32
  226.5 1.6 collective-permute-done.31.low
  228.1 8.0 %collective-permute-done.32.high = bf16[8,128,128]{2,1,0:T(8,128)(2,1)} collective-permute-done((bf16[8,128,128]{2,1,0:T(8,128)(2,1)}, bf16[8,128,128]{2,1,0:T(8,128)(2,1)}, u32[]{:S(2)}, u32[]{:S(2)}) %collective-permute-start.32) | collective-permute-done | bytes 262176 | tf_op jit(solution)/shard_map/ppermute | solution.py:480
  237.1 2.2 copy-done.6
  239.3 13.8 %decode.1 = (f32[8192,128]{1,0:T(8,128)S(1)}, bf16[8,16,128]{2,1,0:T(8,128)(2,1)S(1)}) custom-call(s32[64,2]{1,0:T(8,128)S(1)} %broadcast_subtract_fusion.index, bf16[8,128,128]{2,1,0:T(8,128)(2,1)S(1)} %collective-permute-done.31.low, bf16[16,128,128]{2,1,0:T(8,128)(2,1)S(1)} %bitcast.49, bf16[8,128,128]{2,1,0:T(8,128)(2,1)} %collective-permute-done.32.high, ...), custom_call_target="tpu_custom_call" | custom-call | tf_op jit(solution)/shard_map/decode/pallas_call | solution.py:411
  253.2 8.5 %all_to_all.16.sums = bf16[8,8,16,128]{3,2,1,0:T(8,128)(2,1)S(1)} all-to-all(bf16[8,8,16,128]{3,2,1,0:T(8,128)(2,1)S(1)} %broadcast_in_dim.3), channel_id=1, replica_groups=mesh['seq'=16,'head'=8] {'head'}, dimensions={0} | all-to-all | bytes 524288 | tf_op jit(solution)/shard_map/all_to_all | solution.py:579
  261.7 5.0 %finish.1 = bf16[8192,128]{1,0:T(8,128)(2,1)} custom-call(bf16[8,8,16,128]{3,2,1,0:T(8,128)(2,1)S(1)} %all_to_all.16.sums, f32[8192,128]{1,0:T(8,128)S(1)} %get-tuple-element.14.back, bf16[8192,128]{1,0:T(8,128)(2,1)S(1)} %copy-done.1, f32[1,128]{1,0:T(1,128)S(1)} %bitcast.53), custom_call_target="tpu_custom_call" | custom-call | tf_op jit(solution)/shard_map/finish/pallas_call | solution.py:461
  (133 shorter events, 33.9 us)
Async XLA Ops:
  0.0 15.3 %copy-start.33 = (s32[16,8]{0,1:T(8,128)S(1)}, s32[16,8]{0,1:T(8,128)}, u32[]{:S(2)}) copy-start(s32[16,8]{0,1:T(8,128)} %param.13) | copy-start | bytes 1540
  2.8 25.0 %copy-start.1 = (bf16[8192,128]{1,0:T(8,128)(2,1)S(1)}, bf16[8192,128]{1,0:T(8,128)(2,1)}, u32[]{:S(2)}) copy-start(bf16[8192,128]{1,0:T(8,128)(2,1)} %state.1) | copy-start | bytes 6291460
  2.8 13.3 %collective-permute-start = (bf16[144,1024]{1,0:T(8,128)(2,1)}, bf16[144,1024]{1,0:T(8,128)(2,1)}, u32[]{:S(2)}, u32[]{:S(2)}) collective-permute-start(bf16[144,1024]{1,0:T(8,128)(2,1)} %pad_maximum_fusion), channel_id=1, source_target_pairs={{0,1},{1,0},{2,3},{3,2},{4,5},{5,4},{6,7},{7,6},{8,9},{9,8},{10,11... | collective-permute-start | bytes 884744 | tf_op jit(solution)/shard_map/ppermute | solution.py:484
  4.0 12.2 %collective-permute-start.1 = (bf16[144,1024]{1,0:T(8,128)(2,1)}, bf16[144,1024]{1,0:T(8,128)(2,1)}, u32[]{:S(2)}, u32[]{:S(2)}) collective-permute-start(bf16[144,1024]{1,0:T(8,128)(2,1)} %pad_maximum_fusion), channel_id=1, source_target_pairs={{0,2},{1,3},{2,4},{3,5},{4,6},{5,7},{6,0},{7,1},{8,10},{9,11},{10,... | collective-permute-start | bytes 884744 | tf_op jit(solution)/shard_map/ppermute | solution.py:484
  5.3 16.2 %collective-permute-start.3 = (bf16[144,1024]{1,0:T(8,128)(2,1)}, bf16[144,1024]{1,0:T(8,128)(2,1)}, u32[]{:S(2)}, u32[]{:S(2)}) collective-permute-start(bf16[144,1024]{1,0:T(8,128)(2,1)} %pad_maximum_fusion), channel_id=1, source_target_pairs={{0,6},{1,7},{2,0},{3,1},{4,2},{5,3},{6,4},{7,5},{8,14},{9,15},{10,... | collective-permute-start | bytes 884744 | tf_op jit(solution)/shard_map/ppermute | solution.py:484
  9.0 15.2 %collective-permute-start.18 = (bf16[2048,128]{1,0:T(8,128)(2,1)}, bf16[2048,128]{1,0:T(8,128)(2,1)}, u32[]{:S(2)}, u32[]{:S(2)}) collective-permute-start(bf16[2048,128]{1,0:T(8,128)(2,1)} %get-tuple-element.16), channel_id=1, source_target_pairs={{0,8},{8,16},{16,24},{24,32},{32,40},{40,48},{48,56},{56,64},{64,7... | collective-permute-start | bytes 1572872 | tf_op jit(solution)/shard_map/ppermute | solution.py:480
  13.3 14.4 %collective-permute-start.19 = (bf16[2048,128]{1,0:T(8,128)(2,1)}, bf16[2048,128]{1,0:T(8,128)(2,1)}, u32[]{:S(2)}, u32[]{:S(2)}) collective-permute-start(bf16[2048,128]{1,0:T(8,128)(2,1)} %get-tuple-element.15), channel_id=1, source_target_pairs={{8,0},{16,8},{24,16},{32,24},{40,32},{48,40},{56,48},{64,56},{72,6... | collective-permute-start | bytes 1572872 | tf_op jit(solution)/shard_map/ppermute | solution.py:480
  16.1 18.3 %collective-permute-start.2 = (bf16[144,1024]{1,0:T(8,128)(2,1)}, bf16[144,1024]{1,0:T(8,128)(2,1)S(1)}, u32[]{:S(2)}, u32[]{:S(2)}) collective-permute-start(bf16[144,1024]{1,0:T(8,128)(2,1)} %collective-permute-done), channel_id=1, source_target_pairs={{0,2},{1,3},{2,4},{3,5},{4,6},{5,7},{6,0},{7,1},{8,10},{9,11},{10,... | collective-permute-start | bytes 884744 | tf_op jit(solution)/shard_map/ppermute | solution.py:484
  16.2 18.4 %collective-permute-start.4 = (bf16[144,1024]{1,0:T(8,128)(2,1)}, bf16[144,1024]{1,0:T(8,128)(2,1)S(1)}, u32[]{:S(2)}, u32[]{:S(2)}) collective-permute-start(bf16[144,1024]{1,0:T(8,128)(2,1)} %collective-permute-done), channel_id=1, source_target_pairs={{0,6},{1,7},{2,0},{3,1},{4,2},{5,3},{6,4},{7,5},{8,14},{9,15},{10,... | collective-permute-start | bytes 884744 | tf_op jit(solution)/shard_map/ppermute | solution.py:484
  21.5 19.0 %collective-permute-start.5 = (bf16[72,1024]{1,0:T(8,128)(2,1)S(1)}, bf16[72,1024]{1,0:T(8,128)(2,1)S(1)}, u32[]{:S(2)}, u32[]{:S(2)}) collective-permute-start(bf16[72,1024]{1,0:T(8,128)(2,1)S(1)} %slice.80), channel_id=1, source_target_pairs={{0,2},{1,3},{2,4},{3,5},{4,6},{5,7},{6,0},{7,1},{8,10},{9,11},{10,... | collective-permute-start | bytes 442376 | tf_op jit(solution)/shard_map/ppermute | solution.py:484
  24.2 16.3 %collective-permute-start.6 = (bf16[72,1024]{1,0:T(8,128)(2,1)S(1)}, bf16[72,1024]{1,0:T(8,128)(2,1)S(1)}, u32[]{:S(2)}, u32[]{:S(2)}) collective-permute-start(bf16[72,1024]{1,0:T(8,128)(2,1)S(1)} %slice.81), channel_id=1, source_target_pairs={{0,6},{1,7},{2,0},{3,1},{4,2},{5,3},{6,4},{7,5},{8,14},{9,15},{10,... | collective-permute-start | bytes 442376 | tf_op jit(solution)/shard_map/ppermute | solution.py:484
  34.4 30.8 %copy-start.9 = (bf16[2048,128]{1,0:T(8,128)(2,1)}, bf16[2048,128]{1,0:T(8,128)(2,1)S(1)}, u32[]{:S(2)}) copy-start(bf16[2048,128]{1,0:T(8,128)(2,1)S(1)} %encode.1.s0) | copy-start | bytes 1572868
  34.4 12.6 %collective-permute-start.20 = (bf16[2048,128]{1,0:T(8,128)(2,1)S(1)}, bf16[2048,128]{1,0:T(8,128)(2,1)S(1)}, u32[]{:S(2)}, u32[]{:S(2)}) collective-permute-start(bf16[2048,128]{1,0:T(8,128)(2,1)S(1)} %encode.1.s0), channel_id=1, source_target_pairs={{0,1},{1,0},{2,3},{3,2},{4,5},{5,4},{6,7},{7,6},{8,9},{9,8},{10,11... | collective-permute-start | bytes 1572872 | tf_op jit(solution)/shard_map/ppermute | solution.py:484
  34.5 6.7 %collective-permute-start.7 = (bf16[72,1024]{1,0:T(8,128)(2,1)S(1)}, bf16[72,1024]{1,0:T(8,128)(2,1)S(1)}, u32[]{:S(2)}, u32[]{:S(2)}) collective-permute-start(bf16[72,1024]{1,0:T(8,128)(2,1)S(1)} %slice.82), channel_id=1, source_target_pairs={{0,2},{1,3},{2,4},{3,5},{4,6},{5,7},{6,0},{7,1},{8,10},{9,11},{10,... | collective-permute-start | bytes 442376 | tf_op jit(solution)/shard_map/ppermute | solution.py:484
  34.7 6.5 %collective-permute-start.8 = (bf16[72,1024]{1,0:T(8,128)(2,1)S(1)}, bf16[72,1024]{1,0:T(8,128)(2,1)S(1)}, u32[]{:S(2)}, u32[]{:S(2)}) collective-permute-start(bf16[72,1024]{1,0:T(8,128)(2,1)S(1)} %slice.83), channel_id=1, source_target_pairs={{0,6},{1,7},{2,0},{3,1},{4,2},{5,3},{6,4},{7,5},{8,14},{9,15},{10,... | collective-permute-start | bytes 442376 | tf_op jit(solution)/shard_map/ppermute | solution.py:484
  40.4 12.7 %collective-permute-start.21 = (bf16[2048,128]{1,0:T(8,128)(2,1)S(1)}, bf16[2048,128]{1,0:T(8,128)(2,1)S(1)}, u32[]{:S(2)}, u32[]{:S(2)}) collective-permute-start(bf16[2048,128]{1,0:T(8,128)(2,1)S(1)} %encode.1.s0), channel_id=1, source_target_pairs={{0,2},{1,3},{2,4},{3,5},{4,6},{5,7},{6,0},{7,1},{8,10},{9,11},{10,... | collective-permute-start | bytes 1572872 | tf_op jit(solution)/shard_map/ppermute | solution.py:484
  41.9 66.3 %collective-permute-start.9 = (bf16[8,144,1024]{2,1,0:T(8,128)(2,1)}, bf16[8,144,1024]{2,1,0:T(8,128)(2,1)}, u32[]{:S(2)}, u32[]{:S(2)}) collective-permute-start(bf16[8,144,1024]{2,1,0:T(8,128)(2,1)} %fusion.1.refs_0_), channel_id=1, source_target_pairs={{0,16},{8,24},{16,32},{24,40},{32,48},{40,56},{48,0},{56,8},{64,80... | collective-permute-start | bytes 7077896 | tf_op jit(solution)/shard_map/ppermute | solution.py:484
  41.9 68.0 %collective-permute-start.10 = (bf16[8,144,1024]{2,1,0:T(8,128)(2,1)}, bf16[8,144,1024]{2,1,0:T(8,128)(2,1)}, u32[]{:S(2)}, u32[]{:S(2)}) collective-permute-start(bf16[8,144,1024]{2,1,0:T(8,128)(2,1)} %fusion.1.refs_0_), channel_id=1, source_target_pairs={{0,48},{8,56},{16,0},{24,8},{32,16},{40,24},{48,32},{56,40},{64,11... | collective-permute-start | bytes 7077896 | tf_op jit(solution)/shard_map/ppermute | solution.py:484
  43.4 11.0 %collective-permute-start.23 = (bf16[2048,128]{1,0:T(8,128)(2,1)S(1)}, bf16[2048,128]{1,0:T(8,128)(2,1)S(1)}, u32[]{:S(2)}, u32[]{:S(2)}) collective-permute-start(bf16[2048,128]{1,0:T(8,128)(2,1)S(1)} %encode.1.s0), channel_id=1, source_target_pairs={{0,6},{1,7},{2,0},{3,1},{4,2},{5,3},{6,4},{7,5},{8,14},{9,15},{10,... | collective-permute-start | bytes 1572872 | tf_op jit(solution)/shard_map/ppermute | solution.py:484
  46.9 17.5 %collective-permute-start.22 = (bf16[2048,128]{1,0:T(8,128)(2,1)S(1)}, bf16[2048,128]{1,0:T(8,128)(2,1)S(1)}, u32[]{:S(2)}, u32[]{:S(2)}) collective-permute-start(bf16[2048,128]{1,0:T(8,128)(2,1)S(1)} %collective-permute-done.20.s1), channel_id=1, source_target_pairs={{0,2},{1,3},{2,4},{3,5},{4,6},{5,7},{6,0},{7,1},{8,10},{9,11},{10,... | collective-permute-start | bytes 1572872 | tf_op jit(solution)/shard_map/ppermute | solution.py:484
  53.2 12.5 %copy-start.12 = (bf16[2048,128]{1,0:T(8,128)(2,1)}, bf16[2048,128]{1,0:T(8,128)(2,1)S(1)}, u32[]{:S(2)}) copy-start(bf16[2048,128]{1,0:T(8,128)(2,1)S(1)} %collective-permute-done.21.s2) | copy-start | bytes 1572868
  53.2 12.5 %collective-permute-start.24 = (bf16[2048,128]{1,0:T(8,128)(2,1)S(1)}, bf16[2048,128]{1,0:T(8,128)(2,1)S(1)}, u32[]{:S(2)}, u32[]{:S(2)}) collective-permute-start(bf16[2048,128]{1,0:T(8,128)(2,1)S(1)} %collective-permute-done.20.s1), channel_id=1, source_target_pairs={{0,6},{1,7},{2,0},{3,1},{4,2},{5,3},{6,4},{7,5},{8,14},{9,15},{10,... | collective-permute-start | bytes 1572872 | tf_op jit(solution)/shard_map/ppermute | solution.py:484
  54.4 12.3 %copy-start.14 = (bf16[2048,128]{1,0:T(8,128)(2,1)}, bf16[2048,128]{1,0:T(8,128)(2,1)S(1)}, u32[]{:S(2)}) copy-start(bf16[2048,128]{1,0:T(8,128)(2,1)S(1)} %collective-permute-done.23.s4) | copy-start | bytes 1572868
  54.4 15.6 %collective-permute-start.25 = (bf16[1024,128]{1,0:T(8,128)(2,1)S(1)}, bf16[1024,128]{1,0:T(8,128)(2,1)S(1)}, u32[]{:S(2)}, u32[]{:S(2)}) collective-permute-start(bf16[1024,128]{1,0:T(8,128)(2,1)S(1)} %slice.86), channel_id=1, source_target_pairs={{0,2},{1,3},{2,4},{3,5},{4,6},{5,7},{6,0},{7,1},{8,10},{9,11},{10,... | collective-permute-start | bytes 786440 | tf_op jit(solution)/shard_map/ppermute | solution.py:484
  56.9 21.5 %copy-start.31 = (f32[1024]{0:T(1024)S(1)}, f32[1024]{0:T(1024)}, u32[]{:S(2)}) copy-start(f32[1024]{0:T(1024)} %param.15) | copy-start | bytes 12292
  64.4 3.0 %copy-start.16 = (bf16[2048,128]{1,0:T(8,128)(2,1)}, bf16[2048,128]{1,0:T(8,128)(2,1)S(1)}, u32[]{:S(2)}) copy-start(bf16[2048,128]{1,0:T(8,128)(2,1)S(1)} %collective-permute-done.22.s3) | copy-start | bytes 1572868
  64.4 11.8 %collective-permute-start.26 = (bf16[1024,128]{1,0:T(8,128)(2,1)}, bf16[1024,128]{1,0:T(8,128)(2,1)}, u32[]{:S(2)}, u32[]{:S(2)}) collective-permute-start(bf16[1024,128]{1,0:T(8,128)(2,1)} %slice.87), channel_id=1, source_target_pairs={{0,6},{1,7},{2,0},{3,1},{4,2},{5,3},{6,4},{7,5},{8,14},{9,15},{10,... | collective-permute-start | bytes 786440 | tf_op jit(solution)/shard_map/ppermute | solution.py:484
  65.7 4.3 %copy-start.18 = (bf16[2048,128]{1,0:T(8,128)(2,1)}, bf16[2048,128]{1,0:T(8,128)(2,1)S(1)}, u32[]{:S(2)}) copy-start(bf16[2048,128]{1,0:T(8,128)(2,1)S(1)} %collective-permute-done.24.s5) | copy-start | bytes 1572868
  65.7 10.5 %collective-permute-start.27 = (bf16[1024,128]{1,0:T(8,128)(2,1)}, bf16[1024,128]{1,0:T(8,128)(2,1)}, u32[]{:S(2)}, u32[]{:S(2)}) collective-permute-start(bf16[1024,128]{1,0:T(8,128)(2,1)} %slice.88), channel_id=1, source_target_pairs={{0,2},{1,3},{2,4},{3,5},{4,6},{5,7},{6,0},{7,1},{8,10},{9,11},{10,... | collective-permute-start | bytes 786440 | tf_op jit(solution)/shard_map/ppermute | solution.py:484
  70.0 8.4 %collective-permute-start.28 = (bf16[1024,128]{1,0:T(8,128)(2,1)}, bf16[1024,128]{1,0:T(8,128)(2,1)}, u32[]{:S(2)}, u32[]{:S(2)}) collective-permute-start(bf16[1024,128]{1,0:T(8,128)(2,1)} %slice.89), channel_id=1, source_target_pairs={{0,6},{1,7},{2,0},{3,1},{4,2},{5,3},{6,4},{7,5},{8,14},{9,15},{10,... | collective-permute-start | bytes 786440 | tf_op jit(solution)/shard_map/ppermute | solution.py:484
  94.2 15.5 %copy-start.2 = (bf16[2048,256]{1,0:T(8,128)(2,1)}, bf16[2048,256]{1,0:T(8,128)(2,1)S(1)}, u32[]{:S(2)}) copy-start(bf16[2048,256]{1,0:T(8,128)(2,1)S(1)} %get-tuple-element.11.own) | copy-start | bytes 3145732
  94.2 15.5 %copy-start.24 = (bf16[8,256,128]{2,1,0:T(8,128)(2,1)}, bf16[8,256,128]{2,1,0:T(8,128)(2,1)S(1)}, u32[]{:S(2)}) copy-start(bf16[8,256,128]{2,1,0:T(8,128)(2,1)S(1)} %get-tuple-element.12.refs_11_) | copy-start | bytes 1572868
  94.2 15.5 %copy-start.28 = (bf16[2048,128]{1,0:T(8,128)(2,1)}, bf16[2048,128]{1,0:T(8,128)(2,1)S(1)}, u32[]{:S(2)}) copy-start(bf16[2048,128]{1,0:T(8,128)(2,1)S(1)} %get-tuple-element.10.queries) | copy-start | bytes 1572868
  94.3 18.8 %collective-permute-start.29 = (bf16[1152,256]{1,0:T(8,128)(2,1)S(1)}, bf16[1152,256]{1,0:T(8,128)(2,1)S(1)}, u32[]{:S(2)}, u32[]{:S(2)}) collective-permute-start(bf16[1152,256]{1,0:T(8,128)(2,1)S(1)} %get-tuple-element.18), channel_id=1, source_target_pairs={{0,8},{8,16},{16,24},{24,32},{32,40},{40,48},{48,56},{56,64},{64,7... | collective-permute-start | bytes 1769480 | tf_op jit(solution)/shard_map/ppermute | solution.py:480
  106.2 14.9 %collective-permute-start.30 = (bf16[1152,256]{1,0:T(8,128)(2,1)S(1)}, bf16[1152,256]{1,0:T(8,128)(2,1)S(1)}, u32[]{:S(2)}, u32[]{:S(2)}) collective-permute-start(bf16[1152,256]{1,0:T(8,128)(2,1)S(1)} %get-tuple-element.17), channel_id=1, source_target_pairs={{8,0},{16,8},{24,16},{32,24},{40,32},{48,40},{56,48},{64,56},{72,6... | collective-permute-start | bytes 1769480 | tf_op jit(solution)/shard_map/ppermute | solution.py:480
  108.2 83.1 %collective-permute-start.13 = (bf16[8,144,1024]{2,1,0:T(8,128)(2,1)}, bf16[8,144,1024]{2,1,0:T(8,128)(2,1)}, u32[]{:S(2)}, u32[]{:S(2)}) collective-permute-start(bf16[8,144,1024]{2,1,0:T(8,128)(2,1)} %fusion.1.refs_0_), channel_id=1, source_target_pairs={{0,8},{8,0},{16,24},{24,16},{32,40},{40,32},{48,56},{56,48},{64,72... | collective-permute-start | bytes 7077896 | tf_op jit(solution)/shard_map/ppermute | solution.py:484
  109.7 27.4 %collective-permute-start.11 = (bf16[4,144,1024]{2,1,0:T(8,128)(2,1)S(1)}, bf16[4,144,1024]{2,1,0:T(8,128)(2,1)}, u32[]{:S(2)}, u32[]{:S(2)}) collective-permute-start(bf16[4,144,1024]{2,1,0:T(8,128)(2,1)S(1)} %slice.84), channel_id=1, source_target_pairs={{0,16},{8,24},{16,32},{24,40},{32,48},{40,56},{48,0},{56,8},{64,80... | collective-permute-start | bytes 3538952 | tf_op jit(solution)/shard_map/ppermute | solution.py:484
  109.9 81.3 %collective-permute-start.14 = (bf16[8,144,1024]{2,1,0:T(8,128)(2,1)}, bf16[8,144,1024]{2,1,0:T(8,128)(2,1)}, u32[]{:S(2)}, u32[]{:S(2)}) collective-permute-start(bf16[8,144,1024]{2,1,0:T(8,128)(2,1)} %collective-permute-done.9.refs_1_), channel_id=1, source_target_pairs={{0,8},{8,0},{16,24},{24,16},{32,40},{40,32},{48,56},{56,48},{64,72... | collective-permute-start | bytes 7077896 | tf_op jit(solution)/shard_map/ppermute | solution.py:484
  111.9 79.4 %copy-start.30 = (f32[1024]{0:T(1024)S(1)}, f32[1024]{0:T(1024)}, u32[]{:S(2)}) copy-start(f32[1024]{0:T(1024)} %param.18) | copy-start | bytes 12292
  113.9 77.4 %collective-permute-start.15 = (bf16[8,144,1024]{2,1,0:T(8,128)(2,1)}, bf16[8,144,1024]{2,1,0:T(8,128)(2,1)}, u32[]{:S(2)}, u32[]{:S(2)}) collective-permute-start(bf16[8,144,1024]{2,1,0:T(8,128)(2,1)} %collective-permute-done.10.refs_2_), channel_id=1, source_target_pairs={{0,8},{8,0},{16,24},{24,16},{32,40},{40,32},{48,56},{56,48},{64,72... | collective-permute-start | bytes 7077896 | tf_op jit(solution)/shard_map/ppermute | solution.py:484
  122.0 24.5 %collective-permute-start.12 = (bf16[4,144,1024]{2,1,0:T(8,128)(2,1)S(1)}, bf16[4,144,1024]{2,1,0:T(8,128)(2,1)}, u32[]{:S(2)}, u32[]{:S(2)}) collective-permute-start(bf16[4,144,1024]{2,1,0:T(8,128)(2,1)S(1)} %slice.85), channel_id=1, source_target_pairs={{0,48},{8,56},{16,0},{24,8},{32,16},{40,24},{48,32},{56,40},{64,11... | collective-permute-start | bytes 3538952 | tf_op jit(solution)/shard_map/ppermute | solution.py:484
  137.1 54.2 %collective-permute-start.16 = (bf16[4,144,1024]{2,1,0:T(8,128)(2,1)}, bf16[4,144,1024]{2,1,0:T(8,128)(2,1)}, u32[]{:S(2)}, u32[]{:S(2)}) collective-permute-start(bf16[4,144,1024]{2,1,0:T(8,128)(2,1)} %collective-permute-done.11.refs_3_), channel_id=1, source_target_pairs={{0,8},{8,0},{16,24},{24,16},{32,40},{40,32},{48,56},{56,48},{64,72... | collective-permute-start | bytes 3538952 | tf_op jit(solution)/shard_map/ppermute | solution.py:484
  146.4 44.8 %collective-permute-start.17 = (bf16[4,144,1024]{2,1,0:T(8,128)(2,1)}, bf16[4,144,1024]{2,1,0:T(8,128)(2,1)}, u32[]{:S(2)}, u32[]{:S(2)}) collective-permute-start(bf16[4,144,1024]{2,1,0:T(8,128)(2,1)} %collective-permute-done.12.refs_4_), channel_id=1, source_target_pairs={{0,8},{8,0},{16,24},{24,16},{32,40},{40,32},{48,56},{56,48},{64,72... | collective-permute-start | bytes 3538952 | tf_op jit(solution)/shard_map/ppermute | solution.py:484
  177.7 13.6 %all-to-all-start = ((bf16[8,256,128]{2,1,0:T(8,128)(2,1)}), bf16[8,256,128]{2,1,0:T(8,128)(2,1)}, u32[]{:S(2)}, u32[]{:S(2)}) async-start(bf16[8,256,128]{2,1,0:T(8,128)(2,1)} %bitcast.50), calls=%async_computation | async-start | bytes 1048576 | tf_op jit(solution)/shard_map/all_to_all | solution.py:558
  192.3 34.1 %copy-start.34 = (s32[64,2]{0,1:T(2,128)S(1)}, s32[64,2]{0,1:T(2,128)}, u32[]{:S(2)}) copy-start(s32[64,2]{0,1:T(2,128)} %param.21) | copy-start | bytes 1540
  217.7 10.4 %collective-permute-start.31 = (bf16[8,128,128]{2,1,0:T(8,128)(2,1)}, bf16[8,128,128]{2,1,0:T(8,128)(2,1)S(1)}, u32[]{:S(2)}, u32[]{:S(2)}) collective-permute-start(bf16[8,128,128]{2,1,0:T(8,128)(2,1)} %bitcast.32), channel_id=1, source_target_pairs={{0,8},{8,16},{16,24},{24,32},{32,40},{40,48},{48,56},{56,64},{64,7... | collective-permute-start | bytes 786440 | tf_op jit(solution)/shard_map/ppermute | solution.py:480
  224.5 11.6 %collective-permute-start.32 = (bf16[8,128,128]{2,1,0:T(8,128)(2,1)}, bf16[8,128,128]{2,1,0:T(8,128)(2,1)}, u32[]{:S(2)}, u32[]{:S(2)}) collective-permute-start(bf16[8,128,128]{2,1,0:T(8,128)(2,1)} %bitcast.34), channel_id=1, source_target_pairs={{8,0},{16,8},{24,16},{32,24},{40,32},{48,40},{56,48},{64,56},{72,6... | collective-permute-start | bytes 786440 | tf_op jit(solution)/shard_map/ppermute | solution.py:480
  239.3 22.4 %copy-start.32 = (f32[128]{0:T(128)S(1)}, f32[128]{0:T(128)}, u32[]{:S(2)}) copy-start(f32[128]{0:T(128)} %param.23) | copy-start | bytes 1540
  (21 other events, 23.6 us)

commit v2 on v1

--- a/solution.py
+++ b/solution.py
@@ -27,6 +27,10 @@
 
 def dot(a, b):
     return jnp.dot(a, b, preferred_element_type=F32)
+
+
+def cost(flops, moved, powers=0):
+    return pl.CostEstimate(flops=flops, bytes_accessed=moved, transcendentals=powers)
 
 
 ANY = pl.BlockSpec(memory_space=pl.ANY)
@@ -87,7 +91,8 @@
                 pltpu.SemaphoreType.DMA((3,)),
             ],
         ),
-        compiler_params=params(24),
+        compiler_params=params(56),
+        cost_estimate=cost(540_000_000, 8_000_000),
         name="encode",
     )(index, *shaped, weights)
 
@@ -158,9 +163,10 @@
             ),
             scratch_shapes=[pltpu.VMEM((D, 3 * BLOCK), BF)],
         ),
-        compiler_params=params(24),
+        compiler_params=params(56),
+        cost_estimate=cost(1_600_000_000, 7_000_000),
         name="project",
-    )(order, *slots, gain.reshape(8, 1, BLOCK), weights.reshape(8, BLOCK, 3 * BLOCK))
+    )(order, *slots, gain.reshape(8, 1, BLOCK), weights)
 
 
 TILE = 256
@@ -249,7 +255,8 @@
                 pltpu.SemaphoreType.DMA((6,)),
             ],
         ),
-        compiler_params=params(32),
+        compiler_params=params(56),
+        cost_estimate=cost(10_700_000_000, 4_000_000, 10_500_000),
         name="attend",
     )(edges, queries, low, own, high)
 
@@ -358,7 +365,8 @@
                 pltpu.SemaphoreType.DMA((3, 20)),
             ],
         ),
-        compiler_params=params(48),
+        compiler_params=params(56),
+        cost_estimate=cost(4_800_000_000, 20_000_000, 1_100_000),
         name="forward",
     )(table, *parts, context, share, gain.reshape(1, D))
 
@@ -385,22 +393,23 @@
             c.wait()
 
     slots = weights.shape[1]
-    ones = jnp.ones((2 * EACH, BLOCK), BF)
-    row = lax.broadcasted_iota(jnp.int32, (2 * EACH, BLOCK), 0)
-    held = jnp.zeros((2 * EACH, BLOCK), F32)
+    ones = jnp.ones((BLOCK, BLOCK), BF)
+    row = lax.broadcasted_iota(jnp.int32, (BLOCK, BLOCK), 0)
+    column = lax.broadcasted_iota(jnp.int32, (BLOCK, BLOCK), 1)
+    made = []
     for b in range(EACH):
         left = jnp.concatenate([weights[b, k] for k in range(slots)], axis=1)
         right = jnp.concatenate(
             [source[index[step * EACH + b, k]] for k in range(slots)], axis=0
         )
-        made = dot(left, right)
-        back[b * BLOCK : (b + 1) * BLOCK] = made
-        plain = lax.dot_general(ones, made.astype(BF), NT, preferred_element_type=F32)
-        square = lax.dot_general(
-            ones, (made * made).astype(BF), NT, preferred_element_type=F32
-        )
-        held = jnp.where(row == b, plain, jnp.where(row == EACH + b, square, held))
-    sums[0] = held.astype(BF)
+        made.append(dot(left, right))
+        back[b * BLOCK : (b + 1) * BLOCK] = made[b]
+    kinds = [m.astype(BF) for m in made] + [(m * m).astype(BF) for m in made]
+    held = [
+        jnp.sum(jnp.where(row == column, dot(k, ones), 0.0), axis=0, keepdims=True)
+        for k in kinds
+    ]
+    sums[0] = jnp.concatenate(held, axis=0).astype(BF)
 
 
 def decode(index, low, own, high, weights):
@@ -432,7 +441,8 @@
                 pltpu.SemaphoreType.DMA((3,)),
             ],
         ),
-        compiler_params=params(24),
+        compiler_params=params(56),
+        cost_estimate=cost(540_000_000, 10_000_000),
         name="decode",
     )(index, low, own, high, weights)
 
@@ -471,7 +481,8 @@
             ],
             out_specs=tile,
         ),
-        compiler_params=params(24),
+        compiler_params=params(32),
+        cost_estimate=cost(540_000_000, 8_000_000),
         name="finish",
     )(sums, back, state, gain.reshape(1, BLOCK))
 
@@ -501,16 +512,18 @@
     return (i // 8) * 8 + ((i // 2 + by) % 4) * 2 + i % 2
 
 
-def gathered_weights(packed):
-    s = head_ring(packed)
-    mine = jnp.stack(
-        s[:6] + (jnp.concatenate(s[6:8], axis=0), jnp.concatenate(s[8:10], axis=0))
-    )
-    up = lambda v: among(v, "seq", 16, lambda i: along_z(i, 1))
-    down = lambda v: among(v, "seq", 16, lambda i: along_z(i, -1))
-    a, b = up(mine), down(mine)
-    here = [mine, a, b, up(a[:4]), down(b[4:])]
-    return here + [among(v, "seq", 16, lambda i: i ^ 1) for v in here]
+UP = lambda v: among(v, "seq", 16, lambda i: along_z(i, 1))
+DOWN = lambda v: among(v, "seq", 16, lambda i: along_z(i, -1))
+TWIN = lambda v: among(v, "seq", 16, lambda i: i ^ 1)
+NORTH = lambda v: among(v, "head", 8, lambda i: (i + 2) % 8)
+SOUTH = lambda v: among(v, "head", 8, lambda i: (i - 2) % 8)
+
+
+def weights_of_heads(packed):
+    x = jnp.stack([packed, among(packed, "head", 8, lambda i: i ^ 1)])
+    a, b = NORTH(x), SOUTH(x)
+    far = jnp.stack([NORTH(a[0]), SOUTH(b[1])])
+    return x, a, b, far
 
 
 def on_device(
@@ -534,13 +547,20 @@
     mesh_rows = mesh_blocks * BLOCK
     grid_blocks = grid_state.shape[0] // BLOCK
     rim = mesh_blocks * BLOCK
-    low = shifted(grid_state[-rim:], 1)
-    high = shifted(grid_state[:rim], -1)
+    last, first, expand, shrink, outward, inward = lax.optimization_barrier(
+        (
+            grid_state[-rim:], grid_state[:rim],
+            expand_weights, shrink_weights, project_out, project_in,
+        )
+    )
+    low = shifted(last, 1)
+    high = shifted(first, -1)
 
     position = band % 8
-    parts = gathered_weights(
-        pack_weights(position, expand_weights, shrink_weights, project_out)
-    )
+    packed = pack_weights(position, expand, shrink, outward)
+    inward = inward.reshape(8, BLOCK, 3 * BLOCK)
+    low, high, inward = lax.optimization_barrier((low, high, inward))
+    mine = jnp.concatenate(weights_of_heads(packed), axis=0)
 
     mesh_start = encode(
         encode_index - (band * grid_blocks - mesh_blocks), low, grid_state, high, encode_weights
@@ -550,11 +570,16 @@
     order = jnp.stack(
         [me, partner] + [(v + by) % 8 for by in (6, 2, 4) for v in (me, partner)]
     ).astype(jnp.int32)
-    queries, keys_values, share = project(order, slots, first_gain, project_in)
+    queries, keys_values, share = project(order, slots, first_gain, inward)
     below = shifted(keys_values[mesh_rows - REACH :], 1)
     above = shifted(keys_values[:REACH], -1)
+    up, down = UP(mine), DOWN(mine)
+    far_up, far_down = UP(up[:4]), DOWN(down[4:])
     edges = jnp.stack([band == 0, band == bands - 1]).astype(jnp.int32)
     context = attend(edges, queries, below, keys_values, above)
+    context, far_up, far_down = lax.optimization_barrier((context, far_up, far_down))
+    here = [mine, up, down, far_up, far_down]
+    parts = here + [TWIN(v) for v in here]
     context = lax.all_to_all(
         context.reshape(8, mesh_rows // 8, BLOCK), "head", 0, 0, tiled=True
     )

time: 268 us -> 237 us (0.88)
  local copies, waits for them, and re-layouts: 47.3 us -> 26.9 us
  starting transfers between devices: 56 us -> 44.3 us
  Pallas kernels: 68.7 us -> 75.7 us
  waiting for transfers between devices: 70.1 us -> 65 us
    unnamed x77 -> x45, local copies, waits for them, and re-layouts: 29.3 us -> 9.05 us
    ppermute x6, starting transfers between devices: 28.8 us -> 18 us  [shifted(): lax.ppermute(value, 'seq', [(i, i + by) for i in range(16) if 0 <= i + by...]
    reshape x2 -> x0, local copies, waits for them, and re-layouts: 6 us -> none  [project(): weights.reshape(8, BLOCK, 3 * BLOCK)]
    ppermute x27 -> x23, waiting for transfers between devices: 41.9 us -> 36.6 us  [among(): return lax.ppermute(value, axis, [(i, to(i)) for i in range(count)])]
    pallas_call x1, Pallas kernels: 4.38 us -> 9.44 us  [encode(): pl.pallas_call(encode_kernel, out_shape=jax.ShapeDtypeStruct((count * BLO...]
    optimization_barrier x0 -> x2, local copies, waits for them, and re-layouts: none -> 3.84 us  [the longest x1 2.44 us: on_device(): low, high, inward = lax.optimization_barrier((low, high, inward))]
    pallas_call x1, Pallas kernels: 13.8 us -> 10.1 us  [decode(): pl.pallas_call(decode_kernel, out_shape=(jax.ShapeDtypeStruct((count * BL...]
    ppermute x27 -> x23, starting transfers between devices: 23 us -> 21.6 us  [among(): return lax.ppermute(value, axis, [(i, to(i)) for i in range(count)])]
  transfers between devices with their start and end apart: 34 -> 30, of which waited for: 15 -> 11; matrix products, arithmetic and copies ran while one was open for 9% -> 9% of each run, Pallas kernels for 15% -> 21%
where the time goes in v2:
time: 237 us; the launch traced here: 235 us
  Pallas kernels  75.7 us (32%)
  waiting for transfers between devices  65 us (27%)
  starting transfers between devices  44.3 us (19%)
  local copies, waits for them, and re-layouts  26.9 us (11%)
  blocking collectives  20.3 us (9%)
  other arithmetic  2.74 us (1%)
    ppermute x23, waiting for transfers between devices, among(): return lax.ppermute(value, axis, [(i, to(i)) for i in range(count)])  36.6 us
    pallas_call x1, Pallas kernels, attend(): pl.pallas_call(attend_kernel, out_shape=jax.ShapeDtypeStruct((rows, BLOCK...  28.5 us
    ppermute x23, starting transfers between devices, among(): return lax.ppermute(value, axis, [(i, to(i)) for i in range(count)])  21.6 us
    ppermute x6, waiting for transfers between devices, shifted(): lax.ppermute(value, 'seq', [(i, i + by) for i in range(16) if 0 <= i + by...  19.6 us
    ppermute x6, starting transfers between devices, shifted(): lax.ppermute(value, 'seq', [(i, i + by) for i in range(16) if 0 <= i + by...  18 us
    pallas_call x1, Pallas kernels, forward(): pl.pallas_call(forward_kernel, out_shape=jax.ShapeDtypeStruct((8, rows, B...  12.3 us
    all_to_all x1, blocking collectives, on_device(): mesh_end = lax.all_to_all(mesh_end, 'head', 0, 0, tiled=True)  11.8 us
    pallas_call x1, Pallas kernels, project(): pl.pallas_call(project_kernel, out_shape=(jax.ShapeDtypeStruct((rows, BLO...  10.5 us
  transfers between devices with their start and end apart: 30, of which 11 were waited for; matrix products, arithmetic and copies ran while one was open for 9% of the time, Pallas kernels for 21%

profile of v2, /device:TPU:97, one launch (start us, length us, event | category | flops | bytes accessed | tf_op | source)
XLA Modules:
  0.0 235.3 jit_solution(161247035928849335)
XLA Ops:
  0.0 2.4 %fusion.1 = (bf16[2048,128]{1,0:T(8,128)(2,1)}, bf16[2048,128]{1,0:T(8,128)(2,1)}) fusion(bf16[8192,128]{1,0:T(8,128)(2,1)} %state.1), kind=kLoop, calls=%fused_computation.18 | loop fusion | bytes 2097152 | tf_op jit(solution)/shard_map/slice | solution.py:552
  2.4 0.9 constant_dynamic-slice_fusion
  4.1 1.3 collective-permute-start
  5.4 3.8 %collective-permute-start.7 = (bf16[2048,128]{1,0:T(8,128)(2,1)}, bf16[2048,128]{1,0:T(8,128)(2,1)}, u32[]{:S(2)}, u32[]{:S(2)}) collective-permute-start(bf16[2048,128]{1,0:T(8,128)(2,1)} %get-tuple-element.25), channel_id=1, source_target_pairs={{0,8},{8,16},{16,24},{24,32},{32,40},{40,48},{48,56},{56,64},{64,7... | collective-permute-start | bytes 1572872 | tf_op jit(solution)/shard_map/ppermute | solution.py:491
  9.3 1.9 collective-permute-start.8
  11.2 1.4 copy.24
  12.6 1.1 copy.26
  13.8 1.4 collective-permute-start.1
  15.8 1.5 collective-permute-start.2
  18.7 5.0 %collective-permute-done.8 = bf16[2048,128]{1,0:T(8,128)(2,1)} collective-permute-done((bf16[2048,128]{1,0:T(8,128)(2,1)}, bf16[2048,128]{1,0:T(8,128)(2,1)}, u32[]{:S(2)}, u32[]{:S(2)}) %collective-permute-start.8) | collective-permute-done | bytes 524320 | tf_op jit(solution)/shard_map/ppermute | solution.py:491
  23.7 9.4 %encode.1.s0 = bf16[2048,128]{1,0:T(8,128)(2,1)} custom-call(s32[16,8]{1,0:T(8,128)} %broadcast_subtract_fusion.1.index, bf16[16,128,128]{2,1,0:T(8,128)(2,1)} %bitcast.24.low, bf16[64,128,128]{2,1,0:T(8,128)(2,1)} %bitcast.46, bf16[16,128,128]{2,1,0:T(8,128)(2,1)} %bitcast.26.high, bf16[16,8,128,128]{3,2,1,0:T(8,128)(2,1)} %weights.2), custom_call_target="tpu_custom_call" | custom-call | flops 540000000 | bytes 8000000 | tf_op jit(solution)/shard_map/encode/pallas_call | solution.py:76
  33.2 1.4 collective-permute-start.10
  34.6 1.4 collective-permute-start.3
  36.0 1.4 collective-permute-start.4
  37.5 0.9 constant_dynamic-update-slice_fusion.1
  38.4 0.9 constant_dynamic-update-slice_fusion
  39.2 13.9 %collective-permute-done.3 = bf16[144,1024]{1,0:T(8,128)(2,1)S(1)} collective-permute-done((bf16[144,1024]{1,0:T(8,128)(2,1)S(1)}, bf16[144,1024]{1,0:T(8,128)(2,1)S(1)}, u32[]{:S(2)}, u32[]{:S(2)}) %collective-permute-start.3) | collective-permute-done | bytes 294944 | tf_op jit(solution)/shard_map/ppermute | solution.py:495
  54.6 1.5 collective-permute-start.6
  56.4 1.2 collective-permute-start.11
  57.6 1.5 collective-permute-start.13
  59.1 11.0 %collective-permute-done.12.s4 = bf16[2048,128]{1,0:T(8,128)(2,1)S(1)} collective-permute-done((bf16[2048,128]{1,0:T(8,128)(2,1)S(1)}, bf16[2048,128]{1,0:T(8,128)(2,1)S(1)}, u32[]{:S(2)}, u32[]{:S(2)}) %collective-permute-start.12) | collective-permute-done | bytes 524320 | tf_op jit(solution)/shard_map/ppermute | solution.py:495
  71.4 2.1 collective-permute-start.15
  74.2 7.1 %collective-permute-done.13.s5 = bf16[2048,128]{1,0:T(8,128)(2,1)S(1)} collective-permute-done((bf16[2048,128]{1,0:T(8,128)(2,1)S(1)}, bf16[2048,128]{1,0:T(8,128)(2,1)S(1)}, u32[]{:S(2)}, u32[]{:S(2)}) %collective-permute-start.13) | collective-permute-done | bytes 524320 | tf_op jit(solution)/shard_map/ppermute | solution.py:495
  83.0 2.6 %collective-permute-start.17 = (bf16[1024,128]{1,0:T(8,128)(2,1)}, bf16[1024,128]{1,0:T(8,128)(2,1)}, u32[]{:S(2)}, u32[]{:S(2)}) collective-permute-start(bf16[1024,128]{1,0:T(8,128)(2,1)} %slice.77), channel_id=1, source_target_pairs={{0,6},{1,7},{2,0},{3,1},{4,2},{5,3},{6,4},{7,5},{8,14},{9,15},{10,... | collective-permute-start | bytes 786440 | tf_op jit(solution)/shard_map/ppermute | solution.py:495
  86.1 2.4 %copy.25.weights = bf16[8,128,384]{2,1,0:T(8,128)(2,1)} copy(bf16[8,128,384]{1,0,2:T(8,128)(2,1)} %bitcast.49) | data formatting | bytes 1572864 | tf_op jit(solution)/shard_map/optimization_barrier | solution.py:562
  88.6 1.9 collective-permute-done.16.lo7
  90.5 2.1 collective-permute-done.17.hi7
  92.6 10.5 %project.1 = (bf16[2048,128]{1,0:T(8,128)(2,1)}, bf16[2048,256]{1,0:T(8,128)(2,1)}, bf16[8,256,128]{2,1,0:T(8,128)(2,1)}) custom-call(s32[8]{0:T(128)} %stack.101.order, bf16[2048,128]{1,0:T(8,128)(2,1)} %encode.1.s0, bf16[2048,128]{1,0:T(8,128)(2,1)} %copy-done.17, bf16[2048,128]{1,0:T(8,128)(2,1)} %copy-done.9, bf16[2048,128]{1,0:T(8,128)(2,1)} %copy-done.11, ...), custom_call_target="tpu_custom_call" | custom-call | flops 1600000000 | bytes 7000000 | tf_op jit(solution)/shard_map/project/pallas_call | solution.py:146
  103.1 1.3 fusion.2
  104.4 3.2 %collective-permute-start.18 = (bf16[1152,256]{1,0:T(8,128)(2,1)S(1)}, bf16[1152,256]{1,0:T(8,128)(2,1)S(1)}, u32[]{:S(2)}, u32[]{:S(2)}) collective-permute-start(bf16[1152,256]{1,0:T(8,128)(2,1)S(1)} %get-tuple-element.42), channel_id=1, source_target_pairs={{0,8},{8,16},{16,24},{24,32},{32,40},{40,48},{48,56},{56,64},{64,7... | collective-permute-start | bytes 1769480 | tf_op jit(solution)/shard_map/ppermute | solution.py:491
  107.6 1.9 collective-permute-start.19
  109.6 1.2 slice.78
  110.9 2.4 %slice.79 = bf16[4,144,1024]{2,1,0:T(8,128)(2,1)} slice(bf16[8,144,1024]{2,1,0:T(8,128)(2,1)} %collective-permute-done.6.refs_2_), slice={[4:8], [0:144], [0:1024]} | slice | bytes 2359296 | tf_op jit(solution)/shard_map/slice | solution.py:577
  113.3 1.3 collective-permute-start.21
  114.6 1.4 collective-permute-start.22
  116.6 5.9 %collective-permute-done.19.high = bf16[1152,256]{1,0:T(8,128)(2,1)S(1)} collective-permute-done((bf16[1152,256]{1,0:T(8,128)(2,1)S(1)}, bf16[1152,256]{1,0:T(8,128)(2,1)S(1)}, u32[]{:S(2)}, u32[]{:S(2)}) %collective-permute-start.19) | collective-permute-done | bytes 589856 | tf_op jit(solution)/shard_map/ppermute | solution.py:491
  124.0 28.5 %attend.1 = bf16[2048,128]{1,0:T(8,128)(2,1)} custom-call(s32[2]{0:T(128)} %add_convert_fusion.edges, bf16[2048,128]{1,0:T(8,128)(2,1)} %get-tuple-element.31.queries, bf16[1152,256]{1,0:T(8,128)(2,1)} %copy-done.15, bf16[2048,256]{1,0:T(8,128)(2,1)} %get-tuple-element.32.own, bf16[1152,256]{1,0:T(8,128)(2,1)} %copy-done.16), custom_call_target="tpu_custom_call" | custom-call | flops 10700000256 | bytes 4000000 | tf_op jit(solution)/shard_map/attend/pallas_call | solution.py:243
  153.2 4.7 %all-to-all-start = ((bf16[8,256,128]{2,1,0:T(8,128)(2,1)}), bf16[8,256,128]{2,1,0:T(8,128)(2,1)}, u32[]{:S(2)}, u32[]{:S(2)}) async-start(bf16[8,256,128]{2,1,0:T(8,128)(2,1)} %bitcast.52), calls=%async_computation | async-start | bytes 1048576 | tf_op jit(solution)/shard_map/all_to_all | solution.py:583
  158.6 8.8 %all-to-all-done.refs_10_ = bf16[8,256,128]{2,1,0:T(8,128)(2,1)} async-done(((bf16[8,256,128]{2,1,0:T(8,128)(2,1)}), bf16[8,256,128]{2,1,0:T(8,128)(2,1)}, u32[]{:S(2)}, u32[]{:S(2)}) %all-to-all-start) | async-done | bytes 524320 | tf_op jit(solution)/shard_map/all_to_all | solution.py:583
  167.4 12.3 %forward.1 = bf16[8,256,128]{2,1,0:T(8,128)(2,1)} custom-call(s32[18]{0:T(128)} %concatenate.14.table, bf16[8,144,1024]{2,1,0:T(8,128)(2,1)} %bitcast_dynamic-update-slice_fusion.refs_0_, bf16[8,144,1024]{2,1,0:T(8,128)(2,1)} %copy-done.4, bf16[8,144,1024]{2,1,0:T(8,128)(2,1)} %collective-permute-done.6.refs_2_, ...), custom_call_target="tpu_custom_call" | custom-call | flops 4800000000 | bytes 20000000 | tf_op jit(solution)/shard_map/forward/pallas_call | solution.py:352
  179.7 11.8 %all_to_all.15 = bf16[8,256,128]{2,1,0:T(8,128)(2,1)S(1)} all-to-all(bf16[8,256,128]{2,1,0:T(8,128)(2,1)} %forward.1), channel_id=1, replica_groups=mesh['seq'=16,'head'=8] {'head'}, dimensions={0} | all-to-all | bytes 1048576 | tf_op jit(solution)/shard_map/all_to_all | solution.py:594
  191.5 5.2 %collective-permute-start.27 = (bf16[8,128,128]{2,1,0:T(8,128)(2,1)S(1)}, bf16[8,128,128]{2,1,0:T(8,128)(2,1)S(1)}, u32[]{:S(2)}, u32[]{:S(2)}) collective-permute-start(bf16[8,128,128]{2,1,0:T(8,128)(2,1)S(1)} %bitcast.54), channel_id=1, source_target_pairs={{0,8},{8,16},{16,24},{24,32},{32,40},{40,48},{48,56},{56,64},{64,7... | collective-permute-start | bytes 786440 | tf_op jit(solution)/shard_map/ppermute | solution.py:491
  196.7 1.9 collective-permute-start.28
  200.0 8.0 %collective-permute-done.28.high = bf16[8,128,128]{2,1,0:T(8,128)(2,1)S(1)} collective-permute-done((bf16[8,128,128]{2,1,0:T(8,128)(2,1)S(1)}, bf16[8,128,128]{2,1,0:T(8,128)(2,1)S(1)}, u32[]{:S(2)}, u32[]{:S(2)}) %collective-permute-start.28) | collective-permute-done | bytes 262176 | tf_op jit(solution)/shard_map/ppermute | solution.py:491
  208.8 10.1 %decode.1 = (f32[8192,128]{1,0:T(8,128)}, bf16[8,16,128]{2,1,0:T(8,128)(2,1)}) custom-call(s32[64,2]{1,0:T(8,128)} %broadcast_subtract_fusion.index, bf16[8,128,128]{2,1,0:T(8,128)(2,1)} %copy-done.7, bf16[16,128,128]{2,1,0:T(8,128)(2,1)} %bitcast.48, bf16[8,128,128]{2,1,0:T(8,128)(2,1)} %copy-done.8, bf16[64,2,128,128]{3,2,1,0:T(8,128)(2,1)} %weights.3), custom_call_target="tpu_custom_call" | custom-call | flops 540000000 | bytes 10000000 | tf_op jit(solution)/shard_map/decode/pallas_call | solution.py:420
  219.7 8.5 %all_to_all.16.sums = bf16[8,8,16,128]{3,2,1,0:T(8,128)(2,1)S(1)} all-to-all(bf16[8,8,16,128]{3,2,1,0:T(8,128)(2,1)S(1)} %broadcast_in_dim.3), channel_id=1, replica_groups=mesh['seq'=16,'head'=8] {'head'}, dimensions={0} | all-to-all | bytes 524288 | tf_op jit(solution)/shard_map/all_to_all | solution.py:604
  228.2 2.2 copy-done.2
  230.4 4.9 %finish.1 = bf16[8192,128]{1,0:T(8,128)(2,1)} custom-call(bf16[8,8,16,128]{3,2,1,0:T(8,128)(2,1)S(1)} %all_to_all.16.sums, f32[8192,128]{1,0:T(8,128)S(1)} %copy-done.2, bf16[8192,128]{1,0:T(8,128)(2,1)S(1)} %copy-done.1, f32[1,128]{1,0:T(1,128)S(1)} %bitcast.47), custom_call_target="tpu_custom_call" | custom-call | flops 540000000 | bytes 8000000 | tf_op jit(solution)/shard_map/finish/pallas_call | solution.py:471
  (91 shorter events, 15.8 us)
Async XLA Ops:
  0.0 3.3 %copy-start = (bf16[512,1024]{1,0:T(8,128)(2,1)S(1)}, bf16[512,1024]{1,0:T(8,128)(2,1)}, u32[]{:S(2)}) copy-start(bf16[512,1024]{1,0:T(8,128)(2,1)} %param.20) | copy-start | bytes 3145732
  2.4 11.3 %copy-start.13 = (s32[16,8]{0,1:T(8,128)S(1)}, s32[16,8]{0,1:T(8,128)}, u32[]{:S(2)}) copy-start(s32[16,8]{0,1:T(8,128)} %param.13) | copy-start | bytes 1540
  4.1 9.6 %collective-permute-start = (bf16[144,1024]{1,0:T(8,128)(2,1)S(1)}, bf16[144,1024]{1,0:T(8,128)(2,1)S(1)}, u32[]{:S(2)}, u32[]{:S(2)}) collective-permute-start(bf16[144,1024]{1,0:T(8,128)(2,1)S(1)} %get-tuple-element.48), channel_id=1, source_target_pairs={{0,1},{1,0},{2,3},{3,2},{4,5},{5,4},{6,7},{7,6},{8,9},{9,8},{10,11... | collective-permute-start | bytes 884744 | tf_op jit(solution)/shard_map/ppermute | solution.py:495
  5.4 13.3 %collective-permute-start.7 = (bf16[2048,128]{1,0:T(8,128)(2,1)}, bf16[2048,128]{1,0:T(8,128)(2,1)}, u32[]{:S(2)}, u32[]{:S(2)}) collective-permute-start(bf16[2048,128]{1,0:T(8,128)(2,1)} %get-tuple-element.25), channel_id=1, source_target_pairs={{0,8},{8,16},{16,24},{24,32},{32,40},{40,48},{48,56},{56,64},{64,7... | collective-permute-start | bytes 1572872 | tf_op jit(solution)/shard_map/ppermute | solution.py:491
  9.3 14.4 %collective-permute-start.8 = (bf16[2048,128]{1,0:T(8,128)(2,1)}, bf16[2048,128]{1,0:T(8,128)(2,1)}, u32[]{:S(2)}, u32[]{:S(2)}) collective-permute-start(bf16[2048,128]{1,0:T(8,128)(2,1)} %get-tuple-element.26), channel_id=1, source_target_pairs={{8,0},{16,8},{24,16},{32,24},{40,32},{48,40},{56,48},{64,56},{72,6... | collective-permute-start | bytes 1572872 | tf_op jit(solution)/shard_map/ppermute | solution.py:491
  13.8 20.8 %collective-permute-start.1 = (bf16[2,144,1024]{2,1,0:T(8,128)(2,1)S(1)}, bf16[2,144,1024]{2,1,0:T(8,128)(2,1)S(1)}, u32[]{:S(2)}, u32[]{:S(2)}) collective-permute-start(bf16[2,144,1024]{2,1,0:T(8,128)(2,1)S(1)} %pad_maximum_fusion), channel_id=1, source_target_pairs={{0,2},{1,3},{2,4},{3,5},{4,6},{5,7},{6,0},{7,1},{8,10},{9,11},{10,... | collective-permute-start | bytes 1769480 | tf_op jit(solution)/shard_map/ppermute | solution.py:495
  15.8 20.2 %collective-permute-start.2 = (bf16[2,144,1024]{2,1,0:T(8,128)(2,1)S(1)}, bf16[2,144,1024]{2,1,0:T(8,128)(2,1)S(1)}, u32[]{:S(2)}, u32[]{:S(2)}) collective-permute-start(bf16[2,144,1024]{2,1,0:T(8,128)(2,1)S(1)} %pad_maximum_fusion), channel_id=1, source_target_pairs={{0,6},{1,7},{2,0},{3,1},{4,2},{5,3},{6,4},{7,5},{8,14},{9,15},{10,... | collective-permute-start | bytes 1769480 | tf_op jit(solution)/shard_map/ppermute | solution.py:495
  33.1 22.9 %copy-start.6 = (bf16[2048,128]{1,0:T(8,128)(2,1)S(1)}, bf16[2048,128]{1,0:T(8,128)(2,1)}, u32[]{:S(2)}) copy-start(bf16[2048,128]{1,0:T(8,128)(2,1)} %encode.1.s0) | copy-start | bytes 1572868
  33.2 23.2 %collective-permute-start.9 = (bf16[2048,128]{1,0:T(8,128)(2,1)}, bf16[2048,128]{1,0:T(8,128)(2,1)S(1)}, u32[]{:S(2)}, u32[]{:S(2)}) collective-permute-start(bf16[2048,128]{1,0:T(8,128)(2,1)} %encode.1.s0), channel_id=1, source_target_pairs={{0,1},{1,0},{2,3},{3,2},{4,5},{5,4},{6,7},{7,6},{8,9},{9,8},{10,11... | collective-permute-start | bytes 1572872 | tf_op jit(solution)/shard_map/ppermute | solution.py:495
  33.2 24.3 %collective-permute-start.10 = (bf16[2048,128]{1,0:T(8,128)(2,1)}, bf16[2048,128]{1,0:T(8,128)(2,1)S(1)}, u32[]{:S(2)}, u32[]{:S(2)}) collective-permute-start(bf16[2048,128]{1,0:T(8,128)(2,1)} %encode.1.s0), channel_id=1, source_target_pairs={{0,2},{1,3},{2,4},{3,5},{4,6},{5,7},{6,0},{7,1},{8,10},{9,11},{10,... | collective-permute-start | bytes 1572872 | tf_op jit(solution)/shard_map/ppermute | solution.py:495
  34.6 18.5 %collective-permute-start.3 = (bf16[144,1024]{1,0:T(8,128)(2,1)S(1)}, bf16[144,1024]{1,0:T(8,128)(2,1)S(1)}, u32[]{:S(2)}, u32[]{:S(2)}) collective-permute-start(bf16[144,1024]{1,0:T(8,128)(2,1)S(1)} %slice_bitcast_fusion.1), channel_id=1, source_target_pairs={{0,2},{1,3},{2,4},{3,5},{4,6},{5,7},{6,0},{7,1},{8,10},{9,11},{10,... | collective-permute-start | bytes 884744 | tf_op jit(solution)/shard_map/ppermute | solution.py:495
  36.0 17.8 %collective-permute-start.4 = (bf16[144,1024]{1,0:T(8,128)(2,1)S(1)}, bf16[144,1024]{1,0:T(8,128)(2,1)S(1)}, u32[]{:S(2)}, u32[]{:S(2)}) collective-permute-start(bf16[144,1024]{1,0:T(8,128)(2,1)S(1)} %slice_bitcast_fusion), channel_id=1, source_target_pairs={{0,6},{1,7},{2,0},{3,1},{4,2},{5,3},{6,4},{7,5},{8,14},{9,15},{10,... | collective-permute-start | bytes 884744 | tf_op jit(solution)/shard_map/ppermute | solution.py:495
  54.6 54.9 %collective-permute-start.5 = (bf16[8,144,1024]{2,1,0:T(8,128)(2,1)}, bf16[8,144,1024]{2,1,0:T(8,128)(2,1)S(1)}, u32[]{:S(2)}, u32[]{:S(2)}) collective-permute-start(bf16[8,144,1024]{2,1,0:T(8,128)(2,1)} %bitcast_dynamic-update-slice_fusion.refs_0_), channel_id=1, source_target_pairs={{0,16},{8,24},{16,32},{24,40},{32,48},{40,56},{48,0},{56,8},{64,80... | collective-permute-start | bytes 7077896 | tf_op jit(solution)/shard_map/ppermute | solution.py:495
  54.6 56.3 %collective-permute-start.6 = (bf16[8,144,1024]{2,1,0:T(8,128)(2,1)}, bf16[8,144,1024]{2,1,0:T(8,128)(2,1)}, u32[]{:S(2)}, u32[]{:S(2)}) collective-permute-start(bf16[8,144,1024]{2,1,0:T(8,128)(2,1)} %bitcast_dynamic-update-slice_fusion.refs_0_), channel_id=1, source_target_pairs={{0,48},{8,56},{16,0},{24,8},{32,16},{40,24},{48,32},{56,40},{64,11... | collective-permute-start | bytes 7077896 | tf_op jit(solution)/shard_map/ppermute | solution.py:495
  56.1 14.0 %collective-permute-start.12 = (bf16[2048,128]{1,0:T(8,128)(2,1)S(1)}, bf16[2048,128]{1,0:T(8,128)(2,1)S(1)}, u32[]{:S(2)}, u32[]{:S(2)}) collective-permute-start(bf16[2048,128]{1,0:T(8,128)(2,1)S(1)} %copy-done.6), channel_id=1, source_target_pairs={{0,6},{1,7},{2,0},{3,1},{4,2},{5,3},{6,4},{7,5},{8,14},{9,15},{10,... | collective-permute-start | bytes 1572872 | tf_op jit(solution)/shard_map/ppermute | solution.py:495
  56.4 25.7 %copy-start.17 = (bf16[2048,128]{1,0:T(8,128)(2,1)}, bf16[2048,128]{1,0:T(8,128)(2,1)S(1)}, u32[]{:S(2)}) copy-start(bf16[2048,128]{1,0:T(8,128)(2,1)S(1)} %collective-permute-done.9.s1) | copy-start | bytes 1572868
  56.4 15.0 %collective-permute-start.11 = (bf16[2048,128]{1,0:T(8,128)(2,1)S(1)}, bf16[2048,128]{1,0:T(8,128)(2,1)S(1)}, u32[]{:S(2)}, u32[]{:S(2)}) collective-permute-start(bf16[2048,128]{1,0:T(8,128)(2,1)S(1)} %collective-permute-done.9.s1), channel_id=1, source_target_pairs={{0,2},{1,3},{2,4},{3,5},{4,6},{5,7},{6,0},{7,1},{8,10},{9,11},{10,... | collective-permute-start | bytes 1572872 | tf_op jit(solution)/shard_map/ppermute | solution.py:495
  57.6 24.6 %copy-start.9 = (bf16[2048,128]{1,0:T(8,128)(2,1)}, bf16[2048,128]{1,0:T(8,128)(2,1)S(1)}, u32[]{:S(2)}) copy-start(bf16[2048,128]{1,0:T(8,128)(2,1)S(1)} %collective-permute-done.10.s2) | copy-start | bytes 1572868
  57.6 23.8 %collective-permute-start.13 = (bf16[2048,128]{1,0:T(8,128)(2,1)S(1)}, bf16[2048,128]{1,0:T(8,128)(2,1)S(1)}, u32[]{:S(2)}, u32[]{:S(2)}) collective-permute-start(bf16[2048,128]{1,0:T(8,128)(2,1)S(1)} %collective-permute-done.9.s1), channel_id=1, source_target_pairs={{0,6},{1,7},{2,0},{3,1},{4,2},{5,3},{6,4},{7,5},{8,14},{9,15},{10,... | collective-permute-start | bytes 1572872 | tf_op jit(solution)/shard_map/ppermute | solution.py:495
  70.1 12.0 %copy-start.10 = (bf16[2048,128]{1,0:T(8,128)(2,1)}, bf16[2048,128]{1,0:T(8,128)(2,1)S(1)}, u32[]{:S(2)}) copy-start(bf16[2048,128]{1,0:T(8,128)(2,1)S(1)} %collective-permute-done.12.s4) | copy-start | bytes 1572868
  70.1 12.0 %collective-permute-start.14 = (bf16[1024,128]{1,0:T(8,128)(2,1)S(1)}, bf16[1024,128]{1,0:T(8,128)(2,1)S(1)}, u32[]{:S(2)}, u32[]{:S(2)}) collective-permute-start(bf16[1024,128]{1,0:T(8,128)(2,1)S(1)} %slice.74), channel_id=1, source_target_pairs={{0,2},{1,3},{2,4},{3,5},{4,6},{5,7},{6,0},{7,1},{8,10},{9,11},{10,... | collective-permute-start | bytes 786440 | tf_op jit(solution)/shard_map/ppermute | solution.py:495
  71.4 10.7 %copy-start.11 = (bf16[2048,128]{1,0:T(8,128)(2,1)}, bf16[2048,128]{1,0:T(8,128)(2,1)S(1)}, u32[]{:S(2)}) copy-start(bf16[2048,128]{1,0:T(8,128)(2,1)S(1)} %collective-permute-done.11.s3) | copy-start | bytes 1572868
  71.4 17.2 %collective-permute-start.15 = (bf16[1024,128]{1,0:T(8,128)(2,1)}, bf16[1024,128]{1,0:T(8,128)(2,1)}, u32[]{:S(2)}, u32[]{:S(2)}) collective-permute-start(bf16[1024,128]{1,0:T(8,128)(2,1)} %slice.75), channel_id=1, source_target_pairs={{0,6},{1,7},{2,0},{3,1},{4,2},{5,3},{6,4},{7,5},{8,14},{9,15},{10,... | collective-permute-start | bytes 786440 | tf_op jit(solution)/shard_map/ppermute | solution.py:495
  81.4 0.9 copy-start.12
  81.4 9.1 %collective-permute-start.16 = (bf16[1024,128]{1,0:T(8,128)(2,1)}, bf16[1024,128]{1,0:T(8,128)(2,1)}, u32[]{:S(2)}, u32[]{:S(2)}) collective-permute-start(bf16[1024,128]{1,0:T(8,128)(2,1)} %slice.76), channel_id=1, source_target_pairs={{0,2},{1,3},{2,4},{3,5},{4,6},{5,7},{6,0},{7,1},{8,10},{9,11},{10,... | collective-permute-start | bytes 786440 | tf_op jit(solution)/shard_map/ppermute | solution.py:495
  83.0 9.6 %collective-permute-start.17 = (bf16[1024,128]{1,0:T(8,128)(2,1)}, bf16[1024,128]{1,0:T(8,128)(2,1)}, u32[]{:S(2)}, u32[]{:S(2)}) collective-permute-start(bf16[1024,128]{1,0:T(8,128)(2,1)} %slice.77), channel_id=1, source_target_pairs={{0,6},{1,7},{2,0},{3,1},{4,2},{5,3},{6,4},{7,5},{8,14},{9,15},{10,... | collective-permute-start | bytes 786440 | tf_op jit(solution)/shard_map/ppermute | solution.py:495
  104.4 11.6 %collective-permute-start.18 = (bf16[1152,256]{1,0:T(8,128)(2,1)S(1)}, bf16[1152,256]{1,0:T(8,128)(2,1)S(1)}, u32[]{:S(2)}, u32[]{:S(2)}) collective-permute-start(bf16[1152,256]{1,0:T(8,128)(2,1)S(1)} %get-tuple-element.42), channel_id=1, source_target_pairs={{0,8},{8,16},{16,24},{24,32},{32,40},{40,48},{48,56},{56,64},{64,7... | collective-permute-start | bytes 1769480 | tf_op jit(solution)/shard_map/ppermute | solution.py:491
  107.6 14.9 %collective-permute-start.19 = (bf16[1152,256]{1,0:T(8,128)(2,1)S(1)}, bf16[1152,256]{1,0:T(8,128)(2,1)S(1)}, u32[]{:S(2)}, u32[]{:S(2)}) collective-permute-start(bf16[1152,256]{1,0:T(8,128)(2,1)S(1)} %get-tuple-element.41), channel_id=1, source_target_pairs={{8,0},{16,8},{24,16},{32,24},{40,32},{48,40},{56,48},{64,56},{72,6... | collective-permute-start | bytes 1769480 | tf_op jit(solution)/shard_map/ppermute | solution.py:491
  109.6 6.4 %copy-start.4 = (bf16[8,144,1024]{2,1,0:T(8,128)(2,1)}, bf16[8,144,1024]{2,1,0:T(8,128)(2,1)S(1)}, u32[]{:S(2)}) copy-start(bf16[8,144,1024]{2,1,0:T(8,128)(2,1)S(1)} %collective-permute-done.5.refs_1_) | copy-start | bytes 7077892
  110.7 41.8 %collective-permute-start.20 = (bf16[4,144,1024]{2,1,0:T(8,128)(2,1)}, bf16[4,144,1024]{2,1,0:T(8,128)(2,1)}, u32[]{:S(2)}, u32[]{:S(2)}) collective-permute-start(bf16[4,144,1024]{2,1,0:T(8,128)(2,1)} %slice.78), channel_id=1, source_target_pairs={{0,16},{8,24},{16,32},{24,40},{32,48},{40,56},{48,0},{56,8},{64,80... | collective-permute-start | bytes 3538952 | tf_op jit(solution)/shard_map/ppermute | solution.py:495
  113.3 39.2 %collective-permute-start.21 = (bf16[4,144,1024]{2,1,0:T(8,128)(2,1)}, bf16[4,144,1024]{2,1,0:T(8,128)(2,1)}, u32[]{:S(2)}, u32[]{:S(2)}) collective-permute-start(bf16[4,144,1024]{2,1,0:T(8,128)(2,1)} %slice.79), channel_id=1, source_target_pairs={{0,48},{8,56},{16,0},{24,8},{32,16},{40,24},{48,32},{56,40},{64,11... | collective-permute-start | bytes 3538952 | tf_op jit(solution)/shard_map/ppermute | solution.py:495
  114.6 44.0 %collective-permute-start.22 = (bf16[8,144,1024]{2,1,0:T(8,128)(2,1)}, bf16[8,144,1024]{2,1,0:T(8,128)(2,1)}, u32[]{:S(2)}, u32[]{:S(2)}) collective-permute-start(bf16[8,144,1024]{2,1,0:T(8,128)(2,1)} %bitcast_dynamic-update-slice_fusion.refs_0_), channel_id=1, source_target_pairs={{0,8},{8,0},{16,24},{24,16},{32,40},{40,32},{48,56},{56,48},{64,72... | collective-permute-start | bytes 7077896 | tf_op jit(solution)/shard_map/ppermute | solution.py:495
  116.0 6.5 %copy-start.15 = (bf16[1152,256]{1,0:T(8,128)(2,1)}, bf16[1152,256]{1,0:T(8,128)(2,1)S(1)}, u32[]{:S(2)}) copy-start(bf16[1152,256]{1,0:T(8,128)(2,1)S(1)} %collective-permute-done.18.low) | copy-start | bytes 1769476
  116.0 51.4 %collective-permute-start.23 = (bf16[8,144,1024]{2,1,0:T(8,128)(2,1)S(1)}, bf16[8,144,1024]{2,1,0:T(8,128)(2,1)}, u32[]{:S(2)}, u32[]{:S(2)}) collective-permute-start(bf16[8,144,1024]{2,1,0:T(8,128)(2,1)S(1)} %collective-permute-done.5.refs_1_), channel_id=1, source_target_pairs={{0,8},{8,0},{16,24},{24,16},{32,40},{40,32},{48,56},{56,48},{64,72... | collective-permute-start | bytes 7077896 | tf_op jit(solution)/shard_map/ppermute | solution.py:495
  122.5 0.8 copy-start.16
  123.4 44.0 %collective-permute-start.24 = (bf16[8,144,1024]{2,1,0:T(8,128)(2,1)}, bf16[8,144,1024]{2,1,0:T(8,128)(2,1)}, u32[]{:S(2)}, u32[]{:S(2)}) collective-permute-start(bf16[8,144,1024]{2,1,0:T(8,128)(2,1)} %collective-permute-done.6.refs_2_), channel_id=1, source_target_pairs={{0,8},{8,0},{16,24},{24,16},{32,40},{40,32},{48,56},{56,48},{64,72... | collective-permute-start | bytes 7077896 | tf_op jit(solution)/shard_map/ppermute | solution.py:495
  152.5 14.8 %collective-permute-start.25 = (bf16[4,144,1024]{2,1,0:T(8,128)(2,1)}, bf16[4,144,1024]{2,1,0:T(8,128)(2,1)}, u32[]{:S(2)}, u32[]{:S(2)}) collective-permute-start(bf16[4,144,1024]{2,1,0:T(8,128)(2,1)} %collective-permute-done.20.refs_3_), channel_id=1, source_target_pairs={{0,8},{8,0},{16,24},{24,16},{32,40},{40,32},{48,56},{56,48},{64,72... | collective-permute-start | bytes 3538952 | tf_op jit(solution)/shard_map/ppermute | solution.py:495
  153.1 14.2 %collective-permute-start.26 = (bf16[4,144,1024]{2,1,0:T(8,128)(2,1)}, bf16[4,144,1024]{2,1,0:T(8,128)(2,1)}, u32[]{:S(2)}, u32[]{:S(2)}) collective-permute-start(bf16[4,144,1024]{2,1,0:T(8,128)(2,1)} %collective-permute-done.21.refs_4_), channel_id=1, source_target_pairs={{0,8},{8,0},{16,24},{24,16},{32,40},{40,32},{48,56},{56,48},{64,72... | collective-permute-start | bytes 3538952 | tf_op jit(solution)/shard_map/ppermute | solution.py:495
  153.2 14.1 %all-to-all-start = ((bf16[8,256,128]{2,1,0:T(8,128)(2,1)}), bf16[8,256,128]{2,1,0:T(8,128)(2,1)}, u32[]{:S(2)}, u32[]{:S(2)}) async-start(bf16[8,256,128]{2,1,0:T(8,128)(2,1)} %bitcast.52), calls=%async_computation | async-start | bytes 1048576 | tf_op jit(solution)/shard_map/all_to_all | solution.py:583
  167.4 31.3 %copy-start.14 = (s32[64,2]{0,1:T(2,128)S(1)}, s32[64,2]{0,1:T(2,128)}, u32[]{:S(2)}) copy-start(s32[64,2]{0,1:T(2,128)} %param.21) | copy-start | bytes 1540
  191.5 16.5 %copy-start.5 = (bf16[8,256,128]{2,1,0:T(8,128)(2,1)}, bf16[8,256,128]{2,1,0:T(8,128)(2,1)S(1)}, u32[]{:S(2)}) copy-start(bf16[8,256,128]{2,1,0:T(8,128)(2,1)S(1)} %all_to_all.15) | copy-start | bytes 1572868
  191.5 8.5 %collective-permute-start.27 = (bf16[8,128,128]{2,1,0:T(8,128)(2,1)S(1)}, bf16[8,128,128]{2,1,0:T(8,128)(2,1)S(1)}, u32[]{:S(2)}, u32[]{:S(2)}) collective-permute-start(bf16[8,128,128]{2,1,0:T(8,128)(2,1)S(1)} %bitcast.54), channel_id=1, source_target_pairs={{0,8},{8,16},{16,24},{24,32},{32,40},{40,48},{48,56},{56,64},{64,7... | collective-permute-start | bytes 786440 | tf_op jit(solution)/shard_map/ppermute | solution.py:491
  196.7 11.3 %collective-permute-start.28 = (bf16[8,128,128]{2,1,0:T(8,128)(2,1)S(1)}, bf16[8,128,128]{2,1,0:T(8,128)(2,1)S(1)}, u32[]{:S(2)}, u32[]{:S(2)}) collective-permute-start(bf16[8,128,128]{2,1,0:T(8,128)(2,1)S(1)} %bitcast.53), channel_id=1, source_target_pairs={{8,0},{16,8},{24,16},{32,24},{40,32},{48,40},{56,48},{64,56},{72,6... | collective-permute-start | bytes 786440 | tf_op jit(solution)/shard_map/ppermute | solution.py:491
  200.0 8.0 %copy-start.7 = (bf16[8,128,128]{2,1,0:T(8,128)(2,1)}, bf16[8,128,128]{2,1,0:T(8,128)(2,1)S(1)}, u32[]{:S(2)}) copy-start(bf16[8,128,128]{2,1,0:T(8,128)(2,1)S(1)} %collective-permute-done.27.low) | copy-start | bytes 786436
  208.1 0.7 copy-start.8
  208.8 19.4 %copy-start.1 = (bf16[8192,128]{1,0:T(8,128)(2,1)S(1)}, bf16[8192,128]{1,0:T(8,128)(2,1)}, u32[]{:S(2)}) copy-start(bf16[8192,128]{1,0:T(8,128)(2,1)} %state.1) | copy-start | bytes 6291460
  208.8 19.4 %copy-start.3 = (f32[128]{0:T(128)S(1)}, f32[128]{0:T(128)}, u32[]{:S(2)}) copy-start(f32[128]{0:T(128)} %param.23) | copy-start | bytes 1540
  228.2 2.2 copy-start.2
  (1 other events, 0.7 us)

commit v3 on v2

--- a/solution.py
+++ b/solution.py
@@ -34,42 +34,50 @@
 
 
 ANY = pl.BlockSpec(memory_space=pl.ANY)
+FAR = pl.BlockSpec(memory_space=pltpu.HBM)
 
 
 def whole(shape):
     return pl.BlockSpec(shape, lambda i, *_: (0,) * len(shape))
 
 
-def encode_kernel(index, low, own, high, weights, out, source, sems):
-    step = pl.program_id(0)
-    rim = low.shape[0]
-
-    @pl.when(step == 0)
-    def _():
-        copies = [
-            pltpu.make_async_copy(low, source.at[pl.ds(0, rim)], sems.at[0]),
-            pltpu.make_async_copy(own, source.at[pl.ds(rim, own.shape[0])], sems.at[1]),
-            pltpu.make_async_copy(
-                high, source.at[pl.ds(rim + own.shape[0], rim)], sems.at[2]
-            ),
-        ]
-        for c in copies:
-            c.start()
-        for c in copies:
-            c.wait()
-
-    per, slots = weights.shape[0], weights.shape[1]
-    for b in range(per):
-        left = jnp.concatenate([weights[b, k] for k in range(slots)], axis=1)
-        right = jnp.concatenate(
-            [source[index[step * per + b, k]] for k in range(slots)], axis=0
+def pieces_of(ref, target, start, count, sems, first):
+    length = ref.shape[0] // count
+    return [
+        pltpu.make_async_copy(
+            ref.at[pl.ds(n * length, length)],
+            target.at[pl.ds(start + n * length, length)],
+            sems.at[first + n],
         )
-        out[b * BLOCK : (b + 1) * BLOCK] = dot(left, right).astype(BF)
+        for n in range(count)
+    ]
+
+
+def encode_kernel(index, low, own, high, weights, out, source, held, made, sems):
+    rim, slots = low.shape[0], weights.shape[1]
+    ahead = pieces_of(low, source, 0, 2, sems, 0)
+    ahead += pieces_of(own, source, rim, 4, sems, 2)
+    ahead += pieces_of(high, source, rim + own.shape[0], 2, sems, 6)
+    count = weights.shape[0]
+    blocks = pieces_of(weights, held, 0, count, sems, 8)
+    back = pieces_of(made, out, 0, 4, sems, 8 + count)
+    for c in ahead + blocks:
+        c.start()
+    for c in ahead:
+        c.wait()
+    for b in range(count):
+        blocks[b].wait()
+        left = jnp.concatenate([held[b, k] for k in range(slots)], axis=1)
+        right = jnp.concatenate([source[index[b, k]] for k in range(slots)], axis=0)
+        made[b * BLOCK : (b + 1) * BLOCK] = dot(left, right).astype(BF)
+        if (b + 1) % (count // 4) == 0:
+            back[b // (count // 4)].start()
+    for c in back:
+        c.wait()
 
 
 def encode(index, low, own, high, weights):
     count, slots = weights.shape[:2]
-    per = 2
     blocks = own.shape[0] // BLOCK
     rim = low.shape[0] // BLOCK
     shaped = [v.reshape(-1, BLOCK, BLOCK) for v in (low, own, high)]
@@ -78,17 +86,14 @@
         out_shape=jax.ShapeDtypeStruct((count * BLOCK, BLOCK), BF),
         grid_spec=pltpu.PrefetchScalarGridSpec(
             num_scalar_prefetch=1,
-            grid=(count // per,),
-            in_specs=[
-                ANY,
-                ANY,
-                ANY,
-                pl.BlockSpec((per, slots, BLOCK, BLOCK), lambda i, _: (i, 0, 0, 0)),
-            ],
-            out_specs=pl.BlockSpec((per * BLOCK, BLOCK), lambda i, _: (i, 0)),
+            grid=(1,),
+            in_specs=[ANY, FAR, ANY, FAR],
+            out_specs=ANY,
             scratch_shapes=[
                 pltpu.VMEM((blocks + 2 * rim, BLOCK, BLOCK), BF),
-                pltpu.SemaphoreType.DMA((3,)),
+                pltpu.VMEM((count, slots, BLOCK, BLOCK), BF),
+                pltpu.VMEM((count * BLOCK, BLOCK), BF),
+                pltpu.SemaphoreType.DMA((12 + count,)),
             ],
         ),
         compiler_params=params(56),
@@ -98,7 +103,7 @@
 
 
 def project_kernel(
-    order, s0, s1, s2, s3, s4, s5, lo6, hi6, lo7, hi7, gain, weights,
+    order, s0, s1, s2, s3, s4, s5, lo6, hi6, lo7, hi7, gain, wq, wk, wv,
     queries, keys_values, share, ordered,
 ):
     step = pl.program_id(0)
@@ -107,7 +112,9 @@
     @pl.when(step == 0)
     def _():
         for p in range(8):
-            ordered[p * BLOCK : (p + 1) * BLOCK] = weights[order[p]]
+            ordered[p * BLOCK : (p + 1) * BLOCK] = jnp.concatenate(
+                [w[order[p]] for w in (wq, wk, wv)], axis=1
+            )
 
     early = step < half
     raw = [s[...] for s in (s0, s1, s2, s3, s4, s5)]
@@ -155,7 +162,8 @@
             grid=(8,),
             in_specs=[full] * 6
             + [early, late, early, late]
-            + [whole((8, 1, BLOCK)), whole((8, BLOCK, 3 * BLOCK))],
+            + [whole((8, 1, BLOCK))]
+            + [whole((8, BLOCK, BLOCK))] * 3,
             out_specs=(
                 full,
                 pl.BlockSpec((tile, 2 * BLOCK), lambda i, _: (i, 0)),
@@ -166,7 +174,7 @@
         compiler_params=params(56),
         cost_estimate=cost(1_600_000_000, 7_000_000),
         name="project",
-    )(order, *slots, gain.reshape(8, 1, BLOCK), weights)
+    )(order, *slots, gain.reshape(8, 1, BLOCK), *weights)
 
 
 TILE = 256
@@ -374,42 +382,41 @@
 EACH = 8
 
 
-def decode_kernel(index, low, own, high, weights, back, sums, source, sems):
-    step = pl.program_id(0)
-    rim = low.shape[0]
-
-    @pl.when(step == 0)
-    def _():
-        copies = [
-            pltpu.make_async_copy(low, source.at[pl.ds(0, rim)], sems.at[0]),
-            pltpu.make_async_copy(own, source.at[pl.ds(rim, own.shape[0])], sems.at[1]),
-            pltpu.make_async_copy(
-                high, source.at[pl.ds(rim + own.shape[0], rim)], sems.at[2]
-            ),
-        ]
-        for c in copies:
-            c.start()
-        for c in copies:
-            c.wait()
-
-    slots = weights.shape[1]
+def decode_kernel(index, low, own, high, weights, back, sums, source, held, kept, sems):
+    rim, slots = low.shape[0], weights.shape[1]
+    steps = weights.shape[0] // EACH
+    ahead = pieces_of(low, source, 0, 1, sems, 0)
+    ahead += pieces_of(own, source, rim, 2, sems, 1)
+    ahead += pieces_of(high, source, rim + own.shape[0], 1, sems, 3)
+    blocks = pieces_of(weights, held, 0, 2 * steps, sems, 4)
+    done = pieces_of(kept, back, 0, steps, sems, 4 + 2 * steps)
+    for c in ahead + blocks:
+        c.start()
+    for c in ahead:
+        c.wait()
     ones = jnp.ones((BLOCK, BLOCK), BF)
     row = lax.broadcasted_iota(jnp.int32, (BLOCK, BLOCK), 0)
     column = lax.broadcasted_iota(jnp.int32, (BLOCK, BLOCK), 1)
-    made = []
-    for b in range(EACH):
-        left = jnp.concatenate([weights[b, k] for k in range(slots)], axis=1)
-        right = jnp.concatenate(
-            [source[index[step * EACH + b, k]] for k in range(slots)], axis=0
-        )
-        made.append(dot(left, right))
-        back[b * BLOCK : (b + 1) * BLOCK] = made[b]
-    kinds = [m.astype(BF) for m in made] + [(m * m).astype(BF) for m in made]
-    held = [
-        jnp.sum(jnp.where(row == column, dot(k, ones), 0.0), axis=0, keepdims=True)
-        for k in kinds
-    ]
-    sums[0] = jnp.concatenate(held, axis=0).astype(BF)
+    for step in range(steps):
+        blocks[2 * step].wait()
+        blocks[2 * step + 1].wait()
+        kinds = []
+        for b in range(step * EACH, (step + 1) * EACH):
+            left = jnp.concatenate([held[b, k] for k in range(slots)], axis=1)
+            right = jnp.concatenate([source[index[b, k]] for k in range(slots)], axis=0)
+            made = dot(left, right)
+            plain = made.astype(BF)
+            kept[b * BLOCK : (b + 1) * BLOCK] = plain
+            kinds.append((plain, (made * made).astype(BF)))
+        done[step].start()
+        held_sums = [
+            jnp.sum(jnp.where(row == column, dot(kinds[b][n], ones), 0.0), axis=0, keepdims=True)
+            for n in range(2)
+            for b in range(EACH)
+        ]
+        sums[step] = jnp.concatenate(held_sums, axis=0).astype(BF)
+    for c in done:
+        c.wait()
 
 
 def decode(index, low, own, high, weights):
@@ -420,25 +427,19 @@
     return pl.pallas_call(
         decode_kernel,
         out_shape=(
-            jax.ShapeDtypeStruct((count * BLOCK, BLOCK), F32),
+            jax.ShapeDtypeStruct((count * BLOCK, BLOCK), BF),
             jax.ShapeDtypeStruct((steps, 2 * EACH, BLOCK), BF),
         ),
         grid_spec=pltpu.PrefetchScalarGridSpec(
             num_scalar_prefetch=1,
-            grid=(steps,),
-            in_specs=[
-                ANY,
-                ANY,
-                ANY,
-                pl.BlockSpec((EACH, slots, BLOCK, BLOCK), lambda i, _: (i, 0, 0, 0)),
-            ],
-            out_specs=(
-                pl.BlockSpec((EACH * BLOCK, BLOCK), lambda i, _: (i, 0)),
-                pl.BlockSpec((1, 2 * EACH, BLOCK), lambda i, _: (i, 0, 0)),
-            ),
+            grid=(1,),
+            in_specs=[ANY, ANY, ANY, FAR],
+            out_specs=(ANY, whole((steps, 2 * EACH, BLOCK))),
             scratch_shapes=[
                 pltpu.VMEM((blocks + 2 * rim, BLOCK, BLOCK), BF),
-                pltpu.SemaphoreType.DMA((3,)),
+                pltpu.VMEM((count, slots, BLOCK, BLOCK), BF),
+                pltpu.VMEM((count * BLOCK, BLOCK), BF),
+                pltpu.SemaphoreType.DMA((4 + 3 * steps,)),
             ],
         ),
         compiler_params=params(56),
@@ -447,41 +448,62 @@
     )(index, low, own, high, weights)
 
 
-def finish_kernel(sums, back, state, gain, out):
+def finish_kernel(sums, back, state, gain, out, stats, kept, base, made, sems):
+    steps = sums.shape[1]
     count = sums.shape[0]
-    stats = jnp.concatenate([sums[h, 0] for h in range(count)], axis=0)
+    first = pieces_of(sums, stats, 0, count, sems, 0)
+    backs = pieces_of(back, kept, 0, steps, sems, count)
+    states = pieces_of(state, base, 0, steps, sems, count + steps)
+    outs = pieces_of(made, out, 0, steps, sems, count + 2 * steps)
+    for c in first:
+        c.start()
+    for a, b in zip(backs, states):
+        a.start()
+        b.start()
     depth = count * 2 * EACH
     row = lax.broadcasted_iota(jnp.int32, (depth, 2 * EACH * BLOCK), 0)
     column = lax.broadcasted_iota(jnp.int32, (depth, 2 * EACH * BLOCK), 1)
-    pick = jnp.where((row % (2 * EACH)) == (column // BLOCK), 1.0, 0.0).astype(BF)
-    spread = lax.dot_general(stats, pick, TN, preferred_element_type=F32) * (1.0 / D)
-    for b in range(EACH):
-        rows = slice(b * BLOCK, (b + 1) * BLOCK)
-        average = spread[:, b * BLOCK : (b + 1) * BLOCK]
-        squares = spread[:, (EACH + b) * BLOCK : (EACH + b + 1) * BLOCK]
-        scale = lax.rsqrt(squares - average * average + EPSILON) * gain[...]
-        out[rows] = (
-            state[rows].astype(F32) + (back[rows] - average) * scale
-        ).astype(BF)
+    pick = jnp.where((row % (2 * EACH)) == (column // BLOCK), 1.0 / D, 0.0).astype(BF)
+    for c in first:
+        c.wait()
+    for step in range(steps):
+        parts = jnp.concatenate([stats[h, step] for h in range(count)], axis=0)
+        spread = lax.dot_general(parts, pick, TN, preferred_element_type=F32)
+        backs[step].wait()
+        states[step].wait()
+        for b in range(EACH):
+            at = (step * EACH + b) * BLOCK
+            average = spread[:, b * BLOCK : (b + 1) * BLOCK]
+            squares = spread[:, (EACH + b) * BLOCK : (EACH + b + 1) * BLOCK]
+            scale = lax.rsqrt(squares - average * average + EPSILON) * gain[...]
+            made[at : at + BLOCK] = (
+                base[at : at + BLOCK].astype(F32)
+                + (kept[at : at + BLOCK].astype(F32) - average) * scale
+            ).astype(BF)
+        outs[step].start()
+    for c in outs:
+        c.wait()
 
 
 def finish(sums, back, state, gain):
     rows = state.shape[0]
-    tile = pl.BlockSpec((EACH * BLOCK, BLOCK), lambda i: (i, 0))
+    count, steps = sums.shape[:2]
     return pl.pallas_call(
         finish_kernel,
         out_shape=jax.ShapeDtypeStruct((rows, BLOCK), BF),
         grid_spec=pl.GridSpec(
-            grid=(rows // (EACH * BLOCK),),
-            in_specs=[
-                pl.BlockSpec((sums.shape[0], 1, 2 * EACH, BLOCK), lambda i: (0, i, 0, 0)),
-                tile,
-                tile,
-                pl.BlockSpec((1, BLOCK), lambda i: (0, 0)),
+            grid=(1,),
+            in_specs=[ANY, ANY, FAR, whole((1, BLOCK))],
+            out_specs=ANY,
+            scratch_shapes=[
+                pltpu.VMEM(sums.shape, BF),
+                pltpu.VMEM((rows, BLOCK), BF),
+                pltpu.VMEM((rows, BLOCK), BF),
+                pltpu.VMEM((rows, BLOCK), BF),
+                pltpu.SemaphoreType.DMA((count + 3 * steps,)),
             ],
-            out_specs=tile,
-        ),
-        compiler_params=params(32),
+        ),
+        compiler_params=params(24),
         cost_estimate=cost(540_000_000, 8_000_000),
         name="finish",
     )(sums, back, state, gain.reshape(1, BLOCK))
@@ -493,19 +515,6 @@
 
 def among(value, axis, count, to):
     return lax.ppermute(value, axis, [(i, to(i)) for i in range(count)])
-
-
-def head_ring(x):
-    half = x.shape[0] // 2
-    north = lambda v: among(v, "head", 8, lambda i: (i + 2) % 8)
-    south = lambda v: among(v, "head", 8, lambda i: (i - 2) % 8)
-    y = among(x, "head", 8, lambda i: i ^ 1)
-    xa, xb = north(x), south(x)
-    ya, yb = north(y), south(y)
-    return (
-        x, y, xa, ya, xb, yb,
-        north(xa[:half]), south(xb[half:]), north(ya[:half]), south(yb[half:]),
-    )
 
 
 def along_z(i, by):
@@ -519,11 +528,7 @@
 SOUTH = lambda v: among(v, "head", 8, lambda i: (i - 2) % 8)
 
 
-def weights_of_heads(packed):
-    x = jnp.stack([packed, among(packed, "head", 8, lambda i: i ^ 1)])
-    a, b = NORTH(x), SOUTH(x)
-    far = jnp.stack([NORTH(a[0]), SOUTH(b[1])])
-    return x, a, b, far
+OVER = lambda v: among(v, "head", 8, lambda i: i ^ 1)
 
 
 def on_device(
@@ -558,14 +563,24 @@
 
     position = band % 8
     packed = pack_weights(position, expand, shrink, outward)
-    inward = inward.reshape(8, BLOCK, 3 * BLOCK)
-    low, high, inward = lax.optimization_barrier((low, high, inward))
-    mine = jnp.concatenate(weights_of_heads(packed), axis=0)
+    inward = [inward[:, j, :].reshape(8, BLOCK, BLOCK) for j in range(3)]
+    packed = jnp.stack([packed, OVER(packed)])
+    low, high, packed, *inward = lax.optimization_barrier((low, high, packed, *inward))
+    packed_a, packed_b = NORTH(packed), SOUTH(packed)
 
     mesh_start = encode(
         encode_index - (band * grid_blocks - mesh_blocks), low, grid_state, high, encode_weights
     )
-    slots = head_ring(mesh_start)
+    half = mesh_rows // 2
+    x = mesh_start
+    y, xa, xb = OVER(x), NORTH(x), SOUTH(x)
+    xc, xd = NORTH(xa[:half]), SOUTH(xb[half:])
+    ya, yb = NORTH(y), SOUTH(y)
+    yc, yd = OVER(xc), OVER(xd)
+    slots = (x, y, xa, ya, xb, yb, xc, xd, yc, yd)
+    far = jnp.stack([NORTH(packed_a[0]), SOUTH(packed_b[1])])
+    mine = jnp.concatenate([packed, packed_a, packed_b, far], axis=0)
+    mine, *_ = lax.optimization_barrier((mine, ya, yb, xc, xd))
     partner = me ^ 1
     order = jnp.stack(
         [me, partner] + [(v + by) % 8 for by in (6, 2, 4) for v in (me, partner)]

time: 237 us -> 261 us (1.10)
  waiting for transfers between devices: 65 us -> 99 us
  local copies, waits for them, and re-layouts: 26.9 us -> 21.7 us
  Pallas kernels: 75.7 us -> 71.8 us
  starting transfers between devices: 44.3 us -> 40.7 us
    ppermute x23, waiting for transfers between devices: 36.6 us -> 80.7 us  [among(): return lax.ppermute(value, axis, [(i, to(i)) for i in range(count)])]
    ppermute x6, waiting for transfers between devices: 19.6 us -> 9.45 us  [shifted(): lax.ppermute(value, 'seq', [(i, i + by) for i in range(16) if 0 <= i + by...]
    ppermute x23, starting transfers between devices: 21.6 us -> 17.7 us  [among(): return lax.ppermute(value, axis, [(i, to(i)) for i in range(count)])]
    optimization_barrier x2 -> x0, local copies, waits for them, and re-layouts: 3.84 us -> none  [the longest x1 2.44 us: on_device(): low, high, inward = lax.optimization_barrier((low, high, inward))]
    unnamed x45 -> x46, local copies, waits for them, and re-layouts: 9.05 us -> 8.99 us
  transfers between devices with their start and end apart: 30 -> 30, of which waited for: 11 -> 12; matrix products, arithmetic and copies ran while one was open for 9% -> 6% of each run, Pallas kernels for 21% -> 18%
where the time goes in v3:
time: 261 us; the launch traced here: 258 us
  waiting for transfers between devices  99 us (38%)
  Pallas kernels  71.8 us (28%)
  starting transfers between devices  40.7 us (16%)
  local copies, waits for them, and re-layouts  21.7 us (8%)
  blocking collectives  20.7 us (8%)
  other arithmetic  3.68 us (1%)
    ppermute x23, waiting for transfers between devices, among(): return lax.ppermute(value, axis, [(i, to(i)) for i in range(count)])  80.7 us
    pallas_call x1, Pallas kernels, attend(): pl.pallas_call(attend_kernel, out_shape=jax.ShapeDtypeStruct((rows, BLOCK...  28.5 us
    ppermute x6, starting transfers between devices, shifted(): lax.ppermute(value, 'seq', [(i, i + by) for i in range(16) if 0 <= i + by...  18.8 us
    ppermute x23, starting transfers between devices, among(): return lax.ppermute(value, axis, [(i, to(i)) for i in range(count)])  17.7 us
    pallas_call x1, Pallas kernels, forward(): pl.pallas_call(forward_kernel, out_shape=jax.ShapeDtypeStruct((8, rows, B...  12.3 us
    all_to_all x1, blocking collectives, on_device(): mesh_end = lax.all_to_all(mesh_end, 'head', 0, 0, tiled=True)  12 us
    pallas_call x1, Pallas kernels, project(): pl.pallas_call(project_kernel, out_shape=(jax.ShapeDtypeStruct((rows, BLO...  10.5 us
    ppermute x6, waiting for transfers between devices, shifted(): lax.ppermute(value, 'seq', [(i, i + by) for i in range(16) if 0 <= i + by...  9.45 us
  transfers between devices with their start and end apart: 30, of which 12 were waited for; matrix products, arithmetic and copies ran while one was open for 6% of the time, Pallas kernels for 18%

profile of v3, /device:TPU:97, one launch (start us, length us, event | category | flops | bytes accessed | tf_op | source)
XLA Modules:
  0.0 258.1 jit_solution(8556570831296275330)
XLA Ops:
  0.0 2.4 fusion.1
  2.4 3.8 %collective-permute-start = (bf16[2048,128]{1,0:T(8,128)(2,1)}, bf16[2048,128]{1,0:T(8,128)(2,1)S(1)}, u32[]{:S(2)}, u32[]{:S(2)}) collective-permute-start(bf16[2048,128]{1,0:T(8,128)(2,1)} %get-tuple-element.26), channel_id=1, source_target_pairs={{0,8},{8,16},{16,24},{24,32},{32,40},{40,48},{48,56},{56,64},{64,7... | collective-permute-start | bytes 1572872 | tf_op jit(solution)/shard_map/ppermute | solution.py:513
  6.2 1.9 collective-permute-start.1
  8.2 0.9 constant_dynamic-slice_fusion
  11.1 0.9 fusion.3
  12.0 7.1 %collective-permute-done.2 = bf16[144,1024]{1,0:T(8,128)(2,1)} collective-permute-done((bf16[144,1024]{1,0:T(8,128)(2,1)}, bf16[144,1024]{1,0:T(8,128)(2,1)}, u32[]{:S(2)}, u32[]{:S(2)}) %collective-permute-start.2) | collective-permute-done | bytes 294944 | tf_op jit(solution)/shard_map/ppermute | solution.py:517
  19.1 1.0 pad_maximum_fusion
  20.2 3.0 %collective-permute-done.1 = bf16[2048,128]{1,0:T(8,128)(2,1)S(1)} collective-permute-done((bf16[2048,128]{1,0:T(8,128)(2,1)}, bf16[2048,128]{1,0:T(8,128)(2,1)S(1)}, u32[]{:S(2)}, u32[]{:S(2)}) %collective-permute-start.1) | collective-permute-done | bytes 524320 | tf_op jit(solution)/shard_map/ppermute | solution.py:513
  23.2 1.3 collective-permute-start.3
  25.1 7.2 %encode.1.s0 = bf16[2048,128]{1,0:T(8,128)(2,1)} custom-call(s32[16,8]{1,0:T(8,128)} %broadcast_subtract_fusion.1.index, bf16[16,128,128]{2,1,0:T(8,128)(2,1)} %bitcast.45, bf16[64,128,128]{2,1,0:T(8,128)(2,1)} %bitcast.42, bf16[16,128,128]{2,1,0:T(8,128)(2,1)} %bitcast.46, bf16[16,8,128,128]{3,2,1,0:T(8,128)(2,1)} %weights.2), custom_call_target="tpu_custom_call" | custom-call | flops 540000000 | bytes 8000000 | tf_op jit(solution)/shard_map/encode/pallas_call | solution.py:84
  32.3 1.4 collective-permute-start.10
  33.7 1.4 collective-permute-start.12
  35.5 0.9 constant_dynamic-update-slice_fusion.2
  36.4 13.2 %collective-permute-done.10.s2 = bf16[2048,128]{1,0:T(8,128)(2,1)S(1)} collective-permute-done((bf16[2048,128]{1,0:T(8,128)(2,1)}, bf16[2048,128]{1,0:T(8,128)(2,1)S(1)}, u32[]{:S(2)}, u32[]{:S(2)}) %collective-permute-start.10) | collective-permute-done | bytes 524320 | tf_op jit(solution)/shard_map/ppermute | solution.py:517
  50.0 1.3 collective-permute-start.8
  51.3 1.4 collective-permute-start.9
  53.0 6.7 %collective-permute-done.4 = bf16[2,144,1024]{2,1,0:T(8,128)(2,1)S(1)} collective-permute-done((bf16[2,144,1024]{2,1,0:T(8,128)(2,1)S(1)}, bf16[2,144,1024]{2,1,0:T(8,128)(2,1)S(1)}, u32[]{:S(2)}, u32[]{:S(2)}) %collective-permute-start.4) | collective-permute-done | bytes 589856 | tf_op jit(solution)/shard_map/ppermute | solution.py:517
  59.7 2.6 %collective-permute-start.6 = (bf16[144,1024]{1,0:T(8,128)(2,1)S(1)}, bf16[144,1024]{1,0:T(8,128)(2,1)S(1)}, u32[]{:S(2)}, u32[]{:S(2)}) collective-permute-start(bf16[144,1024]{1,0:T(8,128)(2,1)S(1)} %slice_bitcast_fusion), channel_id=1, source_target_pairs={{0,6},{1,7},{2,0},{3,1},{4,2},{5,3},{6,4},{7,5},{8,14},{9,15},{10,... | collective-permute-start | bytes 884744 | tf_op jit(solution)/shard_map/ppermute | solution.py:517
  62.4 0.9 constant_dynamic-update-slice_fusion.1
  63.2 0.9 constant_dynamic-update-slice_fusion
  64.1 12.4 %collective-permute-done.5 = bf16[144,1024]{1,0:T(8,128)(2,1)S(1)} collective-permute-done((bf16[144,1024]{1,0:T(8,128)(2,1)S(1)}, bf16[144,1024]{1,0:T(8,128)(2,1)S(1)}, u32[]{:S(2)}, u32[]{:S(2)}) %collective-permute-start.5) | collective-permute-done | bytes 294944 | tf_op jit(solution)/shard_map/ppermute | solution.py:517
  78.5 5.6 %collective-permute-done.13.hi6 = bf16[1024,128]{1,0:T(8,128)(2,1)} collective-permute-done((bf16[1024,128]{1,0:T(8,128)(2,1)S(1)}, bf16[1024,128]{1,0:T(8,128)(2,1)}, u32[]{:S(2)}, u32[]{:S(2)}) %collective-permute-start.13) | collective-permute-done | bytes 262176 | tf_op jit(solution)/shard_map/ppermute | solution.py:517
  86.4 1.5 collective-permute-start.17
  88.5 4.2 %collective-permute-done.16.lo7 = bf16[1024,128]{1,0:T(8,128)(2,1)} collective-permute-done((bf16[1024,128]{1,0:T(8,128)(2,1)}, bf16[1024,128]{1,0:T(8,128)(2,1)}, u32[]{:S(2)}, u32[]{:S(2)}) %collective-permute-start.16) | collective-permute-done | bytes 262176 | tf_op jit(solution)/shard_map/ppermute | solution.py:517
  92.7 5.6 %collective-permute-done.17.hi7 = bf16[1024,128]{1,0:T(8,128)(2,1)} collective-permute-done((bf16[1024,128]{1,0:T(8,128)(2,1)}, bf16[1024,128]{1,0:T(8,128)(2,1)}, u32[]{:S(2)}, u32[]{:S(2)}) %collective-permute-start.17) | collective-permute-done | bytes 262176 | tf_op jit(solution)/shard_map/ppermute | solution.py:517
  98.3 10.5 %project.1 = (bf16[2048,128]{1,0:T(8,128)(2,1)}, bf16[2048,256]{1,0:T(8,128)(2,1)}, bf16[8,256,128]{2,1,0:T(8,128)(2,1)}) custom-call(s32[8]{0:T(128)} %stack.101.order, bf16[2048,128]{1,0:T(8,128)(2,1)} %encode.1.s0, bf16[2048,128]{1,0:T(8,128)(2,1)} %copy-done.17, bf16[2048,128]{1,0:T(8,128)(2,1)} %copy-done.11, bf16[2048,128]{1,0:T(8,128)(2,1)} %copy-done.18, ...), custom_call_target="tpu_custom_call" | custom-call | flops 1600000000 | bytes 7000000 | tf_op jit(solution)/shard_map/project/pallas_call | solution.py:153
  108.8 1.3 fusion.2
  110.1 2.4 collective-permute-start.18
  112.6 4.1 %collective-permute-start.19 = (bf16[1152,256]{1,0:T(8,128)(2,1)S(1)}, bf16[1152,256]{1,0:T(8,128)(2,1)S(1)}, u32[]{:S(2)}, u32[]{:S(2)}) collective-permute-start(bf16[1152,256]{1,0:T(8,128)(2,1)S(1)} %get-tuple-element.49), channel_id=1, source_target_pairs={{8,0},{16,8},{24,16},{32,24},{40,32},{48,40},{56,48},{64,56},{72,6... | collective-permute-start | bytes 1769480 | tf_op jit(solution)/shard_map/ppermute | solution.py:513
  116.7 20.0 %collective-permute-done.14.refs_1_ = bf16[8,144,1024]{2,1,0:T(8,128)(2,1)S(1)} collective-permute-done((bf16[8,144,1024]{2,1,0:T(8,128)(2,1)}, bf16[8,144,1024]{2,1,0:T(8,128)(2,1)S(1)}, u32[]{:S(2)}, u32[]{:S(2)}) %collective-permute-start.14) | collective-permute-done | bytes 2359328 | tf_op jit(solution)/shard_map/ppermute | solution.py:517
  136.7 1.2 slice.80
  137.9 1.4 collective-permute-start.20
  139.3 5.8 %collective-permute-done.15.refs_2_ = bf16[8,144,1024]{2,1,0:T(8,128)(2,1)} collective-permute-done((bf16[8,144,1024]{2,1,0:T(8,128)(2,1)}, bf16[8,144,1024]{2,1,0:T(8,128)(2,1)}, u32[]{:S(2)}, u32[]{:S(2)}) %collective-permute-start.15) | collective-permute-done | bytes 2359328 | tf_op jit(solution)/shard_map/ppermute | solution.py:517
  145.1 2.4 slice.81
  147.5 2.2 collective-permute-start.22
  150.4 0.8 copy-done.16
  151.9 28.5 %attend.1 = bf16[2048,128]{1,0:T(8,128)(2,1)} custom-call(s32[2]{0:T(128)} %add_convert_fusion.edges, bf16[2048,128]{1,0:T(8,128)(2,1)} %get-tuple-element.39.queries, bf16[1152,256]{1,0:T(8,128)(2,1)} %copy-done.15, bf16[2048,256]{1,0:T(8,128)(2,1)} %get-tuple-element.40.own, bf16[1152,256]{1,0:T(8,128)(2,1)} %copy-done.16), custom_call_target="tpu_custom_call" | custom-call | flops 10700000256 | bytes 4000000 | tf_op jit(solution)/shard_map/attend/pallas_call | solution.py:251
  181.1 4.1 %all-to-all-start = ((bf16[8,256,128]{2,1,0:T(8,128)(2,1)}), bf16[8,256,128]{2,1,0:T(8,128)(2,1)}, u32[]{:S(2)}, u32[]{:S(2)}) async-start(bf16[8,256,128]{2,1,0:T(8,128)(2,1)} %bitcast.47), calls=%async_computation | async-start | bytes 1048576 | tf_op jit(solution)/shard_map/all_to_all | solution.py:598
  185.9 8.8 %all-to-all-done.refs_10_ = bf16[8,256,128]{2,1,0:T(8,128)(2,1)} async-done(((bf16[8,256,128]{2,1,0:T(8,128)(2,1)}), bf16[8,256,128]{2,1,0:T(8,128)(2,1)}, u32[]{:S(2)}, u32[]{:S(2)}) %all-to-all-start) | async-done | bytes 524320 | tf_op jit(solution)/shard_map/all_to_all | solution.py:598
  194.8 12.3 %forward.1 = bf16[8,256,128]{2,1,0:T(8,128)(2,1)} custom-call(s32[18]{0:T(128)} %concatenate.13.table, bf16[8,144,1024]{2,1,0:T(8,128)(2,1)} %bitcast_dynamic-update-slice_fusion.refs_0_, bf16[8,144,1024]{2,1,0:T(8,128)(2,1)} %copy-done.4, bf16[8,144,1024]{2,1,0:T(8,128)(2,1)} %collective-permute-done.15.refs_2_, ...), custom_call_target="tpu_custom_call" | custom-call | flops 4800000000 | bytes 20000000 | tf_op jit(solution)/shard_map/forward/pallas_call | solution.py:360
  207.1 12.0 %all_to_all.15 = bf16[8,256,128]{2,1,0:T(8,128)(2,1)S(1)} all-to-all(bf16[8,256,128]{2,1,0:T(8,128)(2,1)} %forward.1), channel_id=1, replica_groups=mesh['seq'=16,'head'=8] {'head'}, dimensions={0} | all-to-all | bytes 1048576 | tf_op jit(solution)/shard_map/all_to_all | solution.py:609
  219.2 2.4 collective-permute-start.27
  221.5 4.1 %collective-permute-start.28 = (bf16[8,128,128]{2,1,0:T(8,128)(2,1)S(1)}, bf16[8,128,128]{2,1,0:T(8,128)(2,1)S(1)}, u32[]{:S(2)}, u32[]{:S(2)}) collective-permute-start(bf16[8,128,128]{2,1,0:T(8,128)(2,1)S(1)} %bitcast.51), channel_id=1, source_target_pairs={{8,0},{16,8},{24,16},{32,24},{40,32},{48,40},{56,48},{64,56},{72,6... | collective-permute-start | bytes 786440 | tf_op jit(solution)/shard_map/ppermute | solution.py:513
  226.4 6.4 %collective-permute-done.28.high = bf16[8,128,128]{2,1,0:T(8,128)(2,1)S(1)} collective-permute-done((bf16[8,128,128]{2,1,0:T(8,128)(2,1)S(1)}, bf16[8,128,128]{2,1,0:T(8,128)(2,1)S(1)}, u32[]{:S(2)}, u32[]{:S(2)}) %collective-permute-start.28) | collective-permute-done | bytes 262176 | tf_op jit(solution)/shard_map/ppermute | solution.py:513
  233.6 8.0 %decode.1 = (bf16[8192,128]{1,0:T(8,128)(2,1)}, bf16[8,16,128]{2,1,0:T(8,128)(2,1)}) custom-call(s32[64,2]{1,0:T(8,128)} %broadcast_subtract_fusion.index, bf16[8,128,128]{2,1,0:T(8,128)(2,1)} %copy-done.9, bf16[16,128,128]{2,1,0:T(8,128)(2,1)} %bitcast.44, bf16[8,128,128]{2,1,0:T(8,128)(2,1)} %copy-done.10, bf16[64,2,128,128]{3,2,1,0:T(8,128)(2,1)} %weights.3), custom_call_target="tpu_custom_call" | custom-call | flops 540000000 | bytes 10000000 | tf_op jit(solution)/shard_map/decode/pallas_call | solution.py:427
  242.4 8.8 %all_to_all.16.sums = bf16[8,8,16,128]{3,2,1,0:T(8,128)(2,1)S(1)} all-to-all(bf16[8,8,16,128]{3,2,1,0:T(8,128)(2,1)S(1)} %broadcast_in_dim.3), channel_id=1, replica_groups=mesh['seq'=16,'head'=8] {'head'}, dimensions={0} | all-to-all | bytes 524288 | tf_op jit(solution)/shard_map/all_to_all | solution.py:619
  251.2 1.6 copy-done.2
  252.8 5.2 %finish.1 = bf16[8192,128]{1,0:T(8,128)(2,1)} custom-call(bf16[8,8,16,128]{3,2,1,0:T(8,128)(2,1)S(1)} %all_to_all.16.sums, bf16[8192,128]{1,0:T(8,128)(2,1)S(1)} %copy-done.2, bf16[8192,128]{1,0:T(8,128)(2,1)S(1)} %copy-done.1, f32[1,128]{1,0:T(1,128)S(1)} %bitcast.43), custom_call_target="tpu_custom_call" | custom-call | flops 540000000 | bytes 8000000 | tf_op jit(solution)/shard_map/finish/pallas_call | solution.py:491
  (88 shorter events, 13.6 us)
Async XLA Ops:
  0.0 9.1 %copy-start = (bf16[512,1024]{1,0:T(8,128)(2,1)S(1)}, bf16[512,1024]{1,0:T(8,128)(2,1)}, u32[]{:S(2)}) copy-start(bf16[512,1024]{1,0:T(8,128)(2,1)} %param.20) | copy-start | bytes 3145732
  0.0 11.1 %copy-start.6 = (bf16[1024,3,128]{2,0,1:T(8,128)(2,1)S(1)}, bf16[1024,3,128]{2,0,1:T(8,128)(2,1)}, u32[]{:S(2)}) copy-start(bf16[1024,3,128]{2,0,1:T(8,128)(2,1)} %param.16) | copy-start | bytes 2359300
  0.0 11.0 %copy-start.13 = (s32[16,8]{0,1:T(8,128)S(1)}, s32[16,8]{0,1:T(8,128)}, u32[]{:S(2)}) copy-start(s32[16,8]{0,1:T(8,128)} %param.13) | copy-start | bytes 1540
  2.4 17.7 %collective-permute-start = (bf16[2048,128]{1,0:T(8,128)(2,1)}, bf16[2048,128]{1,0:T(8,128)(2,1)S(1)}, u32[]{:S(2)}, u32[]{:S(2)}) collective-permute-start(bf16[2048,128]{1,0:T(8,128)(2,1)} %get-tuple-element.26), channel_id=1, source_target_pairs={{0,8},{8,16},{16,24},{24,32},{32,40},{40,48},{48,56},{56,64},{64,7... | collective-permute-start | bytes 1572872 | tf_op jit(solution)/shard_map/ppermute | solution.py:513
  6.2 16.9 %collective-permute-start.1 = (bf16[2048,128]{1,0:T(8,128)(2,1)}, bf16[2048,128]{1,0:T(8,128)(2,1)S(1)}, u32[]{:S(2)}, u32[]{:S(2)}) collective-permute-start(bf16[2048,128]{1,0:T(8,128)(2,1)} %get-tuple-element.27), channel_id=1, source_target_pairs={{8,0},{16,8},{24,16},{32,24},{40,32},{48,40},{56,48},{64,56},{72,6... | collective-permute-start | bytes 1572872 | tf_op jit(solution)/shard_map/ppermute | solution.py:513
  10.7 8.4 %collective-permute-start.2 = (bf16[144,1024]{1,0:T(8,128)(2,1)}, bf16[144,1024]{1,0:T(8,128)(2,1)}, u32[]{:S(2)}, u32[]{:S(2)}) collective-permute-start(bf16[144,1024]{1,0:T(8,128)(2,1)} %get-tuple-element.59), channel_id=1, source_target_pairs={{0,1},{1,0},{2,3},{3,2},{4,5},{5,4},{6,7},{7,6},{8,9},{9,8},{10,11... | collective-permute-start | bytes 884744 | tf_op jit(solution)/shard_map/ppermute | solution.py:517
  20.1 4.9 %copy-start.7 = (bf16[2048,128]{1,0:T(8,128)(2,1)}, bf16[2048,128]{1,0:T(8,128)(2,1)S(1)}, u32[]{:S(2)}) copy-start(bf16[2048,128]{1,0:T(8,128)(2,1)S(1)} %collective-permute-done) | copy-start | bytes 1572868
  23.2 1.9 copy-start.8
  23.2 29.6 %collective-permute-start.3 = (bf16[2,144,1024]{2,1,0:T(8,128)(2,1)S(1)}, bf16[2,144,1024]{2,1,0:T(8,128)(2,1)S(1)}, u32[]{:S(2)}, u32[]{:S(2)}) collective-permute-start(bf16[2,144,1024]{2,1,0:T(8,128)(2,1)S(1)} %pad_maximum_fusion), channel_id=1, source_target_pairs={{0,2},{1,3},{2,4},{3,5},{4,6},{5,7},{6,0},{7,1},{8,10},{9,11},{10,... | collective-permute-start | bytes 1769480 | tf_op jit(solution)/shard_map/ppermute | solution.py:517
  32.3 17.2 %collective-permute-start.10 = (bf16[2048,128]{1,0:T(8,128)(2,1)}, bf16[2048,128]{1,0:T(8,128)(2,1)S(1)}, u32[]{:S(2)}, u32[]{:S(2)}) collective-permute-start(bf16[2048,128]{1,0:T(8,128)(2,1)} %encode.1.s0), channel_id=1, source_target_pairs={{0,2},{1,3},{2,4},{3,5},{4,6},{5,7},{6,0},{7,1},{8,10},{9,11},{10,... | collective-permute-start | bytes 1572872 | tf_op jit(solution)/shard_map/ppermute | solution.py:517
  33.7 16.3 %collective-permute-start.7 = (bf16[2048,128]{1,0:T(8,128)(2,1)}, bf16[2048,128]{1,0:T(8,128)(2,1)S(1)}, u32[]{:S(2)}, u32[]{:S(2)}) collective-permute-start(bf16[2048,128]{1,0:T(8,128)(2,1)} %encode.1.s0), channel_id=1, source_target_pairs={{0,1},{1,0},{2,3},{3,2},{4,5},{5,4},{6,7},{7,6},{8,9},{9,8},{10,11... | collective-permute-start | bytes 1572872 | tf_op jit(solution)/shard_map/ppermute | solution.py:517
  33.7 17.6 %collective-permute-start.12 = (bf16[2048,128]{1,0:T(8,128)(2,1)}, bf16[2048,128]{1,0:T(8,128)(2,1)S(1)}, u32[]{:S(2)}, u32[]{:S(2)}) collective-permute-start(bf16[2048,128]{1,0:T(8,128)(2,1)} %encode.1.s0), channel_id=1, source_target_pairs={{0,6},{1,7},{2,0},{3,1},{4,2},{5,3},{6,4},{7,5},{8,14},{9,15},{10,... | collective-permute-start | bytes 1572872 | tf_op jit(solution)/shard_map/ppermute | solution.py:517
  35.1 24.6 %collective-permute-start.4 = (bf16[2,144,1024]{2,1,0:T(8,128)(2,1)S(1)}, bf16[2,144,1024]{2,1,0:T(8,128)(2,1)S(1)}, u32[]{:S(2)}, u32[]{:S(2)}) collective-permute-start(bf16[2,144,1024]{2,1,0:T(8,128)(2,1)S(1)} %pad_maximum_fusion), channel_id=1, source_target_pairs={{0,6},{1,7},{2,0},{3,1},{4,2},{5,3},{6,4},{7,5},{8,14},{9,15},{10,... | collective-permute-start | bytes 1769480 | tf_op jit(solution)/shard_map/ppermute | solution.py:517
  49.5 1.8 copy-start.11
  49.5 28.9 %collective-permute-start.11 = (bf16[1024,128]{1,0:T(8,128)(2,1)S(1)}, bf16[1024,128]{1,0:T(8,128)(2,1)}, u32[]{:S(2)}, u32[]{:S(2)}) collective-permute-start(bf16[1024,128]{1,0:T(8,128)(2,1)S(1)} %slice.78), channel_id=1, source_target_pairs={{0,2},{1,3},{2,4},{3,5},{4,6},{5,7},{6,0},{7,1},{8,10},{9,11},{10,... | collective-permute-start | bytes 786440 | tf_op jit(solution)/shard_map/ppermute | solution.py:517
  50.0 28.5 %copy-start.17 = (bf16[2048,128]{1,0:T(8,128)(2,1)}, bf16[2048,128]{1,0:T(8,128)(2,1)S(1)}, u32[]{:S(2)}) copy-start(bf16[2048,128]{1,0:T(8,128)(2,1)S(1)} %collective-permute-done.7.s1) | copy-start | bytes 1572868
  50.0 34.1 %collective-permute-start.8 = (bf16[2048,128]{1,0:T(8,128)(2,1)S(1)}, bf16[2048,128]{1,0:T(8,128)(2,1)S(1)}, u32[]{:S(2)}, u32[]{:S(2)}) collective-permute-start(bf16[2048,128]{1,0:T(8,128)(2,1)S(1)} %collective-permute-done.7.s1), channel_id=1, source_target_pairs={{0,2},{1,3},{2,4},{3,5},{4,6},{5,7},{6,0},{7,1},{8,10},{9,11},{10,... | collective-permute-start | bytes 1572872 | tf_op jit(solution)/shard_map/ppermute | solution.py:517
  51.3 27.2 %copy-start.12 = (bf16[2048,128]{1,0:T(8,128)(2,1)}, bf16[2048,128]{1,0:T(8,128)(2,1)S(1)}, u32[]{:S(2)}) copy-start(bf16[2048,128]{1,0:T(8,128)(2,1)S(1)} %collective-permute-done.12.s4) | copy-start | bytes 1572868
  51.3 32.8 %collective-permute-start.9 = (bf16[2048,128]{1,0:T(8,128)(2,1)S(1)}, bf16[2048,128]{1,0:T(8,128)(2,1)S(1)}, u32[]{:S(2)}, u32[]{:S(2)}) collective-permute-start(bf16[2048,128]{1,0:T(8,128)(2,1)S(1)} %collective-permute-done.7.s1), channel_id=1, source_target_pairs={{0,6},{1,7},{2,0},{3,1},{4,2},{5,3},{6,4},{7,5},{8,14},{9,15},{10,... | collective-permute-start | bytes 1572872 | tf_op jit(solution)/shard_map/ppermute | solution.py:517
  52.8 23.7 %collective-permute-start.5 = (bf16[144,1024]{1,0:T(8,128)(2,1)S(1)}, bf16[144,1024]{1,0:T(8,128)(2,1)S(1)}, u32[]{:S(2)}, u32[]{:S(2)}) collective-permute-start(bf16[144,1024]{1,0:T(8,128)(2,1)S(1)} %slice_bitcast_fusion.1), channel_id=1, source_target_pairs={{0,2},{1,3},{2,4},{3,5},{4,6},{5,7},{6,0},{7,1},{8,10},{9,11},{10,... | collective-permute-start | bytes 884744 | tf_op jit(solution)/shard_map/ppermute | solution.py:517
  59.7 18.0 %collective-permute-start.6 = (bf16[144,1024]{1,0:T(8,128)(2,1)S(1)}, bf16[144,1024]{1,0:T(8,128)(2,1)S(1)}, u32[]{:S(2)}, u32[]{:S(2)}) collective-permute-start(bf16[144,1024]{1,0:T(8,128)(2,1)S(1)} %slice_bitcast_fusion), channel_id=1, source_target_pairs={{0,6},{1,7},{2,0},{3,1},{4,2},{5,3},{6,4},{7,5},{8,14},{9,15},{10,... | collective-permute-start | bytes 884744 | tf_op jit(solution)/shard_map/ppermute | solution.py:517
  76.5 7.6 %collective-permute-start.13 = (bf16[1024,128]{1,0:T(8,128)(2,1)S(1)}, bf16[1024,128]{1,0:T(8,128)(2,1)}, u32[]{:S(2)}, u32[]{:S(2)}) collective-permute-start(bf16[1024,128]{1,0:T(8,128)(2,1)S(1)} %slice.79), channel_id=1, source_target_pairs={{0,6},{1,7},{2,0},{3,1},{4,2},{5,3},{6,4},{7,5},{8,14},{9,15},{10,... | collective-permute-start | bytes 786440 | tf_op jit(solution)/shard_map/ppermute | solution.py:517
  84.9 0.8 copy-start.19
  84.9 51.8 %collective-permute-start.14 = (bf16[8,144,1024]{2,1,0:T(8,128)(2,1)}, bf16[8,144,1024]{2,1,0:T(8,128)(2,1)S(1)}, u32[]{:S(2)}, u32[]{:S(2)}) collective-permute-start(bf16[8,144,1024]{2,1,0:T(8,128)(2,1)} %bitcast_dynamic-update-slice_fusion.refs_0_), channel_id=1, source_target_pairs={{0,16},{8,24},{16,32},{24,40},{32,48},{40,56},{48,0},{56,8},{64,80... | collective-permute-start | bytes 7077896 | tf_op jit(solution)/shard_map/ppermute | solution.py:517
  85.7 59.4 %collective-permute-start.15 = (bf16[8,144,1024]{2,1,0:T(8,128)(2,1)}, bf16[8,144,1024]{2,1,0:T(8,128)(2,1)}, u32[]{:S(2)}, u32[]{:S(2)}) collective-permute-start(bf16[8,144,1024]{2,1,0:T(8,128)(2,1)} %bitcast_dynamic-update-slice_fusion.refs_0_), channel_id=1, source_target_pairs={{0,48},{8,56},{16,0},{24,8},{32,16},{40,24},{48,32},{56,40},{64,11... | collective-permute-start | bytes 7077896 | tf_op jit(solution)/shard_map/ppermute | solution.py:517
  86.4 6.3 %collective-permute-start.16 = (bf16[1024,128]{1,0:T(8,128)(2,1)}, bf16[1024,128]{1,0:T(8,128)(2,1)}, u32[]{:S(2)}, u32[]{:S(2)}) collective-permute-start(bf16[1024,128]{1,0:T(8,128)(2,1)} %collective-permute-done.11.lo6), channel_id=1, source_target_pairs={{0,1},{1,0},{2,3},{3,2},{4,5},{5,4},{6,7},{7,6},{8,9},{9,8},{10,11... | collective-permute-start | bytes 786440 | tf_op jit(solution)/shard_map/ppermute | solution.py:517
  86.4 11.9 %collective-permute-start.17 = (bf16[1024,128]{1,0:T(8,128)(2,1)}, bf16[1024,128]{1,0:T(8,128)(2,1)}, u32[]{:S(2)}, u32[]{:S(2)}) collective-permute-start(bf16[1024,128]{1,0:T(8,128)(2,1)} %collective-permute-done.13.hi6), channel_id=1, source_target_pairs={{0,1},{1,0},{2,3},{3,2},{4,5},{5,4},{6,7},{7,6},{8,9},{9,8},{10,11... | collective-permute-start | bytes 786440 | tf_op jit(solution)/shard_map/ppermute | solution.py:517
  110.1 39.5 %collective-permute-start.18 = (bf16[1152,256]{1,0:T(8,128)(2,1)S(1)}, bf16[1152,256]{1,0:T(8,128)(2,1)S(1)}, u32[]{:S(2)}, u32[]{:S(2)}) collective-permute-start(bf16[1152,256]{1,0:T(8,128)(2,1)S(1)} %get-tuple-element.50), channel_id=1, source_target_pairs={{0,8},{8,16},{16,24},{24,32},{32,40},{40,48},{48,56},{56,64},{64,7... | collective-permute-start | bytes 1769480 | tf_op jit(solution)/shard_map/ppermute | solution.py:513
  112.6 37.1 %collective-permute-start.19 = (bf16[1152,256]{1,0:T(8,128)(2,1)S(1)}, bf16[1152,256]{1,0:T(8,128)(2,1)S(1)}, u32[]{:S(2)}, u32[]{:S(2)}) collective-permute-start(bf16[1152,256]{1,0:T(8,128)(2,1)S(1)} %get-tuple-element.49), channel_id=1, source_target_pairs={{8,0},{16,8},{24,16},{32,24},{40,32},{48,40},{56,48},{64,56},{72,6... | collective-permute-start | bytes 1769480 | tf_op jit(solution)/shard_map/ppermute | solution.py:513
  136.7 12.9 %copy-start.4 = (bf16[8,144,1024]{2,1,0:T(8,128)(2,1)}, bf16[8,144,1024]{2,1,0:T(8,128)(2,1)S(1)}, u32[]{:S(2)}) copy-start(bf16[8,144,1024]{2,1,0:T(8,128)(2,1)S(1)} %collective-permute-done.14.refs_1_) | copy-start | bytes 7077892
  137.9 42.5 %collective-permute-start.20 = (bf16[4,144,1024]{2,1,0:T(8,128)(2,1)}, bf16[4,144,1024]{2,1,0:T(8,128)(2,1)}, u32[]{:S(2)}, u32[]{:S(2)}) collective-permute-start(bf16[4,144,1024]{2,1,0:T(8,128)(2,1)} %slice.80), channel_id=1, source_target_pairs={{0,16},{8,24},{16,32},{24,40},{32,48},{40,56},{48,0},{56,8},{64,80... | collective-permute-start | bytes 3538952 | tf_op jit(solution)/shard_map/ppermute | solution.py:517
  147.4 33.0 %collective-permute-start.21 = (bf16[4,144,1024]{2,1,0:T(8,128)(2,1)}, bf16[4,144,1024]{2,1,0:T(8,128)(2,1)}, u32[]{:S(2)}, u32[]{:S(2)}) collective-permute-start(bf16[4,144,1024]{2,1,0:T(8,128)(2,1)} %slice.81), channel_id=1, source_target_pairs={{0,48},{8,56},{16,0},{24,8},{32,16},{40,24},{48,32},{56,40},{64,11... | collective-permute-start | bytes 3538952 | tf_op jit(solution)/shard_map/ppermute | solution.py:517
  147.5 38.5 %collective-permute-start.22 = (bf16[8,144,1024]{2,1,0:T(8,128)(2,1)}, bf16[8,144,1024]{2,1,0:T(8,128)(2,1)}, u32[]{:S(2)}, u32[]{:S(2)}) collective-permute-start(bf16[8,144,1024]{2,1,0:T(8,128)(2,1)} %bitcast_dynamic-update-slice_fusion.refs_0_), channel_id=1, source_target_pairs={{0,8},{8,0},{16,24},{24,16},{32,40},{40,32},{48,56},{56,48},{64,72... | collective-permute-start | bytes 7077896 | tf_op jit(solution)/shard_map/ppermute | solution.py:517
  149.6 0.8 copy-start.15
  149.6 45.1 %collective-permute-start.23 = (bf16[8,144,1024]{2,1,0:T(8,128)(2,1)S(1)}, bf16[8,144,1024]{2,1,0:T(8,128)(2,1)}, u32[]{:S(2)}, u32[]{:S(2)}) collective-permute-start(bf16[8,144,1024]{2,1,0:T(8,128)(2,1)S(1)} %collective-permute-done.14.refs_1_), channel_id=1, source_target_pairs={{0,8},{8,0},{16,24},{24,16},{32,40},{40,32},{48,56},{56,48},{64,72... | collective-permute-start | bytes 7077896 | tf_op jit(solution)/shard_map/ppermute | solution.py:517
  150.4 0.8 copy-start.16
  151.3 43.5 %collective-permute-start.24 = (bf16[8,144,1024]{2,1,0:T(8,128)(2,1)}, bf16[8,144,1024]{2,1,0:T(8,128)(2,1)}, u32[]{:S(2)}, u32[]{:S(2)}) collective-permute-start(bf16[8,144,1024]{2,1,0:T(8,128)(2,1)} %collective-permute-done.15.refs_2_), channel_id=1, source_target_pairs={{0,8},{8,0},{16,24},{24,16},{32,40},{40,32},{48,56},{56,48},{64,72... | collective-permute-start | bytes 7077896 | tf_op jit(solution)/shard_map/ppermute | solution.py:517
  180.4 14.3 %collective-permute-start.25 = (bf16[4,144,1024]{2,1,0:T(8,128)(2,1)}, bf16[4,144,1024]{2,1,0:T(8,128)(2,1)}, u32[]{:S(2)}, u32[]{:S(2)}) collective-permute-start(bf16[4,144,1024]{2,1,0:T(8,128)(2,1)} %collective-permute-done.20.refs_3_), channel_id=1, source_target_pairs={{0,8},{8,0},{16,24},{24,16},{32,40},{40,32},{48,56},{56,48},{64,72... | collective-permute-start | bytes 3538952 | tf_op jit(solution)/shard_map/ppermute | solution.py:517
  181.0 13.8 %collective-permute-start.26 = (bf16[4,144,1024]{2,1,0:T(8,128)(2,1)}, bf16[4,144,1024]{2,1,0:T(8,128)(2,1)}, u32[]{:S(2)}, u32[]{:S(2)}) collective-permute-start(bf16[4,144,1024]{2,1,0:T(8,128)(2,1)} %collective-permute-done.21.refs_4_), channel_id=1, source_target_pairs={{0,8},{8,0},{16,24},{24,16},{32,40},{40,32},{48,56},{56,48},{64,72... | collective-permute-start | bytes 3538952 | tf_op jit(solution)/shard_map/ppermute | solution.py:517
  181.1 13.7 %all-to-all-start = ((bf16[8,256,128]{2,1,0:T(8,128)(2,1)}), bf16[8,256,128]{2,1,0:T(8,128)(2,1)}, u32[]{:S(2)}, u32[]{:S(2)}) async-start(bf16[8,256,128]{2,1,0:T(8,128)(2,1)} %bitcast.47), calls=%async_computation | async-start | bytes 1048576 | tf_op jit(solution)/shard_map/all_to_all | solution.py:598
  194.8 30.9 %copy-start.14 = (s32[64,2]{0,1:T(2,128)S(1)}, s32[64,2]{0,1:T(2,128)}, u32[]{:S(2)}) copy-start(s32[64,2]{0,1:T(2,128)} %param.21) | copy-start | bytes 1540
  219.1 13.7 %copy-start.5 = (bf16[8,256,128]{2,1,0:T(8,128)(2,1)}, bf16[8,256,128]{2,1,0:T(8,128)(2,1)S(1)}, u32[]{:S(2)}) copy-start(bf16[8,256,128]{2,1,0:T(8,128)(2,1)S(1)} %all_to_all.15) | copy-start | bytes 1572868
  219.2 7.3 %collective-permute-start.27 = (bf16[8,128,128]{2,1,0:T(8,128)(2,1)S(1)}, bf16[8,128,128]{2,1,0:T(8,128)(2,1)S(1)}, u32[]{:S(2)}, u32[]{:S(2)}) collective-permute-start(bf16[8,128,128]{2,1,0:T(8,128)(2,1)S(1)} %bitcast.52), channel_id=1, source_target_pairs={{0,8},{8,16},{16,24},{24,32},{32,40},{40,48},{48,56},{56,64},{64,7... | collective-permute-start | bytes 786440 | tf_op jit(solution)/shard_map/ppermute | solution.py:513
  221.5 11.3 %collective-permute-start.28 = (bf16[8,128,128]{2,1,0:T(8,128)(2,1)S(1)}, bf16[8,128,128]{2,1,0:T(8,128)(2,1)S(1)}, u32[]{:S(2)}, u32[]{:S(2)}) collective-permute-start(bf16[8,128,128]{2,1,0:T(8,128)(2,1)S(1)} %bitcast.51), channel_id=1, source_target_pairs={{8,0},{16,8},{24,16},{32,24},{40,32},{48,40},{56,48},{64,56},{72,6... | collective-permute-start | bytes 786440 | tf_op jit(solution)/shard_map/ppermute | solution.py:513
  226.4 6.4 %copy-start.9 = (bf16[8,128,128]{2,1,0:T(8,128)(2,1)}, bf16[8,128,128]{2,1,0:T(8,128)(2,1)S(1)}, u32[]{:S(2)}) copy-start(bf16[8,128,128]{2,1,0:T(8,128)(2,1)S(1)} %collective-permute-done.27.low) | copy-start | bytes 786436
  233.5 17.6 %copy-start.1 = (bf16[8192,128]{1,0:T(8,128)(2,1)S(1)}, bf16[8192,128]{1,0:T(8,128)(2,1)}, u32[]{:S(2)}) copy-start(bf16[8192,128]{1,0:T(8,128)(2,1)} %state.1) | copy-start | bytes 6291460
  233.6 17.6 %copy-start.3 = (f32[128]{0:T(128)S(1)}, f32[128]{0:T(128)}, u32[]{:S(2)}) copy-start(f32[128]{0:T(128)} %param.23) | copy-start | bytes 1540
  251.2 1.6 copy-start.2
  (2 other events, 1.5 us)

commit v4 on v3

--- a/solution.py
+++ b/solution.py
@@ -121,10 +121,14 @@
     raw.append(jnp.where(early, lo6[...], hi6[...]))
     raw.append(jnp.where(early, lo7[...], hi7[...]))
 
-    @pl.when(step == order[0])
-    def _():
-        for p in range(8):
-            share[order[p]] = raw[p]
+    tile = share.shape[1]
+    per = raw[0].shape[0] // tile
+    for n in range(per):
+
+        @pl.when(order[0] == step * per + n)
+        def _():
+            for p in range(8):
+                share[order[p]] = raw[p][n * tile : (n + 1) * tile]
 
     pieces = [r.astype(F32) for r in raw]
     total = pieces[0]
@@ -146,10 +150,11 @@
 
 def project(order, slots, gain, weights):
     rows = slots[0].shape[0]
-    tile = rows // 8
-    full = pl.BlockSpec((tile, BLOCK), lambda i, _: (i, 0))
-    early = pl.BlockSpec((tile, BLOCK), lambda i, _: (jnp.minimum(i, 3), 0))
-    late = pl.BlockSpec((tile, BLOCK), lambda i, _: (jnp.maximum(i - 4, 0), 0))
+    tile, steps = rows // 8, 4
+    each = rows // steps
+    full = pl.BlockSpec((each, BLOCK), lambda i, _: (i, 0))
+    early = pl.BlockSpec((each, BLOCK), lambda i, _: (jnp.minimum(i, steps // 2 - 1), 0))
+    late = pl.BlockSpec((each, BLOCK), lambda i, _: (jnp.maximum(i - steps // 2, 0), 0))
     return pl.pallas_call(
         project_kernel,
         out_shape=(
@@ -159,14 +164,14 @@
         ),
         grid_spec=pltpu.PrefetchScalarGridSpec(
             num_scalar_prefetch=1,
-            grid=(8,),
+            grid=(steps,),
             in_specs=[full] * 6
             + [early, late, early, late]
             + [whole((8, 1, BLOCK))]
             + [whole((8, BLOCK, BLOCK))] * 3,
             out_specs=(
                 full,
-                pl.BlockSpec((tile, 2 * BLOCK), lambda i, _: (i, 0)),
+                pl.BlockSpec((each, 2 * BLOCK), lambda i, _: (i, 0)),
                 whole((8, tile, BLOCK)),
             ),
             scratch_shapes=[pltpu.VMEM((D, 3 * BLOCK), BF)],
@@ -292,49 +297,53 @@
 
 
 def forward_kernel(table, *refs):
-    parts = refs[:10]
-    context, share, gain, out, expand, shrink, outward, sems = refs[10:]
+    parts = refs[:8]
+    context, share, gain, out, expand, shrink, outward, sems = refs[8:]
     groups = ([], [], [])
-    width = expand.shape[2]
+    width = expand.shape[3]
     for n, part in enumerate(parts):
-        first = 4 if n % 5 == 4 else 0
-        count = part.shape[0]
         where = table[8 + n]
-        slots = pl.ds(first, count)
-
-        def copy(group, source, target):
-            groups[group].append(
-                pltpu.make_async_copy(source, target, sems.at[group, len(groups[group])])
-            )
-
-        copy(
-            0,
-            part.at[:, pl.ds(ROWS_E + ROWS_S, ROWS_P), :],
-            outward.at[slots, pl.ds(pl.multiple_of(where * ROWS_P, ROWS_P), ROWS_P), :],
-        )
         for side in range(2):
+            slot = 1 - side if n % 4 == 3 else side
+
+            def copy(group, source, target):
+                groups[group].append(
+                    pltpu.make_async_copy(source, target, sems.at[group, len(groups[group])])
+                )
+
             copy(
-                1,
-                part.at[:, pl.ds(0, ROWS_E), pl.ds(side * width, width)],
-                expand.at[
-                    slots,
-                    pl.ds(pl.multiple_of(where * 2 * ROWS_E + side * ROWS_E, ROWS_E), ROWS_E),
-                    :,
+                0,
+                part.at[:, side, pl.ds(ROWS_E + ROWS_S, ROWS_P), :],
+                outward.at[
+                    :, slot, pl.ds(pl.multiple_of(where * ROWS_P, ROWS_P), ROWS_P), :
                 ],
             )
-        copy(
-            2,
-            part.at[:, pl.ds(ROWS_E, ROWS_S), :],
-            shrink.at[slots, pl.ds(pl.multiple_of(where * ROWS_S, ROWS_S), ROWS_S), :],
-        )
+            for piece in range(2):
+                copy(
+                    1,
+                    part.at[:, side, pl.ds(0, ROWS_E), pl.ds(piece * width, width)],
+                    expand.at[
+                        :,
+                        slot,
+                        pl.ds(
+                            pl.multiple_of(where * 2 * ROWS_E + piece * ROWS_E, ROWS_E), ROWS_E
+                        ),
+                        :,
+                    ],
+                )
+            copy(
+                2,
+                part.at[:, side, pl.ds(ROWS_E, ROWS_S), :],
+                shrink.at[:, slot, pl.ds(pl.multiple_of(where * ROWS_S, ROWS_S), ROWS_S), :],
+            )
     for group in groups:
         for c in group:
             c.start()
     for c in groups[0]:
         c.wait()
-    total = dot(context[table[0]], outward[0])
+    total = dot(context[table[0]], outward[0, 0])
     for p in range(1, 8):
-        total = total + dot(context[table[p]], outward[p])
+        total = total + dot(context[table[p]], outward[p // 2, p % 2])
     start = jnp.concatenate([share[h] for h in range(8)], axis=1).astype(F32)
     middle = (start + total).astype(BF).astype(F32)
     average = jnp.mean(middle, axis=1, keepdims=True)
@@ -343,12 +352,12 @@
     normed = (centred * lax.rsqrt(spread + EPSILON) * gain[...]).astype(BF)
     for c in groups[1]:
         c.wait()
-    hidden = [gelu(dot(normed, expand[p])).astype(BF) for p in range(8)]
+    hidden = [gelu(dot(normed, expand[p // 2, p % 2])).astype(BF) for p in range(8)]
     for c in groups[2]:
         c.wait()
     total = middle
     for p in range(8):
-        total = total + dot(hidden[p], shrink[p])
+        total = total + dot(hidden[p], shrink[p // 2, p % 2])
     done = total.astype(BF)
     for h in range(8):
         out[h] = done[:, h * BLOCK : (h + 1) * BLOCK]
@@ -363,14 +372,14 @@
         grid_spec=pltpu.PrefetchScalarGridSpec(
             num_scalar_prefetch=1,
             grid=(1,),
-            in_specs=[ANY] * 10
+            in_specs=[ANY] * 8
             + [whole((8, rows, BLOCK)), whole((8, rows, BLOCK)), whole((1, D))],
             out_specs=whole((8, rows, BLOCK)),
             scratch_shapes=[
-                pltpu.VMEM((8, D, width), BF),
-                pltpu.VMEM((8, width, D), BF),
-                pltpu.VMEM((8, BLOCK, D), BF),
-                pltpu.SemaphoreType.DMA((3, 20)),
+                pltpu.VMEM((4, 2, D, width), BF),
+                pltpu.VMEM((4, 2, width, D), BF),
+                pltpu.VMEM((4, 2, BLOCK, D), BF),
+                pltpu.SemaphoreType.DMA((3, 32)),
             ],
         ),
         compiler_params=params(56),
@@ -523,11 +532,10 @@
 
 UP = lambda v: among(v, "seq", 16, lambda i: along_z(i, 1))
 DOWN = lambda v: among(v, "seq", 16, lambda i: along_z(i, -1))
+ACROSS = lambda v: among(v, ("seq", "head"), 128, lambda i: i ^ 65)
 TWIN = lambda v: among(v, "seq", 16, lambda i: i ^ 1)
 NORTH = lambda v: among(v, "head", 8, lambda i: (i + 2) % 8)
 SOUTH = lambda v: among(v, "head", 8, lambda i: (i - 2) % 8)
-
-
 OVER = lambda v: among(v, "head", 8, lambda i: i ^ 1)
 
 
@@ -561,11 +569,12 @@
     low = shifted(last, 1)
     high = shifted(first, -1)
 
-    position = band % 8
+    core, place = band % 2, (band // 2 + 2 * (band // 8)) % 4
+    position = place * 2 + core
     packed = pack_weights(position, expand, shrink, outward)
     inward = [inward[:, j, :].reshape(8, BLOCK, BLOCK) for j in range(3)]
     packed = jnp.stack([packed, OVER(packed)])
-    low, high, packed, *inward = lax.optimization_barrier((low, high, packed, *inward))
+    low, high, *inward = lax.optimization_barrier((low, high, *inward))
     packed_a, packed_b = NORTH(packed), SOUTH(packed)
 
     mesh_start = encode(
@@ -573,14 +582,16 @@
     )
     half = mesh_rows // 2
     x = mesh_start
-    y, xa, xb = OVER(x), NORTH(x), SOUTH(x)
+    y, xa, xb = lax.optimization_barrier((OVER(x), NORTH(x), SOUTH(x)))
     xc, xd = NORTH(xa[:half]), SOUTH(xb[half:])
     ya, yb = NORTH(y), SOUTH(y)
     yc, yd = OVER(xc), OVER(xd)
     slots = (x, y, xa, ya, xb, yb, xc, xd, yc, yd)
+    packed_a, packed_b, *_ = lax.optimization_barrier(
+        (packed_a, packed_b, xc, xd, ya, yb)
+    )
     far = jnp.stack([NORTH(packed_a[0]), SOUTH(packed_b[1])])
-    mine = jnp.concatenate([packed, packed_a, packed_b, far], axis=0)
-    mine, *_ = lax.optimization_barrier((mine, ya, yb, xc, xd))
+    mine = jnp.stack([packed, packed_a, packed_b, far])
     partner = me ^ 1
     order = jnp.stack(
         [me, partner] + [(v + by) % 8 for by in (6, 2, 4) for v in (me, partner)]
@@ -588,21 +599,17 @@
     queries, keys_values, share = project(order, slots, first_gain, inward)
     below = shifted(keys_values[mesh_rows - REACH :], 1)
     above = shifted(keys_values[:REACH], -1)
-    up, down = UP(mine), DOWN(mine)
-    far_up, far_down = UP(up[:4]), DOWN(down[4:])
+    others = [UP(mine), DOWN(mine), ACROSS(mine)]
     edges = jnp.stack([band == 0, band == bands - 1]).astype(jnp.int32)
     context = attend(edges, queries, below, keys_values, above)
-    context, far_up, far_down = lax.optimization_barrier((context, far_up, far_down))
-    here = [mine, up, down, far_up, far_down]
+    context, *others = lax.optimization_barrier((context, *others))
+    here = [mine, *others]
     parts = here + [TWIN(v) for v in here]
     context = lax.all_to_all(
         context.reshape(8, mesh_rows // 8, BLOCK), "head", 0, 0, tiled=True
     )
-    z, core = position // 2, position % 2
     places = [
-        ((z + by) % 4) * 2 + side
-        for side in (core, 1 - core)
-        for by in (0, 3, 1, 2, 2)
+        ((place + by) % 4) * 2 + side for side in (core, 1 - core) for by in (0, 3, 1, 2)
     ]
     table = jnp.concatenate([order, jnp.stack(places).astype(jnp.int32)])
     mesh_end = forward(table, parts, context, share, second_gain)

time: 261 us -> 253 us (0.969)
  starting transfers between devices: 40.7 us -> 78.6 us
  waiting for transfers between devices: 99 us -> 65.4 us
  local copies, waits for them, and re-layouts: 21.7 us -> 13.6 us
    ppermute x23 -> x21, waiting for transfers between devices: 80.7 us -> 33.1 us  [among(): return lax.ppermute(value, axis, [(i, to(i)) for i in range(count)])]
    ppermute x23 -> x21, starting transfers between devices: 17.7 us -> 52.5 us  [among(): return lax.ppermute(value, axis, [(i, to(i)) for i in range(count)])]
    ppermute x6, waiting for transfers between devices: 9.45 us -> 23.6 us  [shifted(): lax.ppermute(value, 'seq', [(i, i + by) for i in range(16) if 0 <= i + by...]
    unnamed x46 -> x36, local copies, waits for them, and re-layouts: 8.99 us -> 4.09 us
    slice x2 -> x0, local copies, waits for them, and re-layouts: 3.56 us -> none  [on_device(): far_up, far_down = (UP(up[:4]), DOWN(down[4:]))]
    ppermute x6, starting transfers between devices: 18.8 us -> 22 us  [shifted(): lax.ppermute(value, 'seq', [(i, i + by) for i in range(16) if 0 <= i + by...]
  transfers between devices with their start and end apart: 30 -> 28, of which waited for: 12 -> 13; matrix products, arithmetic and copies ran while one was open for 6% -> 4% of each run, Pallas kernels for 18% -> 18%
where the time goes in v4:
time: 253 us; the launch traced here: 252 us
  starting transfers between devices  78.6 us (31%)
  Pallas kernels  70.5 us (28%)
  waiting for transfers between devices  65.4 us (26%)
  blocking collectives  20.4 us (8%)
  local copies, waits for them, and re-layouts  13.6 us (5%)
  other arithmetic  3.09 us (1%)
    ppermute x21, starting transfers between devices, among(): return lax.ppermute(value, axis, [(i, to(i)) for i in range(count)])  52.5 us
    ppermute x21, waiting for transfers between devices, among(): return lax.ppermute(value, axis, [(i, to(i)) for i in range(count)])  33.1 us
    pallas_call x1, Pallas kernels, attend(): pl.pallas_call(attend_kernel, out_shape=jax.ShapeDtypeStruct((rows, BLOCK...  28.5 us
    ppermute x6, waiting for transfers between devices, shifted(): lax.ppermute(value, 'seq', [(i, i + by) for i in range(16) if 0 <= i + by...  23.6 us
    ppermute x6, starting transfers between devices, shifted(): lax.ppermute(value, 'seq', [(i, i + by) for i in range(16) if 0 <= i + by...  22 us
    pallas_call x1, Pallas kernels, forward(): pl.pallas_call(forward_kernel, out_shape=jax.ShapeDtypeStruct((8, rows, B...  12.8 us
    all_to_all x1, blocking collectives, on_device(): mesh_end = lax.all_to_all(mesh_end, 'head', 0, 0, tiled=True)  11.9 us
    pallas_call x1, Pallas kernels, project(): pl.pallas_call(project_kernel, out_shape=(jax.ShapeDtypeStruct((rows, BLO...  8.85 us
  transfers between devices with their start and end apart: 28, of which 13 were waited for; matrix products, arithmetic and copies ran while one was open for 4% of the time, Pallas kernels for 18%

profile of v4, /device:TPU:97, one launch (start us, length us, event | category | flops | bytes accessed | tf_op | source)
XLA Modules:
  0.0 252.3 jit_solution(448091327490571180)
XLA Ops:
  0.0 2.4 fusion.2
  2.4 3.8 %collective-permute-start.3 = (bf16[2048,128]{1,0:T(8,128)(2,1)}, bf16[2048,128]{1,0:T(8,128)(2,1)S(1)}, u32[]{:S(2)}, u32[]{:S(2)}) collective-permute-start(bf16[2048,128]{1,0:T(8,128)(2,1)} %get-tuple-element.33), channel_id=1, source_target_pairs={{0,8},{8,16},{16,24},{24,32},{32,40},{40,48},{48,56},{56,64},{64,7... | collective-permute-start | bytes 1572872 | tf_op jit(solution)/shard_map/ppermute | solution.py:522
  6.2 1.9 collective-permute-start.4
  8.2 0.9 constant_dynamic-slice_fusion
  9.2 0.8 constant_dynamic-slice_fusion.1
  9.9 0.8 fusion.1
  11.1 0.9 fusion.4
  12.7 10.5 %collective-permute-done.4 = bf16[2048,128]{1,0:T(8,128)(2,1)S(1)} collective-permute-done((bf16[2048,128]{1,0:T(8,128)(2,1)}, bf16[2048,128]{1,0:T(8,128)(2,1)S(1)}, u32[]{:S(2)}, u32[]{:S(2)}) %collective-permute-start.4) | collective-permute-done | bytes 524320 | tf_op jit(solution)/shard_map/ppermute | solution.py:522
  23.2 0.8 copy-done.8
  24.0 7.2 %encode.1.s0 = bf16[2048,128]{1,0:T(8,128)(2,1)} custom-call(s32[16,8]{1,0:T(8,128)} %broadcast_subtract_fusion.1.index, bf16[16,128,128]{2,1,0:T(8,128)(2,1)} %bitcast.51, bf16[64,128,128]{2,1,0:T(8,128)(2,1)} %bitcast.46, bf16[16,128,128]{2,1,0:T(8,128)(2,1)} %bitcast.52, bf16[16,8,128,128]{3,2,1,0:T(8,128)(2,1)} %weights.2), custom_call_target="tpu_custom_call" | custom-call | flops 540000000 | bytes 8000000 | tf_op jit(solution)/shard_map/encode/pallas_call | solution.py:84
  31.3 1.4 collective-permute-start.6
  32.7 1.5 collective-permute-start.7
  34.4 2.7 %collective-permute-start.2 = (bf16[2,144,1024]{2,1,0:T(8,128)(2,1)S(1)}, bf16[2,144,1024]{2,1,0:T(8,128)(2,1)S(1)}, u32[]{:S(2)}, u32[]{:S(2)}) collective-permute-start(bf16[2,144,1024]{2,1,0:T(8,128)(2,1)S(1)} %get-tuple-element.65), channel_id=1, source_target_pairs={{0,6},{1,7},{2,0},{3,1},{4,2},{5,3},{6,4},{7,5},{8,14},{9,15},{10,... | collective-permute-start | bytes 1769480 | tf_op jit(solution)/shard_map/ppermute | solution.py:526
  37.0 2.8 %collective-permute-done.5.s1 = bf16[2048,128]{1,0:T(8,128)(2,1)S(1)} collective-permute-done((bf16[2048,128]{1,0:T(8,128)(2,1)}, bf16[2048,128]{1,0:T(8,128)(2,1)S(1)}, u32[]{:S(2)}, u32[]{:S(2)}) %collective-permute-start.5) | collective-permute-done | bytes 524320 | tf_op jit(solution)/shard_map/ppermute | solution.py:526
  39.8 7.0 %collective-permute-done.6.s2 = bf16[2048,128]{1,0:T(8,128)(2,1)S(1)} collective-permute-done((bf16[2048,128]{1,0:T(8,128)(2,1)}, bf16[2048,128]{1,0:T(8,128)(2,1)S(1)}, u32[]{:S(2)}, u32[]{:S(2)}) %collective-permute-start.6) | collective-permute-done | bytes 524320 | tf_op jit(solution)/shard_map/ppermute | solution.py:526
  46.9 1.3 collective-permute-start.10
  48.2 1.4 collective-permute-start.11
  49.8 9.8 %collective-permute-done.1 = bf16[2,144,1024]{2,1,0:T(8,128)(2,1)S(1)} collective-permute-done((bf16[2,144,1024]{2,1,0:T(8,128)(2,1)S(1)}, bf16[2,144,1024]{2,1,0:T(8,128)(2,1)S(1)}, u32[]{:S(2)}, u32[]{:S(2)}) %collective-permute-start.1) | collective-permute-done | bytes 589856 | tf_op jit(solution)/shard_map/ppermute | solution.py:526
  59.6 1.5 collective-permute-start.9
  61.1 9.3 %collective-permute-done.8.lo6 = bf16[1024,128]{1,0:T(8,128)(2,1)} collective-permute-done((bf16[1024,128]{1,0:T(8,128)(2,1)S(1)}, bf16[1024,128]{1,0:T(8,128)(2,1)}, u32[]{:S(2)}, u32[]{:S(2)}) %collective-permute-start.8) | collective-permute-done | bytes 262176 | tf_op jit(solution)/shard_map/ppermute | solution.py:526
  70.7 0.8 copy-done.16
  71.5 1.5 collective-permute-start.12
  73.1 1.3 collective-permute-start.13
  74.4 0.8 collective-permute-start.14
  75.1 0.7 collective-permute-start.15
  75.9 2.5 %collective-permute-done.12 = bf16[144,1024]{1,0:T(8,128)(2,1)S(1)} collective-permute-done((bf16[144,1024]{1,0:T(8,128)(2,1)S(1)}, bf16[144,1024]{1,0:T(8,128)(2,1)S(1)}, u32[]{:S(2)}, u32[]{:S(2)}) %collective-permute-start.12) | collective-permute-done | bytes 294944 | tf_op jit(solution)/shard_map/ppermute | solution.py:526
  78.4 0.8 collective-permute-done.13
  79.6 2.3 collective-permute-start.19
  81.9 1.8 collective-permute-start.20
  84.9 8.9 %project.1 = (bf16[2048,128]{1,0:T(8,128)(2,1)}, bf16[2048,256]{1,0:T(8,128)(2,1)}, bf16[8,256,128]{2,1,0:T(8,128)(2,1)}) custom-call(s32[8]{0:T(128)} %stack.123.order, bf16[2048,128]{1,0:T(8,128)(2,1)} %encode.1.s0, bf16[2048,128]{1,0:T(8,128)(2,1)} %copy-done.15, bf16[2048,128]{1,0:T(8,128)(2,1)} %copy-done.11, bf16[2048,128]{1,0:T(8,128)(2,1)} %copy-done.16, ...), custom_call_target="tpu_custom_call" | custom-call | flops 1600000000 | bytes 7000000 | tf_op jit(solution)/shard_map/project/pallas_call | solution.py:158
  93.7 2.4 fusion.3
  96.1 4.2 %collective-permute-start.16 = (bf16[1152,256]{1,0:T(8,128)(2,1)}, bf16[1152,256]{1,0:T(8,128)(2,1)}, u32[]{:S(2)}, u32[]{:S(2)}) collective-permute-start(bf16[1152,256]{1,0:T(8,128)(2,1)} %get-tuple-element.58), channel_id=1, source_target_pairs={{0,8},{8,16},{16,24},{24,32},{32,40},{40,48},{48,56},{56,64},{64,7... | collective-permute-start | bytes 1769480 | tf_op jit(solution)/shard_map/ppermute | solution.py:522
  100.2 1.9 collective-permute-start.17
  102.8 4.6 %collective-permute-done.16.low = bf16[1152,256]{1,0:T(8,128)(2,1)} collective-permute-done((bf16[1152,256]{1,0:T(8,128)(2,1)}, bf16[1152,256]{1,0:T(8,128)(2,1)}, u32[]{:S(2)}, u32[]{:S(2)}) %collective-permute-start.16) | collective-permute-done | bytes 589856 | tf_op jit(solution)/shard_map/ppermute | solution.py:522
  107.4 33.1 %collective-permute-start.21 = (bf16[4,2,144,1024]{3,2,1,0:T(8,128)(2,1)S(1)}, bf16[4,2,144,1024]{3,2,1,0:T(8,128)(2,1)}, u32[]{:S(2)}, u32[]{:S(2)}) collective-permute-start(bf16[4,2,144,1024]{3,2,1,0:T(8,128)(2,1)S(1)} %pad_maximum_fusion.refs_0_), channel_id=1, source_target_pairs={{0,8},{8,0},{16,24},{24,16},{32,40},{40,32},{48,56},{56,48},{64,72... | collective-permute-start | bytes 7077896 | tf_op jit(solution)/shard_map/ppermute | solution.py:526
  140.5 28.5 %attend.1 = bf16[2048,128]{1,0:T(8,128)(2,1)} custom-call(s32[2]{0:T(128)} %add_convert_fusion.edges, bf16[2048,128]{1,0:T(8,128)(2,1)} %get-tuple-element.46.queries, bf16[1152,256]{1,0:T(8,128)(2,1)} %collective-permute-done.16.low, bf16[2048,256]{1,0:T(8,128)(2,1)} %get-tuple-element.47.own, bf16[1152,256]{1,0:T(8,128)(2,1)} %collective-permute-done.17.high), custom_call_target="tpu_custom_call" | custom-call | flops 10700000256 | bytes 4000000 | tf_op jit(solution)/shard_map/attend/pallas_call | solution.py:256
  169.7 4.1 %all-to-all-start = ((bf16[8,256,128]{2,1,0:T(8,128)(2,1)}), bf16[8,256,128]{2,1,0:T(8,128)(2,1)}, u32[]{:S(2)}, u32[]{:S(2)}) async-start(bf16[8,256,128]{2,1,0:T(8,128)(2,1)} %bitcast.53), calls=%async_computation | async-start | bytes 1048576 | tf_op jit(solution)/shard_map/all_to_all | solution.py:608
  174.6 8.7 %all-to-all-done.refs_8_ = bf16[8,256,128]{2,1,0:T(8,128)(2,1)} async-done(((bf16[8,256,128]{2,1,0:T(8,128)(2,1)}), bf16[8,256,128]{2,1,0:T(8,128)(2,1)}, u32[]{:S(2)}, u32[]{:S(2)}) %all-to-all-start) | async-done | bytes 524320 | tf_op jit(solution)/shard_map/all_to_all | solution.py:608
  183.3 12.8 %forward.1 = bf16[8,256,128]{2,1,0:T(8,128)(2,1)} custom-call(s32[16]{0:T(128)} %concatenate.10.table, bf16[4,2,144,1024]{3,2,1,0:T(8,128)(2,1)} %copy-done.4, bf16[4,2,144,1024]{3,2,1,0:T(8,128)(2,1)} %collective-permute-done.18.refs_1_, bf16[4,2,144,1024]{3,2,1,0:T(8,128)(2,1)} %collective-permute-done.19.refs_2_, ...), custom_call_target="tpu_custom_call" | custom-call | flops 4800000000 | bytes 20000000 | tf_op jit(solution)/shard_map/forward/pallas_call | solution.py:369
  196.1 11.9 %all_to_all.15 = bf16[8,256,128]{2,1,0:T(8,128)(2,1)S(1)} all-to-all(bf16[8,256,128]{2,1,0:T(8,128)(2,1)} %forward.1), channel_id=1, replica_groups=mesh['seq'=16,'head'=8] {'head'}, dimensions={0} | all-to-all | bytes 1048576 | tf_op jit(solution)/shard_map/all_to_all | solution.py:616
  208.0 8.0 %collective-permute-start.25 = (bf16[8,128,128]{2,1,0:T(8,128)(2,1)S(1)}, bf16[8,128,128]{2,1,0:T(8,128)(2,1)S(1)}, u32[]{:S(2)}, u32[]{:S(2)}) collective-permute-start(bf16[8,128,128]{2,1,0:T(8,128)(2,1)S(1)} %bitcast.61), channel_id=1, source_target_pairs={{0,8},{8,16},{16,24},{24,32},{32,40},{40,48},{48,56},{56,64},{64,7... | collective-permute-start | bytes 786440 | tf_op jit(solution)/shard_map/ppermute | solution.py:522
  216.0 2.1 collective-permute-start.26
  219.3 8.0 %collective-permute-done.26.high = bf16[8,128,128]{2,1,0:T(8,128)(2,1)S(1)} collective-permute-done((bf16[8,128,128]{2,1,0:T(8,128)(2,1)S(1)}, bf16[8,128,128]{2,1,0:T(8,128)(2,1)S(1)}, u32[]{:S(2)}, u32[]{:S(2)}) %collective-permute-start.26) | collective-permute-done | bytes 262176 | tf_op jit(solution)/shard_map/ppermute | solution.py:522
  228.0 8.0 %decode.1 = (bf16[8192,128]{1,0:T(8,128)(2,1)}, bf16[8,16,128]{2,1,0:T(8,128)(2,1)}) custom-call(s32[64,2]{1,0:T(8,128)} %broadcast_subtract_fusion.index, bf16[8,128,128]{2,1,0:T(8,128)(2,1)} %copy-done.9, bf16[16,128,128]{2,1,0:T(8,128)(2,1)} %bitcast.48, bf16[8,128,128]{2,1,0:T(8,128)(2,1)} %copy-done.10, bf16[64,2,128,128]{3,2,1,0:T(8,128)(2,1)} %weights.3), custom_call_target="tpu_custom_call" | custom-call | flops 540000000 | bytes 10000000 | tf_op jit(solution)/shard_map/decode/pallas_call | solution.py:436
  236.0 0.8 broadcast_in_dim.3
  236.8 8.5 %all_to_all.16.sums = bf16[8,8,16,128]{3,2,1,0:T(8,128)(2,1)S(1)} all-to-all(bf16[8,8,16,128]{3,2,1,0:T(8,128)(2,1)S(1)} %broadcast_in_dim.3), channel_id=1, replica_groups=mesh['seq'=16,'head'=8] {'head'}, dimensions={0} | all-to-all | bytes 524288 | tf_op jit(solution)/shard_map/all_to_all | solution.py:626
  245.4 1.6 copy-done.2
  247.0 5.2 %finish.1 = bf16[8192,128]{1,0:T(8,128)(2,1)} custom-call(bf16[8,8,16,128]{3,2,1,0:T(8,128)(2,1)S(1)} %all_to_all.16.sums, bf16[8192,128]{1,0:T(8,128)(2,1)S(1)} %copy-done.2, bf16[8192,128]{1,0:T(8,128)(2,1)S(1)} %copy-done.1, f32[1,128]{1,0:T(1,128)S(1)} %bitcast.47), custom_call_target="tpu_custom_call" | custom-call | flops 540000000 | bytes 8000000 | tf_op jit(solution)/shard_map/finish/pallas_call | solution.py:500
  (73 shorter events, 7.3 us)
Async XLA Ops:
  0.0 9.1 %copy-start = (bf16[512,1024]{1,0:T(8,128)(2,1)S(1)}, bf16[512,1024]{1,0:T(8,128)(2,1)}, u32[]{:S(2)}) copy-start(bf16[512,1024]{1,0:T(8,128)(2,1)} %param.20) | copy-start | bytes 3145732
  0.0 11.1 %copy-start.6 = (bf16[1024,3,128]{2,0,1:T(8,128)(2,1)S(1)}, bf16[1024,3,128]{2,0,1:T(8,128)(2,1)}, u32[]{:S(2)}) copy-start(bf16[1024,3,128]{2,0,1:T(8,128)(2,1)} %param.16) | copy-start | bytes 2359300
  0.0 11.0 %copy-start.13 = (s32[16,8]{0,1:T(8,128)S(1)}, s32[16,8]{0,1:T(8,128)}, u32[]{:S(2)}) copy-start(s32[16,8]{0,1:T(8,128)} %param.13) | copy-start | bytes 1540
  2.4 10.3 %collective-permute-start.3 = (bf16[2048,128]{1,0:T(8,128)(2,1)}, bf16[2048,128]{1,0:T(8,128)(2,1)S(1)}, u32[]{:S(2)}, u32[]{:S(2)}) collective-permute-start(bf16[2048,128]{1,0:T(8,128)(2,1)} %get-tuple-element.33), channel_id=1, source_target_pairs={{0,8},{8,16},{16,24},{24,32},{32,40},{40,48},{48,56},{56,64},{64,7... | collective-permute-start | bytes 1572872 | tf_op jit(solution)/shard_map/ppermute | solution.py:522
  6.2 17.0 %collective-permute-start.4 = (bf16[2048,128]{1,0:T(8,128)(2,1)}, bf16[2048,128]{1,0:T(8,128)(2,1)S(1)}, u32[]{:S(2)}, u32[]{:S(2)}) collective-permute-start(bf16[2048,128]{1,0:T(8,128)(2,1)} %get-tuple-element.34), channel_id=1, source_target_pairs={{8,0},{16,8},{24,16},{32,24},{40,32},{48,40},{56,48},{64,56},{72,6... | collective-permute-start | bytes 1572872 | tf_op jit(solution)/shard_map/ppermute | solution.py:522
  10.7 23.5 %collective-permute-start = (bf16[144,1024]{1,0:T(8,128)(2,1)}, bf16[144,1024]{1,0:T(8,128)(2,1)S(1)}, u32[]{:S(2)}, u32[]{:S(2)}) collective-permute-start(bf16[144,1024]{1,0:T(8,128)(2,1)} %get-tuple-element.69), channel_id=1, source_target_pairs={{0,1},{1,0},{2,3},{3,2},{4,5},{5,4},{6,7},{7,6},{8,9},{9,8},{10,11... | collective-permute-start | bytes 884744 | tf_op jit(solution)/shard_map/ppermute | solution.py:526
  12.7 10.5 %copy-start.7 = (bf16[2048,128]{1,0:T(8,128)(2,1)}, bf16[2048,128]{1,0:T(8,128)(2,1)S(1)}, u32[]{:S(2)}) copy-start(bf16[2048,128]{1,0:T(8,128)(2,1)S(1)} %collective-permute-done.3) | copy-start | bytes 1572868
  23.2 0.8 copy-start.8
  31.2 8.6 %collective-permute-start.5 = (bf16[2048,128]{1,0:T(8,128)(2,1)}, bf16[2048,128]{1,0:T(8,128)(2,1)S(1)}, u32[]{:S(2)}, u32[]{:S(2)}) collective-permute-start(bf16[2048,128]{1,0:T(8,128)(2,1)} %encode.1.s0), channel_id=1, source_target_pairs={{0,1},{1,0},{2,3},{3,2},{4,5},{5,4},{6,7},{7,6},{8,9},{9,8},{10,11... | collective-permute-start | bytes 1572872 | tf_op jit(solution)/shard_map/ppermute | solution.py:526
  31.3 15.6 %collective-permute-start.6 = (bf16[2048,128]{1,0:T(8,128)(2,1)}, bf16[2048,128]{1,0:T(8,128)(2,1)S(1)}, u32[]{:S(2)}, u32[]{:S(2)}) collective-permute-start(bf16[2048,128]{1,0:T(8,128)(2,1)} %encode.1.s0), channel_id=1, source_target_pairs={{0,2},{1,3},{2,4},{3,5},{4,6},{5,7},{6,0},{7,1},{8,10},{9,11},{10,... | collective-permute-start | bytes 1572872 | tf_op jit(solution)/shard_map/ppermute | solution.py:526
  32.7 14.2 %collective-permute-start.7 = (bf16[2048,128]{1,0:T(8,128)(2,1)}, bf16[2048,128]{1,0:T(8,128)(2,1)S(1)}, u32[]{:S(2)}, u32[]{:S(2)}) collective-permute-start(bf16[2048,128]{1,0:T(8,128)(2,1)} %encode.1.s0), channel_id=1, source_target_pairs={{0,6},{1,7},{2,0},{3,1},{4,2},{5,3},{6,4},{7,5},{8,14},{9,15},{10,... | collective-permute-start | bytes 1572872 | tf_op jit(solution)/shard_map/ppermute | solution.py:526
  34.3 25.3 %collective-permute-start.1 = (bf16[2,144,1024]{2,1,0:T(8,128)(2,1)S(1)}, bf16[2,144,1024]{2,1,0:T(8,128)(2,1)S(1)}, u32[]{:S(2)}, u32[]{:S(2)}) collective-permute-start(bf16[2,144,1024]{2,1,0:T(8,128)(2,1)S(1)} %get-tuple-element.65), channel_id=1, source_target_pairs={{0,2},{1,3},{2,4},{3,5},{4,6},{5,7},{6,0},{7,1},{8,10},{9,11},{10,... | collective-permute-start | bytes 1769480 | tf_op jit(solution)/shard_map/ppermute | solution.py:526
  34.4 26.7 %collective-permute-start.2 = (bf16[2,144,1024]{2,1,0:T(8,128)(2,1)S(1)}, bf16[2,144,1024]{2,1,0:T(8,128)(2,1)S(1)}, u32[]{:S(2)}, u32[]{:S(2)}) collective-permute-start(bf16[2,144,1024]{2,1,0:T(8,128)(2,1)S(1)} %get-tuple-element.65), channel_id=1, source_target_pairs={{0,6},{1,7},{2,0},{3,1},{4,2},{5,3},{6,4},{7,5},{8,14},{9,15},{10,... | collective-permute-start | bytes 1769480 | tf_op jit(solution)/shard_map/ppermute | solution.py:526
  39.8 39.4 %copy-start.15 = (bf16[2048,128]{1,0:T(8,128)(2,1)}, bf16[2048,128]{1,0:T(8,128)(2,1)S(1)}, u32[]{:S(2)}) copy-start(bf16[2048,128]{1,0:T(8,128)(2,1)S(1)} %collective-permute-done.5.s1) | copy-start | bytes 1572868
  46.9 32.4 %copy-start.11 = (bf16[2048,128]{1,0:T(8,128)(2,1)}, bf16[2048,128]{1,0:T(8,128)(2,1)S(1)}, u32[]{:S(2)}) copy-start(bf16[2048,128]{1,0:T(8,128)(2,1)S(1)} %collective-permute-done.6.s2) | copy-start | bytes 1572868
  46.9 32.3 %copy-start.12 = (bf16[2048,128]{1,0:T(8,128)(2,1)}, bf16[2048,128]{1,0:T(8,128)(2,1)S(1)}, u32[]{:S(2)}) copy-start(bf16[2048,128]{1,0:T(8,128)(2,1)S(1)} %collective-permute-done.7.s4) | copy-start | bytes 1572868
  46.9 23.8 %collective-permute-start.10 = (bf16[2048,128]{1,0:T(8,128)(2,1)S(1)}, bf16[2048,128]{1,0:T(8,128)(2,1)S(1)}, u32[]{:S(2)}, u32[]{:S(2)}) collective-permute-start(bf16[2048,128]{1,0:T(8,128)(2,1)S(1)} %collective-permute-done.5.s1), channel_id=1, source_target_pairs={{0,2},{1,3},{2,4},{3,5},{4,6},{5,7},{6,0},{7,1},{8,10},{9,11},{10,... | collective-permute-start | bytes 1572872 | tf_op jit(solution)/shard_map/ppermute | solution.py:526
  48.2 23.3 %collective-permute-start.11 = (bf16[2048,128]{1,0:T(8,128)(2,1)S(1)}, bf16[2048,128]{1,0:T(8,128)(2,1)}, u32[]{:S(2)}, u32[]{:S(2)}) collective-permute-start(bf16[2048,128]{1,0:T(8,128)(2,1)S(1)} %collective-permute-done.5.s1), channel_id=1, source_target_pairs={{0,6},{1,7},{2,0},{3,1},{4,2},{5,3},{6,4},{7,5},{8,14},{9,15},{10,... | collective-permute-start | bytes 1572872 | tf_op jit(solution)/shard_map/ppermute | solution.py:526
  49.7 20.7 %collective-permute-start.8 = (bf16[1024,128]{1,0:T(8,128)(2,1)S(1)}, bf16[1024,128]{1,0:T(8,128)(2,1)}, u32[]{:S(2)}, u32[]{:S(2)}) collective-permute-start(bf16[1024,128]{1,0:T(8,128)(2,1)S(1)} %slice.58), channel_id=1, source_target_pairs={{0,2},{1,3},{2,4},{3,5},{4,6},{5,7},{6,0},{7,1},{8,10},{9,11},{10,... | collective-permute-start | bytes 786440 | tf_op jit(solution)/shard_map/ppermute | solution.py:526
  59.6 11.1 %collective-permute-start.9 = (bf16[1024,128]{1,0:T(8,128)(2,1)S(1)}, bf16[1024,128]{1,0:T(8,128)(2,1)}, u32[]{:S(2)}, u32[]{:S(2)}) collective-permute-start(bf16[1024,128]{1,0:T(8,128)(2,1)S(1)} %slice.59), channel_id=1, source_target_pairs={{0,6},{1,7},{2,0},{3,1},{4,2},{5,3},{6,4},{7,5},{8,14},{9,15},{10,... | collective-permute-start | bytes 786440 | tf_op jit(solution)/shard_map/ppermute | solution.py:526
  70.7 0.8 copy-start.16
  71.5 6.9 %collective-permute-start.12 = (bf16[144,1024]{1,0:T(8,128)(2,1)S(1)}, bf16[144,1024]{1,0:T(8,128)(2,1)S(1)}, u32[]{:S(2)}, u32[]{:S(2)}) collective-permute-start(bf16[144,1024]{1,0:T(8,128)(2,1)S(1)} %slice_bitcast_fusion.1), channel_id=1, source_target_pairs={{0,2},{1,3},{2,4},{3,5},{4,6},{5,7},{6,0},{7,1},{8,10},{9,11},{10,... | collective-permute-start | bytes 884744 | tf_op jit(solution)/shard_map/ppermute | solution.py:526
  73.1 6.0 %collective-permute-start.13 = (bf16[144,1024]{1,0:T(8,128)(2,1)S(1)}, bf16[144,1024]{1,0:T(8,128)(2,1)S(1)}, u32[]{:S(2)}, u32[]{:S(2)}) collective-permute-start(bf16[144,1024]{1,0:T(8,128)(2,1)S(1)} %slice_bitcast_fusion), channel_id=1, source_target_pairs={{0,6},{1,7},{2,0},{3,1},{4,2},{5,3},{6,4},{7,5},{8,14},{9,15},{10,... | collective-permute-start | bytes 884744 | tf_op jit(solution)/shard_map/ppermute | solution.py:526
  74.4 10.0 %collective-permute-start.14 = (bf16[1024,128]{1,0:T(8,128)(2,1)}, bf16[1024,128]{1,0:T(8,128)(2,1)}, u32[]{:S(2)}, u32[]{:S(2)}) collective-permute-start(bf16[1024,128]{1,0:T(8,128)(2,1)} %collective-permute-done.8.lo6), channel_id=1, source_target_pairs={{0,1},{1,0},{2,3},{3,2},{4,5},{5,4},{6,7},{7,6},{8,9},{9,8},{10,11... | collective-permute-start | bytes 786440 | tf_op jit(solution)/shard_map/ppermute | solution.py:526
  75.1 9.7 %collective-permute-start.15 = (bf16[1024,128]{1,0:T(8,128)(2,1)}, bf16[1024,128]{1,0:T(8,128)(2,1)}, u32[]{:S(2)}, u32[]{:S(2)}) collective-permute-start(bf16[1024,128]{1,0:T(8,128)(2,1)} %collective-permute-done.9.hi6), channel_id=1, source_target_pairs={{0,1},{1,0},{2,3},{3,2},{4,5},{5,4},{6,7},{7,6},{8,9},{9,8},{10,11... | collective-permute-start | bytes 786440 | tf_op jit(solution)/shard_map/ppermute | solution.py:526
  79.6 27.9 %copy-start.4 = (bf16[4,2,144,1024]{3,2,1,0:T(8,128)(2,1)}, bf16[4,2,144,1024]{3,2,1,0:T(8,128)(2,1)S(1)}, u32[]{:S(2)}) copy-start(bf16[4,2,144,1024]{3,2,1,0:T(8,128)(2,1)S(1)} %pad_maximum_fusion.refs_0_) | copy-start | bytes 7077892
  79.6 89.4 %collective-permute-start.18 = (bf16[4,2,144,1024]{3,2,1,0:T(8,128)(2,1)S(1)}, bf16[4,2,144,1024]{3,2,1,0:T(8,128)(2,1)}, u32[]{:S(2)}, u32[]{:S(2)}) collective-permute-start(bf16[4,2,144,1024]{3,2,1,0:T(8,128)(2,1)S(1)} %pad_maximum_fusion.refs_0_), channel_id=1, source_target_pairs={{0,16},{8,24},{16,32},{24,40},{32,48},{40,56},{48,0},{56,8},{64,80... | collective-permute-start | bytes 7077896 | tf_op jit(solution)/shard_map/ppermute | solution.py:526
  79.6 89.3 %collective-permute-start.19 = (bf16[4,2,144,1024]{3,2,1,0:T(8,128)(2,1)S(1)}, bf16[4,2,144,1024]{3,2,1,0:T(8,128)(2,1)}, u32[]{:S(2)}, u32[]{:S(2)}) collective-permute-start(bf16[4,2,144,1024]{3,2,1,0:T(8,128)(2,1)S(1)} %pad_maximum_fusion.refs_0_), channel_id=1, source_target_pairs={{0,48},{8,56},{16,0},{24,8},{32,16},{40,24},{48,32},{56,40},{64,11... | collective-permute-start | bytes 7077896 | tf_op jit(solution)/shard_map/ppermute | solution.py:526
  81.9 87.1 %collective-permute-start.20 = (bf16[4,2,144,1024]{3,2,1,0:T(8,128)(2,1)S(1)}, bf16[4,2,144,1024]{3,2,1,0:T(8,128)(2,1)}, u32[]{:S(2)}, u32[]{:S(2)}) collective-permute-start(bf16[4,2,144,1024]{3,2,1,0:T(8,128)(2,1)S(1)} %pad_maximum_fusion.refs_0_), channel_id=1, source_target_pairs={{0,65},{1,64},{2,67},{3,66},{4,69},{5,68},{6,71},{7,70},{8,73},{9,... | collective-permute-start | bytes 7077896 | tf_op jit(solution)/shard_map/ppermute | solution.py:526
  96.1 11.3 %collective-permute-start.16 = (bf16[1152,256]{1,0:T(8,128)(2,1)}, bf16[1152,256]{1,0:T(8,128)(2,1)}, u32[]{:S(2)}, u32[]{:S(2)}) collective-permute-start(bf16[1152,256]{1,0:T(8,128)(2,1)} %get-tuple-element.58), channel_id=1, source_target_pairs={{0,8},{8,16},{16,24},{24,32},{32,40},{40,48},{48,56},{56,64},{64,7... | collective-permute-start | bytes 1769480 | tf_op jit(solution)/shard_map/ppermute | solution.py:522
  100.2 40.3 %collective-permute-start.17 = (bf16[1152,256]{1,0:T(8,128)(2,1)}, bf16[1152,256]{1,0:T(8,128)(2,1)}, u32[]{:S(2)}, u32[]{:S(2)}) collective-permute-start(bf16[1152,256]{1,0:T(8,128)(2,1)} %get-tuple-element.57), channel_id=1, source_target_pairs={{8,0},{16,8},{24,16},{32,24},{40,32},{48,40},{56,48},{64,56},{72,6... | collective-permute-start | bytes 1769480 | tf_op jit(solution)/shard_map/ppermute | solution.py:522
  107.4 67.2 %collective-permute-start.21 = (bf16[4,2,144,1024]{3,2,1,0:T(8,128)(2,1)S(1)}, bf16[4,2,144,1024]{3,2,1,0:T(8,128)(2,1)}, u32[]{:S(2)}, u32[]{:S(2)}) collective-permute-start(bf16[4,2,144,1024]{3,2,1,0:T(8,128)(2,1)S(1)} %pad_maximum_fusion.refs_0_), channel_id=1, source_target_pairs={{0,8},{8,0},{16,24},{24,16},{32,40},{40,32},{48,56},{56,48},{64,72... | collective-permute-start | bytes 7077896 | tf_op jit(solution)/shard_map/ppermute | solution.py:526
  169.0 14.2 %collective-permute-start.22 = (bf16[4,2,144,1024]{3,2,1,0:T(8,128)(2,1)}, bf16[4,2,144,1024]{3,2,1,0:T(8,128)(2,1)}, u32[]{:S(2)}, u32[]{:S(2)}) collective-permute-start(bf16[4,2,144,1024]{3,2,1,0:T(8,128)(2,1)} %collective-permute-done.18.refs_1_), channel_id=1, source_target_pairs={{0,8},{8,0},{16,24},{24,16},{32,40},{40,32},{48,56},{56,48},{64,72... | collective-permute-start | bytes 7077896 | tf_op jit(solution)/shard_map/ppermute | solution.py:526
  169.1 14.2 %collective-permute-start.23 = (bf16[4,2,144,1024]{3,2,1,0:T(8,128)(2,1)}, bf16[4,2,144,1024]{3,2,1,0:T(8,128)(2,1)}, u32[]{:S(2)}, u32[]{:S(2)}) collective-permute-start(bf16[4,2,144,1024]{3,2,1,0:T(8,128)(2,1)} %collective-permute-done.19.refs_2_), channel_id=1, source_target_pairs={{0,8},{8,0},{16,24},{24,16},{32,40},{40,32},{48,56},{56,48},{64,72... | collective-permute-start | bytes 7077896 | tf_op jit(solution)/shard_map/ppermute | solution.py:526
  169.6 13.7 %collective-permute-start.24 = (bf16[4,2,144,1024]{3,2,1,0:T(8,128)(2,1)}, bf16[4,2,144,1024]{3,2,1,0:T(8,128)(2,1)}, u32[]{:S(2)}, u32[]{:S(2)}) collective-permute-start(bf16[4,2,144,1024]{3,2,1,0:T(8,128)(2,1)} %collective-permute-done.20.refs_3_), channel_id=1, source_target_pairs={{0,8},{8,0},{16,24},{24,16},{32,40},{40,32},{48,56},{56,48},{64,72... | collective-permute-start | bytes 7077896 | tf_op jit(solution)/shard_map/ppermute | solution.py:526
  169.7 13.6 %all-to-all-start = ((bf16[8,256,128]{2,1,0:T(8,128)(2,1)}), bf16[8,256,128]{2,1,0:T(8,128)(2,1)}, u32[]{:S(2)}, u32[]{:S(2)}) async-start(bf16[8,256,128]{2,1,0:T(8,128)(2,1)} %bitcast.53), calls=%async_computation | async-start | bytes 1048576 | tf_op jit(solution)/shard_map/all_to_all | solution.py:608
  183.3 34.9 %copy-start.14 = (s32[64,2]{0,1:T(2,128)S(1)}, s32[64,2]{0,1:T(2,128)}, u32[]{:S(2)}) copy-start(s32[64,2]{0,1:T(2,128)} %param.21) | copy-start | bytes 1540
  207.9 19.4 %copy-start.5 = (bf16[8,256,128]{2,1,0:T(8,128)(2,1)}, bf16[8,256,128]{2,1,0:T(8,128)(2,1)S(1)}, u32[]{:S(2)}) copy-start(bf16[8,256,128]{2,1,0:T(8,128)(2,1)S(1)} %all_to_all.15) | copy-start | bytes 1572868
  208.0 11.3 %collective-permute-start.25 = (bf16[8,128,128]{2,1,0:T(8,128)(2,1)S(1)}, bf16[8,128,128]{2,1,0:T(8,128)(2,1)S(1)}, u32[]{:S(2)}, u32[]{:S(2)}) collective-permute-start(bf16[8,128,128]{2,1,0:T(8,128)(2,1)S(1)} %bitcast.61), channel_id=1, source_target_pairs={{0,8},{8,16},{16,24},{24,32},{32,40},{40,48},{48,56},{56,64},{64,7... | collective-permute-start | bytes 786440 | tf_op jit(solution)/shard_map/ppermute | solution.py:522
  216.0 11.3 %collective-permute-start.26 = (bf16[8,128,128]{2,1,0:T(8,128)(2,1)S(1)}, bf16[8,128,128]{2,1,0:T(8,128)(2,1)S(1)}, u32[]{:S(2)}, u32[]{:S(2)}) collective-permute-start(bf16[8,128,128]{2,1,0:T(8,128)(2,1)S(1)} %bitcast.60), channel_id=1, source_target_pairs={{8,0},{16,8},{24,16},{32,24},{40,32},{48,40},{56,48},{64,56},{72,6... | collective-permute-start | bytes 786440 | tf_op jit(solution)/shard_map/ppermute | solution.py:522
  219.3 8.0 %copy-start.9 = (bf16[8,128,128]{2,1,0:T(8,128)(2,1)}, bf16[8,128,128]{2,1,0:T(8,128)(2,1)S(1)}, u32[]{:S(2)}) copy-start(bf16[8,128,128]{2,1,0:T(8,128)(2,1)S(1)} %collective-permute-done.25.low) | copy-start | bytes 786436
  227.3 0.7 copy-start.10
  228.0 17.4 %copy-start.1 = (bf16[8192,128]{1,0:T(8,128)(2,1)S(1)}, bf16[8192,128]{1,0:T(8,128)(2,1)}, u32[]{:S(2)}) copy-start(bf16[8192,128]{1,0:T(8,128)(2,1)} %state.1) | copy-start | bytes 6291460
  228.0 17.4 %copy-start.3 = (f32[128]{0:T(128)S(1)}, f32[128]{0:T(128)}, u32[]{:S(2)}) copy-start(f32[128]{0:T(128)} %param.23) | copy-start | bytes 1540
  245.4 1.6 copy-start.2

commit v5 on v4

--- a/solution.py
+++ b/solution.py
@@ -103,11 +103,10 @@
 
 
 def project_kernel(
-    order, s0, s1, s2, s3, s4, s5, lo6, hi6, lo7, hi7, gain, wq, wk, wv,
+    order, s0, s1, s2, s3, s4, s5, s6, s7, gain, wq, wk, wv,
     queries, keys_values, share, ordered,
 ):
     step = pl.program_id(0)
-    half = pl.num_programs(0) // 2
 
     @pl.when(step == 0)
     def _():
@@ -116,10 +115,7 @@
                 [w[order[p]] for w in (wq, wk, wv)], axis=1
             )
 
-    early = step < half
-    raw = [s[...] for s in (s0, s1, s2, s3, s4, s5)]
-    raw.append(jnp.where(early, lo6[...], hi6[...]))
-    raw.append(jnp.where(early, lo7[...], hi7[...]))
+    raw = [s[...] for s in (s0, s1, s2, s3, s4, s5, s6, s7)]
 
     tile = share.shape[1]
     per = raw[0].shape[0] // tile
@@ -153,8 +149,7 @@
     tile, steps = rows // 8, 4
     each = rows // steps
     full = pl.BlockSpec((each, BLOCK), lambda i, _: (i, 0))
-    early = pl.BlockSpec((each, BLOCK), lambda i, _: (jnp.minimum(i, steps // 2 - 1), 0))
-    late = pl.BlockSpec((each, BLOCK), lambda i, _: (jnp.maximum(i - steps // 2, 0), 0))
+    second = pl.BlockSpec((each, BLOCK), lambda i, _: (i + steps // 2, 0))
     return pl.pallas_call(
         project_kernel,
         out_shape=(
@@ -165,8 +160,7 @@
         grid_spec=pltpu.PrefetchScalarGridSpec(
             num_scalar_prefetch=1,
             grid=(steps,),
-            in_specs=[full] * 6
-            + [early, late, early, late]
+            in_specs=[full, full, full, second, full, second, full, full]
             + [whole((8, 1, BLOCK))]
             + [whole((8, BLOCK, BLOCK))] * 3,
             out_specs=(
@@ -177,7 +171,6 @@
             scratch_shapes=[pltpu.VMEM((D, 3 * BLOCK), BF)],
         ),
         compiler_params=params(56),
-        cost_estimate=cost(1_600_000_000, 7_000_000),
         name="project",
     )(order, *slots, gain.reshape(8, 1, BLOCK), *weights)
 
@@ -269,7 +262,6 @@
             ],
         ),
         compiler_params=params(56),
-        cost_estimate=cost(10_700_000_000, 4_000_000, 10_500_000),
         name="attend",
     )(edges, queries, low, own, high)
 
@@ -574,24 +566,24 @@
     packed = pack_weights(position, expand, shrink, outward)
     inward = [inward[:, j, :].reshape(8, BLOCK, BLOCK) for j in range(3)]
     packed = jnp.stack([packed, OVER(packed)])
-    low, high, *inward = lax.optimization_barrier((low, high, *inward))
+    low, high, packed, *inward = lax.optimization_barrier((low, high, packed, *inward))
     packed_a, packed_b = NORTH(packed), SOUTH(packed)
 
     mesh_start = encode(
         encode_index - (band * grid_blocks - mesh_blocks), low, grid_state, high, encode_weights
     )
     half = mesh_rows // 2
-    x = mesh_start
-    y, xa, xb = lax.optimization_barrier((OVER(x), NORTH(x), SOUTH(x)))
-    xc, xd = NORTH(xa[:half]), SOUTH(xb[half:])
-    ya, yb = NORTH(y), SOUTH(y)
-    yc, yd = OVER(xc), OVER(xd)
-    slots = (x, y, xa, ya, xb, yb, xc, xd, yc, yd)
-    packed_a, packed_b, *_ = lax.optimization_barrier(
-        (packed_a, packed_b, xc, xd, ya, yb)
-    )
-    far = jnp.stack([NORTH(packed_a[0]), SOUTH(packed_b[1])])
-    mine = jnp.stack([packed, packed_a, packed_b, far])
+    x, packed_a, packed_b = lax.optimization_barrier((mesh_start, packed_a, packed_b))
+    y, xa, xb, far_a, far_b = lax.optimization_barrier(
+        (OVER(x), NORTH(x), SOUTH(x), NORTH(packed_a[0]), SOUTH(packed_b[1]))
+    )
+    mine = jnp.stack([packed, packed_a, packed_b, jnp.stack([far_a, far_b])])
+    mine, y, xa, xb = lax.optimization_barrier((mine, y, xa, xb))
+    others = [UP(mine), DOWN(mine), ACROSS(mine)]
+    from_south = NORTH(jnp.concatenate([xa[:half], y]))
+    from_north = SOUTH(jnp.concatenate([xb[half:], y]))
+    xc = jnp.concatenate([from_south[:half], from_north[:half]])
+    slots = (x, y, xa, from_south, xb, from_north, xc, OVER(xc))
     partner = me ^ 1
     order = jnp.stack(
         [me, partner] + [(v + by) % 8 for by in (6, 2, 4) for v in (me, partner)]
@@ -599,11 +591,9 @@
     queries, keys_values, share = project(order, slots, first_gain, inward)
     below = shifted(keys_values[mesh_rows - REACH :], 1)
     above = shifted(keys_values[:REACH], -1)
-    others = [UP(mine), DOWN(mine), ACROSS(mine)]
     edges = jnp.stack([band == 0, band == bands - 1]).astype(jnp.int32)
     context = attend(edges, queries, below, keys_values, above)
-    context, *others = lax.optimization_barrier((context, *others))
-    here = [mine, *others]
+    context, *here = lax.optimization_barrier((context, mine, *others))
     parts = here + [TWIN(v) for v in here]
     context = lax.all_to_all(
         context.reshape(8, mesh_rows // 8, BLOCK), "head", 0, 0, tiled=True

time: 253 us -> 236 us (0.933)
  starting transfers between devices: 78.6 us -> 41 us
  waiting for transfers between devices: 65.4 us -> 80.4 us
    ppermute x21 -> x18, starting transfers between devices: 52.5 us -> 17.6 us  [among(): return lax.ppermute(value, axis, [(i, to(i)) for i in range(count)])]
    ppermute x21 -> x18, waiting for transfers between devices: 33.1 us -> 52.7 us  [among(): return lax.ppermute(value, axis, [(i, to(i)) for i in range(count)])]
    ppermute x6, waiting for transfers between devices: 23.6 us -> 18.9 us  [shifted(): lax.ppermute(value, 'seq', [(i, i + by) for i in range(16) if 0 <= i + by...]
    ppermute x6, starting transfers between devices: 22 us -> 19.3 us  [shifted(): lax.ppermute(value, 'seq', [(i, i + by) for i in range(16) if 0 <= i + by...]
    unnamed x36 -> x46, local copies, waits for them, and re-layouts: 4.09 us -> 5.1 us
  transfers between devices with their start and end apart: 28 -> 25, of which waited for: 13 -> 12; matrix products, arithmetic and copies ran while one was open for 4% -> 4% of each run, Pallas kernels for 18% -> 19%
where the time goes in v5:
time: 236 us; the launch traced here: 233 us
  waiting for transfers between devices  80.4 us (34%)
  Pallas kernels  70.4 us (30%)
  starting transfers between devices  41 us (17%)
  blocking collectives  21 us (9%)
  local copies, waits for them, and re-layouts  14.6 us (6%)
  other arithmetic  4.87 us (2%)
    ppermute x18, waiting for transfers between devices, among(): return lax.ppermute(value, axis, [(i, to(i)) for i in range(count)])  52.7 us
    pallas_call x1, Pallas kernels, attend(): pl.pallas_call(attend_kernel, out_shape=jax.ShapeDtypeStruct((rows, BLOCK...  28.5 us
    ppermute x6, starting transfers between devices, shifted(): lax.ppermute(value, 'seq', [(i, i + by) for i in range(16) if 0 <= i + by...  19.3 us
    ppermute x6, waiting for transfers between devices, shifted(): lax.ppermute(value, 'seq', [(i, i + by) for i in range(16) if 0 <= i + by...  18.9 us
    ppermute x18, starting transfers between devices, among(): return lax.ppermute(value, axis, [(i, to(i)) for i in range(count)])  17.6 us
    pallas_call x1, Pallas kernels, forward(): pl.pallas_call(forward_kernel, out_shape=jax.ShapeDtypeStruct((8, rows, B...  12.9 us
    all_to_all x1, blocking collectives, on_device(): mesh_end = lax.all_to_all(mesh_end, 'head', 0, 0, tiled=True)  12.5 us
    all_to_all x1, waiting for transfers between devices, on_device(): lax.all_to_all(context.reshape(8, mesh_rows // 8, BLOCK), 'head', 0, 0, t...  8.85 us
  transfers between devices with their start and end apart: 25, of which 12 were waited for; matrix products, arithmetic and copies ran while one was open for 4% of the time, Pallas kernels for 19%

profile of v5, /device:TPU:97, one launch (start us, length us, event | category | flops | bytes accessed | tf_op | source)
XLA Modules:
  0.0 233.1 jit_solution(13311087909091381768)
XLA Ops:
  0.0 2.4 %fusion.1 = (bf16[2048,128]{1,0:T(8,128)(2,1)}, bf16[2048,128]{1,0:T(8,128)(2,1)}) fusion(bf16[8192,128]{1,0:T(8,128)(2,1)} %state.1), kind=kLoop, calls=%fused_computation.17 | loop fusion | bytes 2097152 | tf_op jit(solution)/shard_map/slice | solution.py:557
  2.4 4.0 %collective-permute-start = (bf16[2048,128]{1,0:T(8,128)(2,1)}, bf16[2048,128]{1,0:T(8,128)(2,1)S(1)}, u32[]{:S(2)}, u32[]{:S(2)}) collective-permute-start(bf16[2048,128]{1,0:T(8,128)(2,1)} %get-tuple-element.39), channel_id=1, source_target_pairs={{0,8},{8,16},{16,24},{24,32},{32,40},{40,48},{48,56},{56,64},{64,7... | collective-permute-start | bytes 1572872 | tf_op jit(solution)/shard_map/ppermute | solution.py:514
  6.3 1.9 collective-permute-start.1
  8.3 0.9 constant_dynamic-slice_fusion
  9.3 0.8 constant_dynamic-slice_fusion.1
  10.5 0.9 fusion.3
  11.4 8.4 %collective-permute-done.2 = bf16[144,1024]{1,0:T(8,128)(2,1)S(1)} collective-permute-done((bf16[144,1024]{1,0:T(8,128)(2,1)S(1)}, bf16[144,1024]{1,0:T(8,128)(2,1)S(1)}, u32[]{:S(2)}, u32[]{:S(2)}) %collective-permute-start.2) | collective-permute-done | bytes 294944 | tf_op jit(solution)/shard_map/ppermute | solution.py:518
  19.9 2.5 %collective-permute-done.1 = bf16[2048,128]{1,0:T(8,128)(2,1)S(1)} collective-permute-done((bf16[2048,128]{1,0:T(8,128)(2,1)}, bf16[2048,128]{1,0:T(8,128)(2,1)S(1)}, u32[]{:S(2)}, u32[]{:S(2)}) %collective-permute-start.1) | collective-permute-done | bytes 524320 | tf_op jit(solution)/shard_map/ppermute | solution.py:514
  22.5 0.8 copy-done.17
  23.3 1.3 collective-permute-start.3
  24.6 1.4 collective-permute-start.4
  26.7 7.2 %encode.1.s0 = bf16[2048,128]{1,0:T(8,128)(2,1)} custom-call(s32[16,8]{1,0:T(8,128)} %broadcast_subtract_fusion.1.index, bf16[16,128,128]{2,1,0:T(8,128)(2,1)} %bitcast.55, bf16[64,128,128]{2,1,0:T(8,128)(2,1)} %bitcast.45, bf16[16,128,128]{2,1,0:T(8,128)(2,1)} %bitcast.56, bf16[16,8,128,128]{3,2,1,0:T(8,128)(2,1)} %weights.2), custom_call_target="tpu_custom_call" | custom-call | flops 540000000 | bytes 8000000 | tf_op jit(solution)/shard_map/encode/pallas_call | solution.py:84
  33.9 4.2 %collective-permute-done.3 = bf16[2,144,1024]{2,1,0:T(8,128)(2,1)S(1)} collective-permute-done((bf16[2,144,1024]{2,1,0:T(8,128)(2,1)S(1)}, bf16[2,144,1024]{2,1,0:T(8,128)(2,1)S(1)}, u32[]{:S(2)}, u32[]{:S(2)}) %collective-permute-start.3) | collective-permute-done | bytes 589856 | tf_op jit(solution)/shard_map/ppermute | solution.py:518
  38.5 1.3 collective-permute-start.5
  39.8 1.3 collective-permute-start.6
  41.1 1.4 collective-permute-start.7
  42.6 2.7 %collective-permute-start.9 = (bf16[144,1024]{1,0:T(8,128)(2,1)S(1)}, bf16[144,1024]{1,0:T(8,128)(2,1)S(1)}, u32[]{:S(2)}, u32[]{:S(2)}) collective-permute-start(bf16[144,1024]{1,0:T(8,128)(2,1)S(1)} %slice_bitcast_fusion), channel_id=1, source_target_pairs={{0,6},{1,7},{2,0},{3,1},{4,2},{5,3},{6,4},{7,5},{8,14},{9,15},{10,... | collective-permute-start | bytes 884744 | tf_op jit(solution)/shard_map/ppermute | solution.py:518
  45.3 15.0 %collective-permute-done.8 = bf16[144,1024]{1,0:T(8,128)(2,1)S(1)} collective-permute-done((bf16[144,1024]{1,0:T(8,128)(2,1)S(1)}, bf16[144,1024]{1,0:T(8,128)(2,1)S(1)}, u32[]{:S(2)}, u32[]{:S(2)}) %collective-permute-start.8) | collective-permute-done | bytes 294944 | tf_op jit(solution)/shard_map/ppermute | solution.py:518
  60.5 2.0 pad_maximum_fusion.refs_0_
  62.7 0.7 collective-permute-start.10
  63.4 2.1 collective-permute-start.11
  65.4 1.5 collective-permute-start.16
  66.9 14.6 %collective-permute-done.10.s3 = bf16[3072,128]{1,0:T(8,128)(2,1)S(1)} collective-permute-done((bf16[3072,128]{1,0:T(8,128)(2,1)S(1)}, bf16[3072,128]{1,0:T(8,128)(2,1)S(1)}, u32[]{:S(2)}, u32[]{:S(2)}) %collective-permute-start.10) | collective-permute-done | bytes 786464 | tf_op jit(solution)/shard_map/ppermute | solution.py:518
  81.5 0.9 copy-done.9
  82.5 0.9 copy-done.10
  83.4 0.8 pad_maximum_fusion.4.s6
  84.2 1.0 collective-permute-start.12
  85.8 9.7 %collective-permute-done.12.s7 = bf16[2048,128]{1,0:T(8,128)(2,1)} collective-permute-done((bf16[2048,128]{1,0:T(8,128)(2,1)}, bf16[2048,128]{1,0:T(8,128)(2,1)}, u32[]{:S(2)}, u32[]{:S(2)}) %collective-permute-start.12) | collective-permute-done | bytes 524320 | tf_op jit(solution)/shard_map/ppermute | solution.py:518
  95.5 8.6 %project.1 = (bf16[2048,128]{1,0:T(8,128)(2,1)}, bf16[2048,256]{1,0:T(8,128)(2,1)}, bf16[8,256,128]{2,1,0:T(8,128)(2,1)}) custom-call(s32[8]{0:T(128)} %stack.112.order, bf16[2048,128]{1,0:T(8,128)(2,1)} %encode.1.s0, bf16[2048,128]{1,0:T(8,128)(2,1)} %copy-done.8, bf16[2048,128]{1,0:T(8,128)(2,1)} %copy-done.13, bf16[3072,128]{1,0:T(8,128)(2,1)} %copy-done.9, ...), custom_call_target="tpu_custom_call" | custom-call | tf_op jit(solution)/shard_map/project/pallas_call | solution.py:153
  104.2 2.4 %fusion.2 = (bf16[1152,256]{1,0:T(8,128)(2,1)}, bf16[1152,256]{1,0:T(8,128)(2,1)}) fusion(bf16[2048,256]{1,0:T(8,128)(2,1)} %get-tuple-element.63.own), kind=kLoop, calls=%fused_computation.18 | loop fusion | bytes 2359296 | tf_op jit(solution)/shard_map/slice | solution.py:593
  106.5 1.9 collective-permute-start.13
  108.4 5.4 %collective-permute-start.14 = (bf16[1152,256]{1,0:T(8,128)(2,1)}, bf16[1152,256]{1,0:T(8,128)(2,1)}, u32[]{:S(2)}, u32[]{:S(2)}) collective-permute-start(bf16[1152,256]{1,0:T(8,128)(2,1)} %get-tuple-element.75), channel_id=1, source_target_pairs={{8,0},{16,8},{24,16},{32,24},{40,32},{48,40},{56,48},{64,56},{72,6... | collective-permute-start | bytes 1769480 | tf_op jit(solution)/shard_map/ppermute | solution.py:514
  114.4 1.2 collective-permute-done.13.low
  115.6 8.1 %collective-permute-done.14.high = bf16[1152,256]{1,0:T(8,128)(2,1)} collective-permute-done((bf16[1152,256]{1,0:T(8,128)(2,1)}, bf16[1152,256]{1,0:T(8,128)(2,1)}, u32[]{:S(2)}, u32[]{:S(2)}) %collective-permute-start.14) | collective-permute-done | bytes 589856 | tf_op jit(solution)/shard_map/ppermute | solution.py:514
  123.7 28.5 %attend.1 = bf16[2048,128]{1,0:T(8,128)(2,1)} custom-call(s32[2]{0:T(128)} %add_convert_fusion.edges, bf16[2048,128]{1,0:T(8,128)(2,1)} %get-tuple-element.62.queries, bf16[1152,256]{1,0:T(8,128)(2,1)} %collective-permute-done.13.low, bf16[2048,256]{1,0:T(8,128)(2,1)} %get-tuple-element.63.own, bf16[1152,256]{1,0:T(8,128)(2,1)} %collective-permute-done.14.high), custom_call_target="tpu_custom_call" | custom-call | tf_op jit(solution)/shard_map/attend/pallas_call | solution.py:249
  152.2 1.9 collective-permute-start.18
  154.7 4.1 %all-to-all-start = ((bf16[8,256,128]{2,1,0:T(8,128)(2,1)}), bf16[8,256,128]{2,1,0:T(8,128)(2,1)}, u32[]{:S(2)}, u32[]{:S(2)}) async-start(bf16[8,256,128]{2,1,0:T(8,128)(2,1)} %bitcast.49), calls=%async_computation | async-start | bytes 1048576 | tf_op jit(solution)/shard_map/all_to_all | solution.py:598
  159.5 8.8 %all-to-all-done.refs_8_ = bf16[8,256,128]{2,1,0:T(8,128)(2,1)} async-done(((bf16[8,256,128]{2,1,0:T(8,128)(2,1)}), bf16[8,256,128]{2,1,0:T(8,128)(2,1)}, u32[]{:S(2)}, u32[]{:S(2)}) %all-to-all-start) | async-done | bytes 524320 | tf_op jit(solution)/shard_map/all_to_all | solution.py:598
  168.7 12.9 %forward.1 = bf16[8,256,128]{2,1,0:T(8,128)(2,1)} custom-call(s32[16]{0:T(128)} %concatenate.19.table, bf16[4,2,144,1024]{3,2,1,0:T(8,128)(2,1)} %copy-done.4, bf16[4,2,144,1024]{3,2,1,0:T(8,128)(2,1)} %collective-permute-done.15.refs_1_, bf16[4,2,144,1024]{3,2,1,0:T(8,128)(2,1)} %collective-permute-done.16.refs_2_, ...), custom_call_target="tpu_custom_call" | custom-call | flops 4800000000 | bytes 20000000 | tf_op jit(solution)/shard_map/forward/pallas_call | solution.py:361
  181.7 12.5 %all_to_all.15 = bf16[8,256,128]{2,1,0:T(8,128)(2,1)S(1)} all-to-all(bf16[8,256,128]{2,1,0:T(8,128)(2,1)} %forward.1), channel_id=1, replica_groups=mesh['seq'=16,'head'=8] {'head'}, dimensions={0} | all-to-all | bytes 1048576 | tf_op jit(solution)/shard_map/all_to_all | solution.py:606
  194.2 2.5 %collective-permute-start.22 = (bf16[8,128,128]{2,1,0:T(8,128)(2,1)S(1)}, bf16[8,128,128]{2,1,0:T(8,128)(2,1)S(1)}, u32[]{:S(2)}, u32[]{:S(2)}) collective-permute-start(bf16[8,128,128]{2,1,0:T(8,128)(2,1)S(1)} %bitcast.61), channel_id=1, source_target_pairs={{0,8},{8,16},{16,24},{24,32},{32,40},{40,48},{48,56},{56,64},{64,7... | collective-permute-start | bytes 786440 | tf_op jit(solution)/shard_map/ppermute | solution.py:514
  196.7 3.5 %collective-permute-start.23 = (bf16[8,128,128]{2,1,0:T(8,128)(2,1)S(1)}, bf16[8,128,128]{2,1,0:T(8,128)(2,1)S(1)}, u32[]{:S(2)}, u32[]{:S(2)}) collective-permute-start(bf16[8,128,128]{2,1,0:T(8,128)(2,1)S(1)} %bitcast.60), channel_id=1, source_target_pairs={{8,0},{16,8},{24,16},{32,24},{40,32},{48,40},{56,48},{64,56},{72,6... | collective-permute-start | bytes 786440 | tf_op jit(solution)/shard_map/ppermute | solution.py:514
  201.0 7.0 %collective-permute-done.23.high = bf16[8,128,128]{2,1,0:T(8,128)(2,1)S(1)} collective-permute-done((bf16[8,128,128]{2,1,0:T(8,128)(2,1)S(1)}, bf16[8,128,128]{2,1,0:T(8,128)(2,1)S(1)}, u32[]{:S(2)}, u32[]{:S(2)}) %collective-permute-start.23) | collective-permute-done | bytes 262176 | tf_op jit(solution)/shard_map/ppermute | solution.py:514
  208.7 8.0 %decode.1 = (bf16[8192,128]{1,0:T(8,128)(2,1)}, bf16[8,16,128]{2,1,0:T(8,128)(2,1)}) custom-call(s32[64,2]{1,0:T(8,128)} %broadcast_subtract_fusion.index, bf16[8,128,128]{2,1,0:T(8,128)(2,1)} %copy-done.18, bf16[16,128,128]{2,1,0:T(8,128)(2,1)} %bitcast.47, bf16[8,128,128]{2,1,0:T(8,128)(2,1)} %copy-done.19, bf16[64,2,128,128]{3,2,1,0:T(8,128)(2,1)} %weights.3), custom_call_target="tpu_custom_call" | custom-call | flops 540000000 | bytes 10000000 | tf_op jit(solution)/shard_map/decode/pallas_call | solution.py:428
  216.8 0.8 broadcast_in_dim.3
  217.5 8.5 %all_to_all.16.sums = bf16[8,8,16,128]{3,2,1,0:T(8,128)(2,1)S(1)} all-to-all(bf16[8,8,16,128]{3,2,1,0:T(8,128)(2,1)S(1)} %broadcast_in_dim.3), channel_id=1, replica_groups=mesh['seq'=16,'head'=8] {'head'}, dimensions={0} | all-to-all | bytes 524288 | tf_op jit(solution)/shard_map/all_to_all | solution.py:616
  226.1 1.6 copy-done.2
  227.7 5.2 %finish.1 = bf16[8192,128]{1,0:T(8,128)(2,1)} custom-call(bf16[8,8,16,128]{3,2,1,0:T(8,128)(2,1)S(1)} %all_to_all.16.sums, bf16[8192,128]{1,0:T(8,128)(2,1)S(1)} %copy-done.2, bf16[8192,128]{1,0:T(8,128)(2,1)S(1)} %copy-done.1, f32[1,128]{1,0:T(1,128)S(1)} %bitcast.46), custom_call_target="tpu_custom_call" | custom-call | flops 540000000 | bytes 8000000 | tf_op jit(solution)/shard_map/finish/pallas_call | solution.py:492
  (81 shorter events, 6.3 us)
Async XLA Ops:
  0.0 9.2 %copy-start = (bf16[512,1024]{1,0:T(8,128)(2,1)S(1)}, bf16[512,1024]{1,0:T(8,128)(2,1)}, u32[]{:S(2)}) copy-start(bf16[512,1024]{1,0:T(8,128)(2,1)} %param.20) | copy-start | bytes 3145732
  0.0 10.5 %copy-start.15 = (bf16[1024,3,128]{2,0,1:T(8,128)(2,1)S(1)}, bf16[1024,3,128]{2,0,1:T(8,128)(2,1)}, u32[]{:S(2)}) copy-start(bf16[1024,3,128]{2,0,1:T(8,128)(2,1)} %param.16) | copy-start | bytes 2359300
  2.4 23.6 %copy-start.20 = (s32[16,8]{0,1:T(8,128)S(1)}, s32[16,8]{0,1:T(8,128)}, u32[]{:S(2)}) copy-start(s32[16,8]{0,1:T(8,128)} %param.13) | copy-start | bytes 1540
  2.4 17.5 %collective-permute-start = (bf16[2048,128]{1,0:T(8,128)(2,1)}, bf16[2048,128]{1,0:T(8,128)(2,1)S(1)}, u32[]{:S(2)}, u32[]{:S(2)}) collective-permute-start(bf16[2048,128]{1,0:T(8,128)(2,1)} %get-tuple-element.39), channel_id=1, source_target_pairs={{0,8},{8,16},{16,24},{24,32},{32,40},{40,48},{48,56},{56,64},{64,7... | collective-permute-start | bytes 1572872 | tf_op jit(solution)/shard_map/ppermute | solution.py:514
  6.3 16.1 %collective-permute-start.1 = (bf16[2048,128]{1,0:T(8,128)(2,1)}, bf16[2048,128]{1,0:T(8,128)(2,1)S(1)}, u32[]{:S(2)}, u32[]{:S(2)}) collective-permute-start(bf16[2048,128]{1,0:T(8,128)(2,1)} %get-tuple-element.40), channel_id=1, source_target_pairs={{8,0},{16,8},{24,16},{32,24},{40,32},{48,40},{56,48},{64,56},{72,6... | collective-permute-start | bytes 1572872 | tf_op jit(solution)/shard_map/ppermute | solution.py:514
  10.1 9.7 %collective-permute-start.2 = (bf16[144,1024]{1,0:T(8,128)(2,1)S(1)}, bf16[144,1024]{1,0:T(8,128)(2,1)S(1)}, u32[]{:S(2)}, u32[]{:S(2)}) collective-permute-start(bf16[144,1024]{1,0:T(8,128)(2,1)S(1)} %get-tuple-element.87), channel_id=1, source_target_pairs={{0,1},{1,0},{2,3},{3,2},{4,5},{5,4},{6,7},{7,6},{8,9},{9,8},{10,11... | collective-permute-start | bytes 884744 | tf_op jit(solution)/shard_map/ppermute | solution.py:518
  19.9 14.0 %copy-start.6 = (bf16[2,144,1024]{2,1,0:T(8,128)(2,1)}, bf16[2,144,1024]{2,1,0:T(8,128)(2,1)S(1)}, u32[]{:S(2)}) copy-start(bf16[2,144,1024]{2,1,0:T(8,128)(2,1)S(1)} %pad_maximum_fusion.3) | copy-start | bytes 1769476
  19.9 6.7 %copy-start.16 = (bf16[2048,128]{1,0:T(8,128)(2,1)}, bf16[2048,128]{1,0:T(8,128)(2,1)S(1)}, u32[]{:S(2)}) copy-start(bf16[2048,128]{1,0:T(8,128)(2,1)S(1)} %collective-permute-done) | copy-start | bytes 1572868
  22.5 0.8 copy-start.17
  23.3 14.9 %collective-permute-start.3 = (bf16[2,144,1024]{2,1,0:T(8,128)(2,1)S(1)}, bf16[2,144,1024]{2,1,0:T(8,128)(2,1)S(1)}, u32[]{:S(2)}, u32[]{:S(2)}) collective-permute-start(bf16[2,144,1024]{2,1,0:T(8,128)(2,1)S(1)} %pad_maximum_fusion.3), channel_id=1, source_target_pairs={{0,2},{1,3},{2,4},{3,5},{4,6},{5,7},{6,0},{7,1},{8,10},{9,11},{10,... | collective-permute-start | bytes 1769480 | tf_op jit(solution)/shard_map/ppermute | solution.py:518
  24.6 13.9 %collective-permute-start.4 = (bf16[2,144,1024]{2,1,0:T(8,128)(2,1)S(1)}, bf16[2,144,1024]{2,1,0:T(8,128)(2,1)S(1)}, u32[]{:S(2)}, u32[]{:S(2)}) collective-permute-start(bf16[2,144,1024]{2,1,0:T(8,128)(2,1)S(1)} %pad_maximum_fusion.3), channel_id=1, source_target_pairs={{0,6},{1,7},{2,0},{3,1},{4,2},{5,3},{6,4},{7,5},{8,14},{9,15},{10,... | collective-permute-start | bytes 1769480 | tf_op jit(solution)/shard_map/ppermute | solution.py:518
  38.1 22.3 %copy-start.11 = (bf16[2,144,1024]{2,1,0:T(8,128)(2,1)}, bf16[2,144,1024]{2,1,0:T(8,128)(2,1)S(1)}, u32[]{:S(2)}) copy-start(bf16[2,144,1024]{2,1,0:T(8,128)(2,1)S(1)} %collective-permute-done.3) | copy-start | bytes 1769476
  38.1 22.4 %copy-start.7 = (bf16[2,144,1024]{2,1,0:T(8,128)(2,1)S(1)}, bf16[2,144,1024]{2,1,0:T(8,128)(2,1)}, u32[]{:S(2)}) copy-start(bf16[2,144,1024]{2,1,0:T(8,128)(2,1)} %copy-done.6) | copy-start | bytes 1769476
  38.5 22.0 %copy-start.12 = (bf16[2,144,1024]{2,1,0:T(8,128)(2,1)}, bf16[2,144,1024]{2,1,0:T(8,128)(2,1)S(1)}, u32[]{:S(2)}) copy-start(bf16[2,144,1024]{2,1,0:T(8,128)(2,1)S(1)} %collective-permute-done.4) | copy-start | bytes 1769476
  38.5 21.9 %collective-permute-start.5 = (bf16[2048,128]{1,0:T(8,128)(2,1)}, bf16[2048,128]{1,0:T(8,128)(2,1)S(1)}, u32[]{:S(2)}, u32[]{:S(2)}) collective-permute-start(bf16[2048,128]{1,0:T(8,128)(2,1)} %encode.1.s0), channel_id=1, source_target_pairs={{0,1},{1,0},{2,3},{3,2},{4,5},{5,4},{6,7},{7,6},{8,9},{9,8},{10,11... | collective-permute-start | bytes 1572872 | tf_op jit(solution)/shard_map/ppermute | solution.py:518
  39.8 20.6 %collective-permute-start.6 = (bf16[2048,128]{1,0:T(8,128)(2,1)}, bf16[2048,128]{1,0:T(8,128)(2,1)S(1)}, u32[]{:S(2)}, u32[]{:S(2)}) collective-permute-start(bf16[2048,128]{1,0:T(8,128)(2,1)} %encode.1.s0), channel_id=1, source_target_pairs={{0,2},{1,3},{2,4},{3,5},{4,6},{5,7},{6,0},{7,1},{8,10},{9,11},{10,... | collective-permute-start | bytes 1572872 | tf_op jit(solution)/shard_map/ppermute | solution.py:518
  41.1 19.3 %collective-permute-start.7 = (bf16[2048,128]{1,0:T(8,128)(2,1)}, bf16[2048,128]{1,0:T(8,128)(2,1)S(1)}, u32[]{:S(2)}, u32[]{:S(2)}) collective-permute-start(bf16[2048,128]{1,0:T(8,128)(2,1)} %encode.1.s0), channel_id=1, source_target_pairs={{0,6},{1,7},{2,0},{3,1},{4,2},{5,3},{6,4},{7,5},{8,14},{9,15},{10,... | collective-permute-start | bytes 1572872 | tf_op jit(solution)/shard_map/ppermute | solution.py:518
  42.5 17.8 %collective-permute-start.8 = (bf16[144,1024]{1,0:T(8,128)(2,1)S(1)}, bf16[144,1024]{1,0:T(8,128)(2,1)S(1)}, u32[]{:S(2)}, u32[]{:S(2)}) collective-permute-start(bf16[144,1024]{1,0:T(8,128)(2,1)S(1)} %slice_bitcast_fusion.1), channel_id=1, source_target_pairs={{0,2},{1,3},{2,4},{3,5},{4,6},{5,7},{6,0},{7,1},{8,10},{9,11},{10,... | collective-permute-start | bytes 884744 | tf_op jit(solution)/shard_map/ppermute | solution.py:518
  42.6 17.7 %collective-permute-start.9 = (bf16[144,1024]{1,0:T(8,128)(2,1)S(1)}, bf16[144,1024]{1,0:T(8,128)(2,1)S(1)}, u32[]{:S(2)}, u32[]{:S(2)}) collective-permute-start(bf16[144,1024]{1,0:T(8,128)(2,1)S(1)} %slice_bitcast_fusion), channel_id=1, source_target_pairs={{0,6},{1,7},{2,0},{3,1},{4,2},{5,3},{6,4},{7,5},{8,14},{9,15},{10,... | collective-permute-start | bytes 884744 | tf_op jit(solution)/shard_map/ppermute | solution.py:518
  60.3 2.2 copy-start.8
  60.4 2.1 copy-start.13
  60.4 2.1 copy-start.14
  62.5 89.8 %copy-start.4 = (bf16[4,2,144,1024]{3,2,1,0:T(8,128)(2,1)}, bf16[4,2,144,1024]{3,2,1,0:T(8,128)(2,1)S(1)}, u32[]{:S(2)}) copy-start(bf16[4,2,144,1024]{3,2,1,0:T(8,128)(2,1)S(1)} %pad_maximum_fusion.refs_0_) | copy-start | bytes 7077892
  62.7 18.8 %collective-permute-start.10 = (bf16[3072,128]{1,0:T(8,128)(2,1)S(1)}, bf16[3072,128]{1,0:T(8,128)(2,1)S(1)}, u32[]{:S(2)}, u32[]{:S(2)}) collective-permute-start(bf16[3072,128]{1,0:T(8,128)(2,1)S(1)} %get-tuple-element.85), channel_id=1, source_target_pairs={{0,2},{1,3},{2,4},{3,5},{4,6},{5,7},{6,0},{7,1},{8,10},{9,11},{10,... | collective-permute-start | bytes 2359304 | tf_op jit(solution)/shard_map/ppermute | solution.py:518
  63.4 19.1 %collective-permute-start.11 = (bf16[3072,128]{1,0:T(8,128)(2,1)S(1)}, bf16[3072,128]{1,0:T(8,128)(2,1)S(1)}, u32[]{:S(2)}, u32[]{:S(2)}) collective-permute-start(bf16[3072,128]{1,0:T(8,128)(2,1)S(1)} %get-tuple-element.84), channel_id=1, source_target_pairs={{0,6},{1,7},{2,0},{3,1},{4,2},{5,3},{6,4},{7,5},{8,14},{9,15},{10,... | collective-permute-start | bytes 2359304 | tf_op jit(solution)/shard_map/ppermute | solution.py:518
  65.4 86.8 %collective-permute-start.15 = (bf16[4,2,144,1024]{3,2,1,0:T(8,128)(2,1)S(1)}, bf16[4,2,144,1024]{3,2,1,0:T(8,128)(2,1)}, u32[]{:S(2)}, u32[]{:S(2)}) collective-permute-start(bf16[4,2,144,1024]{3,2,1,0:T(8,128)(2,1)S(1)} %pad_maximum_fusion.refs_0_), channel_id=1, source_target_pairs={{0,16},{8,24},{16,32},{24,40},{32,48},{40,56},{48,0},{56,8},{64,80... | collective-permute-start | bytes 7077896 | tf_op jit(solution)/shard_map/ppermute | solution.py:518
  65.4 86.8 %collective-permute-start.16 = (bf16[4,2,144,1024]{3,2,1,0:T(8,128)(2,1)S(1)}, bf16[4,2,144,1024]{3,2,1,0:T(8,128)(2,1)}, u32[]{:S(2)}, u32[]{:S(2)}) collective-permute-start(bf16[4,2,144,1024]{3,2,1,0:T(8,128)(2,1)S(1)} %pad_maximum_fusion.refs_0_), channel_id=1, source_target_pairs={{0,48},{8,56},{16,0},{24,8},{32,16},{40,24},{48,32},{56,40},{64,11... | collective-permute-start | bytes 7077896 | tf_op jit(solution)/shard_map/ppermute | solution.py:518
  66.9 85.3 %collective-permute-start.17 = (bf16[4,2,144,1024]{3,2,1,0:T(8,128)(2,1)S(1)}, bf16[4,2,144,1024]{3,2,1,0:T(8,128)(2,1)}, u32[]{:S(2)}, u32[]{:S(2)}) collective-permute-start(bf16[4,2,144,1024]{3,2,1,0:T(8,128)(2,1)S(1)} %pad_maximum_fusion.refs_0_), channel_id=1, source_target_pairs={{0,65},{1,64},{2,67},{3,66},{4,69},{5,68},{6,71},{7,70},{8,73},{9,... | collective-permute-start | bytes 7077896 | tf_op jit(solution)/shard_map/ppermute | solution.py:518
  81.5 0.9 copy-start.9
  82.5 0.9 copy-start.10
  84.2 11.3 %collective-permute-start.12 = (bf16[2048,128]{1,0:T(8,128)(2,1)}, bf16[2048,128]{1,0:T(8,128)(2,1)}, u32[]{:S(2)}, u32[]{:S(2)}) collective-permute-start(bf16[2048,128]{1,0:T(8,128)(2,1)} %pad_maximum_fusion.4.s6), channel_id=1, source_target_pairs={{0,1},{1,0},{2,3},{3,2},{4,5},{5,4},{6,7},{7,6},{8,9},{9,8},{10,11... | collective-permute-start | bytes 1572872 | tf_op jit(solution)/shard_map/ppermute | solution.py:518
  106.5 9.1 %collective-permute-start.13 = (bf16[1152,256]{1,0:T(8,128)(2,1)}, bf16[1152,256]{1,0:T(8,128)(2,1)}, u32[]{:S(2)}, u32[]{:S(2)}) collective-permute-start(bf16[1152,256]{1,0:T(8,128)(2,1)} %get-tuple-element.76), channel_id=1, source_target_pairs={{0,8},{8,16},{16,24},{24,32},{32,40},{40,48},{48,56},{56,64},{64,7... | collective-permute-start | bytes 1769480 | tf_op jit(solution)/shard_map/ppermute | solution.py:514
  108.4 15.3 %collective-permute-start.14 = (bf16[1152,256]{1,0:T(8,128)(2,1)}, bf16[1152,256]{1,0:T(8,128)(2,1)}, u32[]{:S(2)}, u32[]{:S(2)}) collective-permute-start(bf16[1152,256]{1,0:T(8,128)(2,1)} %get-tuple-element.75), channel_id=1, source_target_pairs={{8,0},{16,8},{24,16},{32,24},{40,32},{48,40},{56,48},{64,56},{72,6... | collective-permute-start | bytes 1769480 | tf_op jit(solution)/shard_map/ppermute | solution.py:514
  152.2 16.1 %collective-permute-start.18 = (bf16[4,2,144,1024]{3,2,1,0:T(8,128)(2,1)S(1)}, bf16[4,2,144,1024]{3,2,1,0:T(8,128)(2,1)}, u32[]{:S(2)}, u32[]{:S(2)}) collective-permute-start(bf16[4,2,144,1024]{3,2,1,0:T(8,128)(2,1)S(1)} %pad_maximum_fusion.refs_0_), channel_id=1, source_target_pairs={{0,8},{8,0},{16,24},{24,16},{32,40},{40,32},{48,56},{56,48},{64,72... | collective-permute-start | bytes 7077896 | tf_op jit(solution)/shard_map/ppermute | solution.py:518
  154.1 14.3 %collective-permute-start.19 = (bf16[4,2,144,1024]{3,2,1,0:T(8,128)(2,1)}, bf16[4,2,144,1024]{3,2,1,0:T(8,128)(2,1)}, u32[]{:S(2)}, u32[]{:S(2)}) collective-permute-start(bf16[4,2,144,1024]{3,2,1,0:T(8,128)(2,1)} %collective-permute-done.15.refs_1_), channel_id=1, source_target_pairs={{0,8},{8,0},{16,24},{24,16},{32,40},{40,32},{48,56},{56,48},{64,72... | collective-permute-start | bytes 7077896 | tf_op jit(solution)/shard_map/ppermute | solution.py:518
  154.2 14.2 %collective-permute-start.20 = (bf16[4,2,144,1024]{3,2,1,0:T(8,128)(2,1)}, bf16[4,2,144,1024]{3,2,1,0:T(8,128)(2,1)}, u32[]{:S(2)}, u32[]{:S(2)}) collective-permute-start(bf16[4,2,144,1024]{3,2,1,0:T(8,128)(2,1)} %collective-permute-done.16.refs_2_), channel_id=1, source_target_pairs={{0,8},{8,0},{16,24},{24,16},{32,40},{40,32},{48,56},{56,48},{64,72... | collective-permute-start | bytes 7077896 | tf_op jit(solution)/shard_map/ppermute | solution.py:518
  154.6 14.1 %collective-permute-start.21 = (bf16[4,2,144,1024]{3,2,1,0:T(8,128)(2,1)}, bf16[4,2,144,1024]{3,2,1,0:T(8,128)(2,1)}, u32[]{:S(2)}, u32[]{:S(2)}) collective-permute-start(bf16[4,2,144,1024]{3,2,1,0:T(8,128)(2,1)} %collective-permute-done.17.refs_3_), channel_id=1, source_target_pairs={{0,8},{8,0},{16,24},{24,16},{32,40},{40,32},{48,56},{56,48},{64,72... | collective-permute-start | bytes 7077896 | tf_op jit(solution)/shard_map/ppermute | solution.py:518
  154.7 13.7 %all-to-all-start = ((bf16[8,256,128]{2,1,0:T(8,128)(2,1)}), bf16[8,256,128]{2,1,0:T(8,128)(2,1)}, u32[]{:S(2)}, u32[]{:S(2)}) async-start(bf16[8,256,128]{2,1,0:T(8,128)(2,1)} %bitcast.49), calls=%async_computation | async-start | bytes 1048576 | tf_op jit(solution)/shard_map/all_to_all | solution.py:598
  168.7 31.5 %copy-start.21 = (s32[64,2]{0,1:T(2,128)S(1)}, s32[64,2]{0,1:T(2,128)}, u32[]{:S(2)}) copy-start(s32[64,2]{0,1:T(2,128)} %param.21) | copy-start | bytes 1540
  194.1 13.9 %copy-start.5 = (bf16[8,256,128]{2,1,0:T(8,128)(2,1)}, bf16[8,256,128]{2,1,0:T(8,128)(2,1)S(1)}, u32[]{:S(2)}) copy-start(bf16[8,256,128]{2,1,0:T(8,128)(2,1)S(1)} %all_to_all.15) | copy-start | bytes 1572868
  194.2 6.8 %collective-permute-start.22 = (bf16[8,128,128]{2,1,0:T(8,128)(2,1)S(1)}, bf16[8,128,128]{2,1,0:T(8,128)(2,1)S(1)}, u32[]{:S(2)}, u32[]{:S(2)}) collective-permute-start(bf16[8,128,128]{2,1,0:T(8,128)(2,1)S(1)} %bitcast.61), channel_id=1, source_target_pairs={{0,8},{8,16},{16,24},{24,32},{32,40},{40,48},{48,56},{56,64},{64,7... | collective-permute-start | bytes 786440 | tf_op jit(solution)/shard_map/ppermute | solution.py:514
  196.7 11.3 %collective-permute-start.23 = (bf16[8,128,128]{2,1,0:T(8,128)(2,1)S(1)}, bf16[8,128,128]{2,1,0:T(8,128)(2,1)S(1)}, u32[]{:S(2)}, u32[]{:S(2)}) collective-permute-start(bf16[8,128,128]{2,1,0:T(8,128)(2,1)S(1)} %bitcast.60), channel_id=1, source_target_pairs={{8,0},{16,8},{24,16},{32,24},{40,32},{48,40},{56,48},{64,56},{72,6... | collective-permute-start | bytes 786440 | tf_op jit(solution)/shard_map/ppermute | solution.py:514
  201.0 7.0 %copy-start.18 = (bf16[8,128,128]{2,1,0:T(8,128)(2,1)}, bf16[8,128,128]{2,1,0:T(8,128)(2,1)S(1)}, u32[]{:S(2)}) copy-start(bf16[8,128,128]{2,1,0:T(8,128)(2,1)S(1)} %collective-permute-done.22.low) | copy-start | bytes 786436
  208.0 0.7 copy-start.19
  208.7 17.4 %copy-start.1 = (bf16[8192,128]{1,0:T(8,128)(2,1)S(1)}, bf16[8192,128]{1,0:T(8,128)(2,1)}, u32[]{:S(2)}) copy-start(bf16[8192,128]{1,0:T(8,128)(2,1)} %state.1) | copy-start | bytes 6291460
  208.7 17.4 %copy-start.3 = (f32[128]{0:T(128)S(1)}, f32[128]{0:T(128)}, u32[]{:S(2)}) copy-start(f32[128]{0:T(128)} %param.23) | copy-start | bytes 1540
  226.1 1.6 copy-start.2

commit v6 on v5

--- a/solution.py
+++ b/solution.py
@@ -552,34 +552,38 @@
     mesh_rows = mesh_blocks * BLOCK
     grid_blocks = grid_state.shape[0] // BLOCK
     rim = mesh_blocks * BLOCK
-    last, first, expand, shrink, outward, inward = lax.optimization_barrier(
-        (
-            grid_state[-rim:], grid_state[:rim],
-            expand_weights, shrink_weights, project_out, project_in,
-        )
+    core, place = band % 2, (band // 2 + 2 * (band // 8)) % 4
+    position = place * 2 + core
+    packed = pack_weights(position, expand_weights, shrink_weights, project_out)
+    last, first, packed = lax.optimization_barrier(
+        (grid_state[-rim:], grid_state[:rim], packed)
     )
     low = shifted(last, 1)
     high = shifted(first, -1)
-
-    core, place = band % 2, (band // 2 + 2 * (band // 8)) % 4
-    position = place * 2 + core
-    packed = pack_weights(position, expand, shrink, outward)
-    inward = [inward[:, j, :].reshape(8, BLOCK, BLOCK) for j in range(3)]
-    packed = jnp.stack([packed, OVER(packed)])
-    low, high, packed, *inward = lax.optimization_barrier((low, high, packed, *inward))
-    packed_a, packed_b = NORTH(packed), SOUTH(packed)
-
+    swapped, north, south = OVER(packed), NORTH(packed), SOUTH(packed)
+    swapped_north, swapped_south = NORTH(swapped), SOUTH(swapped)
+    far, swapped_far = NORTH(north), SOUTH(swapped_south)
+    inward = [project_in[:, j, :].reshape(8, BLOCK, BLOCK) for j in range(3)]
+    low, high, *inward = lax.optimization_barrier((low, high, *inward))
     mesh_start = encode(
         encode_index - (band * grid_blocks - mesh_blocks), low, grid_state, high, encode_weights
     )
     half = mesh_rows // 2
-    x, packed_a, packed_b = lax.optimization_barrier((mesh_start, packed_a, packed_b))
-    y, xa, xb, far_a, far_b = lax.optimization_barrier(
-        (OVER(x), NORTH(x), SOUTH(x), NORTH(packed_a[0]), SOUTH(packed_b[1]))
-    )
-    mine = jnp.stack([packed, packed_a, packed_b, jnp.stack([far_a, far_b])])
-    mine, y, xa, xb = lax.optimization_barrier((mine, y, xa, xb))
-    others = [UP(mine), DOWN(mine), ACROSS(mine)]
+    mine = jnp.stack(
+        [
+            jnp.stack(pair)
+            for pair in (
+                (packed, swapped),
+                (north, swapped_north),
+                (south, swapped_south),
+                (far, swapped_far),
+            )
+        ]
+    )
+    x, mine = lax.optimization_barrier((mesh_start, mine))
+    up, down = UP(mine), DOWN(mine)
+    y, xa, xb, mine = lax.optimization_barrier((OVER(x), NORTH(x), SOUTH(x), mine))
+    across = ACROSS(mine)
     from_south = NORTH(jnp.concatenate([xa[:half], y]))
     from_north = SOUTH(jnp.concatenate([xb[half:], y]))
     xc = jnp.concatenate([from_south[:half], from_north[:half]])
@@ -589,11 +593,14 @@
         [me, partner] + [(v + by) % 8 for by in (6, 2, 4) for v in (me, partner)]
     ).astype(jnp.int32)
     queries, keys_values, share = project(order, slots, first_gain, inward)
-    below = shifted(keys_values[mesh_rows - REACH :], 1)
-    above = shifted(keys_values[:REACH], -1)
+    upper, lower, up, down = lax.optimization_barrier(
+        (keys_values[mesh_rows - REACH :], keys_values[:REACH], up, down)
+    )
+    below = shifted(upper, 1)
+    above = shifted(lower, -1)
     edges = jnp.stack([band == 0, band == bands - 1]).astype(jnp.int32)
     context = attend(edges, queries, below, keys_values, above)
-    context, *here = lax.optimization_barrier((context, mine, *others))
+    context, *here = lax.optimization_barrier((context, mine, up, down, across))
     parts = here + [TWIN(v) for v in here]
     context = lax.all_to_all(
         context.reshape(8, mesh_rows // 8, BLOCK), "head", 0, 0, tiled=True

time: 236 us -> 224 us (0.949)
  waiting for transfers between devices: 80.4 us -> 66.2 us
  starting transfers between devices: 41 us -> 44.5 us
    ppermute x18 -> x20, waiting for transfers between devices: 52.7 us -> 30.4 us  [among(): return lax.ppermute(value, axis, [(i, to(i)) for i in range(count)])]
    ppermute x6, waiting for transfers between devices: 18.9 us -> 26.3 us  [shifted(): lax.ppermute(value, 'seq', [(i, i + by) for i in range(16) if 0 <= i + by...]
    ppermute x6, starting transfers between devices: 19.3 us -> 24 us  [shifted(): lax.ppermute(value, 'seq', [(i, i + by) for i in range(16) if 0 <= i + by...]
    ppermute x18 -> x20, starting transfers between devices: 17.6 us -> 16.4 us  [among(): return lax.ppermute(value, axis, [(i, to(i)) for i in range(count)])]
    unnamed x46 -> x40, local copies, waits for them, and re-layouts: 5.1 us -> 5.12 us
  transfers between devices with their start and end apart: 25 -> 27, of which waited for: 12 -> 11; matrix products, arithmetic and copies ran while one was open for 4% -> 4% of each run, Pallas kernels for 19% -> 20%
where the time goes in v6:
time: 224 us; the launch traced here: 223 us
  Pallas kernels  70.3 us (31%)
  waiting for transfers between devices  66.2 us (30%)
  starting transfers between devices  44.5 us (20%)
  blocking collectives  21.2 us (9%)
  local copies, waits for them, and re-layouts  14.6 us (7%)
  other arithmetic  5.27 us (2%)
    ppermute x20, waiting for transfers between devices, among(): return lax.ppermute(value, axis, [(i, to(i)) for i in range(count)])  30.4 us
    pallas_call x1, Pallas kernels, attend(): pl.pallas_call(attend_kernel, out_shape=jax.ShapeDtypeStruct((rows, BLOCK...  28.5 us
    ppermute x6, waiting for transfers between devices, shifted(): lax.ppermute(value, 'seq', [(i, i + by) for i in range(16) if 0 <= i + by...  26.3 us
    ppermute x6, starting transfers between devices, shifted(): lax.ppermute(value, 'seq', [(i, i + by) for i in range(16) if 0 <= i + by...  24 us
    ppermute x20, starting transfers between devices, among(): return lax.ppermute(value, axis, [(i, to(i)) for i in range(count)])  16.4 us
    pallas_call x1, Pallas kernels, forward(): pl.pallas_call(forward_kernel, out_shape=jax.ShapeDtypeStruct((8, rows, B...  12.8 us
    all_to_all x1, blocking collectives, on_device(): mesh_end = lax.all_to_all(mesh_end, 'head', 0, 0, tiled=True)  12.7 us
    all_to_all x1, waiting for transfers between devices, on_device(): lax.all_to_all(context.reshape(8, mesh_rows // 8, BLOCK), 'head', 0, 0, t...  9.5 us
  transfers between devices with their start and end apart: 27, of which 11 were waited for; matrix products, arithmetic and copies ran while one was open for 4% of the time, Pallas kernels for 20%

profile of v6, /device:TPU:97, one launch (start us, length us, event | category | flops | bytes accessed | tf_op | source)
XLA Modules:
  0.0 222.8 jit_solution(1101769607351516525)
XLA Ops:
  0.0 2.4 %fusion = (bf16[2048,128]{1,0:T(8,128)(2,1)}, bf16[2048,128]{1,0:T(8,128)(2,1)}) fusion(bf16[8192,128]{1,0:T(8,128)(2,1)} %state.1), kind=kLoop, calls=%fused_computation.16 | loop fusion | bytes 2097152 | tf_op jit(solution)/shard_map/slice | solution.py:559
  2.4 0.9 constant_dynamic-slice_fusion
  3.3 0.8 constant_dynamic-slice_fusion.1
  4.1 1.3 collective-permute-start.2
  5.4 1.3 collective-permute-start.3
  6.7 4.1 %collective-permute-start = (bf16[2048,128]{1,0:T(8,128)(2,1)}, bf16[2048,128]{1,0:T(8,128)(2,1)S(1)}, u32[]{:S(2)}, u32[]{:S(2)}) collective-permute-start(bf16[2048,128]{1,0:T(8,128)(2,1)} %get-tuple-element.33), channel_id=1, source_target_pairs={{0,8},{8,16},{16,24},{24,32},{32,40},{40,48},{48,56},{56,64},{64,7... | collective-permute-start | bytes 1572872 | tf_op jit(solution)/shard_map/ppermute | solution.py:514
  10.8 1.9 collective-permute-start.1
  12.7 0.9 fusion.2
  13.7 1.4 collective-permute-start.6
  15.8 2.6 %collective-permute-start.5 = (bf16[144,1024]{1,0:T(8,128)(2,1)S(1)}, bf16[144,1024]{1,0:T(8,128)(2,1)S(1)}, u32[]{:S(2)}, u32[]{:S(2)}) collective-permute-start(bf16[144,1024]{1,0:T(8,128)(2,1)S(1)} %pad_maximum_fusion.4), channel_id=1, source_target_pairs={{0,6},{1,7},{2,0},{3,1},{4,2},{5,3},{6,4},{7,5},{8,14},{9,15},{10,... | collective-permute-start | bytes 884744 | tf_op jit(solution)/shard_map/ppermute | solution.py:518
  18.4 1.0 maximum_bitcast_fusion
  19.5 5.6 %collective-permute-done.1 = bf16[2048,128]{1,0:T(8,128)(2,1)S(1)} collective-permute-done((bf16[2048,128]{1,0:T(8,128)(2,1)}, bf16[2048,128]{1,0:T(8,128)(2,1)S(1)}, u32[]{:S(2)}, u32[]{:S(2)}) %collective-permute-start.1) | collective-permute-done | bytes 524320 | tf_op jit(solution)/shard_map/ppermute | solution.py:514
  25.1 1.4 collective-permute-start.8
  26.5 7.2 %encode.1.s0 = bf16[2048,128]{1,0:T(8,128)(2,1)} custom-call(s32[16,8]{1,0:T(8,128)} %broadcast_subtract_fusion.1.index, bf16[16,128,128]{2,1,0:T(8,128)(2,1)} %bitcast.55, bf16[64,128,128]{2,1,0:T(8,128)(2,1)} %bitcast.47, bf16[16,128,128]{2,1,0:T(8,128)(2,1)} %bitcast.56, bf16[16,8,128,128]{3,2,1,0:T(8,128)(2,1)} %weights.2), custom_call_target="tpu_custom_call" | custom-call | flops 540000000 | bytes 8000000 | tf_op jit(solution)/shard_map/encode/pallas_call | solution.py:84
  33.8 1.0 maximum_bitcast_fusion.1
  35.3 0.7 copy-done.6
  36.0 0.7 collective-permute-start.10
  36.7 2.0 collective-permute-start.11
  38.7 1.5 collective-permute-start.16
  40.1 7.9 %collective-permute-done.10.s2 = bf16[2048,128]{1,0:T(8,128)(2,1)S(1)} collective-permute-done((bf16[2048,128]{1,0:T(8,128)(2,1)S(1)}, bf16[2048,128]{1,0:T(8,128)(2,1)S(1)}, u32[]{:S(2)}, u32[]{:S(2)}) %collective-permute-start.10) | collective-permute-done | bytes 524320 | tf_op jit(solution)/shard_map/ppermute | solution.py:518
  48.2 0.7 collective-permute-done.9.s1
  49.2 1.1 collective-permute-start.12
  50.2 1.7 collective-permute-start.13
  52.2 13.4 %collective-permute-done.12.s3 = bf16[3072,128]{1,0:T(8,128)(2,1)S(1)} collective-permute-done((bf16[3072,128]{1,0:T(8,128)(2,1)S(1)}, bf16[3072,128]{1,0:T(8,128)(2,1)S(1)}, u32[]{:S(2)}, u32[]{:S(2)}) %collective-permute-start.12) | collective-permute-done | bytes 786464 | tf_op jit(solution)/shard_map/ppermute | solution.py:518
  65.5 0.9 copy-done.8
  66.5 0.9 copy-done.9
  67.4 0.8 pad_maximum_fusion.3.s6
  68.9 8.2 %collective-permute-done.14.s7 = bf16[2048,128]{1,0:T(8,128)(2,1)} collective-permute-done((bf16[2048,128]{1,0:T(8,128)(2,1)}, bf16[2048,128]{1,0:T(8,128)(2,1)}, u32[]{:S(2)}, u32[]{:S(2)}) %collective-permute-start.14) | collective-permute-done | bytes 524320 | tf_op jit(solution)/shard_map/ppermute | solution.py:518
  77.1 8.6 %project.1 = (bf16[2048,128]{1,0:T(8,128)(2,1)}, bf16[2048,256]{1,0:T(8,128)(2,1)}, bf16[8,256,128]{2,1,0:T(8,128)(2,1)}) custom-call(s32[8]{0:T(128)} %stack.130.order, bf16[2048,128]{1,0:T(8,128)(2,1)} %encode.1.s0, bf16[2048,128]{1,0:T(8,128)(2,1)} %copy-done.7, bf16[2048,128]{1,0:T(8,128)(2,1)} %copy-done.10, bf16[3072,128]{1,0:T(8,128)(2,1)} %copy-done.8, ...), custom_call_target="tpu_custom_call" | custom-call | tf_op jit(solution)/shard_map/project/pallas_call | solution.py:153
  85.7 2.4 %fusion.1 = (bf16[1152,256]{1,0:T(8,128)(2,1)}, bf16[1152,256]{1,0:T(8,128)(2,1)}) fusion(bf16[2048,256]{1,0:T(8,128)(2,1)} %get-tuple-element.47.own), kind=kLoop, calls=%fused_computation.17 | loop fusion | bytes 2359296 | tf_op jit(solution)/shard_map/slice | solution.py:597
  88.1 10.0 %collective-permute-start.17 = (bf16[1152,256]{1,0:T(8,128)(2,1)}, bf16[1152,256]{1,0:T(8,128)(2,1)}, u32[]{:S(2)}, u32[]{:S(2)}) collective-permute-start(bf16[1152,256]{1,0:T(8,128)(2,1)} %get-tuple-element.48), channel_id=1, source_target_pairs={{0,8},{8,16},{16,24},{24,32},{32,40},{40,48},{48,56},{56,64},{64,7... | collective-permute-start | bytes 1769480 | tf_op jit(solution)/shard_map/ppermute | solution.py:514
  98.1 2.1 collective-permute-start.18
  100.9 4.4 %collective-permute-done.17.low = bf16[1152,256]{1,0:T(8,128)(2,1)} collective-permute-done((bf16[1152,256]{1,0:T(8,128)(2,1)}, bf16[1152,256]{1,0:T(8,128)(2,1)}, u32[]{:S(2)}, u32[]{:S(2)}) %collective-permute-start.17) | collective-permute-done | bytes 589856 | tf_op jit(solution)/shard_map/ppermute | solution.py:514
  105.3 8.1 %collective-permute-done.18.high = bf16[1152,256]{1,0:T(8,128)(2,1)} collective-permute-done((bf16[1152,256]{1,0:T(8,128)(2,1)}, bf16[1152,256]{1,0:T(8,128)(2,1)}, u32[]{:S(2)}, u32[]{:S(2)}) %collective-permute-start.18) | collective-permute-done | bytes 589856 | tf_op jit(solution)/shard_map/ppermute | solution.py:514
  113.4 28.5 %attend.1 = bf16[2048,128]{1,0:T(8,128)(2,1)} custom-call(s32[2]{0:T(128)} %add_convert_fusion.edges, bf16[2048,128]{1,0:T(8,128)(2,1)} %get-tuple-element.46.queries, bf16[1152,256]{1,0:T(8,128)(2,1)} %collective-permute-done.17.low, bf16[2048,256]{1,0:T(8,128)(2,1)} %get-tuple-element.47.own, bf16[1152,256]{1,0:T(8,128)(2,1)} %collective-permute-done.18.high), custom_call_target="tpu_custom_call" | custom-call | tf_op jit(solution)/shard_map/attend/pallas_call | solution.py:249
  143.0 4.1 %all-to-all-start = ((bf16[8,256,128]{2,1,0:T(8,128)(2,1)}), bf16[8,256,128]{2,1,0:T(8,128)(2,1)}, u32[]{:S(2)}, u32[]{:S(2)}) async-start(bf16[8,256,128]{2,1,0:T(8,128)(2,1)} %bitcast.50), calls=%async_computation | async-start | bytes 1048576 | tf_op jit(solution)/shard_map/all_to_all | solution.py:605
  147.9 9.5 %all-to-all-done.refs_8_ = bf16[8,256,128]{2,1,0:T(8,128)(2,1)} async-done(((bf16[8,256,128]{2,1,0:T(8,128)(2,1)}), bf16[8,256,128]{2,1,0:T(8,128)(2,1)}, u32[]{:S(2)}, u32[]{:S(2)}) %all-to-all-start) | async-done | bytes 524320 | tf_op jit(solution)/shard_map/all_to_all | solution.py:605
  157.4 12.8 %forward.1 = bf16[8,256,128]{2,1,0:T(8,128)(2,1)} custom-call(s32[16]{0:T(128)} %concatenate.19.table, bf16[4,2,144,1024]{3,2,1,0:T(8,128)(2,1)} %copy-done.4, bf16[4,2,144,1024]{3,2,1,0:T(8,128)(2,1)} %collective-permute-done.15.refs_1_, bf16[4,2,144,1024]{3,2,1,0:T(8,128)(2,1)} %collective-permute-done.16.refs_2_, ...), custom_call_target="tpu_custom_call" | custom-call | flops 4800000000 | bytes 20000000 | tf_op jit(solution)/shard_map/forward/pallas_call | solution.py:361
  170.2 12.7 %all_to_all.15 = bf16[8,256,128]{2,1,0:T(8,128)(2,1)S(1)} all-to-all(bf16[8,256,128]{2,1,0:T(8,128)(2,1)} %forward.1), channel_id=1, replica_groups=mesh['seq'=16,'head'=8] {'head'}, dimensions={0} | all-to-all | bytes 1048576 | tf_op jit(solution)/shard_map/all_to_all | solution.py:613
  182.9 3.6 %collective-permute-start.24 = (bf16[8,128,128]{2,1,0:T(8,128)(2,1)S(1)}, bf16[8,128,128]{2,1,0:T(8,128)(2,1)S(1)}, u32[]{:S(2)}, u32[]{:S(2)}) collective-permute-start(bf16[8,128,128]{2,1,0:T(8,128)(2,1)S(1)} %bitcast.63), channel_id=1, source_target_pairs={{0,8},{8,16},{16,24},{24,32},{32,40},{40,48},{48,56},{56,64},{64,7... | collective-permute-start | bytes 786440 | tf_op jit(solution)/shard_map/ppermute | solution.py:514
  186.5 2.3 %collective-permute-start.25 = (bf16[8,128,128]{2,1,0:T(8,128)(2,1)S(1)}, bf16[8,128,128]{2,1,0:T(8,128)(2,1)S(1)}, u32[]{:S(2)}, u32[]{:S(2)}) collective-permute-start(bf16[8,128,128]{2,1,0:T(8,128)(2,1)S(1)} %bitcast.62), channel_id=1, source_target_pairs={{8,0},{16,8},{24,16},{32,24},{40,32},{48,40},{56,48},{64,56},{72,6... | collective-permute-start | bytes 786440 | tf_op jit(solution)/shard_map/ppermute | solution.py:514
  189.8 8.0 %collective-permute-done.25.high = bf16[8,128,128]{2,1,0:T(8,128)(2,1)S(1)} collective-permute-done((bf16[8,128,128]{2,1,0:T(8,128)(2,1)S(1)}, bf16[8,128,128]{2,1,0:T(8,128)(2,1)S(1)}, u32[]{:S(2)}, u32[]{:S(2)}) %collective-permute-start.25) | collective-permute-done | bytes 262176 | tf_op jit(solution)/shard_map/ppermute | solution.py:514
  197.8 0.7 copy-done.16
  198.5 8.0 %decode.1 = (bf16[8192,128]{1,0:T(8,128)(2,1)}, bf16[8,16,128]{2,1,0:T(8,128)(2,1)}) custom-call(s32[64,2]{1,0:T(8,128)} %broadcast_subtract_fusion.index, bf16[8,128,128]{2,1,0:T(8,128)(2,1)} %copy-done.15, bf16[16,128,128]{2,1,0:T(8,128)(2,1)} %bitcast.49, bf16[8,128,128]{2,1,0:T(8,128)(2,1)} %copy-done.16, bf16[64,2,128,128]{3,2,1,0:T(8,128)(2,1)} %weights.3), custom_call_target="tpu_custom_call" | custom-call | flops 540000000 | bytes 10000000 | tf_op jit(solution)/shard_map/decode/pallas_call | solution.py:428
  206.5 0.8 broadcast_in_dim.3
  207.3 8.5 %all_to_all.16.sums = bf16[8,8,16,128]{3,2,1,0:T(8,128)(2,1)S(1)} all-to-all(bf16[8,8,16,128]{3,2,1,0:T(8,128)(2,1)S(1)} %broadcast_in_dim.3), channel_id=1, replica_groups=mesh['seq'=16,'head'=8] {'head'}, dimensions={0} | all-to-all | bytes 524288 | tf_op jit(solution)/shard_map/all_to_all | solution.py:623
  215.9 1.6 copy-done.2
  217.5 5.2 %finish.1 = bf16[8192,128]{1,0:T(8,128)(2,1)} custom-call(bf16[8,8,16,128]{3,2,1,0:T(8,128)(2,1)S(1)} %all_to_all.16.sums, bf16[8192,128]{1,0:T(8,128)(2,1)S(1)} %copy-done.2, bf16[8192,128]{1,0:T(8,128)(2,1)S(1)} %copy-done.1, f32[1,128]{1,0:T(1,128)S(1)} %bitcast.48), custom_call_target="tpu_custom_call" | custom-call | flops 540000000 | bytes 8000000 | tf_op jit(solution)/shard_map/finish/pallas_call | solution.py:492
  (79 shorter events, 6.2 us)
Async XLA Ops:
  0.0 3.3 %copy-start = (bf16[512,1024]{1,0:T(8,128)(2,1)S(1)}, bf16[512,1024]{1,0:T(8,128)(2,1)}, u32[]{:S(2)}) copy-start(bf16[512,1024]{1,0:T(8,128)(2,1)} %param.20) | copy-start | bytes 3145732
  0.0 12.7 %copy-start.12 = (bf16[1024,3,128]{2,0,1:T(8,128)(2,1)S(1)}, bf16[1024,3,128]{2,0,1:T(8,128)(2,1)}, u32[]{:S(2)}) copy-start(bf16[1024,3,128]{2,0,1:T(8,128)(2,1)} %param.16) | copy-start | bytes 2359300
  0.0 13.6 %copy-start.17 = (s32[16,8]{0,1:T(8,128)S(1)}, s32[16,8]{0,1:T(8,128)}, u32[]{:S(2)}) copy-start(s32[16,8]{0,1:T(8,128)} %param.13) | copy-start | bytes 1540
  4.1 9.6 %collective-permute-start.2 = (bf16[144,1024]{1,0:T(8,128)(2,1)S(1)}, bf16[144,1024]{1,0:T(8,128)(2,1)}, u32[]{:S(2)}, u32[]{:S(2)}) collective-permute-start(bf16[144,1024]{1,0:T(8,128)(2,1)S(1)} %pad_maximum_fusion.4), channel_id=1, source_target_pairs={{0,1},{1,0},{2,3},{3,2},{4,5},{5,4},{6,7},{7,6},{8,9},{9,8},{10,11... | collective-permute-start | bytes 884744 | tf_op jit(solution)/shard_map/ppermute | solution.py:518
  5.4 10.4 %collective-permute-start.3 = (bf16[144,1024]{1,0:T(8,128)(2,1)S(1)}, bf16[144,1024]{1,0:T(8,128)(2,1)}, u32[]{:S(2)}, u32[]{:S(2)}) collective-permute-start(bf16[144,1024]{1,0:T(8,128)(2,1)S(1)} %pad_maximum_fusion.4), channel_id=1, source_target_pairs={{0,2},{1,3},{2,4},{3,5},{4,6},{5,7},{6,0},{7,1},{8,10},{9,11},{10,... | collective-permute-start | bytes 884744 | tf_op jit(solution)/shard_map/ppermute | solution.py:518
  6.7 12.7 %collective-permute-start = (bf16[2048,128]{1,0:T(8,128)(2,1)}, bf16[2048,128]{1,0:T(8,128)(2,1)S(1)}, u32[]{:S(2)}, u32[]{:S(2)}) collective-permute-start(bf16[2048,128]{1,0:T(8,128)(2,1)} %get-tuple-element.33), channel_id=1, source_target_pairs={{0,8},{8,16},{16,24},{24,32},{32,40},{40,48},{48,56},{56,64},{64,7... | collective-permute-start | bytes 1572872 | tf_op jit(solution)/shard_map/ppermute | solution.py:514
  10.8 14.3 %collective-permute-start.1 = (bf16[2048,128]{1,0:T(8,128)(2,1)}, bf16[2048,128]{1,0:T(8,128)(2,1)S(1)}, u32[]{:S(2)}, u32[]{:S(2)}) collective-permute-start(bf16[2048,128]{1,0:T(8,128)(2,1)} %get-tuple-element.34), channel_id=1, source_target_pairs={{8,0},{16,8},{24,16},{32,24},{40,32},{48,40},{56,48},{64,56},{72,6... | collective-permute-start | bytes 1572872 | tf_op jit(solution)/shard_map/ppermute | solution.py:514
  13.7 11.4 %collective-permute-start.6 = (bf16[144,1024]{1,0:T(8,128)(2,1)}, bf16[144,1024]{1,0:T(8,128)(2,1)S(1)}, u32[]{:S(2)}, u32[]{:S(2)}) collective-permute-start(bf16[144,1024]{1,0:T(8,128)(2,1)} %collective-permute-done.2), channel_id=1, source_target_pairs={{0,6},{1,7},{2,0},{3,1},{4,2},{5,3},{6,4},{7,5},{8,14},{9,15},{10,... | collective-permute-start | bytes 884744 | tf_op jit(solution)/shard_map/ppermute | solution.py:518
  15.1 18.6 %collective-permute-start.4 = (bf16[144,1024]{1,0:T(8,128)(2,1)}, bf16[144,1024]{1,0:T(8,128)(2,1)S(1)}, u32[]{:S(2)}, u32[]{:S(2)}) collective-permute-start(bf16[144,1024]{1,0:T(8,128)(2,1)} %collective-permute-done.2), channel_id=1, source_target_pairs={{0,2},{1,3},{2,4},{3,5},{4,6},{5,7},{6,0},{7,1},{8,10},{9,11},{10,... | collective-permute-start | bytes 884744 | tf_op jit(solution)/shard_map/ppermute | solution.py:518
  15.8 19.0 %collective-permute-start.5 = (bf16[144,1024]{1,0:T(8,128)(2,1)S(1)}, bf16[144,1024]{1,0:T(8,128)(2,1)S(1)}, u32[]{:S(2)}, u32[]{:S(2)}) collective-permute-start(bf16[144,1024]{1,0:T(8,128)(2,1)S(1)} %pad_maximum_fusion.4), channel_id=1, source_target_pairs={{0,6},{1,7},{2,0},{3,1},{4,2},{5,3},{6,4},{7,5},{8,14},{9,15},{10,... | collective-permute-start | bytes 884744 | tf_op jit(solution)/shard_map/ppermute | solution.py:518
  19.4 7.1 %copy-start.13 = (bf16[2048,128]{1,0:T(8,128)(2,1)}, bf16[2048,128]{1,0:T(8,128)(2,1)S(1)}, u32[]{:S(2)}) copy-start(bf16[2048,128]{1,0:T(8,128)(2,1)S(1)} %collective-permute-done) | copy-start | bytes 1572868
  19.4 15.4 %collective-permute-start.7 = (bf16[144,1024]{1,0:T(8,128)(2,1)}, bf16[144,1024]{1,0:T(8,128)(2,1)S(1)}, u32[]{:S(2)}, u32[]{:S(2)}) collective-permute-start(bf16[144,1024]{1,0:T(8,128)(2,1)} %collective-permute-done.3), channel_id=1, source_target_pairs={{0,2},{1,3},{2,4},{3,5},{4,6},{5,7},{6,0},{7,1},{8,10},{9,11},{10,... | collective-permute-start | bytes 884744 | tf_op jit(solution)/shard_map/ppermute | solution.py:518
  25.1 1.4 copy-start.14
  25.1 9.7 %collective-permute-start.8 = (bf16[144,1024]{1,0:T(8,128)(2,1)S(1)}, bf16[144,1024]{1,0:T(8,128)(2,1)S(1)}, u32[]{:S(2)}, u32[]{:S(2)}) collective-permute-start(bf16[144,1024]{1,0:T(8,128)(2,1)S(1)} %collective-permute-done.6), channel_id=1, source_target_pairs={{0,6},{1,7},{2,0},{3,1},{4,2},{5,3},{6,4},{7,5},{8,14},{9,15},{10,... | collective-permute-start | bytes 884744 | tf_op jit(solution)/shard_map/ppermute | solution.py:518
  34.9 1.0 copy-start.6
  36.0 105.9 %copy-start.4 = (bf16[4,2,144,1024]{3,2,1,0:T(8,128)(2,1)}, bf16[4,2,144,1024]{3,2,1,0:T(8,128)(2,1)S(1)}, u32[]{:S(2)}) copy-start(bf16[4,2,144,1024]{3,2,1,0:T(8,128)(2,1)S(1)} %pad_maximum_fusion.refs_0_) | copy-start | bytes 7077892
  36.0 12.0 %collective-permute-start.10 = (bf16[2048,128]{1,0:T(8,128)(2,1)S(1)}, bf16[2048,128]{1,0:T(8,128)(2,1)S(1)}, u32[]{:S(2)}, u32[]{:S(2)}) collective-permute-start(bf16[2048,128]{1,0:T(8,128)(2,1)S(1)} %copy-done.6), channel_id=1, source_target_pairs={{0,2},{1,3},{2,4},{3,5},{4,6},{5,7},{6,0},{7,1},{8,10},{9,11},{10,... | collective-permute-start | bytes 1572872 | tf_op jit(solution)/shard_map/ppermute | solution.py:518
  36.7 11.5 %collective-permute-start.11 = (bf16[2048,128]{1,0:T(8,128)(2,1)S(1)}, bf16[2048,128]{1,0:T(8,128)(2,1)S(1)}, u32[]{:S(2)}, u32[]{:S(2)}) collective-permute-start(bf16[2048,128]{1,0:T(8,128)(2,1)S(1)} %copy-done.6), channel_id=1, source_target_pairs={{0,6},{1,7},{2,0},{3,1},{4,2},{5,3},{6,4},{7,5},{8,14},{9,15},{10,... | collective-permute-start | bytes 1572872 | tf_op jit(solution)/shard_map/ppermute | solution.py:518
  38.7 10.2 %collective-permute-start.9 = (bf16[2048,128]{1,0:T(8,128)(2,1)S(1)}, bf16[2048,128]{1,0:T(8,128)(2,1)S(1)}, u32[]{:S(2)}, u32[]{:S(2)}) collective-permute-start(bf16[2048,128]{1,0:T(8,128)(2,1)S(1)} %copy-done.6), channel_id=1, source_target_pairs={{0,1},{1,0},{2,3},{3,2},{4,5},{5,4},{6,7},{7,6},{8,9},{9,8},{10,11... | collective-permute-start | bytes 1572872 | tf_op jit(solution)/shard_map/ppermute | solution.py:518
  38.7 49.4 %collective-permute-start.15 = (bf16[4,2,144,1024]{3,2,1,0:T(8,128)(2,1)S(1)}, bf16[4,2,144,1024]{3,2,1,0:T(8,128)(2,1)}, u32[]{:S(2)}, u32[]{:S(2)}) collective-permute-start(bf16[4,2,144,1024]{3,2,1,0:T(8,128)(2,1)S(1)} %pad_maximum_fusion.refs_0_), channel_id=1, source_target_pairs={{0,16},{8,24},{16,32},{24,40},{32,48},{40,56},{48,0},{56,8},{64,80... | collective-permute-start | bytes 7077896 | tf_op jit(solution)/shard_map/ppermute | solution.py:518
  38.7 49.4 %collective-permute-start.16 = (bf16[4,2,144,1024]{3,2,1,0:T(8,128)(2,1)S(1)}, bf16[4,2,144,1024]{3,2,1,0:T(8,128)(2,1)}, u32[]{:S(2)}, u32[]{:S(2)}) collective-permute-start(bf16[4,2,144,1024]{3,2,1,0:T(8,128)(2,1)S(1)} %pad_maximum_fusion.refs_0_), channel_id=1, source_target_pairs={{0,48},{8,56},{16,0},{24,8},{32,16},{40,24},{48,32},{56,40},{64,11... | collective-permute-start | bytes 7077896 | tf_op jit(solution)/shard_map/ppermute | solution.py:518
  48.0 0.9 copy-start.10
  48.2 0.9 copy-start.11
  48.9 18.5 %copy-start.7 = (bf16[2048,128]{1,0:T(8,128)(2,1)}, bf16[2048,128]{1,0:T(8,128)(2,1)S(1)}, u32[]{:S(2)}) copy-start(bf16[2048,128]{1,0:T(8,128)(2,1)S(1)} %collective-permute-done.9.s1) | copy-start | bytes 1572868
  49.2 16.4 %collective-permute-start.12 = (bf16[3072,128]{1,0:T(8,128)(2,1)S(1)}, bf16[3072,128]{1,0:T(8,128)(2,1)S(1)}, u32[]{:S(2)}, u32[]{:S(2)}) collective-permute-start(bf16[3072,128]{1,0:T(8,128)(2,1)S(1)} %get-tuple-element.73), channel_id=1, source_target_pairs={{0,2},{1,3},{2,4},{3,5},{4,6},{5,7},{6,0},{7,1},{8,10},{9,11},{10,... | collective-permute-start | bytes 2359304 | tf_op jit(solution)/shard_map/ppermute | solution.py:518
  50.2 16.3 %collective-permute-start.13 = (bf16[3072,128]{1,0:T(8,128)(2,1)S(1)}, bf16[3072,128]{1,0:T(8,128)(2,1)S(1)}, u32[]{:S(2)}, u32[]{:S(2)}) collective-permute-start(bf16[3072,128]{1,0:T(8,128)(2,1)S(1)} %get-tuple-element.72), channel_id=1, source_target_pairs={{0,6},{1,7},{2,0},{3,1},{4,2},{5,3},{6,4},{7,5},{8,14},{9,15},{10,... | collective-permute-start | bytes 2359304 | tf_op jit(solution)/shard_map/ppermute | solution.py:518
  51.9 90.0 %collective-permute-start.19 = (bf16[4,2,144,1024]{3,2,1,0:T(8,128)(2,1)S(1)}, bf16[4,2,144,1024]{3,2,1,0:T(8,128)(2,1)}, u32[]{:S(2)}, u32[]{:S(2)}) collective-permute-start(bf16[4,2,144,1024]{3,2,1,0:T(8,128)(2,1)S(1)} %pad_maximum_fusion.refs_0_), channel_id=1, source_target_pairs={{0,65},{1,64},{2,67},{3,66},{4,69},{5,68},{6,71},{7,70},{8,73},{9,... | collective-permute-start | bytes 7077896 | tf_op jit(solution)/shard_map/ppermute | solution.py:518
  65.5 0.9 copy-start.8
  66.5 0.9 copy-start.9
  68.2 8.9 %collective-permute-start.14 = (bf16[2048,128]{1,0:T(8,128)(2,1)}, bf16[2048,128]{1,0:T(8,128)(2,1)}, u32[]{:S(2)}, u32[]{:S(2)}) collective-permute-start(bf16[2048,128]{1,0:T(8,128)(2,1)} %pad_maximum_fusion.3.s6), channel_id=1, source_target_pairs={{0,1},{1,0},{2,3},{3,2},{4,5},{5,4},{6,7},{7,6},{8,9},{9,8},{10,11... | collective-permute-start | bytes 1572872 | tf_op jit(solution)/shard_map/ppermute | solution.py:518
  88.1 17.2 %collective-permute-start.17 = (bf16[1152,256]{1,0:T(8,128)(2,1)}, bf16[1152,256]{1,0:T(8,128)(2,1)}, u32[]{:S(2)}, u32[]{:S(2)}) collective-permute-start(bf16[1152,256]{1,0:T(8,128)(2,1)} %get-tuple-element.48), channel_id=1, source_target_pairs={{0,8},{8,16},{16,24},{24,32},{32,40},{40,48},{48,56},{56,64},{64,7... | collective-permute-start | bytes 1769480 | tf_op jit(solution)/shard_map/ppermute | solution.py:514
  98.1 15.2 %collective-permute-start.18 = (bf16[1152,256]{1,0:T(8,128)(2,1)}, bf16[1152,256]{1,0:T(8,128)(2,1)}, u32[]{:S(2)}, u32[]{:S(2)}) collective-permute-start(bf16[1152,256]{1,0:T(8,128)(2,1)} %get-tuple-element.49), channel_id=1, source_target_pairs={{8,0},{16,8},{24,16},{32,24},{40,32},{48,40},{56,48},{64,56},{72,6... | collective-permute-start | bytes 1769480 | tf_op jit(solution)/shard_map/ppermute | solution.py:514
  141.9 15.5 %collective-permute-start.20 = (bf16[4,2,144,1024]{3,2,1,0:T(8,128)(2,1)S(1)}, bf16[4,2,144,1024]{3,2,1,0:T(8,128)(2,1)}, u32[]{:S(2)}, u32[]{:S(2)}) collective-permute-start(bf16[4,2,144,1024]{3,2,1,0:T(8,128)(2,1)S(1)} %pad_maximum_fusion.refs_0_), channel_id=1, source_target_pairs={{0,8},{8,0},{16,24},{24,16},{32,40},{40,32},{48,56},{56,48},{64,72... | collective-permute-start | bytes 7077896 | tf_op jit(solution)/shard_map/ppermute | solution.py:518
  142.0 15.4 %collective-permute-start.21 = (bf16[4,2,144,1024]{3,2,1,0:T(8,128)(2,1)}, bf16[4,2,144,1024]{3,2,1,0:T(8,128)(2,1)}, u32[]{:S(2)}, u32[]{:S(2)}) collective-permute-start(bf16[4,2,144,1024]{3,2,1,0:T(8,128)(2,1)} %collective-permute-done.15.refs_1_), channel_id=1, source_target_pairs={{0,8},{8,0},{16,24},{24,16},{32,40},{40,32},{48,56},{56,48},{64,72... | collective-permute-start | bytes 7077896 | tf_op jit(solution)/shard_map/ppermute | solution.py:518
  142.5 14.9 %collective-permute-start.22 = (bf16[4,2,144,1024]{3,2,1,0:T(8,128)(2,1)}, bf16[4,2,144,1024]{3,2,1,0:T(8,128)(2,1)}, u32[]{:S(2)}, u32[]{:S(2)}) collective-permute-start(bf16[4,2,144,1024]{3,2,1,0:T(8,128)(2,1)} %collective-permute-done.16.refs_2_), channel_id=1, source_target_pairs={{0,8},{8,0},{16,24},{24,16},{32,40},{40,32},{48,56},{56,48},{64,72... | collective-permute-start | bytes 7077896 | tf_op jit(solution)/shard_map/ppermute | solution.py:518
  142.6 14.8 %collective-permute-start.23 = (bf16[4,2,144,1024]{3,2,1,0:T(8,128)(2,1)}, bf16[4,2,144,1024]{3,2,1,0:T(8,128)(2,1)}, u32[]{:S(2)}, u32[]{:S(2)}) collective-permute-start(bf16[4,2,144,1024]{3,2,1,0:T(8,128)(2,1)} %collective-permute-done.19.refs_3_), channel_id=1, source_target_pairs={{0,8},{8,0},{16,24},{24,16},{32,40},{40,32},{48,56},{56,48},{64,72... | collective-permute-start | bytes 7077896 | tf_op jit(solution)/shard_map/ppermute | solution.py:518
  143.0 14.4 %all-to-all-start = ((bf16[8,256,128]{2,1,0:T(8,128)(2,1)}), bf16[8,256,128]{2,1,0:T(8,128)(2,1)}, u32[]{:S(2)}, u32[]{:S(2)}) async-start(bf16[8,256,128]{2,1,0:T(8,128)(2,1)} %bitcast.50), calls=%async_computation | async-start | bytes 1048576 | tf_op jit(solution)/shard_map/all_to_all | solution.py:605
  157.4 31.4 %copy-start.18 = (s32[64,2]{0,1:T(2,128)S(1)}, s32[64,2]{0,1:T(2,128)}, u32[]{:S(2)}) copy-start(s32[64,2]{0,1:T(2,128)} %param.21) | copy-start | bytes 1540
  182.9 14.9 %copy-start.5 = (bf16[8,256,128]{2,1,0:T(8,128)(2,1)}, bf16[8,256,128]{2,1,0:T(8,128)(2,1)S(1)}, u32[]{:S(2)}) copy-start(bf16[8,256,128]{2,1,0:T(8,128)(2,1)S(1)} %all_to_all.15) | copy-start | bytes 1572868
  182.9 6.9 %collective-permute-start.24 = (bf16[8,128,128]{2,1,0:T(8,128)(2,1)S(1)}, bf16[8,128,128]{2,1,0:T(8,128)(2,1)S(1)}, u32[]{:S(2)}, u32[]{:S(2)}) collective-permute-start(bf16[8,128,128]{2,1,0:T(8,128)(2,1)S(1)} %bitcast.63), channel_id=1, source_target_pairs={{0,8},{8,16},{16,24},{24,32},{32,40},{40,48},{48,56},{56,64},{64,7... | collective-permute-start | bytes 786440 | tf_op jit(solution)/shard_map/ppermute | solution.py:514
  186.5 11.3 %collective-permute-start.25 = (bf16[8,128,128]{2,1,0:T(8,128)(2,1)S(1)}, bf16[8,128,128]{2,1,0:T(8,128)(2,1)S(1)}, u32[]{:S(2)}, u32[]{:S(2)}) collective-permute-start(bf16[8,128,128]{2,1,0:T(8,128)(2,1)S(1)} %bitcast.62), channel_id=1, source_target_pairs={{8,0},{16,8},{24,16},{32,24},{40,32},{48,40},{56,48},{64,56},{72,6... | collective-permute-start | bytes 786440 | tf_op jit(solution)/shard_map/ppermute | solution.py:514
  189.8 8.0 %copy-start.15 = (bf16[8,128,128]{2,1,0:T(8,128)(2,1)}, bf16[8,128,128]{2,1,0:T(8,128)(2,1)S(1)}, u32[]{:S(2)}) copy-start(bf16[8,128,128]{2,1,0:T(8,128)(2,1)S(1)} %collective-permute-done.24.low) | copy-start | bytes 786436
  197.8 0.7 copy-start.16
  198.5 17.4 %copy-start.1 = (bf16[8192,128]{1,0:T(8,128)(2,1)S(1)}, bf16[8192,128]{1,0:T(8,128)(2,1)}, u32[]{:S(2)}) copy-start(bf16[8192,128]{1,0:T(8,128)(2,1)} %state.1) | copy-start | bytes 6291460
  198.5 17.4 %copy-start.3 = (f32[128]{0:T(128)S(1)}, f32[128]{0:T(128)}, u32[]{:S(2)}) copy-start(f32[128]{0:T(128)} %param.23) | copy-start | bytes 1540
  215.9 1.6 copy-start.2

commit v7 on v6

--- a/solution.py
+++ b/solution.py
@@ -139,9 +139,9 @@
     normed = jnp.concatenate(
         [(x * spread * gain[order[p]]).astype(BF) for p, x in enumerate(pieces)], axis=1
     )
-    made = dot(normed, ordered[...]).astype(BF)
-    queries[...] = (made[:, :BLOCK].astype(F32) * (HEAD_DIM**-0.5)).astype(BF)
-    keys_values[...] = made[:, BLOCK:]
+    made = dot(normed, ordered[...])
+    queries[...] = (made[:, :BLOCK] * (HEAD_DIM**-0.5 * LOG2E)).astype(BF)
+    keys_values[...] = made[:, BLOCK:].astype(BF)
 
 
 def project(order, slots, gain, weights):
@@ -176,94 +176,194 @@
 
 
 TILE = 256
-SPAN = TILE + 2 * REACH
-CHUNKS = SPAN // TILE
-
-
-def attend_kernel(edges, queries, low, own, high, out, keys, values, scores, sems):
+CHUNKS = 11
+MIDDLE = CHUNKS // 2
+
+
+def columns_of(part, keys, values, start, count, sems, first):
+    length = part.shape[0] // count
+    copies = []
+    for n in range(count):
+        rows = pl.ds(n * length, length)
+        for m, target in enumerate((keys, values)):
+            copies.append(
+                pltpu.make_async_copy(
+                    part.at[rows, pl.ds(m * BLOCK, BLOCK)],
+                    target.at[pl.ds(start + n * length, length), pl.ds(0, BLOCK)],
+                    sems.at[first + 2 * n + m],
+                )
+            )
+    return copies
+
+
+def chunk(c):
+    return (BLOCK, BLOCK) if c == 0 else (0, BLOCK) if c == CHUNKS - 1 else (0, TILE)
+
+
+def stacked_heads(q):
+    lane = lax.broadcasted_iota(jnp.int32, q.shape, 1)
+    zero = jnp.zeros_like(q)
+    return jnp.concatenate(
+        [jnp.where(lane < HEAD_DIM, q, zero), jnp.where(lane < HEAD_DIM, zero, q)], axis=0
+    )
+
+
+def score_chunk(c, stacked, keys, start, scores, highest):
+    skip, width = chunk(c)
+    part = keys[pl.ds(pl.multiple_of(start, BLOCK), width)]
+    s = lax.dot_general(stacked, part, NT, preferred_element_type=F32)
+    if c <= 1 or c >= CHUNKS - 2:
+        row = lax.broadcasted_iota(jnp.int32, s.shape, 0) & (TILE - 1)
+        gap = lax.broadcasted_iota(jnp.int32, s.shape, 1) - row + (c - MIDDLE) * TILE + skip
+        s = jnp.where(gap >= -WINDOW if c <= 1 else gap <= WINDOW, s, -1e30)
+    scores[:, c * TILE : c * TILE + width] = s
+    best = s[:, :BLOCK]
+    if width == TILE:
+        best = jnp.maximum(best, s[:, BLOCK:])
+    highest[...] = jnp.maximum(highest[...], best)
+
+
+def value_chunk(c, peak, values, start, scores, total):
+    _, width = chunk(c)
+    part = values[pl.ds(pl.multiple_of(start, BLOCK), width)]
+    powers = jnp.exp2(scores[:, c * TILE : c * TILE + width] - peak)
+    total[...] += dot(powers.astype(BF), part)
+
+
+def near_kernel(queries, own, out, keys, values, scores, highest, total, sems):
     step = pl.program_id(0)
-    rows = own.shape[0]
+    blocks = pl.num_programs(0)
 
     @pl.when(step == 0)
     def _():
-        copies = []
-        for n, (part, start) in enumerate(
-            ((low, 0), (own, REACH), (high, REACH + rows))
-        ):
-            for m, target in enumerate((keys, values)):
-                copies.append(
-                    pltpu.make_async_copy(
-                        part.at[:, pl.ds(m * BLOCK, BLOCK)],
-                        target.at[pl.ds(start, part.shape[0]), pl.ds(0, BLOCK)],
-                        sems.at[2 * n + m],
-                    )
-                )
+        copies = columns_of(own, keys, values, 0, 4, sems, 0)
         for c in copies:
             c.start()
         values[:, BLOCK:] = jnp.ones((values.shape[0], BLOCK), BF)
-        first = lax.broadcasted_iota(jnp.int32, (keys.shape[0], BLOCK), 1) == 0
-        row = lax.broadcasted_iota(jnp.int32, (keys.shape[0], BLOCK), 0)
-        absent = ((row < REACH) & (edges[0] == 1)) | (
-            (row >= REACH + rows) & (edges[1] == 1)
-        )
-        keys[:, BLOCK:] = jnp.where(first & absent, -1e30, 0.0).astype(BF)
         for c in copies:
             c.wait()
 
+    stacked = stacked_heads(queries[...])
+    highest[...] = jnp.full(highest.shape, -1e30, F32)
+    total[...] = jnp.zeros(total.shape, F32)
+    for c in range(CHUNKS):
+        block = step + c - MIDDLE
+
+        @pl.when((block >= 0) & (block < blocks))
+        def _():
+            score_chunk(c, stacked, keys, block * TILE + chunk(c)[0], scores, highest)
+
+    peak = jnp.max(highest[...], axis=1, keepdims=True)
+    for c in range(CHUNKS):
+        block = step + c - MIDDLE
+
+        @pl.when((block >= 0) & (block < blocks))
+        def _():
+            value_chunk(c, peak, values, block * TILE + chunk(c)[0], scores, total)
+
+    lane = lax.broadcasted_iota(jnp.int32, (2 * TILE, BLOCK), 1)
+    made = total[...]
+    out[:, :BLOCK] = made[:, :BLOCK]
+    out[:, BLOCK:] = jnp.where(lane < HEAD_DIM, made[:, BLOCK:], peak)
+
+
+def far_kernel(edges, queries, near, low, high, out, keys, values, scores, highest, total, sems):
+    step = pl.program_id(0)
+    blocks = pl.num_programs(0)
+
+    @pl.when(step == 0)
+    def _():
+        copies = columns_of(low, keys, values, 0, 3, sems, 0)
+        copies += columns_of(high, keys, values, REACH, 3, sems, 6)
+        for c in copies:
+            c.start()
+        values[:, BLOCK:] = jnp.ones((values.shape[0], BLOCK), BF)
+        for c in copies:
+            c.wait()
+
+    stacked = stacked_heads(queries[...])
+    before = near[:, BLOCK + HEAD_DIM : BLOCK + HEAD_DIM + 1]
+    highest[...] = jnp.broadcast_to(before, highest.shape)
+    places = {}
+    for c in range(CHUNKS):
+        if c == MIDDLE:
+            continue
+        block = step + c - MIDDLE
+        if c < MIDDLE:
+            there = (block < 0) & (edges[0] == 0)
+            start = block * TILE + REACH + chunk(c)[0]
+        else:
+            there = (block >= blocks) & (edges[1] == 0)
+            start = REACH + (block - blocks) * TILE
+        places[c] = there, start
+
+        @pl.when(there)
+        def _():
+            score_chunk(c, stacked, keys, start, scores, highest)
+
+    peak = jnp.max(highest[...], axis=1, keepdims=True)
+    scale = jnp.exp2(before - peak)
+    total[:, :BLOCK] = near[:, :BLOCK] * scale
+    total[:, BLOCK:] = jnp.broadcast_to(near[:, BLOCK : BLOCK + 1] * scale, (2 * TILE, BLOCK))
+    for c, (there, start) in places.items():
+
+        @pl.when(there)
+        def _():
+            value_chunk(c, peak, values, start, scores, total)
+
     lane = lax.broadcasted_iota(jnp.int32, (TILE, BLOCK), 1)
-    q = queries[...]
-    zero = jnp.zeros_like(q)
-    both = jnp.concatenate(
-        [jnp.where(lane < HEAD_DIM, q, zero), jnp.where(lane < HEAD_DIM, zero, q)], axis=0
-    )
-    mark = jnp.where(
-        lax.broadcasted_iota(jnp.int32, (2 * TILE, BLOCK), 1) == 0, 1.0, 0.0
-    ).astype(BF)
-    stacked = jnp.concatenate([both, mark], axis=1)
-    row = lax.broadcasted_iota(jnp.int32, (2 * TILE, TILE), 0) & (TILE - 1)
-    column = lax.broadcasted_iota(jnp.int32, (2 * TILE, TILE), 1)
-    highest = jnp.full((2 * TILE, BLOCK), -1e30, F32)
-    for c in range(CHUNKS):
-        part = keys[pl.ds(pl.multiple_of((step + c) * TILE, TILE), TILE)]
-        s = lax.dot_general(stacked, part, NT, preferred_element_type=F32)
-        least = c * TILE - REACH
-        gap = column - row + least
-        if least - TILE < -WINDOW:
-            s = jnp.where(gap >= -WINDOW, s, -1e30)
-        if least + TILE > WINDOW:
-            s = jnp.where(gap <= WINDOW, s, -1e30)
-        scores[:, c * TILE : (c + 1) * TILE] = s
-        highest = jnp.maximum(highest, jnp.maximum(s[:, :BLOCK], s[:, BLOCK:]))
-    peak = jnp.max(highest, axis=1, keepdims=True) * LOG2E
-    total = jnp.zeros((2 * TILE, 2 * BLOCK), F32)
-    for c in range(CHUNKS):
-        part = values[pl.ds(pl.multiple_of((step + c) * TILE, TILE), TILE)]
-        powers = jnp.exp2(scores[:, c * TILE : (c + 1) * TILE] * LOG2E - peak)
-        total = total + dot(powers.astype(BF), part)
     made = total[:, :BLOCK] / total[:, BLOCK:]
     out[...] = jnp.where(lane < HEAD_DIM, made[:TILE], made[TILE:]).astype(BF)
 
 
-def attend(edges, queries, low, own, high):
+def attention_scratch(rows, copies):
+    return [
+        pltpu.VMEM((rows, BLOCK), BF),
+        pltpu.VMEM((rows, 2 * BLOCK), BF),
+        pltpu.VMEM((2 * TILE, CHUNKS * TILE), F32),
+        pltpu.VMEM((2 * TILE, BLOCK), F32),
+        pltpu.VMEM((2 * TILE, 2 * BLOCK), F32),
+        pltpu.SemaphoreType.DMA((copies,)),
+    ]
+
+
+def attend_near(queries, own):
     rows = own.shape[0]
     return pl.pallas_call(
-        attend_kernel,
+        near_kernel,
+        out_shape=jax.ShapeDtypeStruct((2 * rows, 2 * BLOCK), F32),
+        grid_spec=pl.GridSpec(
+            grid=(rows // TILE,),
+            in_specs=[pl.BlockSpec((TILE, BLOCK), lambda i: (i, 0)), ANY],
+            out_specs=pl.BlockSpec((2 * TILE, 2 * BLOCK), lambda i: (i, 0)),
+            scratch_shapes=attention_scratch(rows, 8),
+        ),
+        compiler_params=params(40),
+        cost_estimate=cost(7_000_000_000, 6_000_000, 7_000_000),
+        name="attend_near",
+    )(queries, own)
+
+
+def attend_far(edges, queries, near, low, high):
+    rows = queries.shape[0]
+    return pl.pallas_call(
+        far_kernel,
         out_shape=jax.ShapeDtypeStruct((rows, BLOCK), BF),
         grid_spec=pltpu.PrefetchScalarGridSpec(
             num_scalar_prefetch=1,
             grid=(rows // TILE,),
-            in_specs=[pl.BlockSpec((TILE, BLOCK), lambda i, _: (i, 0)), ANY, ANY, ANY],
+            in_specs=[
+                pl.BlockSpec((TILE, BLOCK), lambda i, _: (i, 0)),
+                pl.BlockSpec((2 * TILE, 2 * BLOCK), lambda i, _: (i, 0)),
+                ANY,
+                ANY,
+            ],
             out_specs=pl.BlockSpec((TILE, BLOCK), lambda i, _: (i, 0)),
-            scratch_shapes=[
-                pltpu.VMEM((rows + 2 * REACH, 2 * BLOCK), BF),
-                pltpu.VMEM((rows + 2 * REACH, 2 * BLOCK), BF),
-                pltpu.VMEM((2 * TILE, SPAN), F32),
-                pltpu.SemaphoreType.DMA((6,)),
-            ],
-        ),
-        compiler_params=params(56),
-        name="attend",
-    )(edges, queries, low, own, high)
+            scratch_shapes=attention_scratch(2 * REACH, 12),
+        ),
+        compiler_params=params(40),
+        name="attend_far",
+    )(edges, queries, near, low, high)
 
 
 ROWS_E = 64
@@ -410,10 +510,14 @@
             kept[b * BLOCK : (b + 1) * BLOCK] = plain
             kinds.append((plain, (made * made).astype(BF)))
         done[step].start()
+        wide = dot(jnp.concatenate([k[n] for n in range(2) for k in kinds], axis=0), ones)
         held_sums = [
-            jnp.sum(jnp.where(row == column, dot(kinds[b][n], ones), 0.0), axis=0, keepdims=True)
-            for n in range(2)
-            for b in range(EACH)
+            jnp.sum(
+                jnp.where(row == column, wide[n * BLOCK : (n + 1) * BLOCK], 0.0),
+                axis=0,
+                keepdims=True,
+            )
+            for n in range(2 * EACH)
         ]
         sums[step] = jnp.concatenate(held_sums, axis=0).astype(BF)
     for c in done:
@@ -504,7 +608,7 @@
                 pltpu.SemaphoreType.DMA((count + 3 * steps,)),
             ],
         ),
-        compiler_params=params(24),
+        compiler_params=params(56),
         cost_estimate=cost(540_000_000, 8_000_000),
         name="finish",
     )(sums, back, state, gain.reshape(1, BLOCK))
@@ -593,13 +697,14 @@
         [me, partner] + [(v + by) % 8 for by in (6, 2, 4) for v in (me, partner)]
     ).astype(jnp.int32)
     queries, keys_values, share = project(order, slots, first_gain, inward)
-    upper, lower, up, down = lax.optimization_barrier(
-        (keys_values[mesh_rows - REACH :], keys_values[:REACH], up, down)
+    queries, upper, lower, up, down = lax.optimization_barrier(
+        (queries, keys_values[mesh_rows - REACH :], keys_values[:REACH], up, down)
     )
     below = shifted(upper, 1)
     above = shifted(lower, -1)
     edges = jnp.stack([band == 0, band == bands - 1]).astype(jnp.int32)
-    context = attend(edges, queries, below, keys_values, above)
+    near = attend_near(queries, keys_values)
+    context = attend_far(edges, queries, near, below, above)
     context, *here = lax.optimization_barrier((context, mine, up, down, across))
     parts = here + [TWIN(v) for v in here]
     context = lax.all_to_all(

time: 224 us -> 239 us (1.067)
  Pallas kernels: 70.3 us -> 94 us
  waiting for transfers between devices: 66.2 us -> 54.7 us
  starting transfers between devices: 44.5 us -> 49.3 us
  local copies, waits for them, and re-layouts: 14.6 us -> 12 us
    pallas_call x1 -> x2, Pallas kernels: 28.5 us -> 50.4 us  [the longest x1 29.9 us: attend_near(): pl.pallas_call(near_kernel, out_shape=jax.ShapeDtypeStruct((2 * rows, 2 *...]
    ppermute x6, waiting for transfers between devices: 26.3 us -> 14.3 us  [shifted(): lax.ppermute(value, 'seq', [(i, i + by) for i in range(16) if 0 <= i + by...]
    ppermute x6, starting transfers between devices: 24 us -> 28.6 us  [shifted(): lax.ppermute(value, 'seq', [(i, i + by) for i in range(16) if 0 <= i + by...]
    unnamed x40 -> x38, local copies, waits for them, and re-layouts: 5.12 us -> 3.52 us
  transfers between devices with their start and end apart: 27 -> 27, of which waited for: 11 -> 10; matrix products, arithmetic and copies ran while one was open for 4% -> 3% of each run, Pallas kernels for 20% -> 28%
where the time goes in v7:
time: 239 us; the launch traced here: 237 us
  Pallas kernels  94 us (39%)
  waiting for transfers between devices  54.7 us (23%)
  starting transfers between devices  49.3 us (21%)
  blocking collectives  21.9 us (9%)
  local copies, waits for them, and re-layouts  12 us (5%)
  other arithmetic  4.69 us (2%)
    ppermute x20, waiting for transfers between devices, among(): return lax.ppermute(value, axis, [(i, to(i)) for i in range(count)])  31.1 us
    pallas_call x1, Pallas kernels, attend_near(): pl.pallas_call(near_kernel, out_shape=jax.ShapeDtypeStruct((2 * rows, 2 *...  29.9 us
    ppermute x6, starting transfers between devices, shifted(): lax.ppermute(value, 'seq', [(i, i + by) for i in range(16) if 0 <= i + by...  28.6 us
    pallas_call x1, Pallas kernels, attend_far(): pl.pallas_call(far_kernel, out_shape=jax.ShapeDtypeStruct((rows, BLOCK),...  20.5 us
    ppermute x20, starting transfers between devices, among(): return lax.ppermute(value, axis, [(i, to(i)) for i in range(count)])  16.4 us
    ppermute x6, waiting for transfers between devices, shifted(): lax.ppermute(value, 'seq', [(i, i + by) for i in range(16) if 0 <= i + by...  14.3 us
    pallas_call x1, Pallas kernels, forward(): pl.pallas_call(forward_kernel, out_shape=jax.ShapeDtypeStruct((8, rows, B...  12.8 us
    all_to_all x1, blocking collectives, on_device(): mesh_end = lax.all_to_all(mesh_end, 'head', 0, 0, tiled=True)  12.7 us
  transfers between devices with their start and end apart: 27, of which 10 were waited for; matrix products, arithmetic and copies ran while one was open for 3% of the time, Pallas kernels for 28%

profile of v7, /device:TPU:97, one launch (start us, length us, event | category | flops | bytes accessed | tf_op | source)
XLA Modules:
  0.0 237.4 jit_solution(546155366837805305)
XLA Ops:
  0.0 2.4 fusion
  2.4 0.9 constant_dynamic-slice_fusion
  3.3 0.8 constant_dynamic-slice_fusion.1
  4.1 1.3 collective-permute-start.2
  5.4 1.3 collective-permute-start.3
  6.7 4.1 %collective-permute-start = (bf16[2048,128]{1,0:T(8,128)(2,1)}, bf16[2048,128]{1,0:T(8,128)(2,1)S(1)}, u32[]{:S(2)}, u32[]{:S(2)}) collective-permute-start(bf16[2048,128]{1,0:T(8,128)(2,1)} %get-tuple-element.34), channel_id=1, source_target_pairs={{0,8},{8,16},{16,24},{24,32},{32,40},{40,48},{48,56},{56,64},{64,7... | collective-permute-start | bytes 1572872 | tf_op jit(solution)/shard_map/ppermute | solution.py:618
  10.8 1.9 collective-permute-start.1
  12.7 0.9 fusion.2
  13.7 1.4 collective-permute-start.6
  15.8 2.6 %collective-permute-start.5 = (bf16[144,1024]{1,0:T(8,128)(2,1)S(1)}, bf16[144,1024]{1,0:T(8,128)(2,1)S(1)}, u32[]{:S(2)}, u32[]{:S(2)}) collective-permute-start(bf16[144,1024]{1,0:T(8,128)(2,1)S(1)} %pad_maximum_fusion.4), channel_id=1, source_target_pairs={{0,6},{1,7},{2,0},{3,1},{4,2},{5,3},{6,4},{7,5},{8,14},{9,15},{10,... | collective-permute-start | bytes 884744 | tf_op jit(solution)/shard_map/ppermute | solution.py:622
  18.4 1.0 maximum_bitcast_fusion
  19.5 5.6 %collective-permute-done.1 = bf16[2048,128]{1,0:T(8,128)(2,1)S(1)} collective-permute-done((bf16[2048,128]{1,0:T(8,128)(2,1)}, bf16[2048,128]{1,0:T(8,128)(2,1)S(1)}, u32[]{:S(2)}, u32[]{:S(2)}) %collective-permute-start.1) | collective-permute-done | bytes 524320 | tf_op jit(solution)/shard_map/ppermute | solution.py:618
  25.1 1.4 collective-permute-start.8
  26.5 7.2 %encode.1.s0 = bf16[2048,128]{1,0:T(8,128)(2,1)} custom-call(s32[16,8]{1,0:T(8,128)} %broadcast_subtract_fusion.1.index, bf16[16,128,128]{2,1,0:T(8,128)(2,1)} %bitcast.53, bf16[64,128,128]{2,1,0:T(8,128)(2,1)} %bitcast.47, bf16[16,128,128]{2,1,0:T(8,128)(2,1)} %bitcast.54, bf16[16,8,128,128]{3,2,1,0:T(8,128)(2,1)} %weights.2), custom_call_target="tpu_custom_call" | custom-call | flops 540000000 | bytes 8000000 | tf_op jit(solution)/shard_map/encode/pallas_call | solution.py:84
  33.7 1.0 maximum_bitcast_fusion.1
  35.2 0.7 copy-done.5
  36.0 0.7 collective-permute-start.10
  36.7 2.0 collective-permute-start.11
  38.7 1.5 collective-permute-start.16
  40.1 7.9 %collective-permute-done.10.s2 = bf16[2048,128]{1,0:T(8,128)(2,1)S(1)} collective-permute-done((bf16[2048,128]{1,0:T(8,128)(2,1)S(1)}, bf16[2048,128]{1,0:T(8,128)(2,1)S(1)}, u32[]{:S(2)}, u32[]{:S(2)}) %collective-permute-start.10) | collective-permute-done | bytes 524320 | tf_op jit(solution)/shard_map/ppermute | solution.py:622
  48.2 0.7 collective-permute-done.9.s1
  49.1 1.0 collective-permute-start.12
  50.2 1.7 collective-permute-start.13
  52.2 13.4 %collective-permute-done.12.s3 = bf16[3072,128]{1,0:T(8,128)(2,1)S(1)} collective-permute-done((bf16[3072,128]{1,0:T(8,128)(2,1)S(1)}, bf16[3072,128]{1,0:T(8,128)(2,1)S(1)}, u32[]{:S(2)}, u32[]{:S(2)}) %collective-permute-start.12) | collective-permute-done | bytes 786464 | tf_op jit(solution)/shard_map/ppermute | solution.py:622
  65.5 0.9 copy-done.7
  66.5 0.9 copy-done.8
  67.4 0.8 pad_maximum_fusion.3.s6
  68.9 8.2 %collective-permute-done.14.s7 = bf16[2048,128]{1,0:T(8,128)(2,1)} collective-permute-done((bf16[2048,128]{1,0:T(8,128)(2,1)}, bf16[2048,128]{1,0:T(8,128)(2,1)}, u32[]{:S(2)}, u32[]{:S(2)}) %collective-permute-start.14) | collective-permute-done | bytes 524320 | tf_op jit(solution)/shard_map/ppermute | solution.py:622
  77.1 8.6 %project.1 = (bf16[2048,128]{1,0:T(8,128)(2,1)}, bf16[2048,256]{1,0:T(8,128)(2,1)}, bf16[8,256,128]{2,1,0:T(8,128)(2,1)}) custom-call(s32[8]{0:T(128)} %stack.130.order, bf16[2048,128]{1,0:T(8,128)(2,1)} %encode.1.s0, bf16[2048,128]{1,0:T(8,128)(2,1)} %copy-done.6, bf16[2048,128]{1,0:T(8,128)(2,1)} %copy-done.9, bf16[3072,128]{1,0:T(8,128)(2,1)} %copy-done.7, ...), custom_call_target="tpu_custom_call" | custom-call | tf_op jit(solution)/shard_map/project/pallas_call | solution.py:153
  85.7 1.4 fusion.1
  87.2 0.8 collective-permute-done.16.refs_2_
  88.0 10.2 %collective-permute-start.17 = (bf16[1152,256]{1,0:T(8,128)(2,1)S(1)}, bf16[1152,256]{1,0:T(8,128)(2,1)S(1)}, u32[]{:S(2)}, u32[]{:S(2)}) collective-permute-start(bf16[1152,256]{1,0:T(8,128)(2,1)S(1)} %get-tuple-element.50), channel_id=1, source_target_pairs={{0,8},{8,16},{16,24},{24,32},{32,40},{40,48},{48,56},{56,64},{64,7... | collective-permute-start | bytes 1769480 | tf_op jit(solution)/shard_map/ppermute | solution.py:618
  98.2 2.1 collective-permute-start.18
  100.3 29.9 %attend_near.1.near = f32[4096,256]{1,0:T(8,128)S(1)} custom-call(bf16[2048,128]{1,0:T(8,128)(2,1)S(1)} %copy-done.2, bf16[2048,256]{1,0:T(8,128)(2,1)S(1)} %copy-done.1), custom_call_target="tpu_custom_call" | custom-call | flops 7000000000 | bytes 6000000 | tf_op jit(solution)/shard_map/attend_near/pallas_call | solution.py:332
  130.2 20.5 %attend_far.1 = bf16[2048,128]{1,0:T(8,128)(2,1)} custom-call(s32[2]{0:T(128)S(1)} %add_convert_fusion.edges, bf16[2048,128]{1,0:T(8,128)(2,1)S(1)} %copy-done.2, f32[4096,256]{1,0:T(8,128)S(1)} %attend_near.1.near, bf16[1152,256]{1,0:T(8,128)(2,1)S(1)} %collective-permute-done.17.low, bf16[1152,256]{1,0:T(8,128)(2,1)S(1)} %collective-permute-done.18.high), custom_call_target="tpu_custom_call" | custom-call | tf_op jit(solution)/shard_map/attend_far/pallas_call | solution.py:349
  151.8 4.4 %all-to-all-start = ((bf16[8,256,128]{2,1,0:T(8,128)(2,1)}), bf16[8,256,128]{2,1,0:T(8,128)(2,1)}, u32[]{:S(2)}, u32[]{:S(2)}) async-start(bf16[8,256,128]{2,1,0:T(8,128)(2,1)} %bitcast.37), calls=%async_computation | async-start | bytes 1048576 | tf_op jit(solution)/shard_map/all_to_all | solution.py:710
  156.9 9.3 %all-to-all-done.refs_8_ = bf16[8,256,128]{2,1,0:T(8,128)(2,1)} async-done(((bf16[8,256,128]{2,1,0:T(8,128)(2,1)}), bf16[8,256,128]{2,1,0:T(8,128)(2,1)}, u32[]{:S(2)}, u32[]{:S(2)}) %all-to-all-start) | async-done | bytes 524320 | tf_op jit(solution)/shard_map/all_to_all | solution.py:710
  166.2 12.8 %forward.1 = bf16[8,256,128]{2,1,0:T(8,128)(2,1)} custom-call(s32[16]{0:T(128)} %concatenate.19.table, bf16[4,2,144,1024]{3,2,1,0:T(8,128)(2,1)} %copy-done.3, bf16[4,2,144,1024]{3,2,1,0:T(8,128)(2,1)} %collective-permute-done.15.refs_1_, bf16[4,2,144,1024]{3,2,1,0:T(8,128)(2,1)} %collective-permute-done.16.refs_2_, ...), custom_call_target="tpu_custom_call" | custom-call | flops 4800000000 | bytes 20000000 | tf_op jit(solution)/shard_map/forward/pallas_call | solution.py:461
  179.0 12.7 %all_to_all.15 = bf16[8,256,128]{2,1,0:T(8,128)(2,1)S(1)} all-to-all(bf16[8,256,128]{2,1,0:T(8,128)(2,1)} %forward.1), channel_id=1, replica_groups=mesh['seq'=16,'head'=8] {'head'}, dimensions={0} | all-to-all | bytes 1048576 | tf_op jit(solution)/shard_map/all_to_all | solution.py:718
  191.7 8.4 %collective-permute-start.24 = (bf16[8,128,128]{2,1,0:T(8,128)(2,1)S(1)}, bf16[8,128,128]{2,1,0:T(8,128)(2,1)S(1)}, u32[]{:S(2)}, u32[]{:S(2)}) collective-permute-start(bf16[8,128,128]{2,1,0:T(8,128)(2,1)S(1)} %bitcast.61), channel_id=1, source_target_pairs={{0,8},{8,16},{16,24},{24,32},{32,40},{40,48},{48,56},{56,64},{64,7... | collective-permute-start | bytes 786440 | tf_op jit(solution)/shard_map/ppermute | solution.py:618
  200.2 1.9 collective-permute-start.25
  202.8 0.7 collective-permute-done.24.low
  203.4 8.0 %collective-permute-done.25.high = bf16[8,128,128]{2,1,0:T(8,128)(2,1)S(1)} collective-permute-done((bf16[8,128,128]{2,1,0:T(8,128)(2,1)S(1)}, bf16[8,128,128]{2,1,0:T(8,128)(2,1)S(1)}, u32[]{:S(2)}, u32[]{:S(2)}) %collective-permute-start.25) | collective-permute-done | bytes 262176 | tf_op jit(solution)/shard_map/ppermute | solution.py:618
  211.5 0.7 copy-done.15
  212.2 9.0 %decode.1 = (bf16[8192,128]{1,0:T(8,128)(2,1)}, bf16[8,16,128]{2,1,0:T(8,128)(2,1)}) custom-call(s32[64,2]{1,0:T(8,128)} %broadcast_subtract_fusion.index, bf16[8,128,128]{2,1,0:T(8,128)(2,1)} %copy-done.14, bf16[16,128,128]{2,1,0:T(8,128)(2,1)} %bitcast.48, bf16[8,128,128]{2,1,0:T(8,128)(2,1)} %copy-done.15, bf16[64,2,128,128]{3,2,1,0:T(8,128)(2,1)} %weights.3), custom_call_target="tpu_custom_call" | custom-call | flops 540000000 | bytes 10000000 | tf_op jit(solution)/shard_map/decode/pallas_call | solution.py:532
  221.1 0.8 broadcast_in_dim.3
  221.9 9.2 %all_to_all.16.sums = bf16[8,8,16,128]{3,2,1,0:T(8,128)(2,1)} all-to-all(bf16[8,8,16,128]{3,2,1,0:T(8,128)(2,1)S(1)} %broadcast_in_dim.3), channel_id=1, replica_groups=mesh['seq'=16,'head'=8] {'head'}, dimensions={0} | all-to-all | bytes 524288 | tf_op jit(solution)/shard_map/all_to_all | solution.py:728
  231.1 6.1 %finish.1 = bf16[8192,128]{1,0:T(8,128)(2,1)} custom-call(bf16[8,8,16,128]{3,2,1,0:T(8,128)(2,1)} %all_to_all.16.sums, bf16[8192,128]{1,0:T(8,128)(2,1)} %get-tuple-element.62.back, bf16[8192,128]{1,0:T(8,128)(2,1)} %state.1, f32[1,128]{1,0:T(1,128)} %bitcast.64), custom_call_target="tpu_custom_call" | custom-call | flops 540000000 | bytes 8000000 | tf_op jit(solution)/shard_map/finish/pallas_call | solution.py:596
  (78 shorter events, 5.3 us)
Async XLA Ops:
  0.0 3.3 %copy-start = (bf16[512,1024]{1,0:T(8,128)(2,1)S(1)}, bf16[512,1024]{1,0:T(8,128)(2,1)}, u32[]{:S(2)}) copy-start(bf16[512,1024]{1,0:T(8,128)(2,1)} %param.20) | copy-start | bytes 3145732
  0.0 12.7 %copy-start.11 = (bf16[1024,3,128]{2,0,1:T(8,128)(2,1)S(1)}, bf16[1024,3,128]{2,0,1:T(8,128)(2,1)}, u32[]{:S(2)}) copy-start(bf16[1024,3,128]{2,0,1:T(8,128)(2,1)} %param.16) | copy-start | bytes 2359300
  0.0 13.6 %copy-start.16 = (s32[16,8]{0,1:T(8,128)S(1)}, s32[16,8]{0,1:T(8,128)}, u32[]{:S(2)}) copy-start(s32[16,8]{0,1:T(8,128)} %param.13) | copy-start | bytes 1540
  4.1 9.6 %collective-permute-start.2 = (bf16[144,1024]{1,0:T(8,128)(2,1)S(1)}, bf16[144,1024]{1,0:T(8,128)(2,1)}, u32[]{:S(2)}, u32[]{:S(2)}) collective-permute-start(bf16[144,1024]{1,0:T(8,128)(2,1)S(1)} %pad_maximum_fusion.4), channel_id=1, source_target_pairs={{0,1},{1,0},{2,3},{3,2},{4,5},{5,4},{6,7},{7,6},{8,9},{9,8},{10,11... | collective-permute-start | bytes 884744 | tf_op jit(solution)/shard_map/ppermute | solution.py:622
  5.4 10.4 %collective-permute-start.3 = (bf16[144,1024]{1,0:T(8,128)(2,1)S(1)}, bf16[144,1024]{1,0:T(8,128)(2,1)}, u32[]{:S(2)}, u32[]{:S(2)}) collective-permute-start(bf16[144,1024]{1,0:T(8,128)(2,1)S(1)} %pad_maximum_fusion.4), channel_id=1, source_target_pairs={{0,2},{1,3},{2,4},{3,5},{4,6},{5,7},{6,0},{7,1},{8,10},{9,11},{10,... | collective-permute-start | bytes 884744 | tf_op jit(solution)/shard_map/ppermute | solution.py:622
  6.7 12.7 %collective-permute-start = (bf16[2048,128]{1,0:T(8,128)(2,1)}, bf16[2048,128]{1,0:T(8,128)(2,1)S(1)}, u32[]{:S(2)}, u32[]{:S(2)}) collective-permute-start(bf16[2048,128]{1,0:T(8,128)(2,1)} %get-tuple-element.34), channel_id=1, source_target_pairs={{0,8},{8,16},{16,24},{24,32},{32,40},{40,48},{48,56},{56,64},{64,7... | collective-permute-start | bytes 1572872 | tf_op jit(solution)/shard_map/ppermute | solution.py:618
  10.8 14.3 %collective-permute-start.1 = (bf16[2048,128]{1,0:T(8,128)(2,1)}, bf16[2048,128]{1,0:T(8,128)(2,1)S(1)}, u32[]{:S(2)}, u32[]{:S(2)}) collective-permute-start(bf16[2048,128]{1,0:T(8,128)(2,1)} %get-tuple-element.35), channel_id=1, source_target_pairs={{8,0},{16,8},{24,16},{32,24},{40,32},{48,40},{56,48},{64,56},{72,6... | collective-permute-start | bytes 1572872 | tf_op jit(solution)/shard_map/ppermute | solution.py:618
  13.7 11.4 %collective-permute-start.6 = (bf16[144,1024]{1,0:T(8,128)(2,1)}, bf16[144,1024]{1,0:T(8,128)(2,1)S(1)}, u32[]{:S(2)}, u32[]{:S(2)}) collective-permute-start(bf16[144,1024]{1,0:T(8,128)(2,1)} %collective-permute-done.2), channel_id=1, source_target_pairs={{0,6},{1,7},{2,0},{3,1},{4,2},{5,3},{6,4},{7,5},{8,14},{9,15},{10,... | collective-permute-start | bytes 884744 | tf_op jit(solution)/shard_map/ppermute | solution.py:622
  15.1 18.6 %collective-permute-start.4 = (bf16[144,1024]{1,0:T(8,128)(2,1)}, bf16[144,1024]{1,0:T(8,128)(2,1)S(1)}, u32[]{:S(2)}, u32[]{:S(2)}) collective-permute-start(bf16[144,1024]{1,0:T(8,128)(2,1)} %collective-permute-done.2), channel_id=1, source_target_pairs={{0,2},{1,3},{2,4},{3,5},{4,6},{5,7},{6,0},{7,1},{8,10},{9,11},{10,... | collective-permute-start | bytes 884744 | tf_op jit(solution)/shard_map/ppermute | solution.py:622
  15.8 19.0 %collective-permute-start.5 = (bf16[144,1024]{1,0:T(8,128)(2,1)S(1)}, bf16[144,1024]{1,0:T(8,128)(2,1)S(1)}, u32[]{:S(2)}, u32[]{:S(2)}) collective-permute-start(bf16[144,1024]{1,0:T(8,128)(2,1)S(1)} %pad_maximum_fusion.4), channel_id=1, source_target_pairs={{0,6},{1,7},{2,0},{3,1},{4,2},{5,3},{6,4},{7,5},{8,14},{9,15},{10,... | collective-permute-start | bytes 884744 | tf_op jit(solution)/shard_map/ppermute | solution.py:622
  19.4 7.1 %copy-start.12 = (bf16[2048,128]{1,0:T(8,128)(2,1)}, bf16[2048,128]{1,0:T(8,128)(2,1)S(1)}, u32[]{:S(2)}) copy-start(bf16[2048,128]{1,0:T(8,128)(2,1)S(1)} %collective-permute-done) | copy-start | bytes 1572868
  19.4 15.4 %collective-permute-start.7 = (bf16[144,1024]{1,0:T(8,128)(2,1)}, bf16[144,1024]{1,0:T(8,128)(2,1)S(1)}, u32[]{:S(2)}, u32[]{:S(2)}) collective-permute-start(bf16[144,1024]{1,0:T(8,128)(2,1)} %collective-permute-done.3), channel_id=1, source_target_pairs={{0,2},{1,3},{2,4},{3,5},{4,6},{5,7},{6,0},{7,1},{8,10},{9,11},{10,... | collective-permute-start | bytes 884744 | tf_op jit(solution)/shard_map/ppermute | solution.py:622
  25.1 1.4 copy-start.13
  25.1 9.7 %collective-permute-start.8 = (bf16[144,1024]{1,0:T(8,128)(2,1)S(1)}, bf16[144,1024]{1,0:T(8,128)(2,1)S(1)}, u32[]{:S(2)}, u32[]{:S(2)}) collective-permute-start(bf16[144,1024]{1,0:T(8,128)(2,1)S(1)} %collective-permute-done.6), channel_id=1, source_target_pairs={{0,6},{1,7},{2,0},{3,1},{4,2},{5,3},{6,4},{7,5},{8,14},{9,15},{10,... | collective-permute-start | bytes 884744 | tf_op jit(solution)/shard_map/ppermute | solution.py:622
  34.9 1.0 copy-start.5
  36.0 114.7 %copy-start.3 = (bf16[4,2,144,1024]{3,2,1,0:T(8,128)(2,1)}, bf16[4,2,144,1024]{3,2,1,0:T(8,128)(2,1)S(1)}, u32[]{:S(2)}) copy-start(bf16[4,2,144,1024]{3,2,1,0:T(8,128)(2,1)S(1)} %pad_maximum_fusion.refs_0_) | copy-start | bytes 7077892
  36.0 12.0 %collective-permute-start.10 = (bf16[2048,128]{1,0:T(8,128)(2,1)S(1)}, bf16[2048,128]{1,0:T(8,128)(2,1)S(1)}, u32[]{:S(2)}, u32[]{:S(2)}) collective-permute-start(bf16[2048,128]{1,0:T(8,128)(2,1)S(1)} %copy-done.5), channel_id=1, source_target_pairs={{0,2},{1,3},{2,4},{3,5},{4,6},{5,7},{6,0},{7,1},{8,10},{9,11},{10,... | collective-permute-start | bytes 1572872 | tf_op jit(solution)/shard_map/ppermute | solution.py:622
  36.7 11.5 %collective-permute-start.11 = (bf16[2048,128]{1,0:T(8,128)(2,1)S(1)}, bf16[2048,128]{1,0:T(8,128)(2,1)S(1)}, u32[]{:S(2)}, u32[]{:S(2)}) collective-permute-start(bf16[2048,128]{1,0:T(8,128)(2,1)S(1)} %copy-done.5), channel_id=1, source_target_pairs={{0,6},{1,7},{2,0},{3,1},{4,2},{5,3},{6,4},{7,5},{8,14},{9,15},{10,... | collective-permute-start | bytes 1572872 | tf_op jit(solution)/shard_map/ppermute | solution.py:622
  38.6 10.2 %collective-permute-start.9 = (bf16[2048,128]{1,0:T(8,128)(2,1)S(1)}, bf16[2048,128]{1,0:T(8,128)(2,1)S(1)}, u32[]{:S(2)}, u32[]{:S(2)}) collective-permute-start(bf16[2048,128]{1,0:T(8,128)(2,1)S(1)} %copy-done.5), channel_id=1, source_target_pairs={{0,1},{1,0},{2,3},{3,2},{4,5},{5,4},{6,7},{7,6},{8,9},{9,8},{10,11... | collective-permute-start | bytes 1572872 | tf_op jit(solution)/shard_map/ppermute | solution.py:622
  38.7 48.5 %collective-permute-start.15 = (bf16[4,2,144,1024]{3,2,1,0:T(8,128)(2,1)S(1)}, bf16[4,2,144,1024]{3,2,1,0:T(8,128)(2,1)}, u32[]{:S(2)}, u32[]{:S(2)}) collective-permute-start(bf16[4,2,144,1024]{3,2,1,0:T(8,128)(2,1)S(1)} %pad_maximum_fusion.refs_0_), channel_id=1, source_target_pairs={{0,16},{8,24},{16,32},{24,40},{32,48},{40,56},{48,0},{56,8},{64,80... | collective-permute-start | bytes 7077896 | tf_op jit(solution)/shard_map/ppermute | solution.py:622
  38.7 49.3 %collective-permute-start.16 = (bf16[4,2,144,1024]{3,2,1,0:T(8,128)(2,1)S(1)}, bf16[4,2,144,1024]{3,2,1,0:T(8,128)(2,1)}, u32[]{:S(2)}, u32[]{:S(2)}) collective-permute-start(bf16[4,2,144,1024]{3,2,1,0:T(8,128)(2,1)S(1)} %pad_maximum_fusion.refs_0_), channel_id=1, source_target_pairs={{0,48},{8,56},{16,0},{24,8},{32,16},{40,24},{48,32},{56,40},{64,11... | collective-permute-start | bytes 7077896 | tf_op jit(solution)/shard_map/ppermute | solution.py:622
  48.0 0.9 copy-start.9
  48.2 0.8 copy-start.10
  48.9 18.5 %copy-start.6 = (bf16[2048,128]{1,0:T(8,128)(2,1)}, bf16[2048,128]{1,0:T(8,128)(2,1)S(1)}, u32[]{:S(2)}) copy-start(bf16[2048,128]{1,0:T(8,128)(2,1)S(1)} %collective-permute-done.9.s1) | copy-start | bytes 1572868
  49.1 16.4 %collective-permute-start.12 = (bf16[3072,128]{1,0:T(8,128)(2,1)S(1)}, bf16[3072,128]{1,0:T(8,128)(2,1)S(1)}, u32[]{:S(2)}, u32[]{:S(2)}) collective-permute-start(bf16[3072,128]{1,0:T(8,128)(2,1)S(1)} %get-tuple-element.75), channel_id=1, source_target_pairs={{0,2},{1,3},{2,4},{3,5},{4,6},{5,7},{6,0},{7,1},{8,10},{9,11},{10,... | collective-permute-start | bytes 2359304 | tf_op jit(solution)/shard_map/ppermute | solution.py:622
  50.2 16.3 %collective-permute-start.13 = (bf16[3072,128]{1,0:T(8,128)(2,1)S(1)}, bf16[3072,128]{1,0:T(8,128)(2,1)S(1)}, u32[]{:S(2)}, u32[]{:S(2)}) collective-permute-start(bf16[3072,128]{1,0:T(8,128)(2,1)S(1)} %get-tuple-element.74), channel_id=1, source_target_pairs={{0,6},{1,7},{2,0},{3,1},{4,2},{5,3},{6,4},{7,5},{8,14},{9,15},{10,... | collective-permute-start | bytes 2359304 | tf_op jit(solution)/shard_map/ppermute | solution.py:622
  51.9 98.8 %collective-permute-start.19 = (bf16[4,2,144,1024]{3,2,1,0:T(8,128)(2,1)S(1)}, bf16[4,2,144,1024]{3,2,1,0:T(8,128)(2,1)}, u32[]{:S(2)}, u32[]{:S(2)}) collective-permute-start(bf16[4,2,144,1024]{3,2,1,0:T(8,128)(2,1)S(1)} %pad_maximum_fusion.refs_0_), channel_id=1, source_target_pairs={{0,65},{1,64},{2,67},{3,66},{4,69},{5,68},{6,71},{7,70},{8,73},{9,... | collective-permute-start | bytes 7077896 | tf_op jit(solution)/shard_map/ppermute | solution.py:622
  65.5 0.9 copy-start.7
  66.5 0.9 copy-start.8
  68.2 8.9 %collective-permute-start.14 = (bf16[2048,128]{1,0:T(8,128)(2,1)}, bf16[2048,128]{1,0:T(8,128)(2,1)}, u32[]{:S(2)}, u32[]{:S(2)}) collective-permute-start(bf16[2048,128]{1,0:T(8,128)(2,1)} %pad_maximum_fusion.3.s6), channel_id=1, source_target_pairs={{0,1},{1,0},{2,3},{3,2},{4,5},{5,4},{6,7},{7,6},{8,9},{9,8},{10,11... | collective-permute-start | bytes 1572872 | tf_op jit(solution)/shard_map/ppermute | solution.py:622
  85.7 14.5 %copy-start.1 = (bf16[2048,256]{1,0:T(8,128)(2,1)S(1)}, bf16[2048,256]{1,0:T(8,128)(2,1)}, u32[]{:S(2)}) copy-start(bf16[2048,256]{1,0:T(8,128)(2,1)} %get-tuple-element.48.own) | copy-start | bytes 3145732
  85.7 14.5 %copy-start.2 = (bf16[2048,128]{1,0:T(8,128)(2,1)S(1)}, bf16[2048,128]{1,0:T(8,128)(2,1)}, u32[]{:S(2)}) copy-start(bf16[2048,128]{1,0:T(8,128)(2,1)} %get-tuple-element.49.queries) | copy-start | bytes 1572868
  88.0 42.2 %collective-permute-start.17 = (bf16[1152,256]{1,0:T(8,128)(2,1)S(1)}, bf16[1152,256]{1,0:T(8,128)(2,1)S(1)}, u32[]{:S(2)}, u32[]{:S(2)}) collective-permute-start(bf16[1152,256]{1,0:T(8,128)(2,1)S(1)} %get-tuple-element.50), channel_id=1, source_target_pairs={{0,8},{8,16},{16,24},{24,32},{32,40},{40,48},{48,56},{56,64},{64,7... | collective-permute-start | bytes 1769480 | tf_op jit(solution)/shard_map/ppermute | solution.py:618
  98.2 32.0 %collective-permute-start.18 = (bf16[1152,256]{1,0:T(8,128)(2,1)S(1)}, bf16[1152,256]{1,0:T(8,128)(2,1)S(1)}, u32[]{:S(2)}, u32[]{:S(2)}) collective-permute-start(bf16[1152,256]{1,0:T(8,128)(2,1)S(1)} %get-tuple-element.51), channel_id=1, source_target_pairs={{8,0},{16,8},{24,16},{32,24},{40,32},{48,40},{56,48},{64,56},{72,6... | collective-permute-start | bytes 1769480 | tf_op jit(solution)/shard_map/ppermute | solution.py:618
  150.7 15.5 %collective-permute-start.20 = (bf16[4,2,144,1024]{3,2,1,0:T(8,128)(2,1)S(1)}, bf16[4,2,144,1024]{3,2,1,0:T(8,128)(2,1)}, u32[]{:S(2)}, u32[]{:S(2)}) collective-permute-start(bf16[4,2,144,1024]{3,2,1,0:T(8,128)(2,1)S(1)} %pad_maximum_fusion.refs_0_), channel_id=1, source_target_pairs={{0,8},{8,0},{16,24},{24,16},{32,40},{40,32},{48,56},{56,48},{64,72... | collective-permute-start | bytes 7077896 | tf_op jit(solution)/shard_map/ppermute | solution.py:622
  150.8 15.4 %collective-permute-start.21 = (bf16[4,2,144,1024]{3,2,1,0:T(8,128)(2,1)}, bf16[4,2,144,1024]{3,2,1,0:T(8,128)(2,1)}, u32[]{:S(2)}, u32[]{:S(2)}) collective-permute-start(bf16[4,2,144,1024]{3,2,1,0:T(8,128)(2,1)} %collective-permute-done.15.refs_1_), channel_id=1, source_target_pairs={{0,8},{8,0},{16,24},{24,16},{32,40},{40,32},{48,56},{56,48},{64,72... | collective-permute-start | bytes 7077896 | tf_op jit(solution)/shard_map/ppermute | solution.py:622
  151.3 14.9 %collective-permute-start.22 = (bf16[4,2,144,1024]{3,2,1,0:T(8,128)(2,1)}, bf16[4,2,144,1024]{3,2,1,0:T(8,128)(2,1)}, u32[]{:S(2)}, u32[]{:S(2)}) collective-permute-start(bf16[4,2,144,1024]{3,2,1,0:T(8,128)(2,1)} %collective-permute-done.16.refs_2_), channel_id=1, source_target_pairs={{0,8},{8,0},{16,24},{24,16},{32,40},{40,32},{48,56},{56,48},{64,72... | collective-permute-start | bytes 7077896 | tf_op jit(solution)/shard_map/ppermute | solution.py:622
  151.4 14.8 %collective-permute-start.23 = (bf16[4,2,144,1024]{3,2,1,0:T(8,128)(2,1)}, bf16[4,2,144,1024]{3,2,1,0:T(8,128)(2,1)}, u32[]{:S(2)}, u32[]{:S(2)}) collective-permute-start(bf16[4,2,144,1024]{3,2,1,0:T(8,128)(2,1)} %collective-permute-done.19.refs_3_), channel_id=1, source_target_pairs={{0,8},{8,0},{16,24},{24,16},{32,40},{40,32},{48,56},{56,48},{64,72... | collective-permute-start | bytes 7077896 | tf_op jit(solution)/shard_map/ppermute | solution.py:622
  151.8 14.4 %all-to-all-start = ((bf16[8,256,128]{2,1,0:T(8,128)(2,1)}), bf16[8,256,128]{2,1,0:T(8,128)(2,1)}, u32[]{:S(2)}, u32[]{:S(2)}) async-start(bf16[8,256,128]{2,1,0:T(8,128)(2,1)} %bitcast.37), calls=%async_computation | async-start | bytes 1048576 | tf_op jit(solution)/shard_map/all_to_all | solution.py:710
  166.2 35.8 %copy-start.17 = (s32[64,2]{0,1:T(2,128)S(1)}, s32[64,2]{0,1:T(2,128)}, u32[]{:S(2)}) copy-start(s32[64,2]{0,1:T(2,128)} %param.21) | copy-start | bytes 1540
  191.7 19.8 %copy-start.4 = (bf16[8,256,128]{2,1,0:T(8,128)(2,1)}, bf16[8,256,128]{2,1,0:T(8,128)(2,1)S(1)}, u32[]{:S(2)}) copy-start(bf16[8,256,128]{2,1,0:T(8,128)(2,1)S(1)} %all_to_all.15) | copy-start | bytes 1572868
  191.7 11.7 %collective-permute-start.24 = (bf16[8,128,128]{2,1,0:T(8,128)(2,1)S(1)}, bf16[8,128,128]{2,1,0:T(8,128)(2,1)S(1)}, u32[]{:S(2)}, u32[]{:S(2)}) collective-permute-start(bf16[8,128,128]{2,1,0:T(8,128)(2,1)S(1)} %bitcast.61), channel_id=1, source_target_pairs={{0,8},{8,16},{16,24},{24,32},{32,40},{40,48},{48,56},{56,64},{64,7... | collective-permute-start | bytes 786440 | tf_op jit(solution)/shard_map/ppermute | solution.py:618
  200.2 11.3 %collective-permute-start.25 = (bf16[8,128,128]{2,1,0:T(8,128)(2,1)S(1)}, bf16[8,128,128]{2,1,0:T(8,128)(2,1)S(1)}, u32[]{:S(2)}, u32[]{:S(2)}) collective-permute-start(bf16[8,128,128]{2,1,0:T(8,128)(2,1)S(1)} %bitcast.60), channel_id=1, source_target_pairs={{8,0},{16,8},{24,16},{32,24},{40,32},{48,40},{56,48},{64,56},{72,6... | collective-permute-start | bytes 786440 | tf_op jit(solution)/shard_map/ppermute | solution.py:618
  203.4 8.0 %copy-start.14 = (bf16[8,128,128]{2,1,0:T(8,128)(2,1)}, bf16[8,128,128]{2,1,0:T(8,128)(2,1)S(1)}, u32[]{:S(2)}) copy-start(bf16[8,128,128]{2,1,0:T(8,128)(2,1)S(1)} %collective-permute-done.24.low) | copy-start | bytes 786436
  211.5 0.7 copy-start.15

commit v8 on v6

--- a/solution.py
+++ b/solution.py
@@ -139,9 +139,9 @@
     normed = jnp.concatenate(
         [(x * spread * gain[order[p]]).astype(BF) for p, x in enumerate(pieces)], axis=1
     )
-    made = dot(normed, ordered[...]).astype(BF)
-    queries[...] = (made[:, :BLOCK].astype(F32) * (HEAD_DIM**-0.5)).astype(BF)
-    keys_values[...] = made[:, BLOCK:]
+    made = dot(normed, ordered[...])
+    queries[...] = (made[:, :BLOCK] * (HEAD_DIM**-0.5 * LOG2E)).astype(BF)
+    keys_values[...] = made[:, BLOCK:].astype(BF)
 
 
 def project(order, slots, gain, weights):
@@ -180,7 +180,7 @@
 CHUNKS = SPAN // TILE
 
 
-def attend_kernel(edges, queries, low, own, high, out, keys, values, scores, sems):
+def attend_kernel(edges, queries, low, own, high, out, keys, values, scores, powers, sems):
     step = pl.program_id(0)
     rows = own.shape[0]
 
@@ -200,7 +200,6 @@
                 )
         for c in copies:
             c.start()
-        values[:, BLOCK:] = jnp.ones((values.shape[0], BLOCK), BF)
         first = lax.broadcasted_iota(jnp.int32, (keys.shape[0], BLOCK), 1) == 0
         row = lax.broadcasted_iota(jnp.int32, (keys.shape[0], BLOCK), 0)
         absent = ((row < REACH) & (edges[0] == 1)) | (
@@ -209,6 +208,11 @@
         keys[:, BLOCK:] = jnp.where(first & absent, -1e30, 0.0).astype(BF)
         for c in copies:
             c.wait()
+        both = values[:, :BLOCK]
+        left = lax.broadcasted_iota(jnp.int32, both.shape, 1) < HEAD_DIM
+        ones = jnp.ones_like(both)
+        values[:, :BLOCK] = jnp.where(left, both, ones)
+        values[:, BLOCK:] = jnp.where(left, ones, both)
 
     lane = lax.broadcasted_iota(jnp.int32, (TILE, BLOCK), 1)
     q = queries[...]
@@ -234,14 +238,18 @@
             s = jnp.where(gap <= WINDOW, s, -1e30)
         scores[:, c * TILE : (c + 1) * TILE] = s
         highest = jnp.maximum(highest, jnp.maximum(s[:, :BLOCK], s[:, BLOCK:]))
-    peak = jnp.max(highest, axis=1, keepdims=True) * LOG2E
-    total = jnp.zeros((2 * TILE, 2 * BLOCK), F32)
-    for c in range(CHUNKS):
-        part = values[pl.ds(pl.multiple_of((step + c) * TILE, TILE), TILE)]
-        powers = jnp.exp2(scores[:, c * TILE : (c + 1) * TILE] * LOG2E - peak)
-        total = total + dot(powers.astype(BF), part)
-    made = total[:, :BLOCK] / total[:, BLOCK:]
-    out[...] = jnp.where(lane < HEAD_DIM, made[:TILE], made[TILE:]).astype(BF)
+    peak = jnp.max(highest, axis=1, keepdims=True)
+    span = pl.ds(pl.multiple_of(step * TILE, TILE), SPAN)
+    totals = []
+    for h in range(2):
+        rows_of = slice(h * TILE, (h + 1) * TILE)
+        for c in range(CHUNKS):
+            at = slice(c * TILE, (c + 1) * TILE)
+            powers[rows_of, at] = jnp.exp2(scores[rows_of, at] - peak[rows_of]).astype(BF)
+        totals.append(dot(powers[rows_of], values[span, h * BLOCK : (h + 1) * BLOCK]))
+    made = jnp.where(lane < HEAD_DIM, totals[0], totals[1])
+    sums = jnp.where(lane < HEAD_DIM, totals[1], totals[0])
+    out[...] = (made / pltpu.roll(sums, HEAD_DIM, 1)).astype(BF)
 
 
 def attend(edges, queries, low, own, high):
@@ -258,6 +266,7 @@
                 pltpu.VMEM((rows + 2 * REACH, 2 * BLOCK), BF),
                 pltpu.VMEM((rows + 2 * REACH, 2 * BLOCK), BF),
                 pltpu.VMEM((2 * TILE, SPAN), F32),
+                pltpu.VMEM((2 * TILE, SPAN), BF),
                 pltpu.SemaphoreType.DMA((6,)),
             ],
         ),
@@ -395,7 +404,6 @@
         c.start()
     for c in ahead:
         c.wait()
-    ones = jnp.ones((BLOCK, BLOCK), BF)
     row = lax.broadcasted_iota(jnp.int32, (BLOCK, BLOCK), 0)
     column = lax.broadcasted_iota(jnp.int32, (BLOCK, BLOCK), 1)
     for step in range(steps):
@@ -406,12 +414,15 @@
             left = jnp.concatenate([held[b, k] for k in range(slots)], axis=1)
             right = jnp.concatenate([source[index[b, k]] for k in range(slots)], axis=0)
             made = dot(left, right)
-            plain = made.astype(BF)
-            kept[b * BLOCK : (b + 1) * BLOCK] = plain
-            kinds.append((plain, (made * made).astype(BF)))
+            kept[b * BLOCK : (b + 1) * BLOCK] = made.astype(BF)
+            kinds.append((made, made * made))
         done[step].start()
         held_sums = [
-            jnp.sum(jnp.where(row == column, dot(kinds[b][n], ones), 0.0), axis=0, keepdims=True)
+            jnp.sum(
+                jnp.where(row == column, jnp.sum(kinds[b][n], axis=1, keepdims=True), 0.0),
+                axis=0,
+                keepdims=True,
+            )
             for n in range(2)
             for b in range(EACH)
         ]
@@ -504,7 +515,7 @@
                 pltpu.SemaphoreType.DMA((count + 3 * steps,)),
             ],
         ),
-        compiler_params=params(24),
+        compiler_params=params(56),
         cost_estimate=cost(540_000_000, 8_000_000),
         name="finish",
     )(sums, back, state, gain.reshape(1, BLOCK))

time: 224 us -> 215 us (0.960)
  Pallas kernels: 70.3 us -> 62 us
    pallas_call x1, Pallas kernels: 28.5 us -> 19.2 us  [attend(): pl.pallas_call(attend_kernel, out_shape=jax.ShapeDtypeStruct((rows, BLOCK...]
    unnamed x40 -> x34, local copies, waits for them, and re-layouts: 5.12 us -> 3.49 us
  transfers between devices with their start and end apart: 27 -> 27, of which waited for: 11 -> 11; matrix products, arithmetic and copies ran while one was open for 4% -> 5% of each run, Pallas kernels for 20% -> 16%
where the time goes in v8:
time: 215 us; the launch traced here: 213 us
  waiting for transfers between devices  66.3 us (31%)
  Pallas kernels  62 us (29%)
  starting transfers between devices  44.6 us (21%)
  blocking collectives  21.9 us (10%)
  local copies, waits for them, and re-layouts  12.9 us (6%)
  other arithmetic  5.25 us (2%)
    ppermute x20, waiting for transfers between devices, among(): return lax.ppermute(value, axis, [(i, to(i)) for i in range(count)])  30.4 us
    ppermute x6, waiting for transfers between devices, shifted(): lax.ppermute(value, 'seq', [(i, i + by) for i in range(16) if 0 <= i + by...  26.3 us
    ppermute x6, starting transfers between devices, shifted(): lax.ppermute(value, 'seq', [(i, i + by) for i in range(16) if 0 <= i + by...  24.1 us
    pallas_call x1, Pallas kernels, attend(): pl.pallas_call(attend_kernel, out_shape=jax.ShapeDtypeStruct((rows, BLOCK...  19.2 us
    ppermute x20, starting transfers between devices, among(): return lax.ppermute(value, axis, [(i, to(i)) for i in range(count)])  16.4 us
    pallas_call x1, Pallas kernels, forward(): pl.pallas_call(forward_kernel, out_shape=jax.ShapeDtypeStruct((8, rows, B...  12.8 us
    all_to_all x1, blocking collectives, on_device(): mesh_end = lax.all_to_all(mesh_end, 'head', 0, 0, tiled=True)  12.7 us
    all_to_all x1, waiting for transfers between devices, on_device(): lax.all_to_all(context.reshape(8, mesh_rows // 8, BLOCK), 'head', 0, 0, t...  9.54 us
  transfers between devices with their start and end apart: 27, of which 11 were waited for; matrix products, arithmetic and copies ran while one was open for 5% of the time, Pallas kernels for 16%

profile of v8, /device:TPU:97, one launch (start us, length us, event | category | flops | bytes accessed | tf_op | source)
XLA Modules:
  0.0 213.5 jit_solution(17070911217884231551)
XLA Ops:
  0.0 2.4 %fusion = (bf16[2048,128]{1,0:T(8,128)(2,1)}, bf16[2048,128]{1,0:T(8,128)(2,1)}) fusion(bf16[8192,128]{1,0:T(8,128)(2,1)} %state.1), kind=kLoop, calls=%fused_computation.16 | loop fusion | bytes 2097152 | tf_op jit(solution)/shard_map/slice | solution.py:570
  2.4 0.9 constant_dynamic-slice_fusion
  3.3 0.8 constant_dynamic-slice_fusion.1
  4.1 1.3 collective-permute-start.2
  5.4 1.3 collective-permute-start.3
  6.7 4.1 %collective-permute-start = (bf16[2048,128]{1,0:T(8,128)(2,1)}, bf16[2048,128]{1,0:T(8,128)(2,1)S(1)}, u32[]{:S(2)}, u32[]{:S(2)}) collective-permute-start(bf16[2048,128]{1,0:T(8,128)(2,1)} %get-tuple-element.33), channel_id=1, source_target_pairs={{0,8},{8,16},{16,24},{24,32},{32,40},{40,48},{48,56},{56,64},{64,7... | collective-permute-start | bytes 1572872 | tf_op jit(solution)/shard_map/ppermute | solution.py:525
  10.8 1.9 collective-permute-start.1
  12.7 0.9 fusion.2
  13.7 1.4 collective-permute-start.6
  15.8 2.6 %collective-permute-start.5 = (bf16[144,1024]{1,0:T(8,128)(2,1)S(1)}, bf16[144,1024]{1,0:T(8,128)(2,1)S(1)}, u32[]{:S(2)}, u32[]{:S(2)}) collective-permute-start(bf16[144,1024]{1,0:T(8,128)(2,1)S(1)} %pad_maximum_fusion.4), channel_id=1, source_target_pairs={{0,6},{1,7},{2,0},{3,1},{4,2},{5,3},{6,4},{7,5},{8,14},{9,15},{10,... | collective-permute-start | bytes 884744 | tf_op jit(solution)/shard_map/ppermute | solution.py:529
  18.4 1.0 maximum_bitcast_fusion
  19.5 5.6 %collective-permute-done.1 = bf16[2048,128]{1,0:T(8,128)(2,1)S(1)} collective-permute-done((bf16[2048,128]{1,0:T(8,128)(2,1)}, bf16[2048,128]{1,0:T(8,128)(2,1)S(1)}, u32[]{:S(2)}, u32[]{:S(2)}) %collective-permute-start.1) | collective-permute-done | bytes 524320 | tf_op jit(solution)/shard_map/ppermute | solution.py:525
  25.1 1.4 collective-permute-start.8
  26.5 7.2 %encode.1.s0 = bf16[2048,128]{1,0:T(8,128)(2,1)} custom-call(s32[16,8]{1,0:T(8,128)} %broadcast_subtract_fusion.1.index, bf16[16,128,128]{2,1,0:T(8,128)(2,1)} %bitcast.54, bf16[64,128,128]{2,1,0:T(8,128)(2,1)} %bitcast.47, bf16[16,128,128]{2,1,0:T(8,128)(2,1)} %bitcast.55, bf16[16,8,128,128]{3,2,1,0:T(8,128)(2,1)} %weights.2), custom_call_target="tpu_custom_call" | custom-call | flops 540000000 | bytes 8000000 | tf_op jit(solution)/shard_map/encode/pallas_call | solution.py:84
  33.8 1.0 maximum_bitcast_fusion.1
  35.3 0.7 copy-done.3
  36.0 0.7 collective-permute-start.10
  36.7 2.0 collective-permute-start.11
  38.7 1.5 collective-permute-start.16
  40.1 7.9 %collective-permute-done.10.s2 = bf16[2048,128]{1,0:T(8,128)(2,1)S(1)} collective-permute-done((bf16[2048,128]{1,0:T(8,128)(2,1)S(1)}, bf16[2048,128]{1,0:T(8,128)(2,1)S(1)}, u32[]{:S(2)}, u32[]{:S(2)}) %collective-permute-start.10) | collective-permute-done | bytes 524320 | tf_op jit(solution)/shard_map/ppermute | solution.py:529
  48.2 0.7 collective-permute-done.9.s1
  49.1 1.1 collective-permute-start.12
  50.2 1.7 collective-permute-start.13
  52.2 13.4 %collective-permute-done.12.s3 = bf16[3072,128]{1,0:T(8,128)(2,1)S(1)} collective-permute-done((bf16[3072,128]{1,0:T(8,128)(2,1)S(1)}, bf16[3072,128]{1,0:T(8,128)(2,1)S(1)}, u32[]{:S(2)}, u32[]{:S(2)}) %collective-permute-start.12) | collective-permute-done | bytes 786464 | tf_op jit(solution)/shard_map/ppermute | solution.py:529
  65.5 0.9 copy-done.5
  66.5 0.9 copy-done.6
  67.4 0.9 pad_maximum_fusion.3.s6
  68.2 0.6 stack.130.order
  68.9 8.2 %collective-permute-done.14.s7 = bf16[2048,128]{1,0:T(8,128)(2,1)} collective-permute-done((bf16[2048,128]{1,0:T(8,128)(2,1)}, bf16[2048,128]{1,0:T(8,128)(2,1)}, u32[]{:S(2)}, u32[]{:S(2)}) %collective-permute-start.14) | collective-permute-done | bytes 524320 | tf_op jit(solution)/shard_map/ppermute | solution.py:529
  77.1 8.6 %project.1 = (bf16[2048,128]{1,0:T(8,128)(2,1)}, bf16[2048,256]{1,0:T(8,128)(2,1)}, bf16[8,256,128]{2,1,0:T(8,128)(2,1)}) custom-call(s32[8]{0:T(128)} %stack.130.order, bf16[2048,128]{1,0:T(8,128)(2,1)} %encode.1.s0, bf16[2048,128]{1,0:T(8,128)(2,1)} %copy-done.4, bf16[2048,128]{1,0:T(8,128)(2,1)} %copy-done.7, bf16[3072,128]{1,0:T(8,128)(2,1)} %copy-done.5, ...), custom_call_target="tpu_custom_call" | custom-call | tf_op jit(solution)/shard_map/project/pallas_call | solution.py:153
  85.7 2.3 %fusion.1 = (bf16[1152,256]{1,0:T(8,128)(2,1)}, bf16[1152,256]{1,0:T(8,128)(2,1)}) fusion(bf16[2048,256]{1,0:T(8,128)(2,1)} %get-tuple-element.47.own), kind=kLoop, calls=%fused_computation.17 | loop fusion | bytes 2359296 | tf_op jit(solution)/shard_map/slice | solution.py:608
  88.1 10.1 %collective-permute-start.17 = (bf16[1152,256]{1,0:T(8,128)(2,1)}, bf16[1152,256]{1,0:T(8,128)(2,1)}, u32[]{:S(2)}, u32[]{:S(2)}) collective-permute-start(bf16[1152,256]{1,0:T(8,128)(2,1)} %get-tuple-element.48), channel_id=1, source_target_pairs={{0,8},{8,16},{16,24},{24,32},{32,40},{40,48},{48,56},{56,64},{64,7... | collective-permute-start | bytes 1769480 | tf_op jit(solution)/shard_map/ppermute | solution.py:525
  98.1 2.1 collective-permute-start.18
  100.9 4.4 %collective-permute-done.17.low = bf16[1152,256]{1,0:T(8,128)(2,1)} collective-permute-done((bf16[1152,256]{1,0:T(8,128)(2,1)}, bf16[1152,256]{1,0:T(8,128)(2,1)}, u32[]{:S(2)}, u32[]{:S(2)}) %collective-permute-start.17) | collective-permute-done | bytes 589856 | tf_op jit(solution)/shard_map/ppermute | solution.py:525
  105.3 8.1 %collective-permute-done.18.high = bf16[1152,256]{1,0:T(8,128)(2,1)} collective-permute-done((bf16[1152,256]{1,0:T(8,128)(2,1)}, bf16[1152,256]{1,0:T(8,128)(2,1)}, u32[]{:S(2)}, u32[]{:S(2)}) %collective-permute-start.18) | collective-permute-done | bytes 589856 | tf_op jit(solution)/shard_map/ppermute | solution.py:525
  113.4 19.2 %attend.1 = bf16[2048,128]{1,0:T(8,128)(2,1)} custom-call(s32[2]{0:T(128)} %add_convert_fusion.edges, bf16[2048,128]{1,0:T(8,128)(2,1)} %get-tuple-element.46.queries, bf16[1152,256]{1,0:T(8,128)(2,1)} %collective-permute-done.17.low, bf16[2048,256]{1,0:T(8,128)(2,1)} %get-tuple-element.47.own, bf16[1152,256]{1,0:T(8,128)(2,1)} %collective-permute-done.18.high), custom_call_target="tpu_custom_call" | custom-call | tf_op jit(solution)/shard_map/attend/pallas_call | solution.py:257
  133.8 4.1 %all-to-all-start = ((bf16[8,256,128]{2,1,0:T(8,128)(2,1)}), bf16[8,256,128]{2,1,0:T(8,128)(2,1)}, u32[]{:S(2)}, u32[]{:S(2)}) async-start(bf16[8,256,128]{2,1,0:T(8,128)(2,1)} %bitcast.49), calls=%async_computation | async-start | bytes 1048576 | tf_op jit(solution)/shard_map/all_to_all | solution.py:616
  138.6 9.5 %all-to-all-done.refs_8_ = bf16[8,256,128]{2,1,0:T(8,128)(2,1)} async-done(((bf16[8,256,128]{2,1,0:T(8,128)(2,1)}), bf16[8,256,128]{2,1,0:T(8,128)(2,1)}, u32[]{:S(2)}, u32[]{:S(2)}) %all-to-all-start) | async-done | bytes 524320 | tf_op jit(solution)/shard_map/all_to_all | solution.py:616
  148.2 12.8 %forward.1 = bf16[8,256,128]{2,1,0:T(8,128)(2,1)} custom-call(s32[16]{0:T(128)} %concatenate.19.table, bf16[4,2,144,1024]{3,2,1,0:T(8,128)(2,1)} %copy-done.1, bf16[4,2,144,1024]{3,2,1,0:T(8,128)(2,1)} %collective-permute-done.15.refs_1_, bf16[4,2,144,1024]{3,2,1,0:T(8,128)(2,1)} %collective-permute-done.16.refs_2_, ...), custom_call_target="tpu_custom_call" | custom-call | flops 4800000000 | bytes 20000000 | tf_op jit(solution)/shard_map/forward/pallas_call | solution.py:370
  161.0 12.7 %all_to_all.15 = bf16[8,256,128]{2,1,0:T(8,128)(2,1)S(1)} all-to-all(bf16[8,256,128]{2,1,0:T(8,128)(2,1)} %forward.1), channel_id=1, replica_groups=mesh['seq'=16,'head'=8] {'head'}, dimensions={0} | all-to-all | bytes 1048576 | tf_op jit(solution)/shard_map/all_to_all | solution.py:624
  173.7 3.5 %collective-permute-start.24 = (bf16[8,128,128]{2,1,0:T(8,128)(2,1)S(1)}, bf16[8,128,128]{2,1,0:T(8,128)(2,1)S(1)}, u32[]{:S(2)}, u32[]{:S(2)}) collective-permute-start(bf16[8,128,128]{2,1,0:T(8,128)(2,1)S(1)} %bitcast.62), channel_id=1, source_target_pairs={{0,8},{8,16},{16,24},{24,32},{32,40},{40,48},{48,56},{56,64},{64,7... | collective-permute-start | bytes 786440 | tf_op jit(solution)/shard_map/ppermute | solution.py:525
  177.2 2.4 %collective-permute-start.25 = (bf16[8,128,128]{2,1,0:T(8,128)(2,1)S(1)}, bf16[8,128,128]{2,1,0:T(8,128)(2,1)S(1)}, u32[]{:S(2)}, u32[]{:S(2)}) collective-permute-start(bf16[8,128,128]{2,1,0:T(8,128)(2,1)S(1)} %bitcast.61), channel_id=1, source_target_pairs={{8,0},{16,8},{24,16},{32,24},{40,32},{48,40},{56,48},{64,56},{72,6... | collective-permute-start | bytes 786440 | tf_op jit(solution)/shard_map/ppermute | solution.py:525
  180.5 8.0 %collective-permute-done.25.high = bf16[8,128,128]{2,1,0:T(8,128)(2,1)S(1)} collective-permute-done((bf16[8,128,128]{2,1,0:T(8,128)(2,1)S(1)}, bf16[8,128,128]{2,1,0:T(8,128)(2,1)S(1)}, u32[]{:S(2)}, u32[]{:S(2)}) %collective-permute-start.25) | collective-permute-done | bytes 262176 | tf_op jit(solution)/shard_map/ppermute | solution.py:525
  188.5 0.7 copy-done.13
  189.2 8.0 %decode.1 = (bf16[8192,128]{1,0:T(8,128)(2,1)}, bf16[8,16,128]{2,1,0:T(8,128)(2,1)}) custom-call(s32[64,2]{1,0:T(8,128)} %broadcast_subtract_fusion.index, bf16[8,128,128]{2,1,0:T(8,128)(2,1)} %copy-done.12, bf16[16,128,128]{2,1,0:T(8,128)(2,1)} %bitcast.48, bf16[8,128,128]{2,1,0:T(8,128)(2,1)} %copy-done.13, bf16[64,2,128,128]{3,2,1,0:T(8,128)(2,1)} %weights.3), custom_call_target="tpu_custom_call" | custom-call | flops 540000000 | bytes 10000000 | tf_op jit(solution)/shard_map/decode/pallas_call | solution.py:439
  197.2 0.8 broadcast_in_dim.3
  198.0 9.2 %all_to_all.16.sums = bf16[8,8,16,128]{3,2,1,0:T(8,128)(2,1)} all-to-all(bf16[8,8,16,128]{3,2,1,0:T(8,128)(2,1)S(1)} %broadcast_in_dim.3), channel_id=1, replica_groups=mesh['seq'=16,'head'=8] {'head'}, dimensions={0} | all-to-all | bytes 524288 | tf_op jit(solution)/shard_map/all_to_all | solution.py:634
  207.2 6.1 %finish.1 = bf16[8192,128]{1,0:T(8,128)(2,1)} custom-call(bf16[8,8,16,128]{3,2,1,0:T(8,128)(2,1)} %all_to_all.16.sums, bf16[8192,128]{1,0:T(8,128)(2,1)} %get-tuple-element.60.back, bf16[8192,128]{1,0:T(8,128)(2,1)} %state.1, f32[1,128]{1,0:T(1,128)} %bitcast.65), custom_call_target="tpu_custom_call" | custom-call | flops 540000000 | bytes 8000000 | tf_op jit(solution)/shard_map/finish/pallas_call | solution.py:503
  (73 shorter events, 5.4 us)
Async XLA Ops:
  0.0 3.3 %copy-start = (bf16[512,1024]{1,0:T(8,128)(2,1)S(1)}, bf16[512,1024]{1,0:T(8,128)(2,1)}, u32[]{:S(2)}) copy-start(bf16[512,1024]{1,0:T(8,128)(2,1)} %param.20) | copy-start | bytes 3145732
  0.0 12.7 %copy-start.9 = (bf16[1024,3,128]{2,0,1:T(8,128)(2,1)S(1)}, bf16[1024,3,128]{2,0,1:T(8,128)(2,1)}, u32[]{:S(2)}) copy-start(bf16[1024,3,128]{2,0,1:T(8,128)(2,1)} %param.16) | copy-start | bytes 2359300
  0.0 13.6 %copy-start.14 = (s32[16,8]{0,1:T(8,128)S(1)}, s32[16,8]{0,1:T(8,128)}, u32[]{:S(2)}) copy-start(s32[16,8]{0,1:T(8,128)} %param.13) | copy-start | bytes 1540
  4.1 9.6 %collective-permute-start.2 = (bf16[144,1024]{1,0:T(8,128)(2,1)S(1)}, bf16[144,1024]{1,0:T(8,128)(2,1)}, u32[]{:S(2)}, u32[]{:S(2)}) collective-permute-start(bf16[144,1024]{1,0:T(8,128)(2,1)S(1)} %pad_maximum_fusion.4), channel_id=1, source_target_pairs={{0,1},{1,0},{2,3},{3,2},{4,5},{5,4},{6,7},{7,6},{8,9},{9,8},{10,11... | collective-permute-start | bytes 884744 | tf_op jit(solution)/shard_map/ppermute | solution.py:529
  5.4 10.4 %collective-permute-start.3 = (bf16[144,1024]{1,0:T(8,128)(2,1)S(1)}, bf16[144,1024]{1,0:T(8,128)(2,1)}, u32[]{:S(2)}, u32[]{:S(2)}) collective-permute-start(bf16[144,1024]{1,0:T(8,128)(2,1)S(1)} %pad_maximum_fusion.4), channel_id=1, source_target_pairs={{0,2},{1,3},{2,4},{3,5},{4,6},{5,7},{6,0},{7,1},{8,10},{9,11},{10,... | collective-permute-start | bytes 884744 | tf_op jit(solution)/shard_map/ppermute | solution.py:529
  6.7 12.7 %collective-permute-start = (bf16[2048,128]{1,0:T(8,128)(2,1)}, bf16[2048,128]{1,0:T(8,128)(2,1)S(1)}, u32[]{:S(2)}, u32[]{:S(2)}) collective-permute-start(bf16[2048,128]{1,0:T(8,128)(2,1)} %get-tuple-element.33), channel_id=1, source_target_pairs={{0,8},{8,16},{16,24},{24,32},{32,40},{40,48},{48,56},{56,64},{64,7... | collective-permute-start | bytes 1572872 | tf_op jit(solution)/shard_map/ppermute | solution.py:525
  10.8 14.3 %collective-permute-start.1 = (bf16[2048,128]{1,0:T(8,128)(2,1)}, bf16[2048,128]{1,0:T(8,128)(2,1)S(1)}, u32[]{:S(2)}, u32[]{:S(2)}) collective-permute-start(bf16[2048,128]{1,0:T(8,128)(2,1)} %get-tuple-element.34), channel_id=1, source_target_pairs={{8,0},{16,8},{24,16},{32,24},{40,32},{48,40},{56,48},{64,56},{72,6... | collective-permute-start | bytes 1572872 | tf_op jit(solution)/shard_map/ppermute | solution.py:525
  13.7 11.4 %collective-permute-start.6 = (bf16[144,1024]{1,0:T(8,128)(2,1)}, bf16[144,1024]{1,0:T(8,128)(2,1)S(1)}, u32[]{:S(2)}, u32[]{:S(2)}) collective-permute-start(bf16[144,1024]{1,0:T(8,128)(2,1)} %collective-permute-done.2), channel_id=1, source_target_pairs={{0,6},{1,7},{2,0},{3,1},{4,2},{5,3},{6,4},{7,5},{8,14},{9,15},{10,... | collective-permute-start | bytes 884744 | tf_op jit(solution)/shard_map/ppermute | solution.py:529
  15.1 18.6 %collective-permute-start.4 = (bf16[144,1024]{1,0:T(8,128)(2,1)}, bf16[144,1024]{1,0:T(8,128)(2,1)S(1)}, u32[]{:S(2)}, u32[]{:S(2)}) collective-permute-start(bf16[144,1024]{1,0:T(8,128)(2,1)} %collective-permute-done.2), channel_id=1, source_target_pairs={{0,2},{1,3},{2,4},{3,5},{4,6},{5,7},{6,0},{7,1},{8,10},{9,11},{10,... | collective-permute-start | bytes 884744 | tf_op jit(solution)/shard_map/ppermute | solution.py:529
  15.8 19.0 %collective-permute-start.5 = (bf16[144,1024]{1,0:T(8,128)(2,1)S(1)}, bf16[144,1024]{1,0:T(8,128)(2,1)S(1)}, u32[]{:S(2)}, u32[]{:S(2)}) collective-permute-start(bf16[144,1024]{1,0:T(8,128)(2,1)S(1)} %pad_maximum_fusion.4), channel_id=1, source_target_pairs={{0,6},{1,7},{2,0},{3,1},{4,2},{5,3},{6,4},{7,5},{8,14},{9,15},{10,... | collective-permute-start | bytes 884744 | tf_op jit(solution)/shard_map/ppermute | solution.py:529
  19.4 7.1 %copy-start.10 = (bf16[2048,128]{1,0:T(8,128)(2,1)}, bf16[2048,128]{1,0:T(8,128)(2,1)S(1)}, u32[]{:S(2)}) copy-start(bf16[2048,128]{1,0:T(8,128)(2,1)S(1)} %collective-permute-done) | copy-start | bytes 1572868
  19.4 15.4 %collective-permute-start.7 = (bf16[144,1024]{1,0:T(8,128)(2,1)}, bf16[144,1024]{1,0:T(8,128)(2,1)S(1)}, u32[]{:S(2)}, u32[]{:S(2)}) collective-permute-start(bf16[144,1024]{1,0:T(8,128)(2,1)} %collective-permute-done.3), channel_id=1, source_target_pairs={{0,2},{1,3},{2,4},{3,5},{4,6},{5,7},{6,0},{7,1},{8,10},{9,11},{10,... | collective-permute-start | bytes 884744 | tf_op jit(solution)/shard_map/ppermute | solution.py:529
  25.1 1.4 copy-start.11
  25.1 9.7 %collective-permute-start.8 = (bf16[144,1024]{1,0:T(8,128)(2,1)S(1)}, bf16[144,1024]{1,0:T(8,128)(2,1)S(1)}, u32[]{:S(2)}, u32[]{:S(2)}) collective-permute-start(bf16[144,1024]{1,0:T(8,128)(2,1)S(1)} %collective-permute-done.6), channel_id=1, source_target_pairs={{0,6},{1,7},{2,0},{3,1},{4,2},{5,3},{6,4},{7,5},{8,14},{9,15},{10,... | collective-permute-start | bytes 884744 | tf_op jit(solution)/shard_map/ppermute | solution.py:529
  34.9 1.0 copy-start.3
  36.0 96.7 %copy-start.1 = (bf16[4,2,144,1024]{3,2,1,0:T(8,128)(2,1)}, bf16[4,2,144,1024]{3,2,1,0:T(8,128)(2,1)S(1)}, u32[]{:S(2)}) copy-start(bf16[4,2,144,1024]{3,2,1,0:T(8,128)(2,1)S(1)} %pad_maximum_fusion.refs_0_) | copy-start | bytes 7077892
  36.0 12.0 %collective-permute-start.10 = (bf16[2048,128]{1,0:T(8,128)(2,1)S(1)}, bf16[2048,128]{1,0:T(8,128)(2,1)S(1)}, u32[]{:S(2)}, u32[]{:S(2)}) collective-permute-start(bf16[2048,128]{1,0:T(8,128)(2,1)S(1)} %copy-done.3), channel_id=1, source_target_pairs={{0,2},{1,3},{2,4},{3,5},{4,6},{5,7},{6,0},{7,1},{8,10},{9,11},{10,... | collective-permute-start | bytes 1572872 | tf_op jit(solution)/shard_map/ppermute | solution.py:529
  36.7 11.5 %collective-permute-start.11 = (bf16[2048,128]{1,0:T(8,128)(2,1)S(1)}, bf16[2048,128]{1,0:T(8,128)(2,1)S(1)}, u32[]{:S(2)}, u32[]{:S(2)}) collective-permute-start(bf16[2048,128]{1,0:T(8,128)(2,1)S(1)} %copy-done.3), channel_id=1, source_target_pairs={{0,6},{1,7},{2,0},{3,1},{4,2},{5,3},{6,4},{7,5},{8,14},{9,15},{10,... | collective-permute-start | bytes 1572872 | tf_op jit(solution)/shard_map/ppermute | solution.py:529
  38.7 10.2 %collective-permute-start.9 = (bf16[2048,128]{1,0:T(8,128)(2,1)S(1)}, bf16[2048,128]{1,0:T(8,128)(2,1)S(1)}, u32[]{:S(2)}, u32[]{:S(2)}) collective-permute-start(bf16[2048,128]{1,0:T(8,128)(2,1)S(1)} %copy-done.3), channel_id=1, source_target_pairs={{0,1},{1,0},{2,3},{3,2},{4,5},{5,4},{6,7},{7,6},{8,9},{9,8},{10,11... | collective-permute-start | bytes 1572872 | tf_op jit(solution)/shard_map/ppermute | solution.py:529
  38.7 49.4 %collective-permute-start.15 = (bf16[4,2,144,1024]{3,2,1,0:T(8,128)(2,1)S(1)}, bf16[4,2,144,1024]{3,2,1,0:T(8,128)(2,1)}, u32[]{:S(2)}, u32[]{:S(2)}) collective-permute-start(bf16[4,2,144,1024]{3,2,1,0:T(8,128)(2,1)S(1)} %pad_maximum_fusion.refs_0_), channel_id=1, source_target_pairs={{0,16},{8,24},{16,32},{24,40},{32,48},{40,56},{48,0},{56,8},{64,80... | collective-permute-start | bytes 7077896 | tf_op jit(solution)/shard_map/ppermute | solution.py:529
  38.7 49.4 %collective-permute-start.16 = (bf16[4,2,144,1024]{3,2,1,0:T(8,128)(2,1)S(1)}, bf16[4,2,144,1024]{3,2,1,0:T(8,128)(2,1)}, u32[]{:S(2)}, u32[]{:S(2)}) collective-permute-start(bf16[4,2,144,1024]{3,2,1,0:T(8,128)(2,1)S(1)} %pad_maximum_fusion.refs_0_), channel_id=1, source_target_pairs={{0,48},{8,56},{16,0},{24,8},{32,16},{40,24},{48,32},{56,40},{64,11... | collective-permute-start | bytes 7077896 | tf_op jit(solution)/shard_map/ppermute | solution.py:529
  48.0 0.9 copy-start.7
  48.2 0.9 copy-start.8
  48.9 18.5 %copy-start.4 = (bf16[2048,128]{1,0:T(8,128)(2,1)}, bf16[2048,128]{1,0:T(8,128)(2,1)S(1)}, u32[]{:S(2)}) copy-start(bf16[2048,128]{1,0:T(8,128)(2,1)S(1)} %collective-permute-done.9.s1) | copy-start | bytes 1572868
  49.1 16.4 %collective-permute-start.12 = (bf16[3072,128]{1,0:T(8,128)(2,1)S(1)}, bf16[3072,128]{1,0:T(8,128)(2,1)S(1)}, u32[]{:S(2)}, u32[]{:S(2)}) collective-permute-start(bf16[3072,128]{1,0:T(8,128)(2,1)S(1)} %get-tuple-element.73), channel_id=1, source_target_pairs={{0,2},{1,3},{2,4},{3,5},{4,6},{5,7},{6,0},{7,1},{8,10},{9,11},{10,... | collective-permute-start | bytes 2359304 | tf_op jit(solution)/shard_map/ppermute | solution.py:529
  50.2 16.3 %collective-permute-start.13 = (bf16[3072,128]{1,0:T(8,128)(2,1)S(1)}, bf16[3072,128]{1,0:T(8,128)(2,1)S(1)}, u32[]{:S(2)}, u32[]{:S(2)}) collective-permute-start(bf16[3072,128]{1,0:T(8,128)(2,1)S(1)} %get-tuple-element.72), channel_id=1, source_target_pairs={{0,6},{1,7},{2,0},{3,1},{4,2},{5,3},{6,4},{7,5},{8,14},{9,15},{10,... | collective-permute-start | bytes 2359304 | tf_op jit(solution)/shard_map/ppermute | solution.py:529
  51.9 80.7 %collective-permute-start.19 = (bf16[4,2,144,1024]{3,2,1,0:T(8,128)(2,1)S(1)}, bf16[4,2,144,1024]{3,2,1,0:T(8,128)(2,1)}, u32[]{:S(2)}, u32[]{:S(2)}) collective-permute-start(bf16[4,2,144,1024]{3,2,1,0:T(8,128)(2,1)S(1)} %pad_maximum_fusion.refs_0_), channel_id=1, source_target_pairs={{0,65},{1,64},{2,67},{3,66},{4,69},{5,68},{6,71},{7,70},{8,73},{9,... | collective-permute-start | bytes 7077896 | tf_op jit(solution)/shard_map/ppermute | solution.py:529
  65.5 0.9 copy-start.5
  66.5 0.9 copy-start.6
  68.2 8.9 %collective-permute-start.14 = (bf16[2048,128]{1,0:T(8,128)(2,1)}, bf16[2048,128]{1,0:T(8,128)(2,1)}, u32[]{:S(2)}, u32[]{:S(2)}) collective-permute-start(bf16[2048,128]{1,0:T(8,128)(2,1)} %pad_maximum_fusion.3.s6), channel_id=1, source_target_pairs={{0,1},{1,0},{2,3},{3,2},{4,5},{5,4},{6,7},{7,6},{8,9},{9,8},{10,11... | collective-permute-start | bytes 1572872 | tf_op jit(solution)/shard_map/ppermute | solution.py:529
  88.1 17.2 %collective-permute-start.17 = (bf16[1152,256]{1,0:T(8,128)(2,1)}, bf16[1152,256]{1,0:T(8,128)(2,1)}, u32[]{:S(2)}, u32[]{:S(2)}) collective-permute-start(bf16[1152,256]{1,0:T(8,128)(2,1)} %get-tuple-element.48), channel_id=1, source_target_pairs={{0,8},{8,16},{16,24},{24,32},{32,40},{40,48},{48,56},{56,64},{64,7... | collective-permute-start | bytes 1769480 | tf_op jit(solution)/shard_map/ppermute | solution.py:525
  98.1 15.2 %collective-permute-start.18 = (bf16[1152,256]{1,0:T(8,128)(2,1)}, bf16[1152,256]{1,0:T(8,128)(2,1)}, u32[]{:S(2)}, u32[]{:S(2)}) collective-permute-start(bf16[1152,256]{1,0:T(8,128)(2,1)} %get-tuple-element.49), channel_id=1, source_target_pairs={{8,0},{16,8},{24,16},{32,24},{40,32},{48,40},{56,48},{64,56},{72,6... | collective-permute-start | bytes 1769480 | tf_op jit(solution)/shard_map/ppermute | solution.py:525
  132.6 15.5 %collective-permute-start.20 = (bf16[4,2,144,1024]{3,2,1,0:T(8,128)(2,1)S(1)}, bf16[4,2,144,1024]{3,2,1,0:T(8,128)(2,1)}, u32[]{:S(2)}, u32[]{:S(2)}) collective-permute-start(bf16[4,2,144,1024]{3,2,1,0:T(8,128)(2,1)S(1)} %pad_maximum_fusion.refs_0_), channel_id=1, source_target_pairs={{0,8},{8,0},{16,24},{24,16},{32,40},{40,32},{48,56},{56,48},{64,72... | collective-permute-start | bytes 7077896 | tf_op jit(solution)/shard_map/ppermute | solution.py:529
  132.7 15.4 %collective-permute-start.21 = (bf16[4,2,144,1024]{3,2,1,0:T(8,128)(2,1)}, bf16[4,2,144,1024]{3,2,1,0:T(8,128)(2,1)}, u32[]{:S(2)}, u32[]{:S(2)}) collective-permute-start(bf16[4,2,144,1024]{3,2,1,0:T(8,128)(2,1)} %collective-permute-done.15.refs_1_), channel_id=1, source_target_pairs={{0,8},{8,0},{16,24},{24,16},{32,40},{40,32},{48,56},{56,48},{64,72... | collective-permute-start | bytes 7077896 | tf_op jit(solution)/shard_map/ppermute | solution.py:529
  133.2 14.9 %collective-permute-start.22 = (bf16[4,2,144,1024]{3,2,1,0:T(8,128)(2,1)}, bf16[4,2,144,1024]{3,2,1,0:T(8,128)(2,1)}, u32[]{:S(2)}, u32[]{:S(2)}) collective-permute-start(bf16[4,2,144,1024]{3,2,1,0:T(8,128)(2,1)} %collective-permute-done.16.refs_2_), channel_id=1, source_target_pairs={{0,8},{8,0},{16,24},{24,16},{32,40},{40,32},{48,56},{56,48},{64,72... | collective-permute-start | bytes 7077896 | tf_op jit(solution)/shard_map/ppermute | solution.py:529
  133.3 14.8 %collective-permute-start.23 = (bf16[4,2,144,1024]{3,2,1,0:T(8,128)(2,1)}, bf16[4,2,144,1024]{3,2,1,0:T(8,128)(2,1)}, u32[]{:S(2)}, u32[]{:S(2)}) collective-permute-start(bf16[4,2,144,1024]{3,2,1,0:T(8,128)(2,1)} %collective-permute-done.19.refs_3_), channel_id=1, source_target_pairs={{0,8},{8,0},{16,24},{24,16},{32,40},{40,32},{48,56},{56,48},{64,72... | collective-permute-start | bytes 7077896 | tf_op jit(solution)/shard_map/ppermute | solution.py:529
  133.8 14.4 %all-to-all-start = ((bf16[8,256,128]{2,1,0:T(8,128)(2,1)}), bf16[8,256,128]{2,1,0:T(8,128)(2,1)}, u32[]{:S(2)}, u32[]{:S(2)}) async-start(bf16[8,256,128]{2,1,0:T(8,128)(2,1)} %bitcast.49), calls=%async_computation | async-start | bytes 1048576 | tf_op jit(solution)/shard_map/all_to_all | solution.py:616
  148.2 31.4 %copy-start.15 = (s32[64,2]{0,1:T(2,128)S(1)}, s32[64,2]{0,1:T(2,128)}, u32[]{:S(2)}) copy-start(s32[64,2]{0,1:T(2,128)} %param.21) | copy-start | bytes 1540
  173.6 14.9 %copy-start.2 = (bf16[8,256,128]{2,1,0:T(8,128)(2,1)}, bf16[8,256,128]{2,1,0:T(8,128)(2,1)S(1)}, u32[]{:S(2)}) copy-start(bf16[8,256,128]{2,1,0:T(8,128)(2,1)S(1)} %all_to_all.15) | copy-start | bytes 1572868
  173.7 6.8 %collective-permute-start.24 = (bf16[8,128,128]{2,1,0:T(8,128)(2,1)S(1)}, bf16[8,128,128]{2,1,0:T(8,128)(2,1)S(1)}, u32[]{:S(2)}, u32[]{:S(2)}) collective-permute-start(bf16[8,128,128]{2,1,0:T(8,128)(2,1)S(1)} %bitcast.62), channel_id=1, source_target_pairs={{0,8},{8,16},{16,24},{24,32},{32,40},{40,48},{48,56},{56,64},{64,7... | collective-permute-start | bytes 786440 | tf_op jit(solution)/shard_map/ppermute | solution.py:525
  177.2 11.3 %collective-permute-start.25 = (bf16[8,128,128]{2,1,0:T(8,128)(2,1)S(1)}, bf16[8,128,128]{2,1,0:T(8,128)(2,1)S(1)}, u32[]{:S(2)}, u32[]{:S(2)}) collective-permute-start(bf16[8,128,128]{2,1,0:T(8,128)(2,1)S(1)} %bitcast.61), channel_id=1, source_target_pairs={{8,0},{16,8},{24,16},{32,24},{40,32},{48,40},{56,48},{64,56},{72,6... | collective-permute-start | bytes 786440 | tf_op jit(solution)/shard_map/ppermute | solution.py:525
  180.5 8.0 %copy-start.12 = (bf16[8,128,128]{2,1,0:T(8,128)(2,1)}, bf16[8,128,128]{2,1,0:T(8,128)(2,1)S(1)}, u32[]{:S(2)}) copy-start(bf16[8,128,128]{2,1,0:T(8,128)(2,1)S(1)} %collective-permute-done.24.low) | copy-start | bytes 786436
  188.5 0.7 copy-start.13

commit v9 on v8

--- a/solution.py
+++ b/solution.py
@@ -298,44 +298,41 @@
 
 
 def forward_kernel(table, *refs):
-    parts = refs[:8]
-    context, share, gain, out, expand, shrink, outward, sems = refs[8:]
+    parts = refs[:10]
+    context, share, gain, out, expand, shrink, outward, sems = refs[10:]
     groups = ([], [], [])
     width = expand.shape[3]
+
+    def copy(group, source, target):
+        groups[group].append(
+            pltpu.make_async_copy(source, target, sems.at[group, len(groups[group])])
+        )
+
     for n, part in enumerate(parts):
-        where = table[8 + n]
-        for side in range(2):
-            slot = 1 - side if n % 4 == 3 else side
-
-            def copy(group, source, target):
-                groups[group].append(
-                    pltpu.make_async_copy(source, target, sems.at[group, len(groups[group])])
-                )
-
+        place = table[8 + 4 * (n // 5) + min(n % 5, 3)]
+        pairs = pl.ds(2 if n % 5 == 4 else 0, part.shape[0])
+        swaps = ((0, 1), (1, 0)) if n % 5 >= 3 else ((slice(None), slice(None)),)
+        for side, slot in swaps:
             copy(
                 0,
                 part.at[:, side, pl.ds(ROWS_E + ROWS_S, ROWS_P), :],
                 outward.at[
-                    :, slot, pl.ds(pl.multiple_of(where * ROWS_P, ROWS_P), ROWS_P), :
+                    pairs, slot, pl.ds(pl.multiple_of(place * ROWS_P, ROWS_P), ROWS_P), :
                 ],
             )
             for piece in range(2):
+                start = pl.multiple_of(place * 2 * ROWS_E + piece * ROWS_E, ROWS_E)
                 copy(
                     1,
                     part.at[:, side, pl.ds(0, ROWS_E), pl.ds(piece * width, width)],
-                    expand.at[
-                        :,
-                        slot,
-                        pl.ds(
-                            pl.multiple_of(where * 2 * ROWS_E + piece * ROWS_E, ROWS_E), ROWS_E
-                        ),
-                        :,
-                    ],
+                    expand.at[pairs, slot, pl.ds(start, ROWS_E), :],
                 )
             copy(
                 2,
                 part.at[:, side, pl.ds(ROWS_E, ROWS_S), :],
-                shrink.at[:, slot, pl.ds(pl.multiple_of(where * ROWS_S, ROWS_S), ROWS_S), :],
+                shrink.at[
+                    pairs, slot, pl.ds(pl.multiple_of(place * ROWS_S, ROWS_S), ROWS_S), :
+                ],
             )
     for group in groups:
         for c in group:
@@ -373,7 +370,7 @@
         grid_spec=pltpu.PrefetchScalarGridSpec(
             num_scalar_prefetch=1,
             grid=(1,),
-            in_specs=[ANY] * 8
+            in_specs=[ANY] * 10
             + [whole((8, rows, BLOCK)), whole((8, rows, BLOCK)), whole((1, D))],
             out_specs=whole((8, rows, BLOCK)),
             scratch_shapes=[
@@ -594,7 +591,7 @@
     x, mine = lax.optimization_barrier((mesh_start, mine))
     up, down = UP(mine), DOWN(mine)
     y, xa, xb, mine = lax.optimization_barrier((OVER(x), NORTH(x), SOUTH(x), mine))
-    across = ACROSS(mine)
+    across = ACROSS(mine[:2])
     from_south = NORTH(jnp.concatenate([xa[:half], y]))
     from_north = SOUTH(jnp.concatenate([xb[half:], y]))
     xc = jnp.concatenate([from_south[:half], from_north[:half]])
@@ -604,14 +601,15 @@
         [me, partner] + [(v + by) % 8 for by in (6, 2, 4) for v in (me, partner)]
     ).astype(jnp.int32)
     queries, keys_values, share = project(order, slots, first_gain, inward)
-    upper, lower, up, down = lax.optimization_barrier(
-        (keys_values[mesh_rows - REACH :], keys_values[:REACH], up, down)
-    )
-    below = shifted(upper, 1)
-    above = shifted(lower, -1)
+    upper, lower, up, down, across = lax.optimization_barrier(
+        (keys_values[mesh_rows - REACH :], keys_values[:REACH], up, down, across)
+    )
+    below, above, late = lax.optimization_barrier(
+        (shifted(upper, 1), shifted(lower, -1), mine[2:])
+    )
     edges = jnp.stack([band == 0, band == bands - 1]).astype(jnp.int32)
     context = attend(edges, queries, below, keys_values, above)
-    context, *here = lax.optimization_barrier((context, mine, up, down, across))
+    context, *here = lax.optimization_barrier((context, mine, up, down, across, ACROSS(late)))
     parts = here + [TWIN(v) for v in here]
     context = lax.all_to_all(
         context.reshape(8, mesh_rows // 8, BLOCK), "head", 0, 0, tiled=True

time: 215 us -> 224 us (1.042)
  starting transfers between devices: 44.6 us -> 49.9 us
  waiting for transfers between devices: 66.3 us -> 68.9 us
    ppermute x6, starting transfers between devices: 24.1 us -> 29.4 us  [shifted(): lax.ppermute(value, 'seq', [(i, i + by) for i in range(16) if 0 <= i + by...]
    ppermute x20 -> x22, waiting for transfers between devices: 30.4 us -> 33.3 us  [among(): return lax.ppermute(value, axis, [(i, to(i)) for i in range(count)])]
    ppermute x20 -> x22, starting transfers between devices: 16.4 us -> 16.4 us  [among(): return lax.ppermute(value, axis, [(i, to(i)) for i in range(count)])]
  transfers between devices with their start and end apart: 27 -> 29, of which waited for: 11 -> 14; matrix products, arithmetic and copies ran while one was open for 5% -> 5% of each run, Pallas kernels for 16% -> 16%
where the time goes in v9:
time: 224 us; the launch traced here: 223 us
  waiting for transfers between devices  68.9 us (31%)
  Pallas kernels  61.9 us (28%)
  starting transfers between devices  49.9 us (22%)
  blocking collectives  21.4 us (10%)
  local copies, waits for them, and re-layouts  14.6 us (7%)
  other arithmetic  5.26 us (2%)
    ppermute x22, waiting for transfers between devices, among(): return lax.ppermute(value, axis, [(i, to(i)) for i in range(count)])  33.3 us
    ppermute x6, starting transfers between devices, shifted(): lax.ppermute(value, 'seq', [(i, i + by) for i in range(16) if 0 <= i + by...  29.4 us
    ppermute x6, waiting for transfers between devices, shifted(): lax.ppermute(value, 'seq', [(i, i + by) for i in range(16) if 0 <= i + by...  26.9 us
    pallas_call x1, Pallas kernels, attend(): pl.pallas_call(attend_kernel, out_shape=jax.ShapeDtypeStruct((rows, BLOCK...  19.2 us
    ppermute x22, starting transfers between devices, among(): return lax.ppermute(value, axis, [(i, to(i)) for i in range(count)])  16.4 us
    pallas_call x1, Pallas kernels, forward(): pl.pallas_call(forward_kernel, out_shape=jax.ShapeDtypeStruct((8, rows, B...  12.7 us
    all_to_all x1, blocking collectives, on_device(): mesh_end = lax.all_to_all(mesh_end, 'head', 0, 0, tiled=True)  12.2 us
    all_to_all x1, blocking collectives, on_device(): lax.all_to_all(jnp.broadcast_to(sums, (8, *sums.shape)), 'head', 0, 0, ti...  9.2 us
  transfers between devices with their start and end apart: 29, of which 14 were waited for; matrix products, arithmetic and copies ran while one was open for 5% of the time, Pallas kernels for 16%

profile of v9, /device:TPU:97, one launch (start us, length us, event | category | flops | bytes accessed | tf_op | source)
XLA Modules:
  0.0 222.5 jit_solution(6317745367314940642)
XLA Ops:
  0.0 2.4 %fusion.1 = (bf16[2048,128]{1,0:T(8,128)(2,1)}, bf16[2048,128]{1,0:T(8,128)(2,1)}) fusion(bf16[8192,128]{1,0:T(8,128)(2,1)} %state.1), kind=kLoop, calls=%fused_computation.17 | loop fusion | bytes 2097152 | tf_op jit(solution)/shard_map/slice | solution.py:567
  2.4 0.9 constant_dynamic-slice_fusion
  3.3 0.8 constant_dynamic-slice_fusion.1
  4.1 1.3 collective-permute-start.2
  5.4 1.3 collective-permute-start.3
  6.7 4.1 %collective-permute-start = (bf16[2048,128]{1,0:T(8,128)(2,1)}, bf16[2048,128]{1,0:T(8,128)(2,1)S(1)}, u32[]{:S(2)}, u32[]{:S(2)}) collective-permute-start(bf16[2048,128]{1,0:T(8,128)(2,1)} %get-tuple-element.38), channel_id=1, source_target_pairs={{0,8},{8,16},{16,24},{24,32},{32,40},{40,48},{48,56},{56,64},{64,7... | collective-permute-start | bytes 1572872 | tf_op jit(solution)/shard_map/ppermute | solution.py:522
  10.8 1.9 collective-permute-start.1
  12.7 0.9 fusion.3
  13.7 1.4 collective-permute-start.6
  15.8 2.6 %collective-permute-start.5 = (bf16[144,1024]{1,0:T(8,128)(2,1)S(1)}, bf16[144,1024]{1,0:T(8,128)(2,1)S(1)}, u32[]{:S(2)}, u32[]{:S(2)}) collective-permute-start(bf16[144,1024]{1,0:T(8,128)(2,1)S(1)} %pad_maximum_fusion.4), channel_id=1, source_target_pairs={{0,6},{1,7},{2,0},{3,1},{4,2},{5,3},{6,4},{7,5},{8,14},{9,15},{10,... | collective-permute-start | bytes 884744 | tf_op jit(solution)/shard_map/ppermute | solution.py:526
  18.4 1.0 maximum_bitcast_fusion
  19.5 5.6 %collective-permute-done.1 = bf16[2048,128]{1,0:T(8,128)(2,1)S(1)} collective-permute-done((bf16[2048,128]{1,0:T(8,128)(2,1)}, bf16[2048,128]{1,0:T(8,128)(2,1)S(1)}, u32[]{:S(2)}, u32[]{:S(2)}) %collective-permute-start.1) | collective-permute-done | bytes 524320 | tf_op jit(solution)/shard_map/ppermute | solution.py:522
  25.1 1.4 collective-permute-start.8
  26.5 7.2 %encode.1.s0 = bf16[2048,128]{1,0:T(8,128)(2,1)} custom-call(s32[16,8]{1,0:T(8,128)} %broadcast_subtract_fusion.1.index, bf16[16,128,128]{2,1,0:T(8,128)(2,1)} %bitcast.54, bf16[64,128,128]{2,1,0:T(8,128)(2,1)} %bitcast.47, bf16[16,128,128]{2,1,0:T(8,128)(2,1)} %bitcast.55, bf16[16,8,128,128]{3,2,1,0:T(8,128)(2,1)} %weights.2), custom_call_target="tpu_custom_call" | custom-call | flops 540000000 | bytes 8000000 | tf_op jit(solution)/shard_map/encode/pallas_call | solution.py:84
  33.7 1.0 maximum_bitcast_fusion.1
  35.2 0.7 copy-done.3
  36.7 2.0 collective-permute-start.11
  38.6 1.5 collective-permute-start.16
  40.1 7.9 %collective-permute-done.10.s2 = bf16[2048,128]{1,0:T(8,128)(2,1)S(1)} collective-permute-done((bf16[2048,128]{1,0:T(8,128)(2,1)S(1)}, bf16[2048,128]{1,0:T(8,128)(2,1)S(1)}, u32[]{:S(2)}, u32[]{:S(2)}) %collective-permute-start.10) | collective-permute-done | bytes 524320 | tf_op jit(solution)/shard_map/ppermute | solution.py:526
  49.1 0.9 collective-permute-start.12
  50.0 1.8 collective-permute-start.13
  51.8 1.7 fusion
  53.9 11.5 %collective-permute-done.12.s3 = bf16[3072,128]{1,0:T(8,128)(2,1)S(1)} collective-permute-done((bf16[3072,128]{1,0:T(8,128)(2,1)S(1)}, bf16[3072,128]{1,0:T(8,128)(2,1)S(1)}, u32[]{:S(2)}, u32[]{:S(2)}) %collective-permute-start.12) | collective-permute-done | bytes 786464 | tf_op jit(solution)/shard_map/ppermute | solution.py:526
  65.4 0.9 copy-done.5
  66.3 0.9 copy-done.6
  67.2 0.8 pad_maximum_fusion.3.s6
  68.8 8.1 %collective-permute-done.14.s7 = bf16[2048,128]{1,0:T(8,128)(2,1)} collective-permute-done((bf16[2048,128]{1,0:T(8,128)(2,1)}, bf16[2048,128]{1,0:T(8,128)(2,1)}, u32[]{:S(2)}, u32[]{:S(2)}) %collective-permute-start.14) | collective-permute-done | bytes 524320 | tf_op jit(solution)/shard_map/ppermute | solution.py:526
  76.9 8.6 %project.1 = (bf16[2048,128]{1,0:T(8,128)(2,1)}, bf16[2048,256]{1,0:T(8,128)(2,1)}, bf16[8,256,128]{2,1,0:T(8,128)(2,1)}) custom-call(s32[8]{0:T(128)} %stack.130.order, bf16[2048,128]{1,0:T(8,128)(2,1)} %encode.1.s0, bf16[2048,128]{1,0:T(8,128)(2,1)} %copy-done.4, bf16[2048,128]{1,0:T(8,128)(2,1)} %copy-done.7, bf16[3072,128]{1,0:T(8,128)(2,1)} %copy-done.5, ...), custom_call_target="tpu_custom_call" | custom-call | tf_op jit(solution)/shard_map/project/pallas_call | solution.py:153
  85.5 1.3 fusion.2
  86.9 1.1 collective-permute-done.16.refs_2_
  88.0 10.2 %collective-permute-start.18 = (bf16[1152,256]{1,0:T(8,128)(2,1)S(1)}, bf16[1152,256]{1,0:T(8,128)(2,1)}, u32[]{:S(2)}, u32[]{:S(2)}) collective-permute-start(bf16[1152,256]{1,0:T(8,128)(2,1)S(1)} %get-tuple-element.54), channel_id=1, source_target_pairs={{0,8},{8,16},{16,24},{24,32},{32,40},{40,48},{48,56},{56,64},{64,7... | collective-permute-start | bytes 1769480 | tf_op jit(solution)/shard_map/ppermute | solution.py:522
  98.2 1.9 collective-permute-start.19
  100.1 4.9 %collective-permute-done.18.low = bf16[1152,256]{1,0:T(8,128)(2,1)} collective-permute-done((bf16[1152,256]{1,0:T(8,128)(2,1)S(1)}, bf16[1152,256]{1,0:T(8,128)(2,1)}, u32[]{:S(2)}, u32[]{:S(2)}) %collective-permute-start.18) | collective-permute-done | bytes 589856 | tf_op jit(solution)/shard_map/ppermute | solution.py:522
  105.0 8.0 %collective-permute-done.19.high = bf16[1152,256]{1,0:T(8,128)(2,1)S(1)} collective-permute-done((bf16[1152,256]{1,0:T(8,128)(2,1)S(1)}, bf16[1152,256]{1,0:T(8,128)(2,1)S(1)}, u32[]{:S(2)}, u32[]{:S(2)}) %collective-permute-start.19) | collective-permute-done | bytes 589856 | tf_op jit(solution)/shard_map/ppermute | solution.py:522
  113.0 0.9 copy-done.10
  114.5 19.2 %attend.1 = bf16[2048,128]{1,0:T(8,128)(2,1)} custom-call(s32[2]{0:T(128)} %add_convert_fusion.edges, bf16[2048,128]{1,0:T(8,128)(2,1)} %get-tuple-element.51.queries, bf16[1152,256]{1,0:T(8,128)(2,1)} %collective-permute-done.18.low, bf16[2048,256]{1,0:T(8,128)(2,1)} %get-tuple-element.52.own, bf16[1152,256]{1,0:T(8,128)(2,1)} %copy-done.10), custom_call_target="tpu_custom_call" | custom-call | tf_op jit(solution)/shard_map/attend/pallas_call | solution.py:257
  133.7 3.4 %collective-permute-done.20.refs_4_ = bf16[2,2,144,1024]{3,2,1,0:T(8,128)(2,1)} collective-permute-done((bf16[2,2,144,1024]{3,2,1,0:T(8,128)(2,1)}, bf16[2,2,144,1024]{3,2,1,0:T(8,128)(2,1)}, u32[]{:S(2)}, u32[]{:S(2)}) %collective-permute-start.20) | collective-permute-done | bytes 1179680 | tf_op jit(solution)/shard_map/ppermute | solution.py:526
  138.1 4.1 %all-to-all-start = ((bf16[8,256,128]{2,1,0:T(8,128)(2,1)}), bf16[8,256,128]{2,1,0:T(8,128)(2,1)}, u32[]{:S(2)}, u32[]{:S(2)}) async-start(bf16[8,256,128]{2,1,0:T(8,128)(2,1)} %bitcast.49), calls=%async_computation | async-start | bytes 1048576 | tf_op jit(solution)/shard_map/all_to_all | solution.py:614
  143.0 8.6 %all-to-all-done.refs_10_ = bf16[8,256,128]{2,1,0:T(8,128)(2,1)} async-done(((bf16[8,256,128]{2,1,0:T(8,128)(2,1)}), bf16[8,256,128]{2,1,0:T(8,128)(2,1)}, u32[]{:S(2)}, u32[]{:S(2)}) %all-to-all-start) | async-done | bytes 524320 | tf_op jit(solution)/shard_map/all_to_all | solution.py:614
  152.1 12.7 %forward.1 = bf16[8,256,128]{2,1,0:T(8,128)(2,1)} custom-call(s32[16]{0:T(128)} %concatenate.19.table, bf16[4,2,144,1024]{3,2,1,0:T(8,128)(2,1)} %copy-done.1, bf16[4,2,144,1024]{3,2,1,0:T(8,128)(2,1)} %collective-permute-done.15.refs_1_, bf16[4,2,144,1024]{3,2,1,0:T(8,128)(2,1)} %collective-permute-done.16.refs_2_, ...), custom_call_target="tpu_custom_call" | custom-call | flops 4800000000 | bytes 20000000 | tf_op jit(solution)/shard_map/forward/pallas_call | solution.py:367
  164.8 12.2 %all_to_all.15 = bf16[8,256,128]{2,1,0:T(8,128)(2,1)S(1)} all-to-all(bf16[8,256,128]{2,1,0:T(8,128)(2,1)} %forward.1), channel_id=1, replica_groups=mesh['seq'=16,'head'=8] {'head'}, dimensions={0} | all-to-all | bytes 1048576 | tf_op jit(solution)/shard_map/all_to_all | solution.py:622
  177.1 9.1 %collective-permute-start.26 = (bf16[8,128,128]{2,1,0:T(8,128)(2,1)S(1)}, bf16[8,128,128]{2,1,0:T(8,128)(2,1)S(1)}, u32[]{:S(2)}, u32[]{:S(2)}) collective-permute-start(bf16[8,128,128]{2,1,0:T(8,128)(2,1)S(1)} %bitcast.62), channel_id=1, source_target_pairs={{0,8},{8,16},{16,24},{24,32},{32,40},{40,48},{48,56},{56,64},{64,7... | collective-permute-start | bytes 786440 | tf_op jit(solution)/shard_map/ppermute | solution.py:522
  186.2 2.1 collective-permute-start.27
  189.5 8.0 %collective-permute-done.27.high = bf16[8,128,128]{2,1,0:T(8,128)(2,1)S(1)} collective-permute-done((bf16[8,128,128]{2,1,0:T(8,128)(2,1)S(1)}, bf16[8,128,128]{2,1,0:T(8,128)(2,1)S(1)}, u32[]{:S(2)}, u32[]{:S(2)}) %collective-permute-start.27) | collective-permute-done | bytes 262176 | tf_op jit(solution)/shard_map/ppermute | solution.py:522
  198.2 8.0 %decode.1 = (bf16[8192,128]{1,0:T(8,128)(2,1)}, bf16[8,16,128]{2,1,0:T(8,128)(2,1)}) custom-call(s32[64,2]{1,0:T(8,128)} %broadcast_subtract_fusion.index, bf16[8,128,128]{2,1,0:T(8,128)(2,1)} %copy-done.13, bf16[16,128,128]{2,1,0:T(8,128)(2,1)} %bitcast.48, bf16[8,128,128]{2,1,0:T(8,128)(2,1)} %copy-done.14, bf16[64,2,128,128]{3,2,1,0:T(8,128)(2,1)} %weights.3), custom_call_target="tpu_custom_call" | custom-call | flops 540000000 | bytes 10000000 | tf_op jit(solution)/shard_map/decode/pallas_call | solution.py:436
  206.3 0.8 broadcast_in_dim.3
  207.1 9.2 %all_to_all.16.sums = bf16[8,8,16,128]{3,2,1,0:T(8,128)(2,1)} all-to-all(bf16[8,8,16,128]{3,2,1,0:T(8,128)(2,1)S(1)} %broadcast_in_dim.3), channel_id=1, replica_groups=mesh['seq'=16,'head'=8] {'head'}, dimensions={0} | all-to-all | bytes 524288 | tf_op jit(solution)/shard_map/all_to_all | solution.py:632
  216.3 6.1 %finish.1 = bf16[8192,128]{1,0:T(8,128)(2,1)} custom-call(bf16[8,8,16,128]{3,2,1,0:T(8,128)(2,1)} %all_to_all.16.sums, bf16[8192,128]{1,0:T(8,128)(2,1)} %get-tuple-element.70.back, bf16[8192,128]{1,0:T(8,128)(2,1)} %state.1, f32[1,128]{1,0:T(1,128)} %bitcast.65), custom_call_target="tpu_custom_call" | custom-call | flops 540000000 | bytes 8000000 | tf_op jit(solution)/shard_map/finish/pallas_call | solution.py:500
  (80 shorter events, 8.8 us)
Async XLA Ops:
  0.0 3.3 %copy-start = (bf16[512,1024]{1,0:T(8,128)(2,1)S(1)}, bf16[512,1024]{1,0:T(8,128)(2,1)}, u32[]{:S(2)}) copy-start(bf16[512,1024]{1,0:T(8,128)(2,1)} %param.20) | copy-start | bytes 3145732
  0.0 12.7 %copy-start.9 = (bf16[1024,3,128]{2,0,1:T(8,128)(2,1)S(1)}, bf16[1024,3,128]{2,0,1:T(8,128)(2,1)}, u32[]{:S(2)}) copy-start(bf16[1024,3,128]{2,0,1:T(8,128)(2,1)} %param.16) | copy-start | bytes 2359300
  0.0 13.7 %copy-start.15 = (s32[16,8]{0,1:T(8,128)S(1)}, s32[16,8]{0,1:T(8,128)}, u32[]{:S(2)}) copy-start(s32[16,8]{0,1:T(8,128)} %param.13) | copy-start | bytes 1540
  4.1 9.6 %collective-permute-start.2 = (bf16[144,1024]{1,0:T(8,128)(2,1)S(1)}, bf16[144,1024]{1,0:T(8,128)(2,1)}, u32[]{:S(2)}, u32[]{:S(2)}) collective-permute-start(bf16[144,1024]{1,0:T(8,128)(2,1)S(1)} %pad_maximum_fusion.4), channel_id=1, source_target_pairs={{0,1},{1,0},{2,3},{3,2},{4,5},{5,4},{6,7},{7,6},{8,9},{9,8},{10,11... | collective-permute-start | bytes 884744 | tf_op jit(solution)/shard_map/ppermute | solution.py:526
  5.4 10.4 %collective-permute-start.3 = (bf16[144,1024]{1,0:T(8,128)(2,1)S(1)}, bf16[144,1024]{1,0:T(8,128)(2,1)}, u32[]{:S(2)}, u32[]{:S(2)}) collective-permute-start(bf16[144,1024]{1,0:T(8,128)(2,1)S(1)} %pad_maximum_fusion.4), channel_id=1, source_target_pairs={{0,2},{1,3},{2,4},{3,5},{4,6},{5,7},{6,0},{7,1},{8,10},{9,11},{10,... | collective-permute-start | bytes 884744 | tf_op jit(solution)/shard_map/ppermute | solution.py:526
  6.7 12.7 %collective-permute-start = (bf16[2048,128]{1,0:T(8,128)(2,1)}, bf16[2048,128]{1,0:T(8,128)(2,1)S(1)}, u32[]{:S(2)}, u32[]{:S(2)}) collective-permute-start(bf16[2048,128]{1,0:T(8,128)(2,1)} %get-tuple-element.38), channel_id=1, source_target_pairs={{0,8},{8,16},{16,24},{24,32},{32,40},{40,48},{48,56},{56,64},{64,7... | collective-permute-start | bytes 1572872 | tf_op jit(solution)/shard_map/ppermute | solution.py:522
  10.8 14.3 %collective-permute-start.1 = (bf16[2048,128]{1,0:T(8,128)(2,1)}, bf16[2048,128]{1,0:T(8,128)(2,1)S(1)}, u32[]{:S(2)}, u32[]{:S(2)}) collective-permute-start(bf16[2048,128]{1,0:T(8,128)(2,1)} %get-tuple-element.39), channel_id=1, source_target_pairs={{8,0},{16,8},{24,16},{32,24},{40,32},{48,40},{56,48},{64,56},{72,6... | collective-permute-start | bytes 1572872 | tf_op jit(solution)/shard_map/ppermute | solution.py:522
  13.7 11.4 %collective-permute-start.6 = (bf16[144,1024]{1,0:T(8,128)(2,1)}, bf16[144,1024]{1,0:T(8,128)(2,1)S(1)}, u32[]{:S(2)}, u32[]{:S(2)}) collective-permute-start(bf16[144,1024]{1,0:T(8,128)(2,1)} %collective-permute-done.2), channel_id=1, source_target_pairs={{0,6},{1,7},{2,0},{3,1},{4,2},{5,3},{6,4},{7,5},{8,14},{9,15},{10,... | collective-permute-start | bytes 884744 | tf_op jit(solution)/shard_map/ppermute | solution.py:526
  15.1 18.6 %collective-permute-start.4 = (bf16[144,1024]{1,0:T(8,128)(2,1)}, bf16[144,1024]{1,0:T(8,128)(2,1)S(1)}, u32[]{:S(2)}, u32[]{:S(2)}) collective-permute-start(bf16[144,1024]{1,0:T(8,128)(2,1)} %collective-permute-done.2), channel_id=1, source_target_pairs={{0,2},{1,3},{2,4},{3,5},{4,6},{5,7},{6,0},{7,1},{8,10},{9,11},{10,... | collective-permute-start | bytes 884744 | tf_op jit(solution)/shard_map/ppermute | solution.py:526
  15.8 19.0 %collective-permute-start.5 = (bf16[144,1024]{1,0:T(8,128)(2,1)S(1)}, bf16[144,1024]{1,0:T(8,128)(2,1)S(1)}, u32[]{:S(2)}, u32[]{:S(2)}) collective-permute-start(bf16[144,1024]{1,0:T(8,128)(2,1)S(1)} %pad_maximum_fusion.4), channel_id=1, source_target_pairs={{0,6},{1,7},{2,0},{3,1},{4,2},{5,3},{6,4},{7,5},{8,14},{9,15},{10,... | collective-permute-start | bytes 884744 | tf_op jit(solution)/shard_map/ppermute | solution.py:526
  19.4 7.1 %copy-start.11 = (bf16[2048,128]{1,0:T(8,128)(2,1)}, bf16[2048,128]{1,0:T(8,128)(2,1)S(1)}, u32[]{:S(2)}) copy-start(bf16[2048,128]{1,0:T(8,128)(2,1)S(1)} %collective-permute-done) | copy-start | bytes 1572868
  19.4 15.4 %collective-permute-start.7 = (bf16[144,1024]{1,0:T(8,128)(2,1)}, bf16[144,1024]{1,0:T(8,128)(2,1)S(1)}, u32[]{:S(2)}, u32[]{:S(2)}) collective-permute-start(bf16[144,1024]{1,0:T(8,128)(2,1)} %collective-permute-done.3), channel_id=1, source_target_pairs={{0,2},{1,3},{2,4},{3,5},{4,6},{5,7},{6,0},{7,1},{8,10},{9,11},{10,... | collective-permute-start | bytes 884744 | tf_op jit(solution)/shard_map/ppermute | solution.py:526
  25.1 1.4 copy-start.12
  25.1 9.7 %collective-permute-start.8 = (bf16[144,1024]{1,0:T(8,128)(2,1)S(1)}, bf16[144,1024]{1,0:T(8,128)(2,1)S(1)}, u32[]{:S(2)}, u32[]{:S(2)}) collective-permute-start(bf16[144,1024]{1,0:T(8,128)(2,1)S(1)} %collective-permute-done.6), channel_id=1, source_target_pairs={{0,6},{1,7},{2,0},{3,1},{4,2},{5,3},{6,4},{7,5},{8,14},{9,15},{10,... | collective-permute-start | bytes 884744 | tf_op jit(solution)/shard_map/ppermute | solution.py:526
  34.9 1.0 copy-start.3
  36.0 101.2 %copy-start.1 = (bf16[4,2,144,1024]{3,2,1,0:T(8,128)(2,1)}, bf16[4,2,144,1024]{3,2,1,0:T(8,128)(2,1)S(1)}, u32[]{:S(2)}) copy-start(bf16[4,2,144,1024]{3,2,1,0:T(8,128)(2,1)S(1)} %pad_maximum_fusion.refs_0_) | copy-start | bytes 7077892
  36.0 12.0 %collective-permute-start.10 = (bf16[2048,128]{1,0:T(8,128)(2,1)S(1)}, bf16[2048,128]{1,0:T(8,128)(2,1)S(1)}, u32[]{:S(2)}, u32[]{:S(2)}) collective-permute-start(bf16[2048,128]{1,0:T(8,128)(2,1)S(1)} %copy-done.3), channel_id=1, source_target_pairs={{0,2},{1,3},{2,4},{3,5},{4,6},{5,7},{6,0},{7,1},{8,10},{9,11},{10,... | collective-permute-start | bytes 1572872 | tf_op jit(solution)/shard_map/ppermute | solution.py:526
  36.7 11.5 %collective-permute-start.11 = (bf16[2048,128]{1,0:T(8,128)(2,1)S(1)}, bf16[2048,128]{1,0:T(8,128)(2,1)S(1)}, u32[]{:S(2)}, u32[]{:S(2)}) collective-permute-start(bf16[2048,128]{1,0:T(8,128)(2,1)S(1)} %copy-done.3), channel_id=1, source_target_pairs={{0,6},{1,7},{2,0},{3,1},{4,2},{5,3},{6,4},{7,5},{8,14},{9,15},{10,... | collective-permute-start | bytes 1572872 | tf_op jit(solution)/shard_map/ppermute | solution.py:526
  38.6 10.2 %collective-permute-start.9 = (bf16[2048,128]{1,0:T(8,128)(2,1)S(1)}, bf16[2048,128]{1,0:T(8,128)(2,1)S(1)}, u32[]{:S(2)}, u32[]{:S(2)}) collective-permute-start(bf16[2048,128]{1,0:T(8,128)(2,1)S(1)} %copy-done.3), channel_id=1, source_target_pairs={{0,1},{1,0},{2,3},{3,2},{4,5},{5,4},{6,7},{7,6},{8,9},{9,8},{10,11... | collective-permute-start | bytes 1572872 | tf_op jit(solution)/shard_map/ppermute | solution.py:526
  38.6 48.2 %collective-permute-start.15 = (bf16[4,2,144,1024]{3,2,1,0:T(8,128)(2,1)S(1)}, bf16[4,2,144,1024]{3,2,1,0:T(8,128)(2,1)}, u32[]{:S(2)}, u32[]{:S(2)}) collective-permute-start(bf16[4,2,144,1024]{3,2,1,0:T(8,128)(2,1)S(1)} %pad_maximum_fusion.refs_0_), channel_id=1, source_target_pairs={{0,16},{8,24},{16,32},{24,40},{32,48},{40,56},{48,0},{56,8},{64,80... | collective-permute-start | bytes 7077896 | tf_op jit(solution)/shard_map/ppermute | solution.py:526
  38.6 49.3 %collective-permute-start.16 = (bf16[4,2,144,1024]{3,2,1,0:T(8,128)(2,1)S(1)}, bf16[4,2,144,1024]{3,2,1,0:T(8,128)(2,1)}, u32[]{:S(2)}, u32[]{:S(2)}) collective-permute-start(bf16[4,2,144,1024]{3,2,1,0:T(8,128)(2,1)S(1)} %pad_maximum_fusion.refs_0_), channel_id=1, source_target_pairs={{0,48},{8,56},{16,0},{24,8},{32,16},{40,24},{48,32},{56,40},{64,11... | collective-permute-start | bytes 7077896 | tf_op jit(solution)/shard_map/ppermute | solution.py:526
  48.0 1.1 copy-start.7
  48.2 0.9 copy-start.8
  48.9 4.6 %copy-start.4 = (bf16[2048,128]{1,0:T(8,128)(2,1)}, bf16[2048,128]{1,0:T(8,128)(2,1)S(1)}, u32[]{:S(2)}) copy-start(bf16[2048,128]{1,0:T(8,128)(2,1)S(1)} %collective-permute-done.9.s1) | copy-start | bytes 1572868
  49.1 16.3 %collective-permute-start.12 = (bf16[3072,128]{1,0:T(8,128)(2,1)S(1)}, bf16[3072,128]{1,0:T(8,128)(2,1)S(1)}, u32[]{:S(2)}, u32[]{:S(2)}) collective-permute-start(bf16[3072,128]{1,0:T(8,128)(2,1)S(1)} %get-tuple-element.85), channel_id=1, source_target_pairs={{0,2},{1,3},{2,4},{3,5},{4,6},{5,7},{6,0},{7,1},{8,10},{9,11},{10,... | collective-permute-start | bytes 2359304 | tf_op jit(solution)/shard_map/ppermute | solution.py:526
  50.0 16.3 %collective-permute-start.13 = (bf16[3072,128]{1,0:T(8,128)(2,1)S(1)}, bf16[3072,128]{1,0:T(8,128)(2,1)S(1)}, u32[]{:S(2)}, u32[]{:S(2)}) collective-permute-start(bf16[3072,128]{1,0:T(8,128)(2,1)S(1)} %get-tuple-element.84), channel_id=1, source_target_pairs={{0,6},{1,7},{2,0},{3,1},{4,2},{5,3},{6,4},{7,5},{8,14},{9,15},{10,... | collective-permute-start | bytes 2359304 | tf_op jit(solution)/shard_map/ppermute | solution.py:526
  53.5 33.3 %collective-permute-start.17 = (bf16[2,2,144,1024]{3,2,1,0:T(8,128)(2,1)}, bf16[2,2,144,1024]{3,2,1,0:T(8,128)(2,1)}, u32[]{:S(2)}, u32[]{:S(2)}) collective-permute-start(bf16[2,2,144,1024]{3,2,1,0:T(8,128)(2,1)} %get-tuple-element.72), channel_id=1, source_target_pairs={{0,65},{1,64},{2,67},{3,66},{4,69},{5,68},{6,71},{7,70},{8,73},{9,... | collective-permute-start | bytes 3538952 | tf_op jit(solution)/shard_map/ppermute | solution.py:526
  65.4 0.9 copy-start.5
  66.3 0.9 copy-start.6
  68.1 8.8 %collective-permute-start.14 = (bf16[2048,128]{1,0:T(8,128)(2,1)}, bf16[2048,128]{1,0:T(8,128)(2,1)}, u32[]{:S(2)}, u32[]{:S(2)}) collective-permute-start(bf16[2048,128]{1,0:T(8,128)(2,1)} %pad_maximum_fusion.3.s6), channel_id=1, source_target_pairs={{0,1},{1,0},{2,3},{3,2},{4,5},{5,4},{6,7},{7,6},{8,9},{9,8},{10,11... | collective-permute-start | bytes 1572872 | tf_op jit(solution)/shard_map/ppermute | solution.py:526
  88.0 17.0 %collective-permute-start.18 = (bf16[1152,256]{1,0:T(8,128)(2,1)S(1)}, bf16[1152,256]{1,0:T(8,128)(2,1)}, u32[]{:S(2)}, u32[]{:S(2)}) collective-permute-start(bf16[1152,256]{1,0:T(8,128)(2,1)S(1)} %get-tuple-element.54), channel_id=1, source_target_pairs={{0,8},{8,16},{16,24},{24,32},{32,40},{40,48},{48,56},{56,64},{64,7... | collective-permute-start | bytes 1769480 | tf_op jit(solution)/shard_map/ppermute | solution.py:522
  98.2 14.8 %collective-permute-start.19 = (bf16[1152,256]{1,0:T(8,128)(2,1)S(1)}, bf16[1152,256]{1,0:T(8,128)(2,1)S(1)}, u32[]{:S(2)}, u32[]{:S(2)}) collective-permute-start(bf16[1152,256]{1,0:T(8,128)(2,1)S(1)} %get-tuple-element.55), channel_id=1, source_target_pairs={{8,0},{16,8},{24,16},{32,24},{40,32},{48,40},{56,48},{64,56},{72,6... | collective-permute-start | bytes 1769480 | tf_op jit(solution)/shard_map/ppermute | solution.py:522
  113.0 0.9 copy-start.10
  113.8 23.3 %collective-permute-start.20 = (bf16[2,2,144,1024]{3,2,1,0:T(8,128)(2,1)}, bf16[2,2,144,1024]{3,2,1,0:T(8,128)(2,1)}, u32[]{:S(2)}, u32[]{:S(2)}) collective-permute-start(bf16[2,2,144,1024]{3,2,1,0:T(8,128)(2,1)} %get-tuple-element.61), channel_id=1, source_target_pairs={{0,65},{1,64},{2,67},{3,66},{4,69},{5,68},{6,71},{7,70},{8,73},{9,... | collective-permute-start | bytes 3538952 | tf_op jit(solution)/shard_map/ppermute | solution.py:526
  137.1 15.0 %collective-permute-start.21 = (bf16[4,2,144,1024]{3,2,1,0:T(8,128)(2,1)S(1)}, bf16[4,2,144,1024]{3,2,1,0:T(8,128)(2,1)}, u32[]{:S(2)}, u32[]{:S(2)}) collective-permute-start(bf16[4,2,144,1024]{3,2,1,0:T(8,128)(2,1)S(1)} %pad_maximum_fusion.refs_0_), channel_id=1, source_target_pairs={{0,8},{8,0},{16,24},{24,16},{32,40},{40,32},{48,56},{56,48},{64,72... | collective-permute-start | bytes 7077896 | tf_op jit(solution)/shard_map/ppermute | solution.py:526
  137.1 15.0 %collective-permute-start.22 = (bf16[4,2,144,1024]{3,2,1,0:T(8,128)(2,1)}, bf16[4,2,144,1024]{3,2,1,0:T(8,128)(2,1)}, u32[]{:S(2)}, u32[]{:S(2)}) collective-permute-start(bf16[4,2,144,1024]{3,2,1,0:T(8,128)(2,1)} %collective-permute-done.15.refs_1_), channel_id=1, source_target_pairs={{0,8},{8,0},{16,24},{24,16},{32,40},{40,32},{48,56},{56,48},{64,72... | collective-permute-start | bytes 7077896 | tf_op jit(solution)/shard_map/ppermute | solution.py:526
  137.6 14.5 %collective-permute-start.23 = (bf16[4,2,144,1024]{3,2,1,0:T(8,128)(2,1)}, bf16[4,2,144,1024]{3,2,1,0:T(8,128)(2,1)}, u32[]{:S(2)}, u32[]{:S(2)}) collective-permute-start(bf16[4,2,144,1024]{3,2,1,0:T(8,128)(2,1)} %collective-permute-done.16.refs_2_), channel_id=1, source_target_pairs={{0,8},{8,0},{16,24},{24,16},{32,40},{40,32},{48,56},{56,48},{64,72... | collective-permute-start | bytes 7077896 | tf_op jit(solution)/shard_map/ppermute | solution.py:526
  137.6 14.1 %collective-permute-start.24 = (bf16[2,2,144,1024]{3,2,1,0:T(8,128)(2,1)}, bf16[2,2,144,1024]{3,2,1,0:T(8,128)(2,1)}, u32[]{:S(2)}, u32[]{:S(2)}) collective-permute-start(bf16[2,2,144,1024]{3,2,1,0:T(8,128)(2,1)} %collective-permute-done.17.refs_3_), channel_id=1, source_target_pairs={{0,8},{8,0},{16,24},{24,16},{32,40},{40,32},{48,56},{56,48},{64,72... | collective-permute-start | bytes 3538952 | tf_op jit(solution)/shard_map/ppermute | solution.py:526
  138.1 14.0 %collective-permute-start.25 = (bf16[2,2,144,1024]{3,2,1,0:T(8,128)(2,1)}, bf16[2,2,144,1024]{3,2,1,0:T(8,128)(2,1)}, u32[]{:S(2)}, u32[]{:S(2)}) collective-permute-start(bf16[2,2,144,1024]{3,2,1,0:T(8,128)(2,1)} %collective-permute-done.20.refs_4_), channel_id=1, source_target_pairs={{0,8},{8,0},{16,24},{24,16},{32,40},{40,32},{48,56},{56,48},{64,72... | collective-permute-start | bytes 3538952 | tf_op jit(solution)/shard_map/ppermute | solution.py:526
  138.1 13.5 %all-to-all-start = ((bf16[8,256,128]{2,1,0:T(8,128)(2,1)}), bf16[8,256,128]{2,1,0:T(8,128)(2,1)}, u32[]{:S(2)}, u32[]{:S(2)}) async-start(bf16[8,256,128]{2,1,0:T(8,128)(2,1)} %bitcast.49), calls=%async_computation | async-start | bytes 1048576 | tf_op jit(solution)/shard_map/all_to_all | solution.py:614
  164.8 23.6 %copy-start.16 = (s32[64,2]{0,1:T(2,128)S(1)}, s32[64,2]{0,1:T(2,128)}, u32[]{:S(2)}) copy-start(s32[64,2]{0,1:T(2,128)} %param.21) | copy-start | bytes 1540
  177.0 20.5 %copy-start.2 = (bf16[8,256,128]{2,1,0:T(8,128)(2,1)}, bf16[8,256,128]{2,1,0:T(8,128)(2,1)S(1)}, u32[]{:S(2)}) copy-start(bf16[8,256,128]{2,1,0:T(8,128)(2,1)S(1)} %all_to_all.15) | copy-start | bytes 1572868
  177.1 12.4 %collective-permute-start.26 = (bf16[8,128,128]{2,1,0:T(8,128)(2,1)S(1)}, bf16[8,128,128]{2,1,0:T(8,128)(2,1)S(1)}, u32[]{:S(2)}, u32[]{:S(2)}) collective-permute-start(bf16[8,128,128]{2,1,0:T(8,128)(2,1)S(1)} %bitcast.62), channel_id=1, source_target_pairs={{0,8},{8,16},{16,24},{24,32},{32,40},{40,48},{48,56},{56,64},{64,7... | collective-permute-start | bytes 786440 | tf_op jit(solution)/shard_map/ppermute | solution.py:522
  186.2 11.3 %collective-permute-start.27 = (bf16[8,128,128]{2,1,0:T(8,128)(2,1)S(1)}, bf16[8,128,128]{2,1,0:T(8,128)(2,1)S(1)}, u32[]{:S(2)}, u32[]{:S(2)}) collective-permute-start(bf16[8,128,128]{2,1,0:T(8,128)(2,1)S(1)} %bitcast.61), channel_id=1, source_target_pairs={{8,0},{16,8},{24,16},{32,24},{40,32},{48,40},{56,48},{64,56},{72,6... | collective-permute-start | bytes 786440 | tf_op jit(solution)/shard_map/ppermute | solution.py:522
  189.5 8.0 %copy-start.13 = (bf16[8,128,128]{2,1,0:T(8,128)(2,1)}, bf16[8,128,128]{2,1,0:T(8,128)(2,1)S(1)}, u32[]{:S(2)}) copy-start(bf16[8,128,128]{2,1,0:T(8,128)(2,1)S(1)} %collective-permute-done.26.low) | copy-start | bytes 786436
  197.5 0.7 copy-start.14

commit v10 on v8

--- a/solution.py
+++ b/solution.py
@@ -66,7 +66,9 @@
     for c in ahead:
         c.wait()
     for b in range(count):
-        blocks[b].wait()
+        if b % 4 == 0:
+            for c in blocks[b : b + 4]:
+                c.wait()
         left = jnp.concatenate([held[b, k] for k in range(slots)], axis=1)
         right = jnp.concatenate([source[index[b, k]] for k in range(slots)], axis=0)
         made[b * BLOCK : (b + 1) * BLOCK] = dot(left, right).astype(BF)
@@ -104,7 +106,7 @@
 
 def project_kernel(
     order, s0, s1, s2, s3, s4, s5, s6, s7, gain, wq, wk, wv,
-    queries, keys_values, share, ordered,
+    queries, keys_values, share, ordered, normed,
 ):
     step = pl.program_id(0)
 
@@ -115,31 +117,33 @@
                 [w[order[p]] for w in (wq, wk, wv)], axis=1
             )
 
-    raw = [s[...] for s in (s0, s1, s2, s3, s4, s5, s6, s7)]
-
+    slots = (s0, s1, s2, s3, s4, s5, s6, s7)
+    rows = s0.shape[0]
     tile = share.shape[1]
-    per = raw[0].shape[0] // tile
-    for n in range(per):
-
-        @pl.when(order[0] == step * per + n)
+    for n in range(rows // tile):
+
+        @pl.when(order[0] == step * (rows // tile) + n)
         def _():
             for p in range(8):
-                share[order[p]] = raw[p][n * tile : (n + 1) * tile]
-
-    pieces = [r.astype(F32) for r in raw]
-    total = pieces[0]
-    for x in pieces[1:]:
-        total = total + x
-    average = jnp.sum(total, axis=1, keepdims=True) * (1.0 / D)
-    pieces = [x - average for x in pieces]
-    total = pieces[0] * pieces[0]
-    for x in pieces[1:]:
-        total = total + x * x
-    spread = lax.rsqrt(jnp.sum(total, axis=1, keepdims=True) * (1.0 / D) + EPSILON)
-    normed = jnp.concatenate(
-        [(x * spread * gain[order[p]]).astype(BF) for p, x in enumerate(pieces)], axis=1
-    )
-    made = dot(normed, ordered[...])
+                share[order[p]] = slots[p][n * tile : (n + 1) * tile]
+
+    gains = [gain[order[p]] for p in range(8)]
+    few = 32
+    for n in range(rows // few):
+        at = slice(n * few, (n + 1) * few)
+        pieces = [s[at].astype(F32) for s in slots]
+        total = pieces[0]
+        for x in pieces[1:]:
+            total = total + x
+        average = jnp.sum(total, axis=1, keepdims=True) * (1.0 / D)
+        pieces = [x - average for x in pieces]
+        total = pieces[0] * pieces[0]
+        for x in pieces[1:]:
+            total = total + x * x
+        spread = lax.rsqrt(jnp.sum(total, axis=1, keepdims=True) * (1.0 / D) + EPSILON)
+        for p, x in enumerate(pieces):
+            normed[at, p * BLOCK : (p + 1) * BLOCK] = (x * spread * gains[p]).astype(BF)
+    made = dot(normed[...], ordered[...])
     queries[...] = (made[:, :BLOCK] * (HEAD_DIM**-0.5 * LOG2E)).astype(BF)
     keys_values[...] = made[:, BLOCK:].astype(BF)
 
@@ -168,7 +172,7 @@
                 pl.BlockSpec((each, 2 * BLOCK), lambda i, _: (i, 0)),
                 whole((8, tile, BLOCK)),
             ),
-            scratch_shapes=[pltpu.VMEM((D, 3 * BLOCK), BF)],
+            scratch_shapes=[pltpu.VMEM((D, 3 * BLOCK), BF), pltpu.VMEM((each, D), BF)],
         ),
         compiler_params=params(56),
         name="project",

time: 215 us -> 215 us (level)
  waiting for transfers between devices: 66.3 us -> 69.6 us
    ppermute x20, waiting for transfers between devices: 30.4 us -> 33.5 us  [among(): return lax.ppermute(value, axis, [(i, to(i)) for i in range(count)])]
where the time goes in v10:
time: 215 us; the launch traced here: 214 us
  waiting for transfers between devices  69.6 us (32%)
  Pallas kernels  60.1 us (28%)
  starting transfers between devices  43.4 us (20%)
  blocking collectives  21.9 us (10%)
  local copies, waits for them, and re-layouts  12.9 us (6%)
  other arithmetic  5.24 us (2%)
    ppermute x20, waiting for transfers between devices, among(): return lax.ppermute(value, axis, [(i, to(i)) for i in range(count)])  33.5 us
    ppermute x6, waiting for transfers between devices, shifted(): lax.ppermute(value, 'seq', [(i, i + by) for i in range(16) if 0 <= i + by...  26.5 us
    ppermute x6, starting transfers between devices, shifted(): lax.ppermute(value, 'seq', [(i, i + by) for i in range(16) if 0 <= i + by...  22.1 us
    pallas_call x1, Pallas kernels, attend(): pl.pallas_call(attend_kernel, out_shape=jax.ShapeDtypeStruct((rows, BLOCK...  19.2 us
    ppermute x20, starting transfers between devices, among(): return lax.ppermute(value, axis, [(i, to(i)) for i in range(count)])  17.2 us
    pallas_call x1, Pallas kernels, forward(): pl.pallas_call(forward_kernel, out_shape=jax.ShapeDtypeStruct((8, rows, B...  12.8 us
    all_to_all x1, blocking collectives, on_device(): mesh_end = lax.all_to_all(mesh_end, 'head', 0, 0, tiled=True)  12.7 us
    all_to_all x1, waiting for transfers between devices, on_device(): lax.all_to_all(context.reshape(8, mesh_rows // 8, BLOCK), 'head', 0, 0, t...  9.54 us
  transfers between devices with their start and end apart: 27, of which 11 were waited for; matrix products, arithmetic and copies ran while one was open for 5% of the time, Pallas kernels for 16%

profile of v10, /device:TPU:97, one launch (start us, length us, event | category | flops | bytes accessed | tf_op | source)
XLA Modules:
  0.0 213.7 jit_solution(16999964026410874910)
XLA Ops:
  0.0 2.4 %fusion = (bf16[2048,128]{1,0:T(8,128)(2,1)}, bf16[2048,128]{1,0:T(8,128)(2,1)}) fusion(bf16[8192,128]{1,0:T(8,128)(2,1)} %state.1), kind=kLoop, calls=%fused_computation.16 | loop fusion | bytes 2097152 | tf_op jit(solution)/shard_map/slice | solution.py:574
  2.4 0.9 constant_dynamic-slice_fusion
  3.3 0.8 constant_dynamic-slice_fusion.1
  4.1 1.3 collective-permute-start.2
  5.4 1.3 collective-permute-start.3
  6.7 4.1 %collective-permute-start = (bf16[2048,128]{1,0:T(8,128)(2,1)}, bf16[2048,128]{1,0:T(8,128)(2,1)S(1)}, u32[]{:S(2)}, u32[]{:S(2)}) collective-permute-start(bf16[2048,128]{1,0:T(8,128)(2,1)} %get-tuple-element.33), channel_id=1, source_target_pairs={{0,8},{8,16},{16,24},{24,32},{32,40},{40,48},{48,56},{56,64},{64,7... | collective-permute-start | bytes 1572872 | tf_op jit(solution)/shard_map/ppermute | solution.py:529
  10.8 1.9 collective-permute-start.1
  12.7 0.9 fusion.2
  13.7 1.4 collective-permute-start.6
  15.8 2.6 %collective-permute-start.5 = (bf16[144,1024]{1,0:T(8,128)(2,1)S(1)}, bf16[144,1024]{1,0:T(8,128)(2,1)S(1)}, u32[]{:S(2)}, u32[]{:S(2)}) collective-permute-start(bf16[144,1024]{1,0:T(8,128)(2,1)S(1)} %pad_maximum_fusion.4), channel_id=1, source_target_pairs={{0,6},{1,7},{2,0},{3,1},{4,2},{5,3},{6,4},{7,5},{8,14},{9,15},{10,... | collective-permute-start | bytes 884744 | tf_op jit(solution)/shard_map/ppermute | solution.py:533
  18.4 1.0 maximum_bitcast_fusion
  19.5 5.6 %collective-permute-done.1 = bf16[2048,128]{1,0:T(8,128)(2,1)S(1)} collective-permute-done((bf16[2048,128]{1,0:T(8,128)(2,1)}, bf16[2048,128]{1,0:T(8,128)(2,1)S(1)}, u32[]{:S(2)}, u32[]{:S(2)}) %collective-permute-start.1) | collective-permute-done | bytes 524320 | tf_op jit(solution)/shard_map/ppermute | solution.py:529
  25.1 1.4 collective-permute-start.8
  26.5 5.6 %encode.1.s0 = bf16[2048,128]{1,0:T(8,128)(2,1)} custom-call(s32[16,8]{1,0:T(8,128)} %broadcast_subtract_fusion.1.index, bf16[16,128,128]{2,1,0:T(8,128)(2,1)} %bitcast.54, bf16[64,128,128]{2,1,0:T(8,128)(2,1)} %bitcast.47, bf16[16,128,128]{2,1,0:T(8,128)(2,1)} %bitcast.55, bf16[16,8,128,128]{3,2,1,0:T(8,128)(2,1)} %weights.2), custom_call_target="tpu_custom_call" | custom-call | flops 540000000 | bytes 8000000 | tf_op jit(solution)/shard_map/encode/pallas_call | solution.py:86
  32.1 1.0 maximum_bitcast_fusion.1
  33.2 1.0 collective-permute-done.8
  34.6 0.7 copy-done.3
  35.3 1.3 collective-permute-start.10
  36.6 1.4 collective-permute-start.11
  38.3 1.2 collective-permute-start.16
  39.5 8.8 %collective-permute-done.10.s2 = bf16[2048,128]{1,0:T(8,128)(2,1)S(1)} collective-permute-done((bf16[2048,128]{1,0:T(8,128)(2,1)S(1)}, bf16[2048,128]{1,0:T(8,128)(2,1)S(1)}, u32[]{:S(2)}, u32[]{:S(2)}) %collective-permute-start.10) | collective-permute-done | bytes 524320 | tf_op jit(solution)/shard_map/ppermute | solution.py:533
  48.3 0.9 collective-permute-done.9.s1
  50.1 2.1 collective-permute-start.13
  52.2 1.1 collective-permute-start.19
  53.3 13.5 %collective-permute-done.12.s3 = bf16[3072,128]{1,0:T(8,128)(2,1)S(1)} collective-permute-done((bf16[3072,128]{1,0:T(8,128)(2,1)S(1)}, bf16[3072,128]{1,0:T(8,128)(2,1)S(1)}, u32[]{:S(2)}, u32[]{:S(2)}) %collective-permute-start.12) | collective-permute-done | bytes 786464 | tf_op jit(solution)/shard_map/ppermute | solution.py:533
  66.8 0.9 copy-done.5
  67.7 0.9 copy-done.6
  68.6 0.9 pad_maximum_fusion.3.s6
  70.1 9.2 %collective-permute-done.14.s7 = bf16[2048,128]{1,0:T(8,128)(2,1)} collective-permute-done((bf16[2048,128]{1,0:T(8,128)(2,1)}, bf16[2048,128]{1,0:T(8,128)(2,1)}, u32[]{:S(2)}, u32[]{:S(2)}) %collective-permute-start.14) | collective-permute-done | bytes 524320 | tf_op jit(solution)/shard_map/ppermute | solution.py:533
  79.3 8.4 %project.1 = (bf16[2048,128]{1,0:T(8,128)(2,1)}, bf16[2048,256]{1,0:T(8,128)(2,1)}, bf16[8,256,128]{2,1,0:T(8,128)(2,1)}) custom-call(s32[8]{0:T(128)} %stack.130.order, bf16[2048,128]{1,0:T(8,128)(2,1)} %encode.1.s0, bf16[2048,128]{1,0:T(8,128)(2,1)} %copy-done.4, bf16[2048,128]{1,0:T(8,128)(2,1)} %copy-done.7, bf16[3072,128]{1,0:T(8,128)(2,1)} %copy-done.5, ...), custom_call_target="tpu_custom_call" | custom-call | tf_op jit(solution)/shard_map/project/pallas_call | solution.py:157
  87.7 2.3 %fusion.1 = (bf16[1152,256]{1,0:T(8,128)(2,1)}, bf16[1152,256]{1,0:T(8,128)(2,1)}) fusion(bf16[2048,256]{1,0:T(8,128)(2,1)} %get-tuple-element.47.own), kind=kLoop, calls=%fused_computation.17 | loop fusion | bytes 2359296 | tf_op jit(solution)/shard_map/slice | solution.py:612
  90.1 8.1 %collective-permute-start.17 = (bf16[1152,256]{1,0:T(8,128)(2,1)}, bf16[1152,256]{1,0:T(8,128)(2,1)}, u32[]{:S(2)}, u32[]{:S(2)}) collective-permute-start(bf16[1152,256]{1,0:T(8,128)(2,1)} %get-tuple-element.48), channel_id=1, source_target_pairs={{0,8},{8,16},{16,24},{24,32},{32,40},{40,48},{48,56},{56,64},{64,7... | collective-permute-start | bytes 1769480 | tf_op jit(solution)/shard_map/ppermute | solution.py:529
  98.1 2.1 collective-permute-start.18
  100.9 4.4 %collective-permute-done.17.low = bf16[1152,256]{1,0:T(8,128)(2,1)} collective-permute-done((bf16[1152,256]{1,0:T(8,128)(2,1)}, bf16[1152,256]{1,0:T(8,128)(2,1)}, u32[]{:S(2)}, u32[]{:S(2)}) %collective-permute-start.17) | collective-permute-done | bytes 589856 | tf_op jit(solution)/shard_map/ppermute | solution.py:529
  105.3 8.1 %collective-permute-done.18.high = bf16[1152,256]{1,0:T(8,128)(2,1)} collective-permute-done((bf16[1152,256]{1,0:T(8,128)(2,1)}, bf16[1152,256]{1,0:T(8,128)(2,1)}, u32[]{:S(2)}, u32[]{:S(2)}) %collective-permute-start.18) | collective-permute-done | bytes 589856 | tf_op jit(solution)/shard_map/ppermute | solution.py:529
  113.4 19.2 %attend.1 = bf16[2048,128]{1,0:T(8,128)(2,1)} custom-call(s32[2]{0:T(128)} %add_convert_fusion.edges, bf16[2048,128]{1,0:T(8,128)(2,1)} %get-tuple-element.46.queries, bf16[1152,256]{1,0:T(8,128)(2,1)} %collective-permute-done.17.low, bf16[2048,256]{1,0:T(8,128)(2,1)} %get-tuple-element.47.own, bf16[1152,256]{1,0:T(8,128)(2,1)} %collective-permute-done.18.high), custom_call_target="tpu_custom_call" | custom-call | tf_op jit(solution)/shard_map/attend/pallas_call | solution.py:261
  133.8 4.1 %all-to-all-start = ((bf16[8,256,128]{2,1,0:T(8,128)(2,1)}), bf16[8,256,128]{2,1,0:T(8,128)(2,1)}, u32[]{:S(2)}, u32[]{:S(2)}) async-start(bf16[8,256,128]{2,1,0:T(8,128)(2,1)} %bitcast.49), calls=%async_computation | async-start | bytes 1048576 | tf_op jit(solution)/shard_map/all_to_all | solution.py:620
  138.6 9.5 %all-to-all-done.refs_8_ = bf16[8,256,128]{2,1,0:T(8,128)(2,1)} async-done(((bf16[8,256,128]{2,1,0:T(8,128)(2,1)}), bf16[8,256,128]{2,1,0:T(8,128)(2,1)}, u32[]{:S(2)}, u32[]{:S(2)}) %all-to-all-start) | async-done | bytes 524320 | tf_op jit(solution)/shard_map/all_to_all | solution.py:620
  148.2 12.8 %forward.1 = bf16[8,256,128]{2,1,0:T(8,128)(2,1)} custom-call(s32[16]{0:T(128)} %concatenate.19.table, bf16[4,2,144,1024]{3,2,1,0:T(8,128)(2,1)} %copy-done.1, bf16[4,2,144,1024]{3,2,1,0:T(8,128)(2,1)} %collective-permute-done.15.refs_1_, bf16[4,2,144,1024]{3,2,1,0:T(8,128)(2,1)} %collective-permute-done.16.refs_2_, ...), custom_call_target="tpu_custom_call" | custom-call | flops 4800000000 | bytes 20000000 | tf_op jit(solution)/shard_map/forward/pallas_call | solution.py:374
  161.0 12.7 %all_to_all.15 = bf16[8,256,128]{2,1,0:T(8,128)(2,1)S(1)} all-to-all(bf16[8,256,128]{2,1,0:T(8,128)(2,1)} %forward.1), channel_id=1, replica_groups=mesh['seq'=16,'head'=8] {'head'}, dimensions={0} | all-to-all | bytes 1048576 | tf_op jit(solution)/shard_map/all_to_all | solution.py:628
  173.7 3.7 %collective-permute-start.24 = (bf16[8,128,128]{2,1,0:T(8,128)(2,1)S(1)}, bf16[8,128,128]{2,1,0:T(8,128)(2,1)S(1)}, u32[]{:S(2)}, u32[]{:S(2)}) collective-permute-start(bf16[8,128,128]{2,1,0:T(8,128)(2,1)S(1)} %bitcast.62), channel_id=1, source_target_pairs={{0,8},{8,16},{16,24},{24,32},{32,40},{40,48},{48,56},{56,64},{64,7... | collective-permute-start | bytes 786440 | tf_op jit(solution)/shard_map/ppermute | solution.py:529
  177.4 2.2 %collective-permute-start.25 = (bf16[8,128,128]{2,1,0:T(8,128)(2,1)S(1)}, bf16[8,128,128]{2,1,0:T(8,128)(2,1)S(1)}, u32[]{:S(2)}, u32[]{:S(2)}) collective-permute-start(bf16[8,128,128]{2,1,0:T(8,128)(2,1)S(1)} %bitcast.61), channel_id=1, source_target_pairs={{8,0},{16,8},{24,16},{32,24},{40,32},{48,40},{56,48},{64,56},{72,6... | collective-permute-start | bytes 786440 | tf_op jit(solution)/shard_map/ppermute | solution.py:529
  180.7 8.0 %collective-permute-done.25.high = bf16[8,128,128]{2,1,0:T(8,128)(2,1)S(1)} collective-permute-done((bf16[8,128,128]{2,1,0:T(8,128)(2,1)S(1)}, bf16[8,128,128]{2,1,0:T(8,128)(2,1)S(1)}, u32[]{:S(2)}, u32[]{:S(2)}) %collective-permute-start.25) | collective-permute-done | bytes 262176 | tf_op jit(solution)/shard_map/ppermute | solution.py:529
  188.7 0.7 copy-done.13
  189.4 8.0 %decode.1 = (bf16[8192,128]{1,0:T(8,128)(2,1)}, bf16[8,16,128]{2,1,0:T(8,128)(2,1)}) custom-call(s32[64,2]{1,0:T(8,128)} %broadcast_subtract_fusion.index, bf16[8,128,128]{2,1,0:T(8,128)(2,1)} %copy-done.12, bf16[16,128,128]{2,1,0:T(8,128)(2,1)} %bitcast.48, bf16[8,128,128]{2,1,0:T(8,128)(2,1)} %copy-done.13, bf16[64,2,128,128]{3,2,1,0:T(8,128)(2,1)} %weights.3), custom_call_target="tpu_custom_call" | custom-call | flops 540000000 | bytes 10000000 | tf_op jit(solution)/shard_map/decode/pallas_call | solution.py:443
  197.4 0.8 broadcast_in_dim.3
  198.2 9.2 %all_to_all.16.sums = bf16[8,8,16,128]{3,2,1,0:T(8,128)(2,1)} all-to-all(bf16[8,8,16,128]{3,2,1,0:T(8,128)(2,1)S(1)} %broadcast_in_dim.3), channel_id=1, replica_groups=mesh['seq'=16,'head'=8] {'head'}, dimensions={0} | all-to-all | bytes 524288 | tf_op jit(solution)/shard_map/all_to_all | solution.py:638
  207.4 6.1 %finish.1 = bf16[8192,128]{1,0:T(8,128)(2,1)} custom-call(bf16[8,8,16,128]{3,2,1,0:T(8,128)(2,1)} %all_to_all.16.sums, bf16[8192,128]{1,0:T(8,128)(2,1)} %get-tuple-element.60.back, bf16[8192,128]{1,0:T(8,128)(2,1)} %state.1, f32[1,128]{1,0:T(1,128)} %bitcast.65), custom_call_target="tpu_custom_call" | custom-call | flops 540000000 | bytes 8000000 | tf_op jit(solution)/shard_map/finish/pallas_call | solution.py:507
  (73 shorter events, 6.7 us)
Async XLA Ops:
  0.0 3.3 %copy-start = (bf16[512,1024]{1,0:T(8,128)(2,1)S(1)}, bf16[512,1024]{1,0:T(8,128)(2,1)}, u32[]{:S(2)}) copy-start(bf16[512,1024]{1,0:T(8,128)(2,1)} %param.20) | copy-start | bytes 3145732
  0.0 12.7 %copy-start.9 = (bf16[1024,3,128]{2,0,1:T(8,128)(2,1)S(1)}, bf16[1024,3,128]{2,0,1:T(8,128)(2,1)}, u32[]{:S(2)}) copy-start(bf16[1024,3,128]{2,0,1:T(8,128)(2,1)} %param.16) | copy-start | bytes 2359300
  0.0 13.6 %copy-start.14 = (s32[16,8]{0,1:T(8,128)S(1)}, s32[16,8]{0,1:T(8,128)}, u32[]{:S(2)}) copy-start(s32[16,8]{0,1:T(8,128)} %param.13) | copy-start | bytes 1540
  4.1 9.6 %collective-permute-start.2 = (bf16[144,1024]{1,0:T(8,128)(2,1)S(1)}, bf16[144,1024]{1,0:T(8,128)(2,1)}, u32[]{:S(2)}, u32[]{:S(2)}) collective-permute-start(bf16[144,1024]{1,0:T(8,128)(2,1)S(1)} %pad_maximum_fusion.4), channel_id=1, source_target_pairs={{0,1},{1,0},{2,3},{3,2},{4,5},{5,4},{6,7},{7,6},{8,9},{9,8},{10,11... | collective-permute-start | bytes 884744 | tf_op jit(solution)/shard_map/ppermute | solution.py:533
  5.4 10.4 %collective-permute-start.3 = (bf16[144,1024]{1,0:T(8,128)(2,1)S(1)}, bf16[144,1024]{1,0:T(8,128)(2,1)}, u32[]{:S(2)}, u32[]{:S(2)}) collective-permute-start(bf16[144,1024]{1,0:T(8,128)(2,1)S(1)} %pad_maximum_fusion.4), channel_id=1, source_target_pairs={{0,2},{1,3},{2,4},{3,5},{4,6},{5,7},{6,0},{7,1},{8,10},{9,11},{10,... | collective-permute-start | bytes 884744 | tf_op jit(solution)/shard_map/ppermute | solution.py:533
  6.7 12.7 %collective-permute-start = (bf16[2048,128]{1,0:T(8,128)(2,1)}, bf16[2048,128]{1,0:T(8,128)(2,1)S(1)}, u32[]{:S(2)}, u32[]{:S(2)}) collective-permute-start(bf16[2048,128]{1,0:T(8,128)(2,1)} %get-tuple-element.33), channel_id=1, source_target_pairs={{0,8},{8,16},{16,24},{24,32},{32,40},{40,48},{48,56},{56,64},{64,7... | collective-permute-start | bytes 1572872 | tf_op jit(solution)/shard_map/ppermute | solution.py:529
  10.8 14.3 %collective-permute-start.1 = (bf16[2048,128]{1,0:T(8,128)(2,1)}, bf16[2048,128]{1,0:T(8,128)(2,1)S(1)}, u32[]{:S(2)}, u32[]{:S(2)}) collective-permute-start(bf16[2048,128]{1,0:T(8,128)(2,1)} %get-tuple-element.34), channel_id=1, source_target_pairs={{8,0},{16,8},{24,16},{32,24},{40,32},{48,40},{56,48},{64,56},{72,6... | collective-permute-start | bytes 1572872 | tf_op jit(solution)/shard_map/ppermute | solution.py:529
  13.7 11.4 %collective-permute-start.6 = (bf16[144,1024]{1,0:T(8,128)(2,1)}, bf16[144,1024]{1,0:T(8,128)(2,1)S(1)}, u32[]{:S(2)}, u32[]{:S(2)}) collective-permute-start(bf16[144,1024]{1,0:T(8,128)(2,1)} %collective-permute-done.2), channel_id=1, source_target_pairs={{0,6},{1,7},{2,0},{3,1},{4,2},{5,3},{6,4},{7,5},{8,14},{9,15},{10,... | collective-permute-start | bytes 884744 | tf_op jit(solution)/shard_map/ppermute | solution.py:533
  15.1 17.0 %collective-permute-start.4 = (bf16[144,1024]{1,0:T(8,128)(2,1)}, bf16[144,1024]{1,0:T(8,128)(2,1)S(1)}, u32[]{:S(2)}, u32[]{:S(2)}) collective-permute-start(bf16[144,1024]{1,0:T(8,128)(2,1)} %collective-permute-done.2), channel_id=1, source_target_pairs={{0,2},{1,3},{2,4},{3,5},{4,6},{5,7},{6,0},{7,1},{8,10},{9,11},{10,... | collective-permute-start | bytes 884744 | tf_op jit(solution)/shard_map/ppermute | solution.py:533
  15.8 17.3 %collective-permute-start.5 = (bf16[144,1024]{1,0:T(8,128)(2,1)S(1)}, bf16[144,1024]{1,0:T(8,128)(2,1)S(1)}, u32[]{:S(2)}, u32[]{:S(2)}) collective-permute-start(bf16[144,1024]{1,0:T(8,128)(2,1)S(1)} %pad_maximum_fusion.4), channel_id=1, source_target_pairs={{0,6},{1,7},{2,0},{3,1},{4,2},{5,3},{6,4},{7,5},{8,14},{9,15},{10,... | collective-permute-start | bytes 884744 | tf_op jit(solution)/shard_map/ppermute | solution.py:533
  19.4 7.1 %copy-start.10 = (bf16[2048,128]{1,0:T(8,128)(2,1)}, bf16[2048,128]{1,0:T(8,128)(2,1)S(1)}, u32[]{:S(2)}) copy-start(bf16[2048,128]{1,0:T(8,128)(2,1)S(1)} %collective-permute-done) | copy-start | bytes 1572868
  19.4 13.8 %collective-permute-start.7 = (bf16[144,1024]{1,0:T(8,128)(2,1)}, bf16[144,1024]{1,0:T(8,128)(2,1)S(1)}, u32[]{:S(2)}, u32[]{:S(2)}) collective-permute-start(bf16[144,1024]{1,0:T(8,128)(2,1)} %collective-permute-done.3), channel_id=1, source_target_pairs={{0,2},{1,3},{2,4},{3,5},{4,6},{5,7},{6,0},{7,1},{8,10},{9,11},{10,... | collective-permute-start | bytes 884744 | tf_op jit(solution)/shard_map/ppermute | solution.py:533
  25.1 1.4 copy-start.11
  25.1 9.1 %collective-permute-start.8 = (bf16[144,1024]{1,0:T(8,128)(2,1)S(1)}, bf16[144,1024]{1,0:T(8,128)(2,1)S(1)}, u32[]{:S(2)}, u32[]{:S(2)}) collective-permute-start(bf16[144,1024]{1,0:T(8,128)(2,1)S(1)} %collective-permute-done.6), channel_id=1, source_target_pairs={{0,6},{1,7},{2,0},{3,1},{4,2},{5,3},{6,4},{7,5},{8,14},{9,15},{10,... | collective-permute-start | bytes 884744 | tf_op jit(solution)/shard_map/ppermute | solution.py:533
  34.3 1.0 copy-start.3
  35.3 97.3 %copy-start.1 = (bf16[4,2,144,1024]{3,2,1,0:T(8,128)(2,1)}, bf16[4,2,144,1024]{3,2,1,0:T(8,128)(2,1)S(1)}, u32[]{:S(2)}) copy-start(bf16[4,2,144,1024]{3,2,1,0:T(8,128)(2,1)S(1)} %pad_maximum_fusion.refs_0_) | copy-start | bytes 7077892
  35.3 13.0 %collective-permute-start.10 = (bf16[2048,128]{1,0:T(8,128)(2,1)S(1)}, bf16[2048,128]{1,0:T(8,128)(2,1)S(1)}, u32[]{:S(2)}, u32[]{:S(2)}) collective-permute-start(bf16[2048,128]{1,0:T(8,128)(2,1)S(1)} %copy-done.3), channel_id=1, source_target_pairs={{0,2},{1,3},{2,4},{3,5},{4,6},{5,7},{6,0},{7,1},{8,10},{9,11},{10,... | collective-permute-start | bytes 1572872 | tf_op jit(solution)/shard_map/ppermute | solution.py:533
  36.6 11.7 %collective-permute-start.11 = (bf16[2048,128]{1,0:T(8,128)(2,1)S(1)}, bf16[2048,128]{1,0:T(8,128)(2,1)S(1)}, u32[]{:S(2)}, u32[]{:S(2)}) collective-permute-start(bf16[2048,128]{1,0:T(8,128)(2,1)S(1)} %copy-done.3), channel_id=1, source_target_pairs={{0,6},{1,7},{2,0},{3,1},{4,2},{5,3},{6,4},{7,5},{8,14},{9,15},{10,... | collective-permute-start | bytes 1572872 | tf_op jit(solution)/shard_map/ppermute | solution.py:533
  38.0 11.2 %collective-permute-start.9 = (bf16[2048,128]{1,0:T(8,128)(2,1)S(1)}, bf16[2048,128]{1,0:T(8,128)(2,1)S(1)}, u32[]{:S(2)}, u32[]{:S(2)}) collective-permute-start(bf16[2048,128]{1,0:T(8,128)(2,1)S(1)} %copy-done.3), channel_id=1, source_target_pairs={{0,1},{1,0},{2,3},{3,2},{4,5},{5,4},{6,7},{7,6},{8,9},{9,8},{10,11... | collective-permute-start | bytes 1572872 | tf_op jit(solution)/shard_map/ppermute | solution.py:533
  38.0 52.1 %collective-permute-start.15 = (bf16[4,2,144,1024]{3,2,1,0:T(8,128)(2,1)S(1)}, bf16[4,2,144,1024]{3,2,1,0:T(8,128)(2,1)}, u32[]{:S(2)}, u32[]{:S(2)}) collective-permute-start(bf16[4,2,144,1024]{3,2,1,0:T(8,128)(2,1)S(1)} %pad_maximum_fusion.refs_0_), channel_id=1, source_target_pairs={{0,16},{8,24},{16,32},{24,40},{32,48},{40,56},{48,0},{56,8},{64,80... | collective-permute-start | bytes 7077896 | tf_op jit(solution)/shard_map/ppermute | solution.py:533
  38.3 51.8 %collective-permute-start.16 = (bf16[4,2,144,1024]{3,2,1,0:T(8,128)(2,1)S(1)}, bf16[4,2,144,1024]{3,2,1,0:T(8,128)(2,1)}, u32[]{:S(2)}, u32[]{:S(2)}) collective-permute-start(bf16[4,2,144,1024]{3,2,1,0:T(8,128)(2,1)S(1)} %pad_maximum_fusion.refs_0_), channel_id=1, source_target_pairs={{0,48},{8,56},{16,0},{24,8},{32,16},{40,24},{48,32},{56,40},{64,11... | collective-permute-start | bytes 7077896 | tf_op jit(solution)/shard_map/ppermute | solution.py:533
  48.3 0.9 copy-start.7
  48.3 1.0 copy-start.8
  49.2 19.4 %copy-start.4 = (bf16[2048,128]{1,0:T(8,128)(2,1)}, bf16[2048,128]{1,0:T(8,128)(2,1)S(1)}, u32[]{:S(2)}) copy-start(bf16[2048,128]{1,0:T(8,128)(2,1)S(1)} %collective-permute-done.9.s1) | copy-start | bytes 1572868
  49.5 17.3 %collective-permute-start.12 = (bf16[3072,128]{1,0:T(8,128)(2,1)S(1)}, bf16[3072,128]{1,0:T(8,128)(2,1)S(1)}, u32[]{:S(2)}, u32[]{:S(2)}) collective-permute-start(bf16[3072,128]{1,0:T(8,128)(2,1)S(1)} %get-tuple-element.73), channel_id=1, source_target_pairs={{0,2},{1,3},{2,4},{3,5},{4,6},{5,7},{6,0},{7,1},{8,10},{9,11},{10,... | collective-permute-start | bytes 2359304 | tf_op jit(solution)/shard_map/ppermute | solution.py:533
  50.1 17.6 %collective-permute-start.13 = (bf16[3072,128]{1,0:T(8,128)(2,1)S(1)}, bf16[3072,128]{1,0:T(8,128)(2,1)S(1)}, u32[]{:S(2)}, u32[]{:S(2)}) collective-permute-start(bf16[3072,128]{1,0:T(8,128)(2,1)S(1)} %get-tuple-element.72), channel_id=1, source_target_pairs={{0,6},{1,7},{2,0},{3,1},{4,2},{5,3},{6,4},{7,5},{8,14},{9,15},{10,... | collective-permute-start | bytes 2359304 | tf_op jit(solution)/shard_map/ppermute | solution.py:533
  52.2 80.4 %collective-permute-start.19 = (bf16[4,2,144,1024]{3,2,1,0:T(8,128)(2,1)S(1)}, bf16[4,2,144,1024]{3,2,1,0:T(8,128)(2,1)}, u32[]{:S(2)}, u32[]{:S(2)}) collective-permute-start(bf16[4,2,144,1024]{3,2,1,0:T(8,128)(2,1)S(1)} %pad_maximum_fusion.refs_0_), channel_id=1, source_target_pairs={{0,65},{1,64},{2,67},{3,66},{4,69},{5,68},{6,71},{7,70},{8,73},{9,... | collective-permute-start | bytes 7077896 | tf_op jit(solution)/shard_map/ppermute | solution.py:533
  66.8 0.9 copy-start.5
  67.7 0.9 copy-start.6
  69.5 9.8 %collective-permute-start.14 = (bf16[2048,128]{1,0:T(8,128)(2,1)}, bf16[2048,128]{1,0:T(8,128)(2,1)}, u32[]{:S(2)}, u32[]{:S(2)}) collective-permute-start(bf16[2048,128]{1,0:T(8,128)(2,1)} %pad_maximum_fusion.3.s6), channel_id=1, source_target_pairs={{0,1},{1,0},{2,3},{3,2},{4,5},{5,4},{6,7},{7,6},{8,9},{9,8},{10,11... | collective-permute-start | bytes 1572872 | tf_op jit(solution)/shard_map/ppermute | solution.py:533
  90.1 15.2 %collective-permute-start.17 = (bf16[1152,256]{1,0:T(8,128)(2,1)}, bf16[1152,256]{1,0:T(8,128)(2,1)}, u32[]{:S(2)}, u32[]{:S(2)}) collective-permute-start(bf16[1152,256]{1,0:T(8,128)(2,1)} %get-tuple-element.48), channel_id=1, source_target_pairs={{0,8},{8,16},{16,24},{24,32},{32,40},{40,48},{48,56},{56,64},{64,7... | collective-permute-start | bytes 1769480 | tf_op jit(solution)/shard_map/ppermute | solution.py:529
  98.1 15.2 %collective-permute-start.18 = (bf16[1152,256]{1,0:T(8,128)(2,1)}, bf16[1152,256]{1,0:T(8,128)(2,1)}, u32[]{:S(2)}, u32[]{:S(2)}) collective-permute-start(bf16[1152,256]{1,0:T(8,128)(2,1)} %get-tuple-element.49), channel_id=1, source_target_pairs={{8,0},{16,8},{24,16},{32,24},{40,32},{48,40},{56,48},{64,56},{72,6... | collective-permute-start | bytes 1769480 | tf_op jit(solution)/shard_map/ppermute | solution.py:529
  132.6 15.5 %collective-permute-start.20 = (bf16[4,2,144,1024]{3,2,1,0:T(8,128)(2,1)S(1)}, bf16[4,2,144,1024]{3,2,1,0:T(8,128)(2,1)}, u32[]{:S(2)}, u32[]{:S(2)}) collective-permute-start(bf16[4,2,144,1024]{3,2,1,0:T(8,128)(2,1)S(1)} %pad_maximum_fusion.refs_0_), channel_id=1, source_target_pairs={{0,8},{8,0},{16,24},{24,16},{32,40},{40,32},{48,56},{56,48},{64,72... | collective-permute-start | bytes 7077896 | tf_op jit(solution)/shard_map/ppermute | solution.py:533
  132.7 15.4 %collective-permute-start.21 = (bf16[4,2,144,1024]{3,2,1,0:T(8,128)(2,1)}, bf16[4,2,144,1024]{3,2,1,0:T(8,128)(2,1)}, u32[]{:S(2)}, u32[]{:S(2)}) collective-permute-start(bf16[4,2,144,1024]{3,2,1,0:T(8,128)(2,1)} %collective-permute-done.15.refs_1_), channel_id=1, source_target_pairs={{0,8},{8,0},{16,24},{24,16},{32,40},{40,32},{48,56},{56,48},{64,72... | collective-permute-start | bytes 7077896 | tf_op jit(solution)/shard_map/ppermute | solution.py:533
  133.2 14.9 %collective-permute-start.22 = (bf16[4,2,144,1024]{3,2,1,0:T(8,128)(2,1)}, bf16[4,2,144,1024]{3,2,1,0:T(8,128)(2,1)}, u32[]{:S(2)}, u32[]{:S(2)}) collective-permute-start(bf16[4,2,144,1024]{3,2,1,0:T(8,128)(2,1)} %collective-permute-done.16.refs_2_), channel_id=1, source_target_pairs={{0,8},{8,0},{16,24},{24,16},{32,40},{40,32},{48,56},{56,48},{64,72... | collective-permute-start | bytes 7077896 | tf_op jit(solution)/shard_map/ppermute | solution.py:533
  133.3 14.8 %collective-permute-start.23 = (bf16[4,2,144,1024]{3,2,1,0:T(8,128)(2,1)}, bf16[4,2,144,1024]{3,2,1,0:T(8,128)(2,1)}, u32[]{:S(2)}, u32[]{:S(2)}) collective-permute-start(bf16[4,2,144,1024]{3,2,1,0:T(8,128)(2,1)} %collective-permute-done.19.refs_3_), channel_id=1, source_target_pairs={{0,8},{8,0},{16,24},{24,16},{32,40},{40,32},{48,56},{56,48},{64,72... | collective-permute-start | bytes 7077896 | tf_op jit(solution)/shard_map/ppermute | solution.py:533
  133.8 14.4 %all-to-all-start = ((bf16[8,256,128]{2,1,0:T(8,128)(2,1)}), bf16[8,256,128]{2,1,0:T(8,128)(2,1)}, u32[]{:S(2)}, u32[]{:S(2)}) async-start(bf16[8,256,128]{2,1,0:T(8,128)(2,1)} %bitcast.49), calls=%async_computation | async-start | bytes 1048576 | tf_op jit(solution)/shard_map/all_to_all | solution.py:620
  148.2 31.4 %copy-start.15 = (s32[64,2]{0,1:T(2,128)S(1)}, s32[64,2]{0,1:T(2,128)}, u32[]{:S(2)}) copy-start(s32[64,2]{0,1:T(2,128)} %param.21) | copy-start | bytes 1540
  173.6 15.1 %copy-start.2 = (bf16[8,256,128]{2,1,0:T(8,128)(2,1)}, bf16[8,256,128]{2,1,0:T(8,128)(2,1)S(1)}, u32[]{:S(2)}) copy-start(bf16[8,256,128]{2,1,0:T(8,128)(2,1)S(1)} %all_to_all.15) | copy-start | bytes 1572868
  173.7 7.0 %collective-permute-start.24 = (bf16[8,128,128]{2,1,0:T(8,128)(2,1)S(1)}, bf16[8,128,128]{2,1,0:T(8,128)(2,1)S(1)}, u32[]{:S(2)}, u32[]{:S(2)}) collective-permute-start(bf16[8,128,128]{2,1,0:T(8,128)(2,1)S(1)} %bitcast.62), channel_id=1, source_target_pairs={{0,8},{8,16},{16,24},{24,32},{32,40},{40,48},{48,56},{56,64},{64,7... | collective-permute-start | bytes 786440 | tf_op jit(solution)/shard_map/ppermute | solution.py:529
  177.4 11.3 %collective-permute-start.25 = (bf16[8,128,128]{2,1,0:T(8,128)(2,1)S(1)}, bf16[8,128,128]{2,1,0:T(8,128)(2,1)S(1)}, u32[]{:S(2)}, u32[]{:S(2)}) collective-permute-start(bf16[8,128,128]{2,1,0:T(8,128)(2,1)S(1)} %bitcast.61), channel_id=1, source_target_pairs={{8,0},{16,8},{24,16},{32,24},{40,32},{48,40},{56,48},{64,56},{72,6... | collective-permute-start | bytes 786440 | tf_op jit(solution)/shard_map/ppermute | solution.py:529
  180.7 8.0 %copy-start.12 = (bf16[8,128,128]{2,1,0:T(8,128)(2,1)}, bf16[8,128,128]{2,1,0:T(8,128)(2,1)S(1)}, u32[]{:S(2)}) copy-start(bf16[8,128,128]{2,1,0:T(8,128)(2,1)S(1)} %collective-permute-done.24.low) | copy-start | bytes 786436
  188.7 0.7 copy-start.13

commit v11 on v10

--- a/solution.py
+++ b/solution.py
@@ -595,7 +595,7 @@
             )
         ]
     )
-    x, mine = lax.optimization_barrier((mesh_start, mine))
+    x, _, _ = lax.optimization_barrier((mesh_start, swapped_north, swapped_south))
     up, down = UP(mine), DOWN(mine)
     y, xa, xb, mine = lax.optimization_barrier((OVER(x), NORTH(x), SOUTH(x), mine))
     across = ACROSS(mine)

time: 215 us -> 213 us (level)
  starting transfers between devices: 43.4 us -> 39.4 us
    ppermute x6, starting transfers between devices: 22.1 us -> 18.4 us  [shifted(): lax.ppermute(value, 'seq', [(i, i + by) for i in range(16) if 0 <= i + by...]
    ppermute x20, waiting for transfers between devices: 33.5 us -> 36.1 us  [among(): return lax.ppermute(value, axis, [(i, to(i)) for i in range(count)])]
  transfers between devices with their start and end apart: 27 -> 27, of which waited for: 11 -> 10; matrix products, arithmetic and copies ran while one was open for 5% -> 5% of each run, Pallas kernels for 16% -> 16%
where the time goes in v11:
time: 213 us; the launch traced here: 212 us
  waiting for transfers between devices  71.6 us (34%)
  Pallas kernels  60.1 us (28%)
  starting transfers between devices  39.4 us (18%)
  blocking collectives  21.9 us (10%)
  local copies, waits for them, and re-layouts  12.1 us (6%)
  other arithmetic  6.27 us (3%)
    ppermute x20, waiting for transfers between devices, among(): return lax.ppermute(value, axis, [(i, to(i)) for i in range(count)])  36.1 us
    ppermute x6, waiting for transfers between devices, shifted(): lax.ppermute(value, 'seq', [(i, i + by) for i in range(16) if 0 <= i + by...  25.9 us
    pallas_call x1, Pallas kernels, attend(): pl.pallas_call(attend_kernel, out_shape=jax.ShapeDtypeStruct((rows, BLOCK...  19.2 us
    ppermute x6, starting transfers between devices, shifted(): lax.ppermute(value, 'seq', [(i, i + by) for i in range(16) if 0 <= i + by...  18.4 us
    ppermute x20, starting transfers between devices, among(): return lax.ppermute(value, axis, [(i, to(i)) for i in range(count)])  16.9 us
    pallas_call x1, Pallas kernels, forward(): pl.pallas_call(forward_kernel, out_shape=jax.ShapeDtypeStruct((8, rows, B...  12.8 us
    all_to_all x1, blocking collectives, on_device(): mesh_end = lax.all_to_all(mesh_end, 'head', 0, 0, tiled=True)  12.7 us
    all_to_all x1, waiting for transfers between devices, on_device(): lax.all_to_all(context.reshape(8, mesh_rows // 8, BLOCK), 'head', 0, 0, t...  9.54 us
  transfers between devices with their start and end apart: 27, of which 10 were waited for; matrix products, arithmetic and copies ran while one was open for 5% of the time, Pallas kernels for 16%

profile of v11, /device:TPU:97, one launch (start us, length us, event | category | flops | bytes accessed | tf_op | source)
XLA Modules:
  0.0 212.1 jit_solution(13243980764563179984)
XLA Ops:
  0.1 2.4 %fusion = (bf16[2048,128]{1,0:T(8,128)(2,1)}, bf16[2048,128]{1,0:T(8,128)(2,1)}) fusion(bf16[8192,128]{1,0:T(8,128)(2,1)} %state.1), kind=kLoop, calls=%fused_computation.16 | loop fusion | bytes 2097152 | tf_op jit(solution)/shard_map/slice | solution.py:574
  2.4 0.9 constant_dynamic-slice_fusion
  3.4 0.8 constant_dynamic-slice_fusion.1
  4.2 1.3 collective-permute-start.2
  5.4 1.3 collective-permute-start.8
  6.7 1.4 collective-permute-start.9
  8.2 4.3 %collective-permute-start = (bf16[2048,128]{1,0:T(8,128)(2,1)}, bf16[2048,128]{1,0:T(8,128)(2,1)S(1)}, u32[]{:S(2)}, u32[]{:S(2)}) collective-permute-start(bf16[2048,128]{1,0:T(8,128)(2,1)} %get-tuple-element.32), channel_id=1, source_target_pairs={{0,8},{8,16},{16,24},{24,32},{32,40},{40,48},{48,56},{56,64},{64,7... | collective-permute-start | bytes 1572872 | tf_op jit(solution)/shard_map/ppermute | solution.py:529
  12.5 1.9 collective-permute-start.1
  14.5 0.9 fusion.2
  15.4 1.5 collective-permute-start.4
  17.6 1.0 maximum_bitcast_fusion
  19.3 7.5 %collective-permute-done.1 = bf16[2048,128]{1,0:T(8,128)(2,1)S(1)} collective-permute-done((bf16[2048,128]{1,0:T(8,128)(2,1)}, bf16[2048,128]{1,0:T(8,128)(2,1)S(1)}, u32[]{:S(2)}, u32[]{:S(2)}) %collective-permute-start.1) | collective-permute-done | bytes 524320 | tf_op jit(solution)/shard_map/ppermute | solution.py:529
  26.8 1.5 collective-permute-start.11
  28.4 5.6 %encode.1.s0 = bf16[2048,128]{1,0:T(8,128)(2,1)} custom-call(s32[16,8]{1,0:T(8,128)} %broadcast_subtract_fusion.1.index, bf16[16,128,128]{2,1,0:T(8,128)(2,1)} %bitcast.54, bf16[64,128,128]{2,1,0:T(8,128)(2,1)} %bitcast.47, bf16[16,128,128]{2,1,0:T(8,128)(2,1)} %bitcast.55, bf16[16,8,128,128]{3,2,1,0:T(8,128)(2,1)} %weights.2), custom_call_target="tpu_custom_call" | custom-call | flops 540000000 | bytes 8000000 | tf_op jit(solution)/shard_map/encode/pallas_call | solution.py:86
  34.1 2.7 %collective-permute-start.7 = (bf16[2048,128]{1,0:T(8,128)(2,1)}, bf16[2048,128]{1,0:T(8,128)(2,1)S(1)}, u32[]{:S(2)}, u32[]{:S(2)}) collective-permute-start(bf16[2048,128]{1,0:T(8,128)(2,1)} %encode.1.s0), channel_id=1, source_target_pairs={{0,6},{1,7},{2,0},{3,1},{4,2},{5,3},{6,4},{7,5},{8,14},{9,15},{10,... | collective-permute-start | bytes 1572872 | tf_op jit(solution)/shard_map/ppermute | solution.py:533
  36.8 1.0 maximum_bitcast_fusion.1
  37.8 1.0 maximum_bitcast_fusion.2
  39.3 1.5 collective-permute-start.16
  40.8 7.3 %collective-permute-done.5.s1 = bf16[2048,128]{1,0:T(8,128)(2,1)S(1)} collective-permute-done((bf16[2048,128]{1,0:T(8,128)(2,1)}, bf16[2048,128]{1,0:T(8,128)(2,1)S(1)}, u32[]{:S(2)}, u32[]{:S(2)}) %collective-permute-start.5) | collective-permute-done | bytes 524320 | tf_op jit(solution)/shard_map/ppermute | solution.py:533
  48.1 1.2 collective-permute-done.6.s2
  49.5 2.7 %collective-permute-start.13 = (bf16[3072,128]{1,0:T(8,128)(2,1)S(1)}, bf16[3072,128]{1,0:T(8,128)(2,1)S(1)}, u32[]{:S(2)}, u32[]{:S(2)}) collective-permute-start(bf16[3072,128]{1,0:T(8,128)(2,1)S(1)} %get-tuple-element.70), channel_id=1, source_target_pairs={{0,6},{1,7},{2,0},{3,1},{4,2},{5,3},{6,4},{7,5},{8,14},{9,15},{10,... | collective-permute-start | bytes 2359304 | tf_op jit(solution)/shard_map/ppermute | solution.py:533
  52.2 17.1 %collective-permute-done.12.s3 = bf16[3072,128]{1,0:T(8,128)(2,1)S(1)} collective-permute-done((bf16[3072,128]{1,0:T(8,128)(2,1)S(1)}, bf16[3072,128]{1,0:T(8,128)(2,1)S(1)}, u32[]{:S(2)}, u32[]{:S(2)}) %collective-permute-start.12) | collective-permute-done | bytes 786464 | tf_op jit(solution)/shard_map/ppermute | solution.py:533
  69.3 0.9 copy-done.4
  70.2 0.9 copy-done.5
  71.2 0.9 pad_maximum_fusion.3.s6
  72.0 1.2 collective-permute-start.14
  73.9 10.5 %collective-permute-done.14.s7 = bf16[2048,128]{1,0:T(8,128)(2,1)} collective-permute-done((bf16[2048,128]{1,0:T(8,128)(2,1)}, bf16[2048,128]{1,0:T(8,128)(2,1)}, u32[]{:S(2)}, u32[]{:S(2)}) %collective-permute-start.14) | collective-permute-done | bytes 524320 | tf_op jit(solution)/shard_map/ppermute | solution.py:533
  84.4 8.4 %project.1 = (bf16[2048,128]{1,0:T(8,128)(2,1)}, bf16[2048,256]{1,0:T(8,128)(2,1)}, bf16[8,256,128]{2,1,0:T(8,128)(2,1)}) custom-call(s32[8]{0:T(128)} %stack.130.order, bf16[2048,128]{1,0:T(8,128)(2,1)} %encode.1.s0, bf16[2048,128]{1,0:T(8,128)(2,1)} %copy-done.3, bf16[2048,128]{1,0:T(8,128)(2,1)} %copy-done.6, bf16[3072,128]{1,0:T(8,128)(2,1)} %copy-done.4, ...), custom_call_target="tpu_custom_call" | custom-call | tf_op jit(solution)/shard_map/project/pallas_call | solution.py:157
  92.8 2.3 %fusion.1 = (bf16[1152,256]{1,0:T(8,128)(2,1)}, bf16[1152,256]{1,0:T(8,128)(2,1)}) fusion(bf16[2048,256]{1,0:T(8,128)(2,1)} %get-tuple-element.45.own), kind=kLoop, calls=%fused_computation.17 | loop fusion | bytes 2359296 | tf_op jit(solution)/shard_map/slice | solution.py:612
  95.1 1.9 collective-permute-start.17
  97.0 4.4 %collective-permute-start.18 = (bf16[1152,256]{1,0:T(8,128)(2,1)}, bf16[1152,256]{1,0:T(8,128)(2,1)}, u32[]{:S(2)}, u32[]{:S(2)}) collective-permute-start(bf16[1152,256]{1,0:T(8,128)(2,1)} %get-tuple-element.47), channel_id=1, source_target_pairs={{8,0},{16,8},{24,16},{32,24},{40,32},{48,40},{56,48},{64,56},{72,6... | collective-permute-start | bytes 1769480 | tf_op jit(solution)/shard_map/ppermute | solution.py:529
  101.4 0.7 add_convert_fusion.edges
  102.1 2.1 collective-permute-done.17.low
  104.2 8.0 %collective-permute-done.18.high = bf16[1152,256]{1,0:T(8,128)(2,1)} collective-permute-done((bf16[1152,256]{1,0:T(8,128)(2,1)}, bf16[1152,256]{1,0:T(8,128)(2,1)}, u32[]{:S(2)}, u32[]{:S(2)}) %collective-permute-start.18) | collective-permute-done | bytes 589856 | tf_op jit(solution)/shard_map/ppermute | solution.py:529
  112.2 19.2 %attend.1 = bf16[2048,128]{1,0:T(8,128)(2,1)} custom-call(s32[2]{0:T(128)} %add_convert_fusion.edges, bf16[2048,128]{1,0:T(8,128)(2,1)} %get-tuple-element.44.queries, bf16[1152,256]{1,0:T(8,128)(2,1)} %collective-permute-done.17.low, bf16[2048,256]{1,0:T(8,128)(2,1)} %get-tuple-element.45.own, bf16[1152,256]{1,0:T(8,128)(2,1)} %collective-permute-done.18.high), custom_call_target="tpu_custom_call" | custom-call | tf_op jit(solution)/shard_map/attend/pallas_call | solution.py:261
  132.5 4.2 %all-to-all-start = ((bf16[8,256,128]{2,1,0:T(8,128)(2,1)}), bf16[8,256,128]{2,1,0:T(8,128)(2,1)}, u32[]{:S(2)}, u32[]{:S(2)}) async-start(bf16[8,256,128]{2,1,0:T(8,128)(2,1)} %bitcast.49), calls=%async_computation | async-start | bytes 1048576 | tf_op jit(solution)/shard_map/all_to_all | solution.py:620
  136.8 0.6 concatenate.19.table
  137.4 9.5 %all-to-all-done.refs_8_ = bf16[8,256,128]{2,1,0:T(8,128)(2,1)} async-done(((bf16[8,256,128]{2,1,0:T(8,128)(2,1)}), bf16[8,256,128]{2,1,0:T(8,128)(2,1)}, u32[]{:S(2)}, u32[]{:S(2)}) %all-to-all-start) | async-done | bytes 524320 | tf_op jit(solution)/shard_map/all_to_all | solution.py:620
  147.0 12.8 %forward.1 = bf16[8,256,128]{2,1,0:T(8,128)(2,1)} custom-call(s32[16]{0:T(128)} %concatenate.19.table, bf16[4,2,144,1024]{3,2,1,0:T(8,128)(2,1)} %copy-done.1, bf16[4,2,144,1024]{3,2,1,0:T(8,128)(2,1)} %collective-permute-done.15.refs_1_, bf16[4,2,144,1024]{3,2,1,0:T(8,128)(2,1)} %collective-permute-done.16.refs_2_, ...), custom_call_target="tpu_custom_call" | custom-call | flops 4800000000 | bytes 20000000 | tf_op jit(solution)/shard_map/forward/pallas_call | solution.py:374
  159.8 12.7 %all_to_all.15 = bf16[8,256,128]{2,1,0:T(8,128)(2,1)S(1)} all-to-all(bf16[8,256,128]{2,1,0:T(8,128)(2,1)} %forward.1), channel_id=1, replica_groups=mesh['seq'=16,'head'=8] {'head'}, dimensions={0} | all-to-all | bytes 1048576 | tf_op jit(solution)/shard_map/all_to_all | solution.py:628
  172.5 3.3 %collective-permute-start.24 = (bf16[8,128,128]{2,1,0:T(8,128)(2,1)S(1)}, bf16[8,128,128]{2,1,0:T(8,128)(2,1)S(1)}, u32[]{:S(2)}, u32[]{:S(2)}) collective-permute-start(bf16[8,128,128]{2,1,0:T(8,128)(2,1)S(1)} %bitcast.61), channel_id=1, source_target_pairs={{0,8},{8,16},{16,24},{24,32},{32,40},{40,48},{48,56},{56,64},{64,7... | collective-permute-start | bytes 786440 | tf_op jit(solution)/shard_map/ppermute | solution.py:529
  175.8 2.6 %collective-permute-start.25 = (bf16[8,128,128]{2,1,0:T(8,128)(2,1)S(1)}, bf16[8,128,128]{2,1,0:T(8,128)(2,1)S(1)}, u32[]{:S(2)}, u32[]{:S(2)}) collective-permute-start(bf16[8,128,128]{2,1,0:T(8,128)(2,1)S(1)} %bitcast.60), channel_id=1, source_target_pairs={{8,0},{16,8},{24,16},{32,24},{40,32},{48,40},{56,48},{64,56},{72,6... | collective-permute-start | bytes 786440 | tf_op jit(solution)/shard_map/ppermute | solution.py:529
  179.1 8.0 %collective-permute-done.25.high = bf16[8,128,128]{2,1,0:T(8,128)(2,1)S(1)} collective-permute-done((bf16[8,128,128]{2,1,0:T(8,128)(2,1)S(1)}, bf16[8,128,128]{2,1,0:T(8,128)(2,1)S(1)}, u32[]{:S(2)}, u32[]{:S(2)}) %collective-permute-start.25) | collective-permute-done | bytes 262176 | tf_op jit(solution)/shard_map/ppermute | solution.py:529
  187.1 0.7 copy-done.12
  187.8 8.1 %decode.1 = (bf16[8192,128]{1,0:T(8,128)(2,1)}, bf16[8,16,128]{2,1,0:T(8,128)(2,1)}) custom-call(s32[64,2]{1,0:T(8,128)} %broadcast_subtract_fusion.index, bf16[8,128,128]{2,1,0:T(8,128)(2,1)} %copy-done.11, bf16[16,128,128]{2,1,0:T(8,128)(2,1)} %bitcast.48, bf16[8,128,128]{2,1,0:T(8,128)(2,1)} %copy-done.12, bf16[64,2,128,128]{3,2,1,0:T(8,128)(2,1)} %weights.3), custom_call_target="tpu_custom_call" | custom-call | flops 540000000 | bytes 10000000 | tf_op jit(solution)/shard_map/decode/pallas_call | solution.py:443
  195.8 0.8 broadcast_in_dim.3
  196.6 9.2 %all_to_all.16.sums = bf16[8,8,16,128]{3,2,1,0:T(8,128)(2,1)} all-to-all(bf16[8,8,16,128]{3,2,1,0:T(8,128)(2,1)S(1)} %broadcast_in_dim.3), channel_id=1, replica_groups=mesh['seq'=16,'head'=8] {'head'}, dimensions={0} | all-to-all | bytes 524288 | tf_op jit(solution)/shard_map/all_to_all | solution.py:638
  205.8 6.1 %finish.1 = bf16[8192,128]{1,0:T(8,128)(2,1)} custom-call(bf16[8,8,16,128]{3,2,1,0:T(8,128)(2,1)} %all_to_all.16.sums, bf16[8192,128]{1,0:T(8,128)(2,1)} %get-tuple-element.58.back, bf16[8192,128]{1,0:T(8,128)(2,1)} %state.1, f32[1,128]{1,0:T(1,128)} %bitcast.64), custom_call_target="tpu_custom_call" | custom-call | flops 540000000 | bytes 8000000 | tf_op jit(solution)/shard_map/finish/pallas_call | solution.py:507
  (71 shorter events, 4.8 us)
Async XLA Ops:
  0.0 3.3 %copy-start = (bf16[512,1024]{1,0:T(8,128)(2,1)S(1)}, bf16[512,1024]{1,0:T(8,128)(2,1)}, u32[]{:S(2)}) copy-start(bf16[512,1024]{1,0:T(8,128)(2,1)} %param.20) | copy-start | bytes 3145732
  0.0 14.4 %copy-start.13 = (s32[16,8]{0,1:T(8,128)S(1)}, s32[16,8]{0,1:T(8,128)}, u32[]{:S(2)}) copy-start(s32[16,8]{0,1:T(8,128)} %param.13) | copy-start | bytes 1540
  0.0 14.5 %copy-start.8 = (bf16[1024,3,128]{2,0,1:T(8,128)(2,1)S(1)}, bf16[1024,3,128]{2,0,1:T(8,128)(2,1)}, u32[]{:S(2)}) copy-start(bf16[1024,3,128]{2,0,1:T(8,128)(2,1)} %param.16) | copy-start | bytes 2359300
  4.2 11.3 %collective-permute-start.2 = (bf16[144,1024]{1,0:T(8,128)(2,1)S(1)}, bf16[144,1024]{1,0:T(8,128)(2,1)}, u32[]{:S(2)}, u32[]{:S(2)}) collective-permute-start(bf16[144,1024]{1,0:T(8,128)(2,1)S(1)} %pad_maximum_fusion.4), channel_id=1, source_target_pairs={{0,1},{1,0},{2,3},{3,2},{4,5},{5,4},{6,7},{7,6},{8,9},{9,8},{10,11... | collective-permute-start | bytes 884744 | tf_op jit(solution)/shard_map/ppermute | solution.py:533
  5.4 11.5 %collective-permute-start.8 = (bf16[144,1024]{1,0:T(8,128)(2,1)S(1)}, bf16[144,1024]{1,0:T(8,128)(2,1)}, u32[]{:S(2)}, u32[]{:S(2)}) collective-permute-start(bf16[144,1024]{1,0:T(8,128)(2,1)S(1)} %pad_maximum_fusion.4), channel_id=1, source_target_pairs={{0,2},{1,3},{2,4},{3,5},{4,6},{5,7},{6,0},{7,1},{8,10},{9,11},{10,... | collective-permute-start | bytes 884744 | tf_op jit(solution)/shard_map/ppermute | solution.py:533
  6.7 27.4 %collective-permute-start.9 = (bf16[144,1024]{1,0:T(8,128)(2,1)S(1)}, bf16[144,1024]{1,0:T(8,128)(2,1)}, u32[]{:S(2)}, u32[]{:S(2)}) collective-permute-start(bf16[144,1024]{1,0:T(8,128)(2,1)S(1)} %pad_maximum_fusion.4), channel_id=1, source_target_pairs={{0,6},{1,7},{2,0},{3,1},{4,2},{5,3},{6,4},{7,5},{8,14},{9,15},{10,... | collective-permute-start | bytes 884744 | tf_op jit(solution)/shard_map/ppermute | solution.py:533
  8.2 10.7 %collective-permute-start = (bf16[2048,128]{1,0:T(8,128)(2,1)}, bf16[2048,128]{1,0:T(8,128)(2,1)S(1)}, u32[]{:S(2)}, u32[]{:S(2)}) collective-permute-start(bf16[2048,128]{1,0:T(8,128)(2,1)} %get-tuple-element.32), channel_id=1, source_target_pairs={{0,8},{8,16},{16,24},{24,32},{32,40},{40,48},{48,56},{56,64},{64,7... | collective-permute-start | bytes 1572872 | tf_op jit(solution)/shard_map/ppermute | solution.py:529
  12.5 14.3 %collective-permute-start.1 = (bf16[2048,128]{1,0:T(8,128)(2,1)}, bf16[2048,128]{1,0:T(8,128)(2,1)S(1)}, u32[]{:S(2)}, u32[]{:S(2)}) collective-permute-start(bf16[2048,128]{1,0:T(8,128)(2,1)} %get-tuple-element.33), channel_id=1, source_target_pairs={{8,0},{16,8},{24,16},{32,24},{40,32},{48,40},{56,48},{64,56},{72,6... | collective-permute-start | bytes 1572872 | tf_op jit(solution)/shard_map/ppermute | solution.py:529
  15.4 11.4 %collective-permute-start.4 = (bf16[144,1024]{1,0:T(8,128)(2,1)}, bf16[144,1024]{1,0:T(8,128)(2,1)S(1)}, u32[]{:S(2)}, u32[]{:S(2)}) collective-permute-start(bf16[144,1024]{1,0:T(8,128)(2,1)} %collective-permute-done.2), channel_id=1, source_target_pairs={{0,6},{1,7},{2,0},{3,1},{4,2},{5,3},{6,4},{7,5},{8,14},{9,15},{10,... | collective-permute-start | bytes 884744 | tf_op jit(solution)/shard_map/ppermute | solution.py:533
  17.0 17.0 %collective-permute-start.3 = (bf16[144,1024]{1,0:T(8,128)(2,1)}, bf16[144,1024]{1,0:T(8,128)(2,1)S(1)}, u32[]{:S(2)}, u32[]{:S(2)}) collective-permute-start(bf16[144,1024]{1,0:T(8,128)(2,1)} %collective-permute-done.2), channel_id=1, source_target_pairs={{0,2},{1,3},{2,4},{3,5},{4,6},{5,7},{6,0},{7,1},{8,10},{9,11},{10,... | collective-permute-start | bytes 884744 | tf_op jit(solution)/shard_map/ppermute | solution.py:533
  18.9 9.4 %copy-start.9 = (bf16[2048,128]{1,0:T(8,128)(2,1)}, bf16[2048,128]{1,0:T(8,128)(2,1)S(1)}, u32[]{:S(2)}) copy-start(bf16[2048,128]{1,0:T(8,128)(2,1)S(1)} %collective-permute-done) | copy-start | bytes 1572868
  18.9 19.9 %collective-permute-start.10 = (bf16[144,1024]{1,0:T(8,128)(2,1)}, bf16[144,1024]{1,0:T(8,128)(2,1)S(1)}, u32[]{:S(2)}, u32[]{:S(2)}) collective-permute-start(bf16[144,1024]{1,0:T(8,128)(2,1)} %collective-permute-done.8), channel_id=1, source_target_pairs={{0,2},{1,3},{2,4},{3,5},{4,6},{5,7},{6,0},{7,1},{8,10},{9,11},{10,... | collective-permute-start | bytes 884744 | tf_op jit(solution)/shard_map/ppermute | solution.py:533
  26.8 1.5 copy-start.10
  26.8 12.0 %collective-permute-start.11 = (bf16[144,1024]{1,0:T(8,128)(2,1)S(1)}, bf16[144,1024]{1,0:T(8,128)(2,1)S(1)}, u32[]{:S(2)}, u32[]{:S(2)}) collective-permute-start(bf16[144,1024]{1,0:T(8,128)(2,1)S(1)} %collective-permute-done.4), channel_id=1, source_target_pairs={{0,6},{1,7},{2,0},{3,1},{4,2},{5,3},{6,4},{7,5},{8,14},{9,15},{10,... | collective-permute-start | bytes 884744 | tf_op jit(solution)/shard_map/ppermute | solution.py:533
  34.0 14.1 %collective-permute-start.5 = (bf16[2048,128]{1,0:T(8,128)(2,1)}, bf16[2048,128]{1,0:T(8,128)(2,1)S(1)}, u32[]{:S(2)}, u32[]{:S(2)}) collective-permute-start(bf16[2048,128]{1,0:T(8,128)(2,1)} %encode.1.s0), channel_id=1, source_target_pairs={{0,1},{1,0},{2,3},{3,2},{4,5},{5,4},{6,7},{7,6},{8,9},{9,8},{10,11... | collective-permute-start | bytes 1572872 | tf_op jit(solution)/shard_map/ppermute | solution.py:533
  34.0 15.2 %collective-permute-start.6 = (bf16[2048,128]{1,0:T(8,128)(2,1)}, bf16[2048,128]{1,0:T(8,128)(2,1)S(1)}, u32[]{:S(2)}, u32[]{:S(2)}) collective-permute-start(bf16[2048,128]{1,0:T(8,128)(2,1)} %encode.1.s0), channel_id=1, source_target_pairs={{0,2},{1,3},{2,4},{3,5},{4,6},{5,7},{6,0},{7,1},{8,10},{9,11},{10,... | collective-permute-start | bytes 1572872 | tf_op jit(solution)/shard_map/ppermute | solution.py:533
  34.1 15.1 %collective-permute-start.7 = (bf16[2048,128]{1,0:T(8,128)(2,1)}, bf16[2048,128]{1,0:T(8,128)(2,1)S(1)}, u32[]{:S(2)}, u32[]{:S(2)}) collective-permute-start(bf16[2048,128]{1,0:T(8,128)(2,1)} %encode.1.s0), channel_id=1, source_target_pairs={{0,6},{1,7},{2,0},{3,1},{4,2},{5,3},{6,4},{7,5},{8,14},{9,15},{10,... | collective-permute-start | bytes 1572872 | tf_op jit(solution)/shard_map/ppermute | solution.py:533
  39.2 92.2 %copy-start.1 = (bf16[4,2,144,1024]{3,2,1,0:T(8,128)(2,1)}, bf16[4,2,144,1024]{3,2,1,0:T(8,128)(2,1)S(1)}, u32[]{:S(2)}) copy-start(bf16[4,2,144,1024]{3,2,1,0:T(8,128)(2,1)S(1)} %pad_maximum_fusion.refs_0_) | copy-start | bytes 7077892
  39.2 55.9 %collective-permute-start.15 = (bf16[4,2,144,1024]{3,2,1,0:T(8,128)(2,1)S(1)}, bf16[4,2,144,1024]{3,2,1,0:T(8,128)(2,1)}, u32[]{:S(2)}, u32[]{:S(2)}) collective-permute-start(bf16[4,2,144,1024]{3,2,1,0:T(8,128)(2,1)S(1)} %pad_maximum_fusion.refs_0_), channel_id=1, source_target_pairs={{0,16},{8,24},{16,32},{24,40},{32,48},{40,56},{48,0},{56,8},{64,80... | collective-permute-start | bytes 7077896 | tf_op jit(solution)/shard_map/ppermute | solution.py:533
  39.3 55.8 %collective-permute-start.16 = (bf16[4,2,144,1024]{3,2,1,0:T(8,128)(2,1)S(1)}, bf16[4,2,144,1024]{3,2,1,0:T(8,128)(2,1)}, u32[]{:S(2)}, u32[]{:S(2)}) collective-permute-start(bf16[4,2,144,1024]{3,2,1,0:T(8,128)(2,1)S(1)} %pad_maximum_fusion.refs_0_), channel_id=1, source_target_pairs={{0,48},{8,56},{16,0},{24,8},{32,16},{40,24},{48,32},{56,40},{64,11... | collective-permute-start | bytes 7077896 | tf_op jit(solution)/shard_map/ppermute | solution.py:533
  48.1 23.0 %copy-start.3 = (bf16[2048,128]{1,0:T(8,128)(2,1)}, bf16[2048,128]{1,0:T(8,128)(2,1)S(1)}, u32[]{:S(2)}) copy-start(bf16[2048,128]{1,0:T(8,128)(2,1)S(1)} %collective-permute-done.5.s1) | copy-start | bytes 1572868
  49.3 21.9 %copy-start.6 = (bf16[2048,128]{1,0:T(8,128)(2,1)}, bf16[2048,128]{1,0:T(8,128)(2,1)S(1)}, u32[]{:S(2)}) copy-start(bf16[2048,128]{1,0:T(8,128)(2,1)S(1)} %collective-permute-done.6.s2) | copy-start | bytes 1572868
  49.3 22.7 %copy-start.7 = (bf16[2048,128]{1,0:T(8,128)(2,1)}, bf16[2048,128]{1,0:T(8,128)(2,1)S(1)}, u32[]{:S(2)}) copy-start(bf16[2048,128]{1,0:T(8,128)(2,1)S(1)} %collective-permute-done.7.s4) | copy-start | bytes 1572868
  49.4 19.9 %collective-permute-start.12 = (bf16[3072,128]{1,0:T(8,128)(2,1)S(1)}, bf16[3072,128]{1,0:T(8,128)(2,1)S(1)}, u32[]{:S(2)}, u32[]{:S(2)}) collective-permute-start(bf16[3072,128]{1,0:T(8,128)(2,1)S(1)} %get-tuple-element.71), channel_id=1, source_target_pairs={{0,2},{1,3},{2,4},{3,5},{4,6},{5,7},{6,0},{7,1},{8,10},{9,11},{10,... | collective-permute-start | bytes 2359304 | tf_op jit(solution)/shard_map/ppermute | solution.py:533
  49.5 20.7 %collective-permute-start.13 = (bf16[3072,128]{1,0:T(8,128)(2,1)S(1)}, bf16[3072,128]{1,0:T(8,128)(2,1)S(1)}, u32[]{:S(2)}, u32[]{:S(2)}) collective-permute-start(bf16[3072,128]{1,0:T(8,128)(2,1)S(1)} %get-tuple-element.70), channel_id=1, source_target_pairs={{0,6},{1,7},{2,0},{3,1},{4,2},{5,3},{6,4},{7,5},{8,14},{9,15},{10,... | collective-permute-start | bytes 2359304 | tf_op jit(solution)/shard_map/ppermute | solution.py:533
  52.2 79.2 %collective-permute-start.19 = (bf16[4,2,144,1024]{3,2,1,0:T(8,128)(2,1)S(1)}, bf16[4,2,144,1024]{3,2,1,0:T(8,128)(2,1)}, u32[]{:S(2)}, u32[]{:S(2)}) collective-permute-start(bf16[4,2,144,1024]{3,2,1,0:T(8,128)(2,1)S(1)} %pad_maximum_fusion.refs_0_), channel_id=1, source_target_pairs={{0,65},{1,64},{2,67},{3,66},{4,69},{5,68},{6,71},{7,70},{8,73},{9,... | collective-permute-start | bytes 7077896 | tf_op jit(solution)/shard_map/ppermute | solution.py:533
  69.3 0.9 copy-start.4
  70.2 0.9 copy-start.5
  72.0 12.4 %collective-permute-start.14 = (bf16[2048,128]{1,0:T(8,128)(2,1)}, bf16[2048,128]{1,0:T(8,128)(2,1)}, u32[]{:S(2)}, u32[]{:S(2)}) collective-permute-start(bf16[2048,128]{1,0:T(8,128)(2,1)} %pad_maximum_fusion.3.s6), channel_id=1, source_target_pairs={{0,1},{1,0},{2,3},{3,2},{4,5},{5,4},{6,7},{7,6},{8,9},{9,8},{10,11... | collective-permute-start | bytes 1572872 | tf_op jit(solution)/shard_map/ppermute | solution.py:533
  95.1 9.1 %collective-permute-start.17 = (bf16[1152,256]{1,0:T(8,128)(2,1)}, bf16[1152,256]{1,0:T(8,128)(2,1)}, u32[]{:S(2)}, u32[]{:S(2)}) collective-permute-start(bf16[1152,256]{1,0:T(8,128)(2,1)} %get-tuple-element.46), channel_id=1, source_target_pairs={{0,8},{8,16},{16,24},{24,32},{32,40},{40,48},{48,56},{56,64},{64,7... | collective-permute-start | bytes 1769480 | tf_op jit(solution)/shard_map/ppermute | solution.py:529
  97.0 15.1 %collective-permute-start.18 = (bf16[1152,256]{1,0:T(8,128)(2,1)}, bf16[1152,256]{1,0:T(8,128)(2,1)}, u32[]{:S(2)}, u32[]{:S(2)}) collective-permute-start(bf16[1152,256]{1,0:T(8,128)(2,1)} %get-tuple-element.47), channel_id=1, source_target_pairs={{8,0},{16,8},{24,16},{32,24},{40,32},{48,40},{56,48},{64,56},{72,6... | collective-permute-start | bytes 1769480 | tf_op jit(solution)/shard_map/ppermute | solution.py:529
  131.4 15.5 %collective-permute-start.20 = (bf16[4,2,144,1024]{3,2,1,0:T(8,128)(2,1)S(1)}, bf16[4,2,144,1024]{3,2,1,0:T(8,128)(2,1)}, u32[]{:S(2)}, u32[]{:S(2)}) collective-permute-start(bf16[4,2,144,1024]{3,2,1,0:T(8,128)(2,1)S(1)} %pad_maximum_fusion.refs_0_), channel_id=1, source_target_pairs={{0,8},{8,0},{16,24},{24,16},{32,40},{40,32},{48,56},{56,48},{64,72... | collective-permute-start | bytes 7077896 | tf_op jit(solution)/shard_map/ppermute | solution.py:533
  131.5 15.4 %collective-permute-start.21 = (bf16[4,2,144,1024]{3,2,1,0:T(8,128)(2,1)}, bf16[4,2,144,1024]{3,2,1,0:T(8,128)(2,1)}, u32[]{:S(2)}, u32[]{:S(2)}) collective-permute-start(bf16[4,2,144,1024]{3,2,1,0:T(8,128)(2,1)} %collective-permute-done.15.refs_1_), channel_id=1, source_target_pairs={{0,8},{8,0},{16,24},{24,16},{32,40},{40,32},{48,56},{56,48},{64,72... | collective-permute-start | bytes 7077896 | tf_op jit(solution)/shard_map/ppermute | solution.py:533
  132.0 14.9 %collective-permute-start.22 = (bf16[4,2,144,1024]{3,2,1,0:T(8,128)(2,1)}, bf16[4,2,144,1024]{3,2,1,0:T(8,128)(2,1)}, u32[]{:S(2)}, u32[]{:S(2)}) collective-permute-start(bf16[4,2,144,1024]{3,2,1,0:T(8,128)(2,1)} %collective-permute-done.16.refs_2_), channel_id=1, source_target_pairs={{0,8},{8,0},{16,24},{24,16},{32,40},{40,32},{48,56},{56,48},{64,72... | collective-permute-start | bytes 7077896 | tf_op jit(solution)/shard_map/ppermute | solution.py:533
  132.1 14.8 %collective-permute-start.23 = (bf16[4,2,144,1024]{3,2,1,0:T(8,128)(2,1)}, bf16[4,2,144,1024]{3,2,1,0:T(8,128)(2,1)}, u32[]{:S(2)}, u32[]{:S(2)}) collective-permute-start(bf16[4,2,144,1024]{3,2,1,0:T(8,128)(2,1)} %collective-permute-done.19.refs_3_), channel_id=1, source_target_pairs={{0,8},{8,0},{16,24},{24,16},{32,40},{40,32},{48,56},{56,48},{64,72... | collective-permute-start | bytes 7077896 | tf_op jit(solution)/shard_map/ppermute | solution.py:533
  132.5 14.4 %all-to-all-start = ((bf16[8,256,128]{2,1,0:T(8,128)(2,1)}), bf16[8,256,128]{2,1,0:T(8,128)(2,1)}, u32[]{:S(2)}, u32[]{:S(2)}) async-start(bf16[8,256,128]{2,1,0:T(8,128)(2,1)} %bitcast.49), calls=%async_computation | async-start | bytes 1048576 | tf_op jit(solution)/shard_map/all_to_all | solution.py:620
  147.0 31.4 %copy-start.14 = (s32[64,2]{0,1:T(2,128)S(1)}, s32[64,2]{0,1:T(2,128)}, u32[]{:S(2)}) copy-start(s32[64,2]{0,1:T(2,128)} %param.21) | copy-start | bytes 1540
  172.4 14.6 %copy-start.2 = (bf16[8,256,128]{2,1,0:T(8,128)(2,1)}, bf16[8,256,128]{2,1,0:T(8,128)(2,1)S(1)}, u32[]{:S(2)}) copy-start(bf16[8,256,128]{2,1,0:T(8,128)(2,1)S(1)} %all_to_all.15) | copy-start | bytes 1572868
  172.5 6.6 %collective-permute-start.24 = (bf16[8,128,128]{2,1,0:T(8,128)(2,1)S(1)}, bf16[8,128,128]{2,1,0:T(8,128)(2,1)S(1)}, u32[]{:S(2)}, u32[]{:S(2)}) collective-permute-start(bf16[8,128,128]{2,1,0:T(8,128)(2,1)S(1)} %bitcast.61), channel_id=1, source_target_pairs={{0,8},{8,16},{16,24},{24,32},{32,40},{40,48},{48,56},{56,64},{64,7... | collective-permute-start | bytes 786440 | tf_op jit(solution)/shard_map/ppermute | solution.py:529
  175.8 11.3 %collective-permute-start.25 = (bf16[8,128,128]{2,1,0:T(8,128)(2,1)S(1)}, bf16[8,128,128]{2,1,0:T(8,128)(2,1)S(1)}, u32[]{:S(2)}, u32[]{:S(2)}) collective-permute-start(bf16[8,128,128]{2,1,0:T(8,128)(2,1)S(1)} %bitcast.60), channel_id=1, source_target_pairs={{8,0},{16,8},{24,16},{32,24},{40,32},{48,40},{56,48},{64,56},{72,6... | collective-permute-start | bytes 786440 | tf_op jit(solution)/shard_map/ppermute | solution.py:529
  179.1 8.0 %copy-start.11 = (bf16[8,128,128]{2,1,0:T(8,128)(2,1)}, bf16[8,128,128]{2,1,0:T(8,128)(2,1)S(1)}, u32[]{:S(2)}) copy-start(bf16[8,128,128]{2,1,0:T(8,128)(2,1)S(1)} %collective-permute-done.24.low) | copy-start | bytes 786436
  187.1 0.7 copy-start.12

commit v12 on v11

--- a/solution.py
+++ b/solution.py
@@ -106,7 +106,7 @@
 
 def project_kernel(
     order, s0, s1, s2, s3, s4, s5, s6, s7, gain, wq, wk, wv,
-    queries, keys_values, share, ordered, normed,
+    queries, keys_values, share, lower, upper, ordered, normed,
 ):
     step = pl.program_id(0)
 
@@ -145,7 +145,18 @@
             normed[at, p * BLOCK : (p + 1) * BLOCK] = (x * spread * gains[p]).astype(BF)
     made = dot(normed[...], ordered[...])
     queries[...] = (made[:, :BLOCK] * (HEAD_DIM**-0.5 * LOG2E)).astype(BF)
-    keys_values[...] = made[:, BLOCK:].astype(BF)
+    both = made[:, BLOCK:].astype(BF)
+    keys_values[...] = both
+    for n in range(4):
+        start, stop = n * rows, (n + 1) * rows
+        skip = 4 * rows - REACH
+
+        @pl.when(step == n)
+        def _():
+            if start < REACH:
+                lower[start : min(stop, REACH)] = both[: min(stop, REACH) - start]
+            if stop > skip:
+                upper[max(start, skip) - skip : stop - skip] = both[max(start, skip) - start :]
 
 
 def project(order, slots, gain, weights):
@@ -160,6 +171,8 @@
             jax.ShapeDtypeStruct((rows, BLOCK), BF),
             jax.ShapeDtypeStruct((rows, 2 * BLOCK), BF),
             jax.ShapeDtypeStruct((8, tile, BLOCK), BF),
+            jax.ShapeDtypeStruct((REACH, 2 * BLOCK), BF),
+            jax.ShapeDtypeStruct((REACH, 2 * BLOCK), BF),
         ),
         grid_spec=pltpu.PrefetchScalarGridSpec(
             num_scalar_prefetch=1,
@@ -171,6 +184,8 @@
                 full,
                 pl.BlockSpec((each, 2 * BLOCK), lambda i, _: (i, 0)),
                 whole((8, tile, BLOCK)),
+                whole((REACH, 2 * BLOCK)),
+                whole((REACH, 2 * BLOCK)),
             ),
             scratch_shapes=[pltpu.VMEM((D, 3 * BLOCK), BF), pltpu.VMEM((each, D), BF)],
         ),
@@ -607,9 +622,9 @@
     order = jnp.stack(
         [me, partner] + [(v + by) % 8 for by in (6, 2, 4) for v in (me, partner)]
     ).astype(jnp.int32)
-    queries, keys_values, share = project(order, slots, first_gain, inward)
+    queries, keys_values, share, lower, upper = project(order, slots, first_gain, inward)
     upper, lower, up, down = lax.optimization_barrier(
-        (keys_values[mesh_rows - REACH :], keys_values[:REACH], up, down)
+        (upper, lower, up, down)
     )
     below = shifted(upper, 1)
     above = shifted(lower, -1)

time: 213 us -> 211 us (level)
  waiting for transfers between devices: 71.6 us -> 66.7 us
  starting transfers between devices: 39.4 us -> 44 us
  local copies, waits for them, and re-layouts: 12.1 us -> 9.87 us
    ppermute x20, waiting for transfers between devices: 36.1 us -> 31.4 us  [among(): return lax.ppermute(value, axis, [(i, to(i)) for i in range(count)])]
    ppermute x20, starting transfers between devices: 16.9 us -> 20.6 us  [among(): return lax.ppermute(value, axis, [(i, to(i)) for i in range(count)])]
    slice x1 -> x0, local copies, waits for them, and re-layouts: 2.33 us -> none  [on_device(): keys_values[:REACH]]
  transfers between devices with their start and end apart: 27 -> 27, of which waited for: 10 -> 10; matrix products, arithmetic and copies ran while one was open for 5% -> 4% of each run, Pallas kernels for 16% -> 16%
where the time goes in v12:
time: 211 us; the launch traced here: 209 us
  waiting for transfers between devices  66.7 us (32%)
  Pallas kernels  60.8 us (29%)
  starting transfers between devices  44 us (21%)
  blocking collectives  22.1 us (10%)
  local copies, waits for them, and re-layouts  9.87 us (5%)
  other arithmetic  5.25 us (2%)
    ppermute x20, waiting for transfers between devices, among(): return lax.ppermute(value, axis, [(i, to(i)) for i in range(count)])  31.4 us
    ppermute x6, waiting for transfers between devices, shifted(): lax.ppermute(value, 'seq', [(i, i + by) for i in range(16) if 0 <= i + by...  25.9 us
    ppermute x20, starting transfers between devices, among(): return lax.ppermute(value, axis, [(i, to(i)) for i in range(count)])  20.6 us
    ppermute x6, starting transfers between devices, shifted(): lax.ppermute(value, 'seq', [(i, i + by) for i in range(16) if 0 <= i + by...  19.3 us
    pallas_call x1, Pallas kernels, attend(): pl.pallas_call(attend_kernel, out_shape=jax.ShapeDtypeStruct((rows, BLOCK...  19.2 us
    all_to_all x1, blocking collectives, on_device(): mesh_end = lax.all_to_all(mesh_end, 'head', 0, 0, tiled=True)  12.9 us
    pallas_call x1, Pallas kernels, forward(): pl.pallas_call(forward_kernel, out_shape=jax.ShapeDtypeStruct((8, rows, B...  12.8 us
    all_to_all x1, waiting for transfers between devices, on_device(): lax.all_to_all(context.reshape(8, mesh_rows // 8, BLOCK), 'head', 0, 0, t...  9.33 us
  transfers between devices with their start and end apart: 27, of which 10 were waited for; matrix products, arithmetic and copies ran while one was open for 4% of the time, Pallas kernels for 16%

profile of v12, /device:TPU:97, one launch (start us, length us, event | category | flops | bytes accessed | tf_op | source)
XLA Modules:
  0.0 209.4 jit_solution(12564056267862186151)
XLA Ops:
  0.0 2.4 %fusion = (bf16[2048,128]{1,0:T(8,128)(2,1)}, bf16[2048,128]{1,0:T(8,128)(2,1)}) fusion(bf16[8192,128]{1,0:T(8,128)(2,1)} %state.1), kind=kLoop, calls=%fused_computation.16 | loop fusion | bytes 2097152 | tf_op jit(solution)/shard_map/slice | solution.py:589
  2.4 0.9 constant_dynamic-slice_fusion
  3.3 0.8 constant_dynamic-slice_fusion.1
  4.1 1.3 collective-permute-start.2
  5.4 1.3 collective-permute-start.8
  6.7 4.1 %collective-permute-start = (bf16[2048,128]{1,0:T(8,128)(2,1)}, bf16[2048,128]{1,0:T(8,128)(2,1)S(1)}, u32[]{:S(2)}, u32[]{:S(2)}) collective-permute-start(bf16[2048,128]{1,0:T(8,128)(2,1)} %get-tuple-element.34), channel_id=1, source_target_pairs={{0,8},{8,16},{16,24},{24,32},{32,40},{40,48},{48,56},{56,64},{64,7... | collective-permute-start | bytes 1572872 | tf_op jit(solution)/shard_map/ppermute | solution.py:544
  10.8 1.9 collective-permute-start.1
  12.7 0.9 fusion.1
  13.7 1.4 collective-permute-start.4
  15.8 2.6 %collective-permute-start.9 = (bf16[144,1024]{1,0:T(8,128)(2,1)S(1)}, bf16[144,1024]{1,0:T(8,128)(2,1)S(1)}, u32[]{:S(2)}, u32[]{:S(2)}) collective-permute-start(bf16[144,1024]{1,0:T(8,128)(2,1)S(1)} %pad_maximum_fusion.4), channel_id=1, source_target_pairs={{0,6},{1,7},{2,0},{3,1},{4,2},{5,3},{6,4},{7,5},{8,14},{9,15},{10,... | collective-permute-start | bytes 884744 | tf_op jit(solution)/shard_map/ppermute | solution.py:548
  18.4 1.0 maximum_bitcast_fusion
  19.5 5.6 %collective-permute-done.1 = bf16[2048,128]{1,0:T(8,128)(2,1)S(1)} collective-permute-done((bf16[2048,128]{1,0:T(8,128)(2,1)}, bf16[2048,128]{1,0:T(8,128)(2,1)S(1)}, u32[]{:S(2)}, u32[]{:S(2)}) %collective-permute-start.1) | collective-permute-done | bytes 524320 | tf_op jit(solution)/shard_map/ppermute | solution.py:544
  25.1 1.4 collective-permute-start.11
  26.5 5.6 %encode.1.s0 = bf16[2048,128]{1,0:T(8,128)(2,1)} custom-call(s32[16,8]{1,0:T(8,128)} %broadcast_subtract_fusion.1.index, bf16[16,128,128]{2,1,0:T(8,128)(2,1)} %bitcast.54, bf16[64,128,128]{2,1,0:T(8,128)(2,1)} %bitcast.47, bf16[16,128,128]{2,1,0:T(8,128)(2,1)} %bitcast.55, bf16[16,8,128,128]{3,2,1,0:T(8,128)(2,1)} %weights.2), custom_call_target="tpu_custom_call" | custom-call | flops 540000000 | bytes 8000000 | tf_op jit(solution)/shard_map/encode/pallas_call | solution.py:86
  32.2 0.8 collective-permute-start.6
  33.0 1.0 maximum_bitcast_fusion.1
  34.0 2.1 collective-permute-start.7
  36.6 1.5 collective-permute-start.16
  38.0 5.0 %collective-permute-done.5.s1 = bf16[2048,128]{1,0:T(8,128)(2,1)S(1)} collective-permute-done((bf16[2048,128]{1,0:T(8,128)(2,1)}, bf16[2048,128]{1,0:T(8,128)(2,1)S(1)}, u32[]{:S(2)}, u32[]{:S(2)}) %collective-permute-start.5) | collective-permute-done | bytes 524320 | tf_op jit(solution)/shard_map/ppermute | solution.py:548
  43.1 1.2 collective-permute-done.7.s4
  44.6 3.1 %collective-permute-start.12 = (bf16[3072,128]{1,0:T(8,128)(2,1)S(1)}, bf16[3072,128]{1,0:T(8,128)(2,1)S(1)}, u32[]{:S(2)}, u32[]{:S(2)}) collective-permute-start(bf16[3072,128]{1,0:T(8,128)(2,1)S(1)} %get-tuple-element.73), channel_id=1, source_target_pairs={{0,2},{1,3},{2,4},{3,5},{4,6},{5,7},{6,0},{7,1},{8,10},{9,11},{10,... | collective-permute-start | bytes 2359304 | tf_op jit(solution)/shard_map/ppermute | solution.py:548
  47.6 14.4 %collective-permute-done.12.s3 = bf16[3072,128]{1,0:T(8,128)(2,1)S(1)} collective-permute-done((bf16[3072,128]{1,0:T(8,128)(2,1)S(1)}, bf16[3072,128]{1,0:T(8,128)(2,1)S(1)}, u32[]{:S(2)}, u32[]{:S(2)}) %collective-permute-start.12) | collective-permute-done | bytes 786464 | tf_op jit(solution)/shard_map/ppermute | solution.py:548
  62.0 0.9 copy-done.4
  62.9 1.1 collective-permute-done.13.s5
  64.0 0.9 copy-done.5
  65.0 0.8 pad_maximum_fusion.3.s6
  65.8 3.8 %collective-permute-start.14 = (bf16[2048,128]{1,0:T(8,128)(2,1)}, bf16[2048,128]{1,0:T(8,128)(2,1)}, u32[]{:S(2)}, u32[]{:S(2)}) collective-permute-start(bf16[2048,128]{1,0:T(8,128)(2,1)} %pad_maximum_fusion.3.s6), channel_id=1, source_target_pairs={{0,1},{1,0},{2,3},{3,2},{4,5},{5,4},{6,7},{7,6},{8,9},{9,8},{10,11... | collective-permute-start | bytes 1572872 | tf_op jit(solution)/shard_map/ppermute | solution.py:548
  70.2 9.6 %collective-permute-done.14.s7 = bf16[2048,128]{1,0:T(8,128)(2,1)} collective-permute-done((bf16[2048,128]{1,0:T(8,128)(2,1)}, bf16[2048,128]{1,0:T(8,128)(2,1)}, u32[]{:S(2)}, u32[]{:S(2)}) %collective-permute-start.14) | collective-permute-done | bytes 524320 | tf_op jit(solution)/shard_map/ppermute | solution.py:548
  79.9 9.1 %project.1 = (bf16[2048,128]{1,0:T(8,128)(2,1)}, bf16[2048,256]{1,0:T(8,128)(2,1)}, bf16[8,256,128]{2,1,0:T(8,128)(2,1)}, bf16[1152,256]{1,0:T(8,128)(2,1)}, bf16[1152,256]{1,0:T(8,128)(2,1)}) custom-call(s32[8]{0:T(128)} %stack.130.order, bf16[2048,128]{1,0:T(8,128)(2,1)} %encode.1.s0, bf16[2048,128]{1,0:T(8,128)(2,1)} %copy-done.3, ...), custom_call_target="tpu_custom_call" | custom-call | tf_op jit(solution)/shard_map/project/pallas_call | solution.py:168
  89.0 5.3 %collective-permute-start.17 = (bf16[1152,256]{1,0:T(8,128)(2,1)}, bf16[1152,256]{1,0:T(8,128)(2,1)}, u32[]{:S(2)}, u32[]{:S(2)}) collective-permute-start(bf16[1152,256]{1,0:T(8,128)(2,1)} %get-tuple-element.49), channel_id=1, source_target_pairs={{0,8},{8,16},{16,24},{24,32},{32,40},{40,48},{48,56},{56,64},{64,7... | collective-permute-start | bytes 1769480 | tf_op jit(solution)/shard_map/ppermute | solution.py:544
  94.3 2.1 %collective-permute-start.18 = (bf16[1152,256]{1,0:T(8,128)(2,1)}, bf16[1152,256]{1,0:T(8,128)(2,1)}, u32[]{:S(2)}, u32[]{:S(2)}) collective-permute-start(bf16[1152,256]{1,0:T(8,128)(2,1)} %get-tuple-element.51), channel_id=1, source_target_pairs={{8,0},{16,8},{24,16},{32,24},{40,32},{48,40},{56,48},{64,56},{72,6... | collective-permute-start | bytes 1769480 | tf_op jit(solution)/shard_map/ppermute | solution.py:544
  96.4 0.7 add_convert_fusion.edges
  97.1 4.4 %collective-permute-done.17.low = bf16[1152,256]{1,0:T(8,128)(2,1)} collective-permute-done((bf16[1152,256]{1,0:T(8,128)(2,1)}, bf16[1152,256]{1,0:T(8,128)(2,1)}, u32[]{:S(2)}, u32[]{:S(2)}) %collective-permute-start.17) | collective-permute-done | bytes 589856 | tf_op jit(solution)/shard_map/ppermute | solution.py:544
  101.4 8.0 %collective-permute-done.18.high = bf16[1152,256]{1,0:T(8,128)(2,1)} collective-permute-done((bf16[1152,256]{1,0:T(8,128)(2,1)}, bf16[1152,256]{1,0:T(8,128)(2,1)}, u32[]{:S(2)}, u32[]{:S(2)}) %collective-permute-start.18) | collective-permute-done | bytes 589856 | tf_op jit(solution)/shard_map/ppermute | solution.py:544
  109.4 19.2 %attend.1 = bf16[2048,128]{1,0:T(8,128)(2,1)} custom-call(s32[2]{0:T(128)} %add_convert_fusion.edges, bf16[2048,128]{1,0:T(8,128)(2,1)} %get-tuple-element.46.queries, bf16[1152,256]{1,0:T(8,128)(2,1)} %collective-permute-done.17.low, bf16[2048,256]{1,0:T(8,128)(2,1)} %get-tuple-element.50.own, bf16[1152,256]{1,0:T(8,128)(2,1)} %collective-permute-done.18.high), custom_call_target="tpu_custom_call" | custom-call | tf_op jit(solution)/shard_map/attend/pallas_call | solution.py:276
  129.8 4.1 %all-to-all-start = ((bf16[8,256,128]{2,1,0:T(8,128)(2,1)}), bf16[8,256,128]{2,1,0:T(8,128)(2,1)}, u32[]{:S(2)}, u32[]{:S(2)}) async-start(bf16[8,256,128]{2,1,0:T(8,128)(2,1)} %bitcast.49), calls=%async_computation | async-start | bytes 1048576 | tf_op jit(solution)/shard_map/all_to_all | solution.py:635
  134.0 0.7 concatenate.19.table
  134.7 9.3 %all-to-all-done.refs_8_ = bf16[8,256,128]{2,1,0:T(8,128)(2,1)} async-done(((bf16[8,256,128]{2,1,0:T(8,128)(2,1)}), bf16[8,256,128]{2,1,0:T(8,128)(2,1)}, u32[]{:S(2)}, u32[]{:S(2)}) %all-to-all-start) | async-done | bytes 524320 | tf_op jit(solution)/shard_map/all_to_all | solution.py:635
  144.0 12.8 %forward.1 = bf16[8,256,128]{2,1,0:T(8,128)(2,1)} custom-call(s32[16]{0:T(128)} %concatenate.19.table, bf16[4,2,144,1024]{3,2,1,0:T(8,128)(2,1)} %copy-done.1, bf16[4,2,144,1024]{3,2,1,0:T(8,128)(2,1)} %collective-permute-done.15.refs_1_, bf16[4,2,144,1024]{3,2,1,0:T(8,128)(2,1)} %collective-permute-done.16.refs_2_, ...), custom_call_target="tpu_custom_call" | custom-call | flops 4800000000 | bytes 20000000 | tf_op jit(solution)/shard_map/forward/pallas_call | solution.py:389
  156.8 12.9 %all_to_all.15 = bf16[8,256,128]{2,1,0:T(8,128)(2,1)S(1)} all-to-all(bf16[8,256,128]{2,1,0:T(8,128)(2,1)} %forward.1), channel_id=1, replica_groups=mesh['seq'=16,'head'=8] {'head'}, dimensions={0} | all-to-all | bytes 1048576 | tf_op jit(solution)/shard_map/all_to_all | solution.py:643
  169.8 3.3 %collective-permute-start.24 = (bf16[8,128,128]{2,1,0:T(8,128)(2,1)S(1)}, bf16[8,128,128]{2,1,0:T(8,128)(2,1)S(1)}, u32[]{:S(2)}, u32[]{:S(2)}) collective-permute-start(bf16[8,128,128]{2,1,0:T(8,128)(2,1)S(1)} %bitcast.62), channel_id=1, source_target_pairs={{0,8},{8,16},{16,24},{24,32},{32,40},{40,48},{48,56},{56,64},{64,7... | collective-permute-start | bytes 786440 | tf_op jit(solution)/shard_map/ppermute | solution.py:544
  173.1 2.6 %collective-permute-start.25 = (bf16[8,128,128]{2,1,0:T(8,128)(2,1)S(1)}, bf16[8,128,128]{2,1,0:T(8,128)(2,1)S(1)}, u32[]{:S(2)}, u32[]{:S(2)}) collective-permute-start(bf16[8,128,128]{2,1,0:T(8,128)(2,1)S(1)} %bitcast.61), channel_id=1, source_target_pairs={{8,0},{16,8},{24,16},{32,24},{40,32},{48,40},{56,48},{64,56},{72,6... | collective-permute-start | bytes 786440 | tf_op jit(solution)/shard_map/ppermute | solution.py:544
  176.5 8.0 %collective-permute-done.25.high = bf16[8,128,128]{2,1,0:T(8,128)(2,1)S(1)} collective-permute-done((bf16[8,128,128]{2,1,0:T(8,128)(2,1)S(1)}, bf16[8,128,128]{2,1,0:T(8,128)(2,1)S(1)}, u32[]{:S(2)}, u32[]{:S(2)}) %collective-permute-start.25) | collective-permute-done | bytes 262176 | tf_op jit(solution)/shard_map/ppermute | solution.py:544
  184.4 0.7 copy-done.12
  185.1 8.0 %decode.1 = (bf16[8192,128]{1,0:T(8,128)(2,1)}, bf16[8,16,128]{2,1,0:T(8,128)(2,1)}) custom-call(s32[64,2]{1,0:T(8,128)} %broadcast_subtract_fusion.index, bf16[8,128,128]{2,1,0:T(8,128)(2,1)} %copy-done.11, bf16[16,128,128]{2,1,0:T(8,128)(2,1)} %bitcast.48, bf16[8,128,128]{2,1,0:T(8,128)(2,1)} %copy-done.12, bf16[64,2,128,128]{3,2,1,0:T(8,128)(2,1)} %weights.3), custom_call_target="tpu_custom_call" | custom-call | flops 540000000 | bytes 10000000 | tf_op jit(solution)/shard_map/decode/pallas_call | solution.py:458
  193.2 0.8 broadcast_in_dim.3
  194.0 9.2 %all_to_all.16.sums = bf16[8,8,16,128]{3,2,1,0:T(8,128)(2,1)} all-to-all(bf16[8,8,16,128]{3,2,1,0:T(8,128)(2,1)S(1)} %broadcast_in_dim.3), channel_id=1, replica_groups=mesh['seq'=16,'head'=8] {'head'}, dimensions={0} | all-to-all | bytes 524288 | tf_op jit(solution)/shard_map/all_to_all | solution.py:653
  203.2 6.1 %finish.1 = bf16[8192,128]{1,0:T(8,128)(2,1)} custom-call(bf16[8,8,16,128]{3,2,1,0:T(8,128)(2,1)} %all_to_all.16.sums, bf16[8192,128]{1,0:T(8,128)(2,1)} %get-tuple-element.62.back, bf16[8192,128]{1,0:T(8,128)(2,1)} %state.1, f32[1,128]{1,0:T(1,128)} %bitcast.65), custom_call_target="tpu_custom_call" | custom-call | flops 540000000 | bytes 8000000 | tf_op jit(solution)/shard_map/finish/pallas_call | solution.py:522
  (70 shorter events, 4.3 us)
Async XLA Ops:
  0.0 3.3 %copy-start = (bf16[512,1024]{1,0:T(8,128)(2,1)S(1)}, bf16[512,1024]{1,0:T(8,128)(2,1)}, u32[]{:S(2)}) copy-start(bf16[512,1024]{1,0:T(8,128)(2,1)} %param.20) | copy-start | bytes 3145732
  0.0 12.7 %copy-start.8 = (bf16[1024,3,128]{2,0,1:T(8,128)(2,1)S(1)}, bf16[1024,3,128]{2,0,1:T(8,128)(2,1)}, u32[]{:S(2)}) copy-start(bf16[1024,3,128]{2,0,1:T(8,128)(2,1)} %param.16) | copy-start | bytes 2359300
  0.0 13.7 %copy-start.13 = (s32[16,8]{0,1:T(8,128)S(1)}, s32[16,8]{0,1:T(8,128)}, u32[]{:S(2)}) copy-start(s32[16,8]{0,1:T(8,128)} %param.13) | copy-start | bytes 1540
  4.1 9.6 %collective-permute-start.2 = (bf16[144,1024]{1,0:T(8,128)(2,1)S(1)}, bf16[144,1024]{1,0:T(8,128)(2,1)}, u32[]{:S(2)}, u32[]{:S(2)}) collective-permute-start(bf16[144,1024]{1,0:T(8,128)(2,1)S(1)} %pad_maximum_fusion.4), channel_id=1, source_target_pairs={{0,1},{1,0},{2,3},{3,2},{4,5},{5,4},{6,7},{7,6},{8,9},{9,8},{10,11... | collective-permute-start | bytes 884744 | tf_op jit(solution)/shard_map/ppermute | solution.py:548
  5.4 10.4 %collective-permute-start.8 = (bf16[144,1024]{1,0:T(8,128)(2,1)S(1)}, bf16[144,1024]{1,0:T(8,128)(2,1)}, u32[]{:S(2)}, u32[]{:S(2)}) collective-permute-start(bf16[144,1024]{1,0:T(8,128)(2,1)S(1)} %pad_maximum_fusion.4), channel_id=1, source_target_pairs={{0,2},{1,3},{2,4},{3,5},{4,6},{5,7},{6,0},{7,1},{8,10},{9,11},{10,... | collective-permute-start | bytes 884744 | tf_op jit(solution)/shard_map/ppermute | solution.py:548
  6.7 12.7 %collective-permute-start = (bf16[2048,128]{1,0:T(8,128)(2,1)}, bf16[2048,128]{1,0:T(8,128)(2,1)S(1)}, u32[]{:S(2)}, u32[]{:S(2)}) collective-permute-start(bf16[2048,128]{1,0:T(8,128)(2,1)} %get-tuple-element.34), channel_id=1, source_target_pairs={{0,8},{8,16},{16,24},{24,32},{32,40},{40,48},{48,56},{56,64},{64,7... | collective-permute-start | bytes 1572872 | tf_op jit(solution)/shard_map/ppermute | solution.py:544
  10.8 14.3 %collective-permute-start.1 = (bf16[2048,128]{1,0:T(8,128)(2,1)}, bf16[2048,128]{1,0:T(8,128)(2,1)S(1)}, u32[]{:S(2)}, u32[]{:S(2)}) collective-permute-start(bf16[2048,128]{1,0:T(8,128)(2,1)} %get-tuple-element.35), channel_id=1, source_target_pairs={{8,0},{16,8},{24,16},{32,24},{40,32},{48,40},{56,48},{64,56},{72,6... | collective-permute-start | bytes 1572872 | tf_op jit(solution)/shard_map/ppermute | solution.py:544
  13.7 11.4 %collective-permute-start.4 = (bf16[144,1024]{1,0:T(8,128)(2,1)}, bf16[144,1024]{1,0:T(8,128)(2,1)S(1)}, u32[]{:S(2)}, u32[]{:S(2)}) collective-permute-start(bf16[144,1024]{1,0:T(8,128)(2,1)} %collective-permute-done.2), channel_id=1, source_target_pairs={{0,6},{1,7},{2,0},{3,1},{4,2},{5,3},{6,4},{7,5},{8,14},{9,15},{10,... | collective-permute-start | bytes 884744 | tf_op jit(solution)/shard_map/ppermute | solution.py:548
  15.1 17.0 %collective-permute-start.3 = (bf16[144,1024]{1,0:T(8,128)(2,1)}, bf16[144,1024]{1,0:T(8,128)(2,1)S(1)}, u32[]{:S(2)}, u32[]{:S(2)}) collective-permute-start(bf16[144,1024]{1,0:T(8,128)(2,1)} %collective-permute-done.2), channel_id=1, source_target_pairs={{0,2},{1,3},{2,4},{3,5},{4,6},{5,7},{6,0},{7,1},{8,10},{9,11},{10,... | collective-permute-start | bytes 884744 | tf_op jit(solution)/shard_map/ppermute | solution.py:548
  15.8 18.2 %collective-permute-start.9 = (bf16[144,1024]{1,0:T(8,128)(2,1)S(1)}, bf16[144,1024]{1,0:T(8,128)(2,1)S(1)}, u32[]{:S(2)}, u32[]{:S(2)}) collective-permute-start(bf16[144,1024]{1,0:T(8,128)(2,1)S(1)} %pad_maximum_fusion.4), channel_id=1, source_target_pairs={{0,6},{1,7},{2,0},{3,1},{4,2},{5,3},{6,4},{7,5},{8,14},{9,15},{10,... | collective-permute-start | bytes 884744 | tf_op jit(solution)/shard_map/ppermute | solution.py:548
  19.4 7.1 %copy-start.9 = (bf16[2048,128]{1,0:T(8,128)(2,1)}, bf16[2048,128]{1,0:T(8,128)(2,1)S(1)}, u32[]{:S(2)}) copy-start(bf16[2048,128]{1,0:T(8,128)(2,1)S(1)} %collective-permute-done) | copy-start | bytes 1572868
  19.4 16.7 %collective-permute-start.10 = (bf16[144,1024]{1,0:T(8,128)(2,1)}, bf16[144,1024]{1,0:T(8,128)(2,1)S(1)}, u32[]{:S(2)}, u32[]{:S(2)}) collective-permute-start(bf16[144,1024]{1,0:T(8,128)(2,1)} %collective-permute-done.8), channel_id=1, source_target_pairs={{0,2},{1,3},{2,4},{3,5},{4,6},{5,7},{6,0},{7,1},{8,10},{9,11},{10,... | collective-permute-start | bytes 884744 | tf_op jit(solution)/shard_map/ppermute | solution.py:548
  25.1 1.4 copy-start.10
  25.1 11.0 %collective-permute-start.11 = (bf16[144,1024]{1,0:T(8,128)(2,1)S(1)}, bf16[144,1024]{1,0:T(8,128)(2,1)S(1)}, u32[]{:S(2)}, u32[]{:S(2)}) collective-permute-start(bf16[144,1024]{1,0:T(8,128)(2,1)S(1)} %collective-permute-done.4), channel_id=1, source_target_pairs={{0,6},{1,7},{2,0},{3,1},{4,2},{5,3},{6,4},{7,5},{8,14},{9,15},{10,... | collective-permute-start | bytes 884744 | tf_op jit(solution)/shard_map/ppermute | solution.py:548
  32.1 11.0 %collective-permute-start.5 = (bf16[2048,128]{1,0:T(8,128)(2,1)}, bf16[2048,128]{1,0:T(8,128)(2,1)S(1)}, u32[]{:S(2)}, u32[]{:S(2)}) collective-permute-start(bf16[2048,128]{1,0:T(8,128)(2,1)} %encode.1.s0), channel_id=1, source_target_pairs={{0,1},{1,0},{2,3},{3,2},{4,5},{5,4},{6,7},{7,6},{8,9},{9,8},{10,11... | collective-permute-start | bytes 1572872 | tf_op jit(solution)/shard_map/ppermute | solution.py:548
  32.2 10.9 %collective-permute-start.6 = (bf16[2048,128]{1,0:T(8,128)(2,1)}, bf16[2048,128]{1,0:T(8,128)(2,1)S(1)}, u32[]{:S(2)}, u32[]{:S(2)}) collective-permute-start(bf16[2048,128]{1,0:T(8,128)(2,1)} %encode.1.s0), channel_id=1, source_target_pairs={{0,2},{1,3},{2,4},{3,5},{4,6},{5,7},{6,0},{7,1},{8,10},{9,11},{10,... | collective-permute-start | bytes 1572872 | tf_op jit(solution)/shard_map/ppermute | solution.py:548
  34.0 10.3 %collective-permute-start.7 = (bf16[2048,128]{1,0:T(8,128)(2,1)}, bf16[2048,128]{1,0:T(8,128)(2,1)S(1)}, u32[]{:S(2)}, u32[]{:S(2)}) collective-permute-start(bf16[2048,128]{1,0:T(8,128)(2,1)} %encode.1.s0), channel_id=1, source_target_pairs={{0,6},{1,7},{2,0},{3,1},{4,2},{5,3},{6,4},{7,5},{8,14},{9,15},{10,... | collective-permute-start | bytes 1572872 | tf_op jit(solution)/shard_map/ppermute | solution.py:548
  36.5 92.2 %copy-start.1 = (bf16[4,2,144,1024]{3,2,1,0:T(8,128)(2,1)}, bf16[4,2,144,1024]{3,2,1,0:T(8,128)(2,1)S(1)}, u32[]{:S(2)}) copy-start(bf16[4,2,144,1024]{3,2,1,0:T(8,128)(2,1)S(1)} %pad_maximum_fusion.refs_0_) | copy-start | bytes 7077892
  36.5 52.5 %collective-permute-start.15 = (bf16[4,2,144,1024]{3,2,1,0:T(8,128)(2,1)S(1)}, bf16[4,2,144,1024]{3,2,1,0:T(8,128)(2,1)}, u32[]{:S(2)}, u32[]{:S(2)}) collective-permute-start(bf16[4,2,144,1024]{3,2,1,0:T(8,128)(2,1)S(1)} %pad_maximum_fusion.refs_0_), channel_id=1, source_target_pairs={{0,16},{8,24},{16,32},{24,40},{32,48},{40,56},{48,0},{56,8},{64,80... | collective-permute-start | bytes 7077896 | tf_op jit(solution)/shard_map/ppermute | solution.py:548
  36.6 52.4 %collective-permute-start.16 = (bf16[4,2,144,1024]{3,2,1,0:T(8,128)(2,1)S(1)}, bf16[4,2,144,1024]{3,2,1,0:T(8,128)(2,1)}, u32[]{:S(2)}, u32[]{:S(2)}) collective-permute-start(bf16[4,2,144,1024]{3,2,1,0:T(8,128)(2,1)S(1)} %pad_maximum_fusion.refs_0_), channel_id=1, source_target_pairs={{0,48},{8,56},{16,0},{24,8},{32,16},{40,24},{48,32},{56,40},{64,11... | collective-permute-start | bytes 7077896 | tf_op jit(solution)/shard_map/ppermute | solution.py:548
  43.1 21.9 %copy-start.3 = (bf16[2048,128]{1,0:T(8,128)(2,1)}, bf16[2048,128]{1,0:T(8,128)(2,1)S(1)}, u32[]{:S(2)}) copy-start(bf16[2048,128]{1,0:T(8,128)(2,1)S(1)} %collective-permute-done.5.s1) | copy-start | bytes 1572868
  43.1 21.9 %copy-start.6 = (bf16[2048,128]{1,0:T(8,128)(2,1)}, bf16[2048,128]{1,0:T(8,128)(2,1)S(1)}, u32[]{:S(2)}) copy-start(bf16[2048,128]{1,0:T(8,128)(2,1)S(1)} %collective-permute-done.6.s2) | copy-start | bytes 1572868
  44.3 21.5 %copy-start.7 = (bf16[2048,128]{1,0:T(8,128)(2,1)}, bf16[2048,128]{1,0:T(8,128)(2,1)S(1)}, u32[]{:S(2)}) copy-start(bf16[2048,128]{1,0:T(8,128)(2,1)S(1)} %collective-permute-done.7.s4) | copy-start | bytes 1572868
  44.4 84.3 %collective-permute-start.19 = (bf16[4,2,144,1024]{3,2,1,0:T(8,128)(2,1)S(1)}, bf16[4,2,144,1024]{3,2,1,0:T(8,128)(2,1)}, u32[]{:S(2)}, u32[]{:S(2)}) collective-permute-start(bf16[4,2,144,1024]{3,2,1,0:T(8,128)(2,1)S(1)} %pad_maximum_fusion.refs_0_), channel_id=1, source_target_pairs={{0,65},{1,64},{2,67},{3,66},{4,69},{5,68},{6,71},{7,70},{8,73},{9,... | collective-permute-start | bytes 7077896 | tf_op jit(solution)/shard_map/ppermute | solution.py:548
  44.6 17.5 %collective-permute-start.12 = (bf16[3072,128]{1,0:T(8,128)(2,1)S(1)}, bf16[3072,128]{1,0:T(8,128)(2,1)S(1)}, u32[]{:S(2)}, u32[]{:S(2)}) collective-permute-start(bf16[3072,128]{1,0:T(8,128)(2,1)S(1)} %get-tuple-element.73), channel_id=1, source_target_pairs={{0,2},{1,3},{2,4},{3,5},{4,6},{5,7},{6,0},{7,1},{8,10},{9,11},{10,... | collective-permute-start | bytes 2359304 | tf_op jit(solution)/shard_map/ppermute | solution.py:548
  47.6 16.4 %collective-permute-start.13 = (bf16[3072,128]{1,0:T(8,128)(2,1)S(1)}, bf16[3072,128]{1,0:T(8,128)(2,1)S(1)}, u32[]{:S(2)}, u32[]{:S(2)}) collective-permute-start(bf16[3072,128]{1,0:T(8,128)(2,1)S(1)} %get-tuple-element.72), channel_id=1, source_target_pairs={{0,6},{1,7},{2,0},{3,1},{4,2},{5,3},{6,4},{7,5},{8,14},{9,15},{10,... | collective-permute-start | bytes 2359304 | tf_op jit(solution)/shard_map/ppermute | solution.py:548
  62.0 0.9 copy-start.4
  64.0 0.9 copy-start.5
  65.8 14.1 %collective-permute-start.14 = (bf16[2048,128]{1,0:T(8,128)(2,1)}, bf16[2048,128]{1,0:T(8,128)(2,1)}, u32[]{:S(2)}, u32[]{:S(2)}) collective-permute-start(bf16[2048,128]{1,0:T(8,128)(2,1)} %pad_maximum_fusion.3.s6), channel_id=1, source_target_pairs={{0,1},{1,0},{2,3},{3,2},{4,5},{5,4},{6,7},{7,6},{8,9},{9,8},{10,11... | collective-permute-start | bytes 1572872 | tf_op jit(solution)/shard_map/ppermute | solution.py:548
  89.0 12.4 %collective-permute-start.17 = (bf16[1152,256]{1,0:T(8,128)(2,1)}, bf16[1152,256]{1,0:T(8,128)(2,1)}, u32[]{:S(2)}, u32[]{:S(2)}) collective-permute-start(bf16[1152,256]{1,0:T(8,128)(2,1)} %get-tuple-element.49), channel_id=1, source_target_pairs={{0,8},{8,16},{16,24},{24,32},{32,40},{40,48},{48,56},{56,64},{64,7... | collective-permute-start | bytes 1769480 | tf_op jit(solution)/shard_map/ppermute | solution.py:544
  94.3 15.1 %collective-permute-start.18 = (bf16[1152,256]{1,0:T(8,128)(2,1)}, bf16[1152,256]{1,0:T(8,128)(2,1)}, u32[]{:S(2)}, u32[]{:S(2)}) collective-permute-start(bf16[1152,256]{1,0:T(8,128)(2,1)} %get-tuple-element.51), channel_id=1, source_target_pairs={{8,0},{16,8},{24,16},{32,24},{40,32},{48,40},{56,48},{64,56},{72,6... | collective-permute-start | bytes 1769480 | tf_op jit(solution)/shard_map/ppermute | solution.py:544
  128.7 15.3 %collective-permute-start.20 = (bf16[4,2,144,1024]{3,2,1,0:T(8,128)(2,1)S(1)}, bf16[4,2,144,1024]{3,2,1,0:T(8,128)(2,1)}, u32[]{:S(2)}, u32[]{:S(2)}) collective-permute-start(bf16[4,2,144,1024]{3,2,1,0:T(8,128)(2,1)S(1)} %pad_maximum_fusion.refs_0_), channel_id=1, source_target_pairs={{0,8},{8,0},{16,24},{24,16},{32,40},{40,32},{48,56},{56,48},{64,72... | collective-permute-start | bytes 7077896 | tf_op jit(solution)/shard_map/ppermute | solution.py:548
  128.8 15.2 %collective-permute-start.21 = (bf16[4,2,144,1024]{3,2,1,0:T(8,128)(2,1)}, bf16[4,2,144,1024]{3,2,1,0:T(8,128)(2,1)}, u32[]{:S(2)}, u32[]{:S(2)}) collective-permute-start(bf16[4,2,144,1024]{3,2,1,0:T(8,128)(2,1)} %collective-permute-done.15.refs_1_), channel_id=1, source_target_pairs={{0,8},{8,0},{16,24},{24,16},{32,40},{40,32},{48,56},{56,48},{64,72... | collective-permute-start | bytes 7077896 | tf_op jit(solution)/shard_map/ppermute | solution.py:548
  129.3 14.7 %collective-permute-start.22 = (bf16[4,2,144,1024]{3,2,1,0:T(8,128)(2,1)}, bf16[4,2,144,1024]{3,2,1,0:T(8,128)(2,1)}, u32[]{:S(2)}, u32[]{:S(2)}) collective-permute-start(bf16[4,2,144,1024]{3,2,1,0:T(8,128)(2,1)} %collective-permute-done.16.refs_2_), channel_id=1, source_target_pairs={{0,8},{8,0},{16,24},{24,16},{32,40},{40,32},{48,56},{56,48},{64,72... | collective-permute-start | bytes 7077896 | tf_op jit(solution)/shard_map/ppermute | solution.py:548
  129.4 14.6 %collective-permute-start.23 = (bf16[4,2,144,1024]{3,2,1,0:T(8,128)(2,1)}, bf16[4,2,144,1024]{3,2,1,0:T(8,128)(2,1)}, u32[]{:S(2)}, u32[]{:S(2)}) collective-permute-start(bf16[4,2,144,1024]{3,2,1,0:T(8,128)(2,1)} %collective-permute-done.19.refs_3_), channel_id=1, source_target_pairs={{0,8},{8,0},{16,24},{24,16},{32,40},{40,32},{48,56},{56,48},{64,72... | collective-permute-start | bytes 7077896 | tf_op jit(solution)/shard_map/ppermute | solution.py:548
  129.8 14.2 %all-to-all-start = ((bf16[8,256,128]{2,1,0:T(8,128)(2,1)}), bf16[8,256,128]{2,1,0:T(8,128)(2,1)}, u32[]{:S(2)}, u32[]{:S(2)}) async-start(bf16[8,256,128]{2,1,0:T(8,128)(2,1)} %bitcast.49), calls=%async_computation | async-start | bytes 1048576 | tf_op jit(solution)/shard_map/all_to_all | solution.py:635
  144.0 31.7 %copy-start.14 = (s32[64,2]{0,1:T(2,128)S(1)}, s32[64,2]{0,1:T(2,128)}, u32[]{:S(2)}) copy-start(s32[64,2]{0,1:T(2,128)} %param.21) | copy-start | bytes 1540
  169.8 14.7 %copy-start.2 = (bf16[8,256,128]{2,1,0:T(8,128)(2,1)}, bf16[8,256,128]{2,1,0:T(8,128)(2,1)S(1)}, u32[]{:S(2)}) copy-start(bf16[8,256,128]{2,1,0:T(8,128)(2,1)S(1)} %all_to_all.15) | copy-start | bytes 1572868
  169.8 6.6 %collective-permute-start.24 = (bf16[8,128,128]{2,1,0:T(8,128)(2,1)S(1)}, bf16[8,128,128]{2,1,0:T(8,128)(2,1)S(1)}, u32[]{:S(2)}, u32[]{:S(2)}) collective-permute-start(bf16[8,128,128]{2,1,0:T(8,128)(2,1)S(1)} %bitcast.62), channel_id=1, source_target_pairs={{0,8},{8,16},{16,24},{24,32},{32,40},{40,48},{48,56},{56,64},{64,7... | collective-permute-start | bytes 786440 | tf_op jit(solution)/shard_map/ppermute | solution.py:544
  173.1 11.3 %collective-permute-start.25 = (bf16[8,128,128]{2,1,0:T(8,128)(2,1)S(1)}, bf16[8,128,128]{2,1,0:T(8,128)(2,1)S(1)}, u32[]{:S(2)}, u32[]{:S(2)}) collective-permute-start(bf16[8,128,128]{2,1,0:T(8,128)(2,1)S(1)} %bitcast.61), channel_id=1, source_target_pairs={{8,0},{16,8},{24,16},{32,24},{40,32},{48,40},{56,48},{64,56},{72,6... | collective-permute-start | bytes 786440 | tf_op jit(solution)/shard_map/ppermute | solution.py:544
  176.5 8.0 %copy-start.11 = (bf16[8,128,128]{2,1,0:T(8,128)(2,1)}, bf16[8,128,128]{2,1,0:T(8,128)(2,1)S(1)}, u32[]{:S(2)}) copy-start(bf16[8,128,128]{2,1,0:T(8,128)(2,1)S(1)} %collective-permute-done.24.low) | copy-start | bytes 786436
  184.4 0.7 copy-start.12

commit v13 on v12

--- a/solution.py
+++ b/solution.py
@@ -426,8 +426,9 @@
     row = lax.broadcasted_iota(jnp.int32, (BLOCK, BLOCK), 0)
     column = lax.broadcasted_iota(jnp.int32, (BLOCK, BLOCK), 1)
     for step in range(steps):
-        blocks[2 * step].wait()
-        blocks[2 * step + 1].wait()
+        if step % 2 == 0:
+            for c in blocks[2 * step : 2 * step + 4]:
+                c.wait()
         kinds = []
         for b in range(step * EACH, (step + 1) * EACH):
             left = jnp.concatenate([held[b, k] for k in range(slots)], axis=1)
@@ -500,8 +501,9 @@
     for step in range(steps):
         parts = jnp.concatenate([stats[h, step] for h in range(count)], axis=0)
         spread = lax.dot_general(parts, pick, TN, preferred_element_type=F32)
-        backs[step].wait()
-        states[step].wait()
+        if step % 2 == 0:
+            for c in backs[step : step + 2] + states[step : step + 2]:
+                c.wait()
         for b in range(EACH):
             at = (step * EACH + b) * BLOCK
             average = spread[:, b * BLOCK : (b + 1) * BLOCK]

time: 211 us -> 209 us (level)
  no operation moved by 1% of the time
where the time goes in v13:
time: 209 us; the launch traced here: 208 us
  waiting for transfers between devices  66.7 us (32%)
  Pallas kernels  59.4 us (28%)
  starting transfers between devices  44 us (21%)
  blocking collectives  22.1 us (11%)
  local copies, waits for them, and re-layouts  9.87 us (5%)
  other arithmetic  5.25 us (3%)
    ppermute x20, waiting for transfers between devices, among(): return lax.ppermute(value, axis, [(i, to(i)) for i in range(count)])  31.4 us
    ppermute x6, waiting for transfers between devices, shifted(): lax.ppermute(value, 'seq', [(i, i + by) for i in range(16) if 0 <= i + by...  25.9 us
    ppermute x20, starting transfers between devices, among(): return lax.ppermute(value, axis, [(i, to(i)) for i in range(count)])  20.6 us
    ppermute x6, starting transfers between devices, shifted(): lax.ppermute(value, 'seq', [(i, i + by) for i in range(16) if 0 <= i + by...  19.3 us
    pallas_call x1, Pallas kernels, attend(): pl.pallas_call(attend_kernel, out_shape=jax.ShapeDtypeStruct((rows, BLOCK...  19.2 us
    all_to_all x1, blocking collectives, on_device(): mesh_end = lax.all_to_all(mesh_end, 'head', 0, 0, tiled=True)  12.9 us
    pallas_call x1, Pallas kernels, forward(): pl.pallas_call(forward_kernel, out_shape=jax.ShapeDtypeStruct((8, rows, B...  12.8 us
    all_to_all x1, waiting for transfers between devices, on_device(): lax.all_to_all(context.reshape(8, mesh_rows // 8, BLOCK), 'head', 0, 0, t...  9.33 us
  transfers between devices with their start and end apart: 27, of which 10 were waited for; matrix products, arithmetic and copies ran while one was open for 4% of the time, Pallas kernels for 16%

profile of v13, /device:TPU:97, one launch (start us, length us, event | category | flops | bytes accessed | tf_op | source)
XLA Modules:
  0.0 208.0 jit_solution(4220304004034801731)
XLA Ops:
  0.0 2.4 %fusion = (bf16[2048,128]{1,0:T(8,128)(2,1)}, bf16[2048,128]{1,0:T(8,128)(2,1)}) fusion(bf16[8192,128]{1,0:T(8,128)(2,1)} %state.1), kind=kLoop, calls=%fused_computation.16 | loop fusion | bytes 2097152 | tf_op jit(solution)/shard_map/slice | solution.py:591
  2.4 0.9 constant_dynamic-slice_fusion
  3.3 0.8 constant_dynamic-slice_fusion.1
  4.1 1.3 collective-permute-start.2
  5.4 1.3 collective-permute-start.8
  6.7 4.1 %collective-permute-start = (bf16[2048,128]{1,0:T(8,128)(2,1)}, bf16[2048,128]{1,0:T(8,128)(2,1)S(1)}, u32[]{:S(2)}, u32[]{:S(2)}) collective-permute-start(bf16[2048,128]{1,0:T(8,128)(2,1)} %get-tuple-element.34), channel_id=1, source_target_pairs={{0,8},{8,16},{16,24},{24,32},{32,40},{40,48},{48,56},{56,64},{64,7... | collective-permute-start | bytes 1572872 | tf_op jit(solution)/shard_map/ppermute | solution.py:546
  10.8 1.9 collective-permute-start.1
  12.7 0.9 fusion.1
  13.7 1.4 collective-permute-start.4
  15.8 2.6 %collective-permute-start.9 = (bf16[144,1024]{1,0:T(8,128)(2,1)S(1)}, bf16[144,1024]{1,0:T(8,128)(2,1)S(1)}, u32[]{:S(2)}, u32[]{:S(2)}) collective-permute-start(bf16[144,1024]{1,0:T(8,128)(2,1)S(1)} %pad_maximum_fusion.4), channel_id=1, source_target_pairs={{0,6},{1,7},{2,0},{3,1},{4,2},{5,3},{6,4},{7,5},{8,14},{9,15},{10,... | collective-permute-start | bytes 884744 | tf_op jit(solution)/shard_map/ppermute | solution.py:550
  18.4 1.0 maximum_bitcast_fusion
  19.5 5.6 %collective-permute-done.1 = bf16[2048,128]{1,0:T(8,128)(2,1)S(1)} collective-permute-done((bf16[2048,128]{1,0:T(8,128)(2,1)}, bf16[2048,128]{1,0:T(8,128)(2,1)S(1)}, u32[]{:S(2)}, u32[]{:S(2)}) %collective-permute-start.1) | collective-permute-done | bytes 524320 | tf_op jit(solution)/shard_map/ppermute | solution.py:546
  25.1 1.4 collective-permute-start.11
  26.5 5.6 %encode.1.s0 = bf16[2048,128]{1,0:T(8,128)(2,1)} custom-call(s32[16,8]{1,0:T(8,128)} %broadcast_subtract_fusion.1.index, bf16[16,128,128]{2,1,0:T(8,128)(2,1)} %bitcast.54, bf16[64,128,128]{2,1,0:T(8,128)(2,1)} %bitcast.47, bf16[16,128,128]{2,1,0:T(8,128)(2,1)} %bitcast.55, bf16[16,8,128,128]{3,2,1,0:T(8,128)(2,1)} %weights.2), custom_call_target="tpu_custom_call" | custom-call | flops 540000000 | bytes 8000000 | tf_op jit(solution)/shard_map/encode/pallas_call | solution.py:86
  32.2 0.8 collective-permute-start.6
  33.0 1.0 maximum_bitcast_fusion.1
  34.0 2.1 collective-permute-start.7
  36.6 1.5 collective-permute-start.16
  38.0 5.0 %collective-permute-done.5.s1 = bf16[2048,128]{1,0:T(8,128)(2,1)S(1)} collective-permute-done((bf16[2048,128]{1,0:T(8,128)(2,1)}, bf16[2048,128]{1,0:T(8,128)(2,1)S(1)}, u32[]{:S(2)}, u32[]{:S(2)}) %collective-permute-start.5) | collective-permute-done | bytes 524320 | tf_op jit(solution)/shard_map/ppermute | solution.py:550
  43.1 1.2 collective-permute-done.7.s4
  44.6 3.1 %collective-permute-start.12 = (bf16[3072,128]{1,0:T(8,128)(2,1)S(1)}, bf16[3072,128]{1,0:T(8,128)(2,1)S(1)}, u32[]{:S(2)}, u32[]{:S(2)}) collective-permute-start(bf16[3072,128]{1,0:T(8,128)(2,1)S(1)} %get-tuple-element.73), channel_id=1, source_target_pairs={{0,2},{1,3},{2,4},{3,5},{4,6},{5,7},{6,0},{7,1},{8,10},{9,11},{10,... | collective-permute-start | bytes 2359304 | tf_op jit(solution)/shard_map/ppermute | solution.py:550
  47.6 14.4 %collective-permute-done.12.s3 = bf16[3072,128]{1,0:T(8,128)(2,1)S(1)} collective-permute-done((bf16[3072,128]{1,0:T(8,128)(2,1)S(1)}, bf16[3072,128]{1,0:T(8,128)(2,1)S(1)}, u32[]{:S(2)}, u32[]{:S(2)}) %collective-permute-start.12) | collective-permute-done | bytes 786464 | tf_op jit(solution)/shard_map/ppermute | solution.py:550
  62.0 0.9 copy-done.4
  62.9 1.1 collective-permute-done.13.s5
  64.0 0.9 copy-done.5
  65.0 0.8 pad_maximum_fusion.3.s6
  65.8 3.8 %collective-permute-start.14 = (bf16[2048,128]{1,0:T(8,128)(2,1)}, bf16[2048,128]{1,0:T(8,128)(2,1)}, u32[]{:S(2)}, u32[]{:S(2)}) collective-permute-start(bf16[2048,128]{1,0:T(8,128)(2,1)} %pad_maximum_fusion.3.s6), channel_id=1, source_target_pairs={{0,1},{1,0},{2,3},{3,2},{4,5},{5,4},{6,7},{7,6},{8,9},{9,8},{10,11... | collective-permute-start | bytes 1572872 | tf_op jit(solution)/shard_map/ppermute | solution.py:550
  70.2 9.6 %collective-permute-done.14.s7 = bf16[2048,128]{1,0:T(8,128)(2,1)} collective-permute-done((bf16[2048,128]{1,0:T(8,128)(2,1)}, bf16[2048,128]{1,0:T(8,128)(2,1)}, u32[]{:S(2)}, u32[]{:S(2)}) %collective-permute-start.14) | collective-permute-done | bytes 524320 | tf_op jit(solution)/shard_map/ppermute | solution.py:550
  79.9 9.1 %project.1 = (bf16[2048,128]{1,0:T(8,128)(2,1)}, bf16[2048,256]{1,0:T(8,128)(2,1)}, bf16[8,256,128]{2,1,0:T(8,128)(2,1)}, bf16[1152,256]{1,0:T(8,128)(2,1)}, bf16[1152,256]{1,0:T(8,128)(2,1)}) custom-call(s32[8]{0:T(128)} %stack.130.order, bf16[2048,128]{1,0:T(8,128)(2,1)} %encode.1.s0, bf16[2048,128]{1,0:T(8,128)(2,1)} %copy-done.3, ...), custom_call_target="tpu_custom_call" | custom-call | tf_op jit(solution)/shard_map/project/pallas_call | solution.py:168
  89.0 5.3 %collective-permute-start.17 = (bf16[1152,256]{1,0:T(8,128)(2,1)}, bf16[1152,256]{1,0:T(8,128)(2,1)}, u32[]{:S(2)}, u32[]{:S(2)}) collective-permute-start(bf16[1152,256]{1,0:T(8,128)(2,1)} %get-tuple-element.49), channel_id=1, source_target_pairs={{0,8},{8,16},{16,24},{24,32},{32,40},{40,48},{48,56},{56,64},{64,7... | collective-permute-start | bytes 1769480 | tf_op jit(solution)/shard_map/ppermute | solution.py:546
  94.3 2.1 %collective-permute-start.18 = (bf16[1152,256]{1,0:T(8,128)(2,1)}, bf16[1152,256]{1,0:T(8,128)(2,1)}, u32[]{:S(2)}, u32[]{:S(2)}) collective-permute-start(bf16[1152,256]{1,0:T(8,128)(2,1)} %get-tuple-element.51), channel_id=1, source_target_pairs={{8,0},{16,8},{24,16},{32,24},{40,32},{48,40},{56,48},{64,56},{72,6... | collective-permute-start | bytes 1769480 | tf_op jit(solution)/shard_map/ppermute | solution.py:546
  96.4 0.7 add_convert_fusion.edges
  97.1 4.4 %collective-permute-done.17.low = bf16[1152,256]{1,0:T(8,128)(2,1)} collective-permute-done((bf16[1152,256]{1,0:T(8,128)(2,1)}, bf16[1152,256]{1,0:T(8,128)(2,1)}, u32[]{:S(2)}, u32[]{:S(2)}) %collective-permute-start.17) | collective-permute-done | bytes 589856 | tf_op jit(solution)/shard_map/ppermute | solution.py:546
  101.4 8.0 %collective-permute-done.18.high = bf16[1152,256]{1,0:T(8,128)(2,1)} collective-permute-done((bf16[1152,256]{1,0:T(8,128)(2,1)}, bf16[1152,256]{1,0:T(8,128)(2,1)}, u32[]{:S(2)}, u32[]{:S(2)}) %collective-permute-start.18) | collective-permute-done | bytes 589856 | tf_op jit(solution)/shard_map/ppermute | solution.py:546
  109.4 19.2 %attend.1 = bf16[2048,128]{1,0:T(8,128)(2,1)} custom-call(s32[2]{0:T(128)} %add_convert_fusion.edges, bf16[2048,128]{1,0:T(8,128)(2,1)} %get-tuple-element.46.queries, bf16[1152,256]{1,0:T(8,128)(2,1)} %collective-permute-done.17.low, bf16[2048,256]{1,0:T(8,128)(2,1)} %get-tuple-element.50.own, bf16[1152,256]{1,0:T(8,128)(2,1)} %collective-permute-done.18.high), custom_call_target="tpu_custom_call" | custom-call | tf_op jit(solution)/shard_map/attend/pallas_call | solution.py:276
  129.8 4.1 %all-to-all-start = ((bf16[8,256,128]{2,1,0:T(8,128)(2,1)}), bf16[8,256,128]{2,1,0:T(8,128)(2,1)}, u32[]{:S(2)}, u32[]{:S(2)}) async-start(bf16[8,256,128]{2,1,0:T(8,128)(2,1)} %bitcast.49), calls=%async_computation | async-start | bytes 1048576 | tf_op jit(solution)/shard_map/all_to_all | solution.py:637
  134.0 0.7 concatenate.19.table
  134.7 9.3 %all-to-all-done.refs_8_ = bf16[8,256,128]{2,1,0:T(8,128)(2,1)} async-done(((bf16[8,256,128]{2,1,0:T(8,128)(2,1)}), bf16[8,256,128]{2,1,0:T(8,128)(2,1)}, u32[]{:S(2)}, u32[]{:S(2)}) %all-to-all-start) | async-done | bytes 524320 | tf_op jit(solution)/shard_map/all_to_all | solution.py:637
  144.0 12.8 %forward.1 = bf16[8,256,128]{2,1,0:T(8,128)(2,1)} custom-call(s32[16]{0:T(128)} %concatenate.19.table, bf16[4,2,144,1024]{3,2,1,0:T(8,128)(2,1)} %copy-done.1, bf16[4,2,144,1024]{3,2,1,0:T(8,128)(2,1)} %collective-permute-done.15.refs_1_, bf16[4,2,144,1024]{3,2,1,0:T(8,128)(2,1)} %collective-permute-done.16.refs_2_, ...), custom_call_target="tpu_custom_call" | custom-call | flops 4800000000 | bytes 20000000 | tf_op jit(solution)/shard_map/forward/pallas_call | solution.py:389
  156.8 12.9 %all_to_all.15 = bf16[8,256,128]{2,1,0:T(8,128)(2,1)S(1)} all-to-all(bf16[8,256,128]{2,1,0:T(8,128)(2,1)} %forward.1), channel_id=1, replica_groups=mesh['seq'=16,'head'=8] {'head'}, dimensions={0} | all-to-all | bytes 1048576 | tf_op jit(solution)/shard_map/all_to_all | solution.py:645
  169.8 3.3 %collective-permute-start.24 = (bf16[8,128,128]{2,1,0:T(8,128)(2,1)S(1)}, bf16[8,128,128]{2,1,0:T(8,128)(2,1)S(1)}, u32[]{:S(2)}, u32[]{:S(2)}) collective-permute-start(bf16[8,128,128]{2,1,0:T(8,128)(2,1)S(1)} %bitcast.62), channel_id=1, source_target_pairs={{0,8},{8,16},{16,24},{24,32},{32,40},{40,48},{48,56},{56,64},{64,7... | collective-permute-start | bytes 786440 | tf_op jit(solution)/shard_map/ppermute | solution.py:546
  173.1 2.6 %collective-permute-start.25 = (bf16[8,128,128]{2,1,0:T(8,128)(2,1)S(1)}, bf16[8,128,128]{2,1,0:T(8,128)(2,1)S(1)}, u32[]{:S(2)}, u32[]{:S(2)}) collective-permute-start(bf16[8,128,128]{2,1,0:T(8,128)(2,1)S(1)} %bitcast.61), channel_id=1, source_target_pairs={{8,0},{16,8},{24,16},{32,24},{40,32},{48,40},{56,48},{64,56},{72,6... | collective-permute-start | bytes 786440 | tf_op jit(solution)/shard_map/ppermute | solution.py:546
  176.5 8.0 %collective-permute-done.25.high = bf16[8,128,128]{2,1,0:T(8,128)(2,1)S(1)} collective-permute-done((bf16[8,128,128]{2,1,0:T(8,128)(2,1)S(1)}, bf16[8,128,128]{2,1,0:T(8,128)(2,1)S(1)}, u32[]{:S(2)}, u32[]{:S(2)}) %collective-permute-start.25) | collective-permute-done | bytes 262176 | tf_op jit(solution)/shard_map/ppermute | solution.py:546
  184.4 0.7 copy-done.12
  185.1 7.1 %decode.1 = (bf16[8192,128]{1,0:T(8,128)(2,1)}, bf16[8,16,128]{2,1,0:T(8,128)(2,1)}) custom-call(s32[64,2]{1,0:T(8,128)} %broadcast_subtract_fusion.index, bf16[8,128,128]{2,1,0:T(8,128)(2,1)} %copy-done.11, bf16[16,128,128]{2,1,0:T(8,128)(2,1)} %bitcast.48, bf16[8,128,128]{2,1,0:T(8,128)(2,1)} %copy-done.12, bf16[64,2,128,128]{3,2,1,0:T(8,128)(2,1)} %weights.3), custom_call_target="tpu_custom_call" | custom-call | flops 540000000 | bytes 10000000 | tf_op jit(solution)/shard_map/decode/pallas_call | solution.py:459
  192.3 0.8 broadcast_in_dim.3
  193.0 9.2 %all_to_all.16.sums = bf16[8,8,16,128]{3,2,1,0:T(8,128)(2,1)} all-to-all(bf16[8,8,16,128]{3,2,1,0:T(8,128)(2,1)S(1)} %broadcast_in_dim.3), channel_id=1, replica_groups=mesh['seq'=16,'head'=8] {'head'}, dimensions={0} | all-to-all | bytes 524288 | tf_op jit(solution)/shard_map/all_to_all | solution.py:655
  202.3 5.6 %finish.1 = bf16[8192,128]{1,0:T(8,128)(2,1)} custom-call(bf16[8,8,16,128]{3,2,1,0:T(8,128)(2,1)} %all_to_all.16.sums, bf16[8192,128]{1,0:T(8,128)(2,1)} %get-tuple-element.62.back, bf16[8192,128]{1,0:T(8,128)(2,1)} %state.1, f32[1,128]{1,0:T(1,128)} %bitcast.65), custom_call_target="tpu_custom_call" | custom-call | flops 540000000 | bytes 8000000 | tf_op jit(solution)/shard_map/finish/pallas_call | solution.py:524
  (70 shorter events, 4.3 us)
Async XLA Ops:
  0.0 3.3 %copy-start = (bf16[512,1024]{1,0:T(8,128)(2,1)S(1)}, bf16[512,1024]{1,0:T(8,128)(2,1)}, u32[]{:S(2)}) copy-start(bf16[512,1024]{1,0:T(8,128)(2,1)} %param.20) | copy-start | bytes 3145732
  0.0 12.7 %copy-start.8 = (bf16[1024,3,128]{2,0,1:T(8,128)(2,1)S(1)}, bf16[1024,3,128]{2,0,1:T(8,128)(2,1)}, u32[]{:S(2)}) copy-start(bf16[1024,3,128]{2,0,1:T(8,128)(2,1)} %param.16) | copy-start | bytes 2359300
  0.0 13.7 %copy-start.13 = (s32[16,8]{0,1:T(8,128)S(1)}, s32[16,8]{0,1:T(8,128)}, u32[]{:S(2)}) copy-start(s32[16,8]{0,1:T(8,128)} %param.13) | copy-start | bytes 1540
  4.1 9.6 %collective-permute-start.2 = (bf16[144,1024]{1,0:T(8,128)(2,1)S(1)}, bf16[144,1024]{1,0:T(8,128)(2,1)}, u32[]{:S(2)}, u32[]{:S(2)}) collective-permute-start(bf16[144,1024]{1,0:T(8,128)(2,1)S(1)} %pad_maximum_fusion.4), channel_id=1, source_target_pairs={{0,1},{1,0},{2,3},{3,2},{4,5},{5,4},{6,7},{7,6},{8,9},{9,8},{10,11... | collective-permute-start | bytes 884744 | tf_op jit(solution)/shard_map/ppermute | solution.py:550
  5.4 10.4 %collective-permute-start.8 = (bf16[144,1024]{1,0:T(8,128)(2,1)S(1)}, bf16[144,1024]{1,0:T(8,128)(2,1)}, u32[]{:S(2)}, u32[]{:S(2)}) collective-permute-start(bf16[144,1024]{1,0:T(8,128)(2,1)S(1)} %pad_maximum_fusion.4), channel_id=1, source_target_pairs={{0,2},{1,3},{2,4},{3,5},{4,6},{5,7},{6,0},{7,1},{8,10},{9,11},{10,... | collective-permute-start | bytes 884744 | tf_op jit(solution)/shard_map/ppermute | solution.py:550
  6.7 12.7 %collective-permute-start = (bf16[2048,128]{1,0:T(8,128)(2,1)}, bf16[2048,128]{1,0:T(8,128)(2,1)S(1)}, u32[]{:S(2)}, u32[]{:S(2)}) collective-permute-start(bf16[2048,128]{1,0:T(8,128)(2,1)} %get-tuple-element.34), channel_id=1, source_target_pairs={{0,8},{8,16},{16,24},{24,32},{32,40},{40,48},{48,56},{56,64},{64,7... | collective-permute-start | bytes 1572872 | tf_op jit(solution)/shard_map/ppermute | solution.py:546
  10.8 14.3 %collective-permute-start.1 = (bf16[2048,128]{1,0:T(8,128)(2,1)}, bf16[2048,128]{1,0:T(8,128)(2,1)S(1)}, u32[]{:S(2)}, u32[]{:S(2)}) collective-permute-start(bf16[2048,128]{1,0:T(8,128)(2,1)} %get-tuple-element.35), channel_id=1, source_target_pairs={{8,0},{16,8},{24,16},{32,24},{40,32},{48,40},{56,48},{64,56},{72,6... | collective-permute-start | bytes 1572872 | tf_op jit(solution)/shard_map/ppermute | solution.py:546
  13.7 11.4 %collective-permute-start.4 = (bf16[144,1024]{1,0:T(8,128)(2,1)}, bf16[144,1024]{1,0:T(8,128)(2,1)S(1)}, u32[]{:S(2)}, u32[]{:S(2)}) collective-permute-start(bf16[144,1024]{1,0:T(8,128)(2,1)} %collective-permute-done.2), channel_id=1, source_target_pairs={{0,6},{1,7},{2,0},{3,1},{4,2},{5,3},{6,4},{7,5},{8,14},{9,15},{10,... | collective-permute-start | bytes 884744 | tf_op jit(solution)/shard_map/ppermute | solution.py:550
  15.1 17.0 %collective-permute-start.3 = (bf16[144,1024]{1,0:T(8,128)(2,1)}, bf16[144,1024]{1,0:T(8,128)(2,1)S(1)}, u32[]{:S(2)}, u32[]{:S(2)}) collective-permute-start(bf16[144,1024]{1,0:T(8,128)(2,1)} %collective-permute-done.2), channel_id=1, source_target_pairs={{0,2},{1,3},{2,4},{3,5},{4,6},{5,7},{6,0},{7,1},{8,10},{9,11},{10,... | collective-permute-start | bytes 884744 | tf_op jit(solution)/shard_map/ppermute | solution.py:550
  15.8 18.2 %collective-permute-start.9 = (bf16[144,1024]{1,0:T(8,128)(2,1)S(1)}, bf16[144,1024]{1,0:T(8,128)(2,1)S(1)}, u32[]{:S(2)}, u32[]{:S(2)}) collective-permute-start(bf16[144,1024]{1,0:T(8,128)(2,1)S(1)} %pad_maximum_fusion.4), channel_id=1, source_target_pairs={{0,6},{1,7},{2,0},{3,1},{4,2},{5,3},{6,4},{7,5},{8,14},{9,15},{10,... | collective-permute-start | bytes 884744 | tf_op jit(solution)/shard_map/ppermute | solution.py:550
  19.4 7.1 %copy-start.9 = (bf16[2048,128]{1,0:T(8,128)(2,1)}, bf16[2048,128]{1,0:T(8,128)(2,1)S(1)}, u32[]{:S(2)}) copy-start(bf16[2048,128]{1,0:T(8,128)(2,1)S(1)} %collective-permute-done) | copy-start | bytes 1572868
  19.4 16.7 %collective-permute-start.10 = (bf16[144,1024]{1,0:T(8,128)(2,1)}, bf16[144,1024]{1,0:T(8,128)(2,1)S(1)}, u32[]{:S(2)}, u32[]{:S(2)}) collective-permute-start(bf16[144,1024]{1,0:T(8,128)(2,1)} %collective-permute-done.8), channel_id=1, source_target_pairs={{0,2},{1,3},{2,4},{3,5},{4,6},{5,7},{6,0},{7,1},{8,10},{9,11},{10,... | collective-permute-start | bytes 884744 | tf_op jit(solution)/shard_map/ppermute | solution.py:550
  25.1 1.4 copy-start.10
  25.1 11.0 %collective-permute-start.11 = (bf16[144,1024]{1,0:T(8,128)(2,1)S(1)}, bf16[144,1024]{1,0:T(8,128)(2,1)S(1)}, u32[]{:S(2)}, u32[]{:S(2)}) collective-permute-start(bf16[144,1024]{1,0:T(8,128)(2,1)S(1)} %collective-permute-done.4), channel_id=1, source_target_pairs={{0,6},{1,7},{2,0},{3,1},{4,2},{5,3},{6,4},{7,5},{8,14},{9,15},{10,... | collective-permute-start | bytes 884744 | tf_op jit(solution)/shard_map/ppermute | solution.py:550
  32.1 11.0 %collective-permute-start.5 = (bf16[2048,128]{1,0:T(8,128)(2,1)}, bf16[2048,128]{1,0:T(8,128)(2,1)S(1)}, u32[]{:S(2)}, u32[]{:S(2)}) collective-permute-start(bf16[2048,128]{1,0:T(8,128)(2,1)} %encode.1.s0), channel_id=1, source_target_pairs={{0,1},{1,0},{2,3},{3,2},{4,5},{5,4},{6,7},{7,6},{8,9},{9,8},{10,11... | collective-permute-start | bytes 1572872 | tf_op jit(solution)/shard_map/ppermute | solution.py:550
  32.2 10.9 %collective-permute-start.6 = (bf16[2048,128]{1,0:T(8,128)(2,1)}, bf16[2048,128]{1,0:T(8,128)(2,1)S(1)}, u32[]{:S(2)}, u32[]{:S(2)}) collective-permute-start(bf16[2048,128]{1,0:T(8,128)(2,1)} %encode.1.s0), channel_id=1, source_target_pairs={{0,2},{1,3},{2,4},{3,5},{4,6},{5,7},{6,0},{7,1},{8,10},{9,11},{10,... | collective-permute-start | bytes 1572872 | tf_op jit(solution)/shard_map/ppermute | solution.py:550
  34.0 10.3 %collective-permute-start.7 = (bf16[2048,128]{1,0:T(8,128)(2,1)}, bf16[2048,128]{1,0:T(8,128)(2,1)S(1)}, u32[]{:S(2)}, u32[]{:S(2)}) collective-permute-start(bf16[2048,128]{1,0:T(8,128)(2,1)} %encode.1.s0), channel_id=1, source_target_pairs={{0,6},{1,7},{2,0},{3,1},{4,2},{5,3},{6,4},{7,5},{8,14},{9,15},{10,... | collective-permute-start | bytes 1572872 | tf_op jit(solution)/shard_map/ppermute | solution.py:550
  36.5 92.2 %copy-start.1 = (bf16[4,2,144,1024]{3,2,1,0:T(8,128)(2,1)}, bf16[4,2,144,1024]{3,2,1,0:T(8,128)(2,1)S(1)}, u32[]{:S(2)}) copy-start(bf16[4,2,144,1024]{3,2,1,0:T(8,128)(2,1)S(1)} %pad_maximum_fusion.refs_0_) | copy-start | bytes 7077892
  36.5 52.5 %collective-permute-start.15 = (bf16[4,2,144,1024]{3,2,1,0:T(8,128)(2,1)S(1)}, bf16[4,2,144,1024]{3,2,1,0:T(8,128)(2,1)}, u32[]{:S(2)}, u32[]{:S(2)}) collective-permute-start(bf16[4,2,144,1024]{3,2,1,0:T(8,128)(2,1)S(1)} %pad_maximum_fusion.refs_0_), channel_id=1, source_target_pairs={{0,16},{8,24},{16,32},{24,40},{32,48},{40,56},{48,0},{56,8},{64,80... | collective-permute-start | bytes 7077896 | tf_op jit(solution)/shard_map/ppermute | solution.py:550
  36.6 52.4 %collective-permute-start.16 = (bf16[4,2,144,1024]{3,2,1,0:T(8,128)(2,1)S(1)}, bf16[4,2,144,1024]{3,2,1,0:T(8,128)(2,1)}, u32[]{:S(2)}, u32[]{:S(2)}) collective-permute-start(bf16[4,2,144,1024]{3,2,1,0:T(8,128)(2,1)S(1)} %pad_maximum_fusion.refs_0_), channel_id=1, source_target_pairs={{0,48},{8,56},{16,0},{24,8},{32,16},{40,24},{48,32},{56,40},{64,11... | collective-permute-start | bytes 7077896 | tf_op jit(solution)/shard_map/ppermute | solution.py:550
  43.1 21.9 %copy-start.3 = (bf16[2048,128]{1,0:T(8,128)(2,1)}, bf16[2048,128]{1,0:T(8,128)(2,1)S(1)}, u32[]{:S(2)}) copy-start(bf16[2048,128]{1,0:T(8,128)(2,1)S(1)} %collective-permute-done.5.s1) | copy-start | bytes 1572868
  43.1 21.9 %copy-start.6 = (bf16[2048,128]{1,0:T(8,128)(2,1)}, bf16[2048,128]{1,0:T(8,128)(2,1)S(1)}, u32[]{:S(2)}) copy-start(bf16[2048,128]{1,0:T(8,128)(2,1)S(1)} %collective-permute-done.6.s2) | copy-start | bytes 1572868
  44.3 21.5 %copy-start.7 = (bf16[2048,128]{1,0:T(8,128)(2,1)}, bf16[2048,128]{1,0:T(8,128)(2,1)S(1)}, u32[]{:S(2)}) copy-start(bf16[2048,128]{1,0:T(8,128)(2,1)S(1)} %collective-permute-done.7.s4) | copy-start | bytes 1572868
  44.4 84.3 %collective-permute-start.19 = (bf16[4,2,144,1024]{3,2,1,0:T(8,128)(2,1)S(1)}, bf16[4,2,144,1024]{3,2,1,0:T(8,128)(2,1)}, u32[]{:S(2)}, u32[]{:S(2)}) collective-permute-start(bf16[4,2,144,1024]{3,2,1,0:T(8,128)(2,1)S(1)} %pad_maximum_fusion.refs_0_), channel_id=1, source_target_pairs={{0,65},{1,64},{2,67},{3,66},{4,69},{5,68},{6,71},{7,70},{8,73},{9,... | collective-permute-start | bytes 7077896 | tf_op jit(solution)/shard_map/ppermute | solution.py:550
  44.6 17.5 %collective-permute-start.12 = (bf16[3072,128]{1,0:T(8,128)(2,1)S(1)}, bf16[3072,128]{1,0:T(8,128)(2,1)S(1)}, u32[]{:S(2)}, u32[]{:S(2)}) collective-permute-start(bf16[3072,128]{1,0:T(8,128)(2,1)S(1)} %get-tuple-element.73), channel_id=1, source_target_pairs={{0,2},{1,3},{2,4},{3,5},{4,6},{5,7},{6,0},{7,1},{8,10},{9,11},{10,... | collective-permute-start | bytes 2359304 | tf_op jit(solution)/shard_map/ppermute | solution.py:550
  47.6 16.4 %collective-permute-start.13 = (bf16[3072,128]{1,0:T(8,128)(2,1)S(1)}, bf16[3072,128]{1,0:T(8,128)(2,1)S(1)}, u32[]{:S(2)}, u32[]{:S(2)}) collective-permute-start(bf16[3072,128]{1,0:T(8,128)(2,1)S(1)} %get-tuple-element.72), channel_id=1, source_target_pairs={{0,6},{1,7},{2,0},{3,1},{4,2},{5,3},{6,4},{7,5},{8,14},{9,15},{10,... | collective-permute-start | bytes 2359304 | tf_op jit(solution)/shard_map/ppermute | solution.py:550
  62.0 0.9 copy-start.4
  64.0 0.9 copy-start.5
  65.8 14.1 %collective-permute-start.14 = (bf16[2048,128]{1,0:T(8,128)(2,1)}, bf16[2048,128]{1,0:T(8,128)(2,1)}, u32[]{:S(2)}, u32[]{:S(2)}) collective-permute-start(bf16[2048,128]{1,0:T(8,128)(2,1)} %pad_maximum_fusion.3.s6), channel_id=1, source_target_pairs={{0,1},{1,0},{2,3},{3,2},{4,5},{5,4},{6,7},{7,6},{8,9},{9,8},{10,11... | collective-permute-start | bytes 1572872 | tf_op jit(solution)/shard_map/ppermute | solution.py:550
  89.0 12.4 %collective-permute-start.17 = (bf16[1152,256]{1,0:T(8,128)(2,1)}, bf16[1152,256]{1,0:T(8,128)(2,1)}, u32[]{:S(2)}, u32[]{:S(2)}) collective-permute-start(bf16[1152,256]{1,0:T(8,128)(2,1)} %get-tuple-element.49), channel_id=1, source_target_pairs={{0,8},{8,16},{16,24},{24,32},{32,40},{40,48},{48,56},{56,64},{64,7... | collective-permute-start | bytes 1769480 | tf_op jit(solution)/shard_map/ppermute | solution.py:546
  94.3 15.1 %collective-permute-start.18 = (bf16[1152,256]{1,0:T(8,128)(2,1)}, bf16[1152,256]{1,0:T(8,128)(2,1)}, u32[]{:S(2)}, u32[]{:S(2)}) collective-permute-start(bf16[1152,256]{1,0:T(8,128)(2,1)} %get-tuple-element.51), channel_id=1, source_target_pairs={{8,0},{16,8},{24,16},{32,24},{40,32},{48,40},{56,48},{64,56},{72,6... | collective-permute-start | bytes 1769480 | tf_op jit(solution)/shard_map/ppermute | solution.py:546
  128.7 15.3 %collective-permute-start.20 = (bf16[4,2,144,1024]{3,2,1,0:T(8,128)(2,1)S(1)}, bf16[4,2,144,1024]{3,2,1,0:T(8,128)(2,1)}, u32[]{:S(2)}, u32[]{:S(2)}) collective-permute-start(bf16[4,2,144,1024]{3,2,1,0:T(8,128)(2,1)S(1)} %pad_maximum_fusion.refs_0_), channel_id=1, source_target_pairs={{0,8},{8,0},{16,24},{24,16},{32,40},{40,32},{48,56},{56,48},{64,72... | collective-permute-start | bytes 7077896 | tf_op jit(solution)/shard_map/ppermute | solution.py:550
  128.8 15.2 %collective-permute-start.21 = (bf16[4,2,144,1024]{3,2,1,0:T(8,128)(2,1)}, bf16[4,2,144,1024]{3,2,1,0:T(8,128)(2,1)}, u32[]{:S(2)}, u32[]{:S(2)}) collective-permute-start(bf16[4,2,144,1024]{3,2,1,0:T(8,128)(2,1)} %collective-permute-done.15.refs_1_), channel_id=1, source_target_pairs={{0,8},{8,0},{16,24},{24,16},{32,40},{40,32},{48,56},{56,48},{64,72... | collective-permute-start | bytes 7077896 | tf_op jit(solution)/shard_map/ppermute | solution.py:550
  129.3 14.7 %collective-permute-start.22 = (bf16[4,2,144,1024]{3,2,1,0:T(8,128)(2,1)}, bf16[4,2,144,1024]{3,2,1,0:T(8,128)(2,1)}, u32[]{:S(2)}, u32[]{:S(2)}) collective-permute-start(bf16[4,2,144,1024]{3,2,1,0:T(8,128)(2,1)} %collective-permute-done.16.refs_2_), channel_id=1, source_target_pairs={{0,8},{8,0},{16,24},{24,16},{32,40},{40,32},{48,56},{56,48},{64,72... | collective-permute-start | bytes 7077896 | tf_op jit(solution)/shard_map/ppermute | solution.py:550
  129.4 14.6 %collective-permute-start.23 = (bf16[4,2,144,1024]{3,2,1,0:T(8,128)(2,1)}, bf16[4,2,144,1024]{3,2,1,0:T(8,128)(2,1)}, u32[]{:S(2)}, u32[]{:S(2)}) collective-permute-start(bf16[4,2,144,1024]{3,2,1,0:T(8,128)(2,1)} %collective-permute-done.19.refs_3_), channel_id=1, source_target_pairs={{0,8},{8,0},{16,24},{24,16},{32,40},{40,32},{48,56},{56,48},{64,72... | collective-permute-start | bytes 7077896 | tf_op jit(solution)/shard_map/ppermute | solution.py:550
  129.8 14.2 %all-to-all-start = ((bf16[8,256,128]{2,1,0:T(8,128)(2,1)}), bf16[8,256,128]{2,1,0:T(8,128)(2,1)}, u32[]{:S(2)}, u32[]{:S(2)}) async-start(bf16[8,256,128]{2,1,0:T(8,128)(2,1)} %bitcast.49), calls=%async_computation | async-start | bytes 1048576 | tf_op jit(solution)/shard_map/all_to_all | solution.py:637
  144.0 31.7 %copy-start.14 = (s32[64,2]{0,1:T(2,128)S(1)}, s32[64,2]{0,1:T(2,128)}, u32[]{:S(2)}) copy-start(s32[64,2]{0,1:T(2,128)} %param.21) | copy-start | bytes 1540
  169.8 14.7 %copy-start.2 = (bf16[8,256,128]{2,1,0:T(8,128)(2,1)}, bf16[8,256,128]{2,1,0:T(8,128)(2,1)S(1)}, u32[]{:S(2)}) copy-start(bf16[8,256,128]{2,1,0:T(8,128)(2,1)S(1)} %all_to_all.15) | copy-start | bytes 1572868
  169.8 6.6 %collective-permute-start.24 = (bf16[8,128,128]{2,1,0:T(8,128)(2,1)S(1)}, bf16[8,128,128]{2,1,0:T(8,128)(2,1)S(1)}, u32[]{:S(2)}, u32[]{:S(2)}) collective-permute-start(bf16[8,128,128]{2,1,0:T(8,128)(2,1)S(1)} %bitcast.62), channel_id=1, source_target_pairs={{0,8},{8,16},{16,24},{24,32},{32,40},{40,48},{48,56},{56,64},{64,7... | collective-permute-start | bytes 786440 | tf_op jit(solution)/shard_map/ppermute | solution.py:546
  173.1 11.3 %collective-permute-start.25 = (bf16[8,128,128]{2,1,0:T(8,128)(2,1)S(1)}, bf16[8,128,128]{2,1,0:T(8,128)(2,1)S(1)}, u32[]{:S(2)}, u32[]{:S(2)}) collective-permute-start(bf16[8,128,128]{2,1,0:T(8,128)(2,1)S(1)} %bitcast.61), channel_id=1, source_target_pairs={{8,0},{16,8},{24,16},{32,24},{40,32},{48,40},{56,48},{64,56},{72,6... | collective-permute-start | bytes 786440 | tf_op jit(solution)/shard_map/ppermute | solution.py:546
  176.5 8.0 %copy-start.11 = (bf16[8,128,128]{2,1,0:T(8,128)(2,1)}, bf16[8,128,128]{2,1,0:T(8,128)(2,1)S(1)}, u32[]{:S(2)}) copy-start(bf16[8,128,128]{2,1,0:T(8,128)(2,1)S(1)} %collective-permute-done.24.low) | copy-start | bytes 786436
  184.4 0.7 copy-start.12
